TPU v7x, 32 devices: a whole 2x2x4 slice. The times are simulated.
32 devices in a mesh: tile: 8 (over z, y), rep: 4 (over x, core).
Axes of the slice: x: 2, y: 2, z: 4, core: 2. Of those that a mesh axis runs over, the one named last changes fastest.
Arguments:
- inputs: bfloat16 [4, 32, 64, 4, 8, 128], P('rep', 'tile'), may hold values from -20 to 20
- w_spatial: bfloat16 [9, 64, 64], replicated, may hold values from -0.25 to 0.25
- w_temporal: bfloat16 [2, 3, 64, 64], replicated, may hold values from -0.4375 to 0.4375
- w_head: bfloat16 [64], replicated, may hold values from -0.75 to 0.75
- targets: bfloat16 [4, 32, 4096], P('rep', None, 'tile'), may hold values from 0 to 1
- valid: int32 [4, 32], P('rep'), may hold values 0 or 1
Outputs:
- logits: bfloat16 [4, 32, 4096], P('rep', None, 'tile')
- grad_inputs: bfloat16 [4, 32, 64, 4, 8, 128], P('rep', 'tile')
- grad_spatial: float32 [9, 64, 64], P(None, 'rep')
- grad_temporal: float32 [2, 3, 64, 64], P(None, None, 'rep')
- grad_head: float32 [64], P('rep')
All inputs are finite; a program needn't handle non-finite values. No bound on the sum of `valid` on one device may be relied on, other than what follows from the above.
Results may differ from a plain program's by a relative error of at most 0.024.
Values may be sent and summed in bfloat16 or wider, within the bound.
No kernel may reach another device: no remote copies, remote signals or barrier semaphores. Data moves between devices by JAX's collectives and lax.ppermute only.
A program may use at most 128 MiB of HBM per device.

v0:
```python
import functools

import jax
import jax.numpy as jnp
from jax import lax
from jax.experimental import pallas as pl
from jax.experimental.pallas import tpu as pltpu
from jax.sharding import PartitionSpec as P

EPS = 1e-06
HALO = 6
F32 = jnp.float32
BF16 = jnp.bfloat16


def sigmoid(u):
    return 0.5 * jnp.tanh(0.5 * u) + 0.5


def dot_nn(a, b):
    return jnp.dot(a, b, preferred_element_type=F32)


def dot_nt(a, b):
    return lax.dot_general(a, b, (((1,), (1,)), ((), ())), preferred_element_type=F32)


def channel_sum(v):
    return jnp.sum(v, axis=0, keepdims=True)


def layer_kernel(
    dims,
    meta_ref,
    weight_ref,
    x_ref,
    wf_ref,
    wb_ref,
    wt_ref,
    wtb_ref,
    wh_ref,
    whc_ref,
    tgt_ref,
    logit_ref,
    dx_ref,
    gs_ref,
    gt_ref,
    gh_ref,
    xt,
    xs,
    xtmp,
    ds,
    feats,
    spre,
    n0,
    inv0,
    h1,
    n1,
    inv1,
    sp0,
    dh2,
    dm1,
    dm0,
):
    own, chans, rows, width, total = dims
    vox = rows * width
    step = 2 * width
    lo, hi = HALO, HALO + own
    first = meta_ref[0]
    lane = lax.broadcasted_iota(jnp.int32, (chans, width), 1)
    not_first = (lane > 0).astype(F32)
    not_last = (lane < width - 1).astype(F32)

    def frame_ok(f):
        g = first + f - HALO
        return jnp.where((g >= 0) & (g < total), 1.0, 0.0).astype(F32)

    def spread(row, dst, r, order):
        prev = pltpu.roll(row, 1, 1) * not_first
        nxt = pltpu.roll(row, width - 1, 1) * not_last
        parts = (prev, row, nxt) if order > 0 else (nxt, row, prev)
        for j in range(3):
            dst[j * chans : (j + 1) * chans, r * width : (r + 1) * width] = parts[j].astype(BF16)

    def conv(w_ref, src, sign):
        outs = [dot_nn(w_ref[...], src[:, p * step : (p + 1) * step]) for p in range(vox // step)]

        def piece(i, r):
            block = outs[r // 2]
            return block[i * chans : (i + 1) * chans, (r % 2) * width : (r % 2 + 1) * width]

        result = []
        for r in range(rows):
            acc = piece(1, r)
            for i in (-1, 1):
                rr = r + sign * i
                if 0 <= rr < rows:
                    acc = acc + piece(i + 1, rr)
            result.append(acc)
        return result

    def forward(f, keep):
        xt[...] = x_ref[f].astype(F32)
        dst = xs.at[f - HALO] if keep else xtmp
        for r in range(rows):
            spread(xt[pl.ds(r, chans, stride=rows), :], dst, r, 1)
        pre_rows = conv(wf_ref, dst, 1)
        for r in range(rows):
            cols = slice(r * width, (r + 1) * width)
            pre = pre_rows[r]
            s = sigmoid(pre)
            y = pre * s
            feat = y.astype(BF16)
            feats[f, :, cols] = feat
            if keep:
                spre[f - HALO, :, cols] = s + y * (1.0 - s)
            hid = feat.astype(F32)
            inv = lax.rsqrt(channel_sum(hid * hid) * (1.0 / chans) + EPS)
            n0[f, :, cols] = (hid * inv).astype(BF16)
            if keep:
                inv0[f - HALO, :, cols] = inv

    def loop(a, b, fn):
        lax.fori_loop(a, b, lambda f, c: (fn(f), c)[1], 0)

    loop(0, lo, lambda f: forward(f, False))
    loop(lo, hi, lambda f: forward(f, True))
    loop(hi, hi + HALO, lambda f: forward(f, False))

    def stack(ref, f0, f1, f2, cols):
        return jnp.concatenate([ref[f0, :, cols], ref[f1, :, cols], ref[f2, :, cols]], axis=0)

    chunks = [slice(p * step, (p + 1) * step) for p in range(vox // step)]

    def layer0(f):
        ok = frame_ok(f)
        for cols in chunks:
            mixed = dot_nn(wt_ref[0], stack(n0, f - 1, f, f + 1, cols))
            s = sigmoid(mixed)
            y = mixed * s
            hid = feats[f, :, cols].astype(F32) + y
            inv = lax.rsqrt(channel_sum(hid * hid) * (1.0 / chans) + EPS) * ok
            h1[f, :, cols] = hid
            n1[f, :, cols] = (hid * inv).astype(BF16)
            inv1[f, :, cols] = inv
            sp0[f, :, cols] = s + y * (1.0 - s)

    loop(1, hi + HALO - 1, layer0)

    gh_ref[...] = jnp.zeros_like(gh_ref)
    gt_ref[...] = jnp.zeros_like(gt_ref)
    gs_ref[...] = jnp.zeros_like(gs_ref)

    def layer1(f):
        weight = weight_ref[f - 3]
        mine = jnp.where((f >= lo) & (f < hi), 1.0, 0.0).astype(F32)
        for cols in chunks:
            mixed = dot_nn(wt_ref[1], stack(n1, f - 2, f, f + 2, cols))
            s = sigmoid(mixed)
            y = mixed * s
            hid = h1[f, :, cols] + y
            inv = lax.rsqrt(channel_sum(hid * hid) * (1.0 / chans) + EPS)
            unit = hid * inv
            final = unit.astype(BF16)
            logit = dot_nn(wh_ref[...], final)[0:1]
            logit_ref[f - 3, :, cols] = logit
            dlogit = weight * (sigmoid(logit) - tgt_ref[f - 3, :, cols].astype(F32))
            gh_ref[...] += dot_nt(jnp.broadcast_to((dlogit * mine).astype(BF16), (16, step)), final)
            dhid = (inv * dlogit) * (whc_ref[...] - unit * (logit * (1.0 / chans)))
            dh2[f, :, cols] = dhid
            dm1[f, :, cols] = (dhid * (s + y * (1.0 - s))).astype(BF16)

    loop(3, hi + 3, layer1)

    def back1(f):
        ok = frame_ok(f)
        for cols in chunks:
            dnorm = dot_nn(wtb_ref[1], stack(dm1, f + 2, f, f - 2, cols))
            unit = n1[f, :, cols].astype(F32)
            mean = channel_sum(dnorm * unit) * (1.0 / chans)
            dhid = dh2[f, :, cols] + inv1[f, :, cols] * (dnorm - unit * mean)
            dh2[f, :, cols] = dhid
            dm0[f, :, cols] = (dhid * (sp0[f, :, cols] * ok)).astype(BF16)

    loop(lo - 1, hi + 1, back1)

    def back0(f):
        b = f - HALO
        for p, cols in enumerate(chunks):
            near0 = stack(dm0, f + 1, f, f - 1, cols)
            dnorm = dot_nn(wtb_ref[0], near0)
            unit = n0[f, :, cols].astype(F32)
            mean = channel_sum(dnorm * unit) * (1.0 / chans)
            dhid = dh2[f, :, cols] + inv0[b, :, cols] * (dnorm - unit * mean)
            dfeat = dhid.astype(BF16).astype(F32)
            dpre = (dfeat * spre[b, :, cols]).astype(BF16).astype(F32)
            for r in range(2):
                spread(dpre[:, r * width : (r + 1) * width], ds, 2 * p + r, -1)
        dx_rows = conv(wb_ref, ds, -1)
        for r in range(rows):
            xt[pl.ds(r, chans, stride=rows), :] = dx_rows[r]
        dx_ref[b] = xt[...].astype(BF16)
        center = ds[chans : 2 * chans, :]
        blank = jnp.zeros((chans, width), BF16)
        taller = jnp.concatenate([center[:, width:], blank], axis=1)
        lower = jnp.concatenate([blank, center[:, :-width]], axis=1)
        gs_ref[...] += dot_nt(jnp.concatenate([taller, center, lower], axis=0), xs[b])
        every = slice(0, vox)
        gt_ref[0] += dot_nt(dm0[f], stack(n0, f - 1, f, f + 1, every))
        gt_ref[1] += dot_nt(dm1[f], stack(n1, f - 2, f, f + 2, every))

    loop(lo, hi, back0)


def run_layer(meta, weights, x, wf, wb, wt, wtb, wh, whc, tgt, dims):
    own, chans, rows, width, total = dims
    vox = rows * width
    every = own + 2 * HALO
    sds = jax.ShapeDtypeStruct
    smem = pl.BlockSpec(memory_space=pltpu.SMEM)
    vmem = pl.BlockSpec(memory_space=pltpu.VMEM)
    return pl.pallas_call(
        functools.partial(layer_kernel, dims),
        name="block",
        out_shape=(
            sds((own + 6, 1, vox), F32),
            sds((own, chans * rows, width), BF16),
            sds((3 * chans, 3 * chans), F32),
            sds((2, chans, 3 * chans), F32),
            sds((16, chans), F32),
        ),
        in_specs=[smem, smem] + [vmem] * 8,
        out_specs=[vmem] * 5,
        scratch_shapes=[
            pltpu.VMEM((chans * rows, width), F32),
            pltpu.VMEM((own, 3 * chans, vox), BF16),
            pltpu.VMEM((3 * chans, vox), BF16),
            pltpu.VMEM((3 * chans, vox), BF16),
            pltpu.VMEM((every, chans, vox), BF16),
            pltpu.VMEM((own, chans, vox), F32),
            pltpu.VMEM((every, chans, vox), BF16),
            pltpu.VMEM((own, 1, vox), F32),
            pltpu.VMEM((every, chans, vox), F32),
            pltpu.VMEM((every, chans, vox), BF16),
            pltpu.VMEM((every, 1, vox), F32),
            pltpu.VMEM((every, chans, vox), F32),
            pltpu.VMEM((every, chans, vox), F32),
            pltpu.VMEM((every, chans, vox), BF16),
            pltpu.VMEM((every, chans, vox), BF16),
        ],
        compiler_params=pltpu.CompilerParams(vmem_limit_bytes=56 * 1024 * 1024),
        cost_estimate=pl.CostEstimate(
            flops=4_000_000_000, bytes_accessed=6_000_000, transcendentals=1_000_000
        ),
    )(meta, weights, x, wf, wb, wt, wtb, wh, whc, tgt)


def group_size(tiles, frames_here, layers):
    for g in range(1, layers + 1):
        if layers % g == 0 and tiles % g == 0 and g * frames_here >= HALO:
            return g
    return layers


def pick(parts, start):
    doubled = jnp.stack(parts + parts)
    return lax.dynamic_slice_in_dim(doubled, start, len(parts), 0)


def body(inputs, w_spatial, w_temporal, w_head, targets, valid):
    _, here, chans, layers, rows, width = inputs.shape
    tiles = lax.axis_size("tile")
    total = here * tiles
    g = group_size(tiles, here, layers)
    per = layers // g
    own = g * here
    groups = tiles // g
    vox = rows * width
    t = lax.axis_index("tile")
    q, m = t // g, t % g
    spot = targets.shape[2]
    share = tiles // g
    x = inputs[0].reshape(here, chans, layers, rows * width)
    x = x.reshape(here, chans, g, per, rows, width)

    def swap(value, s):
        pairs = [(a, a // g * g + (a % g + s) % g) for a in range(tiles)]
        return lax.ppermute(value, "tile", pairs)

    def hop(value, d):
        pairs = [(a, a + d * g) for a in range(tiles) if 0 <= a + d * g < tiles]
        return lax.ppermute(value, "tile", pairs)

    def of_member(k):
        return lax.dynamic_index_in_dim(x, k % g, 2, False)

    w9 = w_spatial.reshape(3, 3, chans, chans)
    wf = w9.transpose(0, 2, 1, 3).reshape(3 * chans, 3 * chans)
    wb = w9.transpose(0, 3, 1, 2).reshape(3 * chans, 3 * chans)
    wt = w_temporal.transpose(0, 2, 1, 3).reshape(2, chans, 3 * chans)
    wtb = w_temporal.transpose(0, 3, 1, 2).reshape(2, chans, 3 * chans)
    wh = jnp.broadcast_to(w_head[None, :], (16, chans))
    whc = w_head.astype(F32)[:, None]

    around = lax.all_gather(targets[0], "tile", axis=0, tiled=False)
    mine = lax.dynamic_slice_in_dim(around, m * share, share, 0)
    mine = mine.transpose(1, 0, 2).reshape(total, per, vox)
    mine = jnp.pad(mine, ((3, 3), (0, 0), (0, 0)))
    mine = lax.dynamic_slice_in_dim(mine, q * own, own + 6, 0)
    frame_weight = jnp.pad(valid[0].astype(F32) / total, (3, 3))
    frame_weight = lax.dynamic_slice_in_dim(frame_weight, q * own, own + 6, 0)
    meta = (q * own)[None].astype(jnp.int32)

    dims = (own, chans, rows, width, total)
    results = []
    for layer in range(per):
        pieces = [of_member(m)[:, :, layer]]
        for s in range(1, g):
            pieces.append(swap(of_member(m + s)[:, :, layer], s))
        block = pick(pieces[::-1], g - 1 - m).reshape(own, chans, rows, width)
        before, after = [], []
        left = HALO
        d = 1
        while left > 0:
            n = min(left, own)
            before.insert(0, hop(block[own - n :], d))
            after.append(hop(block[:n], -d))
            left -= n
            d += 1
        full = jnp.concatenate(before + [block] + after, axis=0)
        full = full.reshape(own + 2 * HALO, chans * rows, width)
        results.append(
            run_layer(
                meta, frame_weight, full, wf, wb, wt, wtb, wh, whc, mine[:, layer][:, None], dims
            )
        )

    back = []
    for layer in range(per):
        dx = results[layer][1].reshape(g, here, chans, rows, width)
        parts = [lax.dynamic_index_in_dim(dx, m, 0, False)]
        for s in range(1, g):
            parts.append(swap(lax.dynamic_index_in_dim(dx, (m - s) % g, 0, False), -s))
        back.append(pick(parts, (g - m) % g))
    grad = jnp.stack(back, axis=3)
    grad = grad.transpose(1, 2, 0, 3, 4, 5).reshape(1, here, chans, layers, rows, width)

    logits = jnp.concatenate([r[0][3 : 3 + own, 0] for r in results], axis=1).astype(BF16)
    logits = lax.all_gather(logits, "tile", axis=0, tiled=False)
    logits = logits.reshape(groups, g, own, share, spot)
    logits = lax.dynamic_index_in_dim(logits, t // share, 1, False)
    logits = lax.dynamic_index_in_dim(logits, t % share, 2, False)
    logits = logits.reshape(1, total, spot)

    gs = sum(r[2] for r in results).reshape(3, chans, 3, chans).transpose(1, 0, 2, 3)
    gt = sum(r[3] for r in results).reshape(2, chans, 3, chans).transpose(1, 0, 2, 3)
    gh = sum(r[4] for r in results)[0][:, None]
    flat = jnp.concatenate([gs.reshape(chans, -1), gt.reshape(chans, -1), gh], axis=1)
    flat = lax.psum_scatter(flat.astype(BF16), "rep", scatter_dimension=0, tiled=True)
    flat = lax.psum(flat, "tile").astype(F32)
    part = flat.shape[0]
    gs = flat[:, : 9 * chans].reshape(part, 9, chans).transpose(1, 0, 2)
    gt = flat[:, 9 * chans : 15 * chans].reshape(part, 2, 3, chans).transpose(1, 2, 0, 3)
    return logits, grad, gs, gt, flat[:, 15 * chans]


def solution(mesh):
    placed = (
        P("rep", "tile", None, None, None, None),
        P(),
        P(),
        P(),
        P("rep", None, "tile"),
        P("rep", None),
    )
    return jax.shard_map(
        body,
        mesh=mesh,
        in_specs=placed,
        out_specs=(
            P("rep", None, "tile"),
            P("rep", "tile", None, None, None, None),
            P(None, "rep", None),
            P(None, None, "rep", None),
            P("rep"),
        ),
        check_vma=False,
    )
```

profile of v0, /device:TPU:0, one launch (start us, length us, event | category | flops | bytes accessed | tf_op | source)
XLA Modules:
  0.0 273.7 jit_solution(12926544035694314633)
XLA Ops:
  7.2 0.0 reduce-scatter.4.cloned.1.call-start
  7.3 1.9 constant_dynamic-slice_fusion.2
  9.2 0.0 copy-start.5
  9.2 0.2 copy.91
  9.4 1.1 slice_bitcast_fusion.3
  10.5 3.0 %collective-permute-start = (bf16[4,64,8,128]{3,2,1,0:T(8,128)(2,1)}, bf16[4,64,8,128]{3,2,1,0:T(8,128)(2,1)S(1)}, u32[]{:S(2)}, u32[]{:S(2)}) collective-permute-start(bf16[4,64,8,128]{3,2,1,0:T(8,128)(2,1)} %get-tuple-element.50), channel_id=1, source_target_pairs={{0,4},{4,0},{8,12},{12,8},{16,20},{20,16},{24,28},{28,24},{1,5},{5... | collective-permute-start | bytes 1572872 | tf_op jit(solution)/shard_map/ppermute | solution.py:288
  13.4 0.0 collective-permute-start.3
  13.5 48.3 %all_gather.7 = bf16[8,32,512]{2,1,0:T(8,128)(2,1)S(1)} all-gather(bf16[1,32,512]{2,1,0:T(8,128)(2,1)S(1)} %copy-done.5), channel_id=1, replica_groups=mesh['tile'=8,'rep'=4] {'tile'}, dimensions={0}, use_global_device_ids=true | all-gather | bytes 294912 | tf_op jit(solution)/shard_map/all_gather | solution.py:305
  61.8 0.2 copy.90
  62.0 0.5 bitcast_convert_fusion
  62.5 0.1 slice_bitcast_fusion.2
  62.6 2.5 fusion.10
  65.1 0.0 copy-start
  65.2 1.4 fusion.16
  66.5 1.3 collective-permute-start.1
  67.9 1.3 collective-permute-start.2
  69.3 0.2 copy.62
  69.4 0.1 copy.92
  69.6 1.4 copy.67.whc_ref
  71.0 1.6 copy.66.wtb_ref
  72.6 1.0 copy.63
  73.6 0.7 copy.65.wt_ref
  74.3 0.8 reshape.124.wb_ref
  75.1 0.8 reshape.123.wf_ref
  75.9 0.1 copy.64
  76.0 0.1 reshape.127
  76.1 0.8 pad_dynamic-slice_fusion.16
  76.9 0.7 multiply_bitcast_fusion
  77.6 0.2 fusion.17
  77.8 4.6 %collective-permute-start.4 = (bf16[6,64,8,128]{3,2,1,0:T(8,128)(2,1)S(1)}, bf16[6,64,8,128]{3,2,1,0:T(8,128)(2,1)S(1)}, u32[]{:S(2)}, u32[]{:S(2)}) collective-permute-start(bf16[6,64,8,128]{3,2,1,0:T(8,128)(2,1)S(1)} %get-tuple-element.52), channel_id=1, source_target_pairs={{0,8},{4,12},{8,16},{12,20},{16,24},{20,28},{1,9},{5,13},{9,17},{1... | collective-permute-start | bytes 2359304 | tf_op jit(solution)/shard_map/ppermute | solution.py:292
  82.4 1.5 collective-permute-start.5
  83.9 0.6 pad_dynamic-slice_fusion.18.weight_ref
  84.5 2.1 collective-permute-done.2
  86.7 2.9 %pad_maximum_fusion.x_ref = bf16[20,512,128]{2,1,0:T(8,128)(2,1)} fusion(bf16[6,512,128]{2,1,0:T(8,128)(2,1)} %bitcast.12, bf16[8,512,128]{2,1,0:T(8,128)(2,1)S(1)} %bitcast.88, bf16[6,512,128]{2,1,0:T(8,128)(2,1)S(1)} %bitcast.96), kind=kLoop, calls=%fused_computation | loop fusion | flops 2621440 | bytes 5242880 | tf_op jit(solution)/shard_map/concatenate | solution.py:330
  89.6 0.6 broadcast_in_dim.15.wh_ref
  90.2 41.3 %block.2 = (f32[14,1,1024]{2,1,0:T(1,128)}, bf16[8,512,128]{2,1,0:T(8,128)(2,1)}, f32[192,192]{1,0:T(8,128)}, f32[2,64,192]{2,1,0:T(8,128)}, f32[16,64]{1,0:T(8,128)}) custom-call(s32[1]{0:T(128)} %bitcast.1.meta_ref, f32[14]{0:T(128)} %pad_dynamic-slice_fusion.18.weight_ref, bf16[20,512,128]{2,1,0:T(8,128)(2,1)} %pad_maximum_fusion.x_ref, ...), custom_call_target="tpu_custom_call" | custom-call | flops 4000000000 | bytes 6000000 | tf_op jit(solution)/shard_map/block/pallas_call | solution.py:222
  131.5 0.8 slice.96
  132.3 1.3 dynamic-slice_bitcast_fusion.1
  133.6 0.2 collective-permute-start.6
  133.8 1.8 pad_maximum_fusion.1.x_ref
  135.5 41.3 %block.3 = (f32[14,1,1024]{2,1,0:T(1,128)}, bf16[8,512,128]{2,1,0:T(8,128)(2,1)}, f32[192,192]{1,0:T(8,128)}, f32[2,64,192]{2,1,0:T(8,128)}, f32[16,64]{1,0:T(8,128)}) custom-call(s32[1]{0:T(128)} %bitcast.1.meta_ref, f32[14]{0:T(128)} %pad_dynamic-slice_fusion.18.weight_ref, bf16[20,512,128]{2,1,0:T(8,128)(2,1)} %pad_maximum_fusion.1.x_ref, ...), custom_call_target="tpu_custom_call" | custom-call | flops 4000000000 | bytes 6000000 | tf_op jit(solution)/shard_map/block/pallas_call | solution.py:222
  176.9 0.8 slice.95
  177.7 2.1 dynamic-slice_bitcast_fusion
  179.8 0.1 copy.73
  180.0 0.1 reshape.134
  180.1 0.2 copy.72
  180.3 0.7 fusion.15
  181.0 0.1 pad_maximum_fusion.2
  181.1 0.8 copy.78
  181.9 0.0 reduce-scatter.4.cloned.1.call-update
  181.9 1.9 collective-permute-start.7
  183.8 36.1 %all_gather.8 = bf16[8,8,2048]{2,1,0:T(8,128)(2,1)S(1)} all-gather(bf16[1,8,2048]{2,1,0:T(8,128)(2,1)S(1)} %pad_maximum_fusion.3), channel_id=1, replica_groups=mesh['tile'=8,'rep'=4] {'tile'}, dimensions={0}, use_global_device_ids=true | all-gather | bytes 294912 | tf_op jit(solution)/shard_map/all_gather | solution.py:349
  219.9 0.6 dynamic-slice_bitcast_fusion.3
  220.6 0.9 copy.79
  221.5 38.3 %psum.7 = bf16[16,961]{0,1:T(8,128)(2,1)S(1)} all-reduce(bf16[16,961]{0,1:T(8,128)(2,1)S(1)} %copy.79), channel_id=1, replica_groups=mesh['tile'=8,'rep'=4] {'tile'}, use_global_device_ids=true, to_apply=%region_1.2 | all-reduce | flops 15376 | bytes 61504 | tf_op jit(solution)/shard_map/psum | solution.py:360
  259.9 0.8 convert_element_type.22
  260.7 0.1 copy.82
  260.8 0.6 copy.77
  261.5 0.8 copy.76
  262.2 1.2 slice_bitcast_fusion.4
  263.4 0.7 fusion.7
  264.2 0.7 fusion.3
  264.9 0.2 maximum_bitcast_fusion
  265.1 1.7 copy.71
  (30 shorter events, 0.2 us)
Async XLA Ops:
  7.2 213.4 %reduce-scatter.4.cloned.1.call-start = ((), (), s32[]{:S(2)}) async-start(), calls=%async_computation.1 | async-start | bytes 163840
  9.2 4.3 %copy-start.5 = (bf16[1,32,512]{2,1,0:T(8,128)(2,1)S(1)}, bf16[1,32,512]{2,1,0:T(8,128)(2,1)}, u32[]{:S(2)}) copy-start(bf16[1,32,512]{2,1,0:T(8,128)(2,1)} %param.10) | copy-start | bytes 98308
  9.4 52.6 %copy-start.6 = (bf16[64]{0:T(256)(128)(2,1)S(1)}, bf16[64]{0:T(256)(128)(2,1)}, u32[]{:S(2)}) copy-start(bf16[64]{0:T(256)(128)(2,1)} %param.9) | copy-start | bytes 388
  10.5 52.1 %collective-permute-start = (bf16[4,64,8,128]{3,2,1,0:T(8,128)(2,1)}, bf16[4,64,8,128]{3,2,1,0:T(8,128)(2,1)S(1)}, u32[]{:S(2)}, u32[]{:S(2)}) collective-permute-start(bf16[4,64,8,128]{3,2,1,0:T(8,128)(2,1)} %get-tuple-element.50), channel_id=1, source_target_pairs={{0,4},{4,0},{8,12},{12,8},{16,20},{20,16},{24,28},{28,24},{1,5},{5... | collective-permute-start | bytes 1572872 | tf_op jit(solution)/shard_map/ppermute | solution.py:288
  13.4 49.2 %collective-permute-start.3 = (bf16[4,64,8,128]{3,2,1,0:T(8,128)(2,1)}, bf16[4,64,8,128]{3,2,1,0:T(8,128)(2,1)}, u32[]{:S(2)}, u32[]{:S(2)}) collective-permute-start(bf16[4,64,8,128]{3,2,1,0:T(8,128)(2,1)} %get-tuple-element.51), channel_id=1, source_target_pairs={{0,4},{4,0},{8,12},{12,8},{16,20},{20,16},{24,28},{28,24},{1,5},{5... | collective-permute-start | bytes 1572872 | tf_op jit(solution)/shard_map/ppermute | solution.py:288
  65.1 4.1 %copy-start = (bf16[9,64,64]{2,1,0:T(8,128)(2,1)S(1)}, bf16[9,64,64]{2,1,0:T(8,128)(2,1)}, u32[]{:S(2)}) copy-start(bf16[9,64,64]{2,1,0:T(8,128)(2,1)} %param.7) | copy-start | bytes 221188
  66.5 18.0 %collective-permute-start.1 = (bf16[6,64,8,128]{3,2,1,0:T(8,128)(2,1)}, bf16[6,64,8,128]{3,2,1,0:T(8,128)(2,1)S(1)}, u32[]{:S(2)}, u32[]{:S(2)}) collective-permute-start(bf16[6,64,8,128]{3,2,1,0:T(8,128)(2,1)} %get-tuple-element.46), channel_id=1, source_target_pairs={{0,8},{4,12},{8,16},{12,20},{16,24},{20,28},{1,9},{5,13},{9,17},{1... | collective-permute-start | bytes 2359304 | tf_op jit(solution)/shard_map/ppermute | solution.py:292
  67.9 18.8 %collective-permute-start.2 = (bf16[6,64,8,128]{3,2,1,0:T(8,128)(2,1)}, bf16[6,64,8,128]{3,2,1,0:T(8,128)(2,1)}, u32[]{:S(2)}, u32[]{:S(2)}) collective-permute-start(bf16[6,64,8,128]{3,2,1,0:T(8,128)(2,1)} %get-tuple-element.47), channel_id=1, source_target_pairs={{8,0},{12,4},{16,8},{20,12},{24,16},{28,20},{9,1},{13,5},{17,9},{2... | collective-permute-start | bytes 2359304 | tf_op jit(solution)/shard_map/ppermute | solution.py:292
  77.8 55.9 %collective-permute-start.4 = (bf16[6,64,8,128]{3,2,1,0:T(8,128)(2,1)S(1)}, bf16[6,64,8,128]{3,2,1,0:T(8,128)(2,1)S(1)}, u32[]{:S(2)}, u32[]{:S(2)}) collective-permute-start(bf16[6,64,8,128]{3,2,1,0:T(8,128)(2,1)S(1)} %get-tuple-element.52), channel_id=1, source_target_pairs={{0,8},{4,12},{8,16},{12,20},{16,24},{20,28},{1,9},{5,13},{9,17},{1... | collective-permute-start | bytes 2359304 | tf_op jit(solution)/shard_map/ppermute | solution.py:292
  82.4 51.3 %collective-permute-start.5 = (bf16[6,64,8,128]{3,2,1,0:T(8,128)(2,1)S(1)}, bf16[6,64,8,128]{3,2,1,0:T(8,128)(2,1)S(1)}, u32[]{:S(2)}, u32[]{:S(2)}) collective-permute-start(bf16[6,64,8,128]{3,2,1,0:T(8,128)(2,1)S(1)} %get-tuple-element.53), channel_id=1, source_target_pairs={{8,0},{12,4},{16,8},{20,12},{24,16},{28,20},{9,1},{13,5},{17,9},{2... | collective-permute-start | bytes 2359304 | tf_op jit(solution)/shard_map/ppermute | solution.py:292
  86.7 2.9 %copy-start.7 = (bf16[64]{0:T(256)(128)(2,1)S(1)}, bf16[64]{0:T(256)(128)(2,1)}, u32[]{:S(2)}) copy-start(bf16[64]{0:T(256)(128)(2,1)} %param.9) | copy-start | bytes 388
  133.6 129.9 %collective-permute-start.6 = (bf16[4,64,8,128]{3,2,1,0:T(8,128)(2,1)S(1)}, bf16[4,64,8,128]{3,2,1,0:T(8,128)(2,1)S(1)}, u32[]{:S(2)}, u32[]{:S(2)}) collective-permute-start(bf16[4,64,8,128]{3,2,1,0:T(8,128)(2,1)S(1)} %get-tuple-element.42), channel_id=1, source_target_pairs={{0,4},{4,0},{8,12},{12,8},{16,20},{20,16},{24,28},{28,24},{1,5},{5... | collective-permute-start | bytes 1572872 | tf_op jit(solution)/shard_map/ppermute | solution.py:288
  176.8 3.0 %copy-start.3 = (f32[2,64,192]{2,1,0:T(8,128)S(1)}, f32[2,64,192]{2,1,0:T(8,128)}, u32[]{:S(2)}) copy-start(f32[2,64,192]{2,1,0:T(8,128)} %get-tuple-element.21) | copy-start | bytes 294916
  176.8 3.0 %copy-start.4 = (f32[2,64,192]{2,1,0:T(8,128)S(1)}, f32[2,64,192]{2,1,0:T(8,128)}, u32[]{:S(2)}) copy-start(f32[2,64,192]{2,1,0:T(8,128)} %get-tuple-element.22) | copy-start | bytes 294916
  176.8 3.1 %copy-start.1 = (f32[192,192]{1,0:T(8,128)S(1)}, f32[192,192]{1,0:T(8,128)}, u32[]{:S(2)}) copy-start(f32[192,192]{1,0:T(8,128)} %get-tuple-element.19) | copy-start | bytes 442372
  176.9 3.1 %copy-start.2 = (f32[192,192]{1,0:T(8,128)S(1)}, f32[192,192]{1,0:T(8,128)}, u32[]{:S(2)}) copy-start(f32[192,192]{1,0:T(8,128)} %get-tuple-element.20) | copy-start | bytes 442372
  181.9 82.3 %collective-permute-start.7 = (bf16[4,64,8,128]{3,2,1,0:T(8,128)(2,1)}, bf16[4,64,8,128]{3,2,1,0:T(8,128)(2,1)S(1)}, u32[]{:S(2)}, u32[]{:S(2)}) collective-permute-start(bf16[4,64,8,128]{3,2,1,0:T(8,128)(2,1)} %get-tuple-element.44), channel_id=1, source_target_pairs={{0,4},{4,0},{8,12},{12,8},{16,20},{20,16},{24,28},{28,24},{1,5},{5... | collective-permute-start | bytes 1572872 | tf_op jit(solution)/shard_map/ppermute | solution.py:288
Sparse Core Ops, SparseCore 0:
  182.0 23.1 reduce-scatter.3
where the time goes:
time: 274 us
  blocking collectives  123 us (45%)
  Pallas kernels  82.5 us (30%)
  local copies, waits for them, and re-layouts  26.1 us (10%)
  between operations  14.5 us (5%)
  starting transfers between devices  13.8 us (5%)
  other arithmetic  11.7 us (4%)
    pallas_call x2, Pallas kernels, run_layer(): pl.pallas_call(functools.partial(layer_kernel, dims), name='block', out_s...  82.5 us
    all_gather x1, blocking collectives, body(): around = lax.all_gather(targets[0], 'tile', axis=0, tiled=False)  48.3 us
    psum x1, blocking collectives, body(): flat = lax.psum(flat, 'tile').astype(F32)  38.3 us
    all_gather x1, blocking collectives, body(): logits = lax.all_gather(logits, 'tile', axis=0, tiled=False)  36.1 us
    ppermute x4, starting transfers between devices, hop(): return lax.ppermute(value, 'tile', pairs)  8.69 us
  transfers between devices with their start and end apart: 9, of which 1 were waited for; matrix products, arithmetic and copies ran while one was open for 10% of the time, Pallas kernels for 30%

commit v1 on v0

v1 whole, which is shorter than its diff:
```python
import functools

import jax
import jax.numpy as jnp
from jax import lax
from jax.experimental import pallas as pl
from jax.experimental.pallas import tpu as pltpu
from jax.sharding import PartitionSpec as P

EPS = 1e-06
HALO = 6
F32 = jnp.float32
BF16 = jnp.bfloat16
VMEM_LIMIT = 52 * 1024 * 1024


def sigmoid(u):
    return 0.5 * jnp.tanh(0.5 * u) + 0.5


def dot_nn(a, b):
    return jnp.dot(a, b, preferred_element_type=F32)


def dot_nt(a, b):
    return lax.dot_general(a, b, (((1,), (1,)), ((), ())), preferred_element_type=F32)


def channel_sum(v):
    return jnp.sum(v, axis=0, keepdims=True)


def spread(row, dst, r, order):
    chans, width = row.shape
    lane = lax.broadcasted_iota(jnp.int32, (chans, width), 1)
    prev = jnp.where(lane > 0, pltpu.roll(row, 1, 1), 0.0)
    nxt = jnp.where(lane < width - 1, pltpu.roll(row, width - 1, 1), 0.0)
    parts = (prev, row, nxt) if order > 0 else (nxt, row, prev)
    for j in range(3):
        dst[j * chans : (j + 1) * chans, r * width : (r + 1) * width] = parts[j].astype(BF16)


def conv_rows(w_ref, src, sign, rows, chans, width):
    step = 2 * width
    outs = [dot_nn(w_ref[...], src[:, p * step : (p + 1) * step]) for p in range(rows // 2)]

    def piece(i, r):
        half = slice((r % 2) * width, (r % 2 + 1) * width)
        return outs[r // 2][i * chans : (i + 1) * chans, half]

    result = []
    for r in range(rows):
        acc = piece(1, r)
        for i in (-1, 1):
            if 0 <= r + sign * i < rows:
                acc = acc + piece(i + 1, r + sign * i)
        result.append(acc)
    return result


def forward_kernel(meta_ref, x_ref, wf_ref, feat_ref, slope_ref, xs_ref, xt):
    _, chans, _, rows, width = x_ref.shape
    xt[...] = x_ref[0, :, 0].astype(F32).reshape(chans * rows, width)
    dst = xs_ref.at[0]
    for r in range(rows):
        spread(xt[pl.ds(r, chans, stride=rows), :], dst, r, 1)
    for r, pre in enumerate(conv_rows(wf_ref, dst, 1, rows, chans, width)):
        cols = slice(r * width, (r + 1) * width)
        s = sigmoid(pre)
        y = pre * s
        feat_ref[0, :, cols] = y.astype(BF16)
        slope_ref[0, :, cols] = (s + y * (1.0 - s)).astype(BF16)


def run_forward(layer, x, wf):
    n, chans, _, rows, width = x.shape
    vox = rows * width
    sds = jax.ShapeDtypeStruct
    return pl.pallas_call(
        forward_kernel,
        name="conv_forward",
        out_shape=(
            sds((n, chans, vox), BF16),
            sds((n, chans, vox), BF16),
            sds((n, 3 * chans, vox), BF16),
        ),
        grid_spec=pltpu.PrefetchScalarGridSpec(
            num_scalar_prefetch=1,
            grid=(n,),
            in_specs=[
                pl.BlockSpec((1, chans, 1, rows, width), lambda f, meta: (f, 0, meta[0], 0, 0)),
                pl.BlockSpec((3 * chans, 3 * chans), lambda f, meta: (0, 0)),
            ],
            out_specs=[
                pl.BlockSpec((1, chans, vox), lambda f, meta: (f, 0, 0)),
                pl.BlockSpec((1, chans, vox), lambda f, meta: (f, 0, 0)),
                pl.BlockSpec((1, 3 * chans, vox), lambda f, meta: (f, 0, 0)),
            ],
            scratch_shapes=[pltpu.VMEM((chans * rows, width), F32)],
        ),
        cost_estimate=pl.CostEstimate(
            flops=2 * n * 9 * chans * chans * vox,
            bytes_accessed=n * chans * vox * 12,
            transcendentals=n * chans * vox,
        ),
    )(layer, x, wf)


def backward_kernel(aliased, meta_ref, dpre_ref, wb_ref, *rest):
    dx_ref, ds, xt = rest[-3:]
    _, chans, _, rows, width = dx_ref.shape
    for r in range(rows):
        spread(dpre_ref[0, :, r * width : (r + 1) * width].astype(F32), ds, r, -1)
    for r, row in enumerate(conv_rows(wb_ref, ds, -1, rows, chans, width)):
        xt[pl.ds(r, chans, stride=rows), :] = row
    dx_ref[0, :, 0] = xt[...].astype(BF16).reshape(chans, rows, width)


def run_backward(meta, dpre, wb, n, layers, rows, into):
    chans, vox = dpre.shape[1:]
    width = vox // rows
    aliased = into is not None
    return pl.pallas_call(
        functools.partial(backward_kernel, aliased),
        name="conv_backward",
        out_shape=jax.ShapeDtypeStruct((n, chans, layers, rows, width), BF16),
        grid_spec=pltpu.PrefetchScalarGridSpec(
            num_scalar_prefetch=1,
            grid=(n,),
            in_specs=[
                pl.BlockSpec((1, chans, vox), lambda f, meta: (meta[0] + f, 0, 0)),
                pl.BlockSpec((3 * chans, 3 * chans), lambda f, meta: (0, 0)),
            ]
            + [pl.BlockSpec(memory_space=pl.ANY)] * aliased,
            out_specs=pl.BlockSpec(
                (1, chans, 1, rows, width), lambda f, meta: (f, 0, meta[1], 0, 0)
            ),
            scratch_shapes=[
                pltpu.VMEM((3 * chans, vox), BF16),
                pltpu.VMEM((chans * rows, width), F32),
            ],
        ),
        input_output_aliases={3: 0} if aliased else {},
        cost_estimate=pl.CostEstimate(
            flops=2 * n * 9 * chans * chans * vox,
            bytes_accessed=n * chans * vox * 4,
            transcendentals=0,
        ),
    )(meta, dpre, wb, *([into] if aliased else []))


def temporal_kernel(
    counts,
    dims,
    meta_ref,
    weight_ref,
    wt_ref,
    wtb_ref,
    whc_ref,
    tgt_ref,
    init_ref,
    *rest,
):
    own, chans, vox, total, members, width = dims
    here = own // members
    pieces = rest[: len(counts)]
    slope_in = rest[len(counts) : len(counts) + members]
    xs_in = rest[len(counts) + members : len(counts) + 2 * members]
    (
        logit_ref,
        dpre_ref,
        grad_ref,
        feats,
        slope,
        xs,
        n0,
        inv0,
        h1,
        n1,
        inv1,
        sp0,
        dh2,
        dm1,
        dm0,
        final_ref,
        dlog,
        sems,
    ) = rest[len(counts) + 2 * members :]
    step = min(256, vox)
    lo, hi = HALO, HALO + own
    first = meta_ref[0]
    chunks = [slice(p * step, (p + 1) * step) for p in range(vox // step)]
    whole = slice(0, vox)

    early = [
        pltpu.make_async_copy(src, feats.at[pl.ds(meta_ref[1 + k], n)], sems.at[k])
        for k, (src, n) in enumerate(zip(pieces, counts))
    ]
    late = []
    for k in range(members):
        spot = pl.ds(meta_ref[1 + k] - HALO, here)
        late.append(pltpu.make_async_copy(slope_in[k], slope.at[spot], sems.at[len(early) + k]))
        late.append(
            pltpu.make_async_copy(xs_in[k], xs.at[spot], sems.at[len(early) + members + k])
        )
    for copy in early + late:
        copy.start()
    for copy in early:
        copy.wait()

    def frame_ok(f):
        g = first + f - HALO
        return jnp.where((g >= 0) & (g < total), 1.0, 0.0).astype(F32)

    def loop(a, b, *fns):
        def every(f, carry):
            for fn in fns:
                fn(f)
            return carry

        lax.fori_loop(a, b, every, 0)

    def stack(ref, f0, f1, f2, cols):
        return jnp.concatenate([ref[f0, :, cols], ref[f1, :, cols], ref[f2, :, cols]], axis=0)

    def rms(hid):
        return lax.rsqrt(channel_sum(hid * hid) * (1.0 / chans) + EPS)

    def norm0(f):
        for cols in chunks:
            hid = feats[f, :, cols].astype(F32)
            inv = rms(hid)
            n0[f, :, cols] = (hid * inv).astype(BF16)
            inv0[f, :, cols] = inv

    def layer0(f):
        ok = frame_ok(f)
        for cols in chunks:
            mixed = dot_nn(wt_ref[0], stack(n0, f - 1, f, f + 1, cols))
            s = sigmoid(mixed)
            y = mixed * s
            hid = feats[f, :, cols].astype(F32) + y
            inv = rms(hid) * ok
            h1[f, :, cols] = hid
            n1[f, :, cols] = (hid * inv).astype(BF16)
            inv1[f, :, cols] = inv
            sp0[f, :, cols] = s + y * (1.0 - s)

    def layer1(f):
        weight = weight_ref[f - 3]
        for cols in chunks:
            mixed = dot_nn(wt_ref[1], stack(n1, f - 2, f, f + 2, cols))
            s = sigmoid(mixed)
            y = mixed * s
            hid = h1[f, :, cols] + y
            inv = rms(hid)
            unit = hid * inv
            final = unit.astype(BF16)
            logit = channel_sum(final.astype(F32) * whc_ref[...])
            logit_ref[f - 3, :, cols] = logit
            dlogit = weight * (sigmoid(logit) - tgt_ref[f - 3, :, cols].astype(F32))
            final_ref[f, :, cols] = final
            dlog[f, :, cols] = dlogit
            dhid = (inv * dlogit) * (whc_ref[...] - unit * (logit * (1.0 / chans)))
            dh2[f, :, cols] = dhid
            dm1[f, :, cols] = (dhid * (s + y * (1.0 - s))).astype(BF16)

    def back1(f):
        ok = frame_ok(f)
        for cols in chunks:
            dnorm = dot_nn(wtb_ref[1], stack(dm1, f + 2, f, f - 2, cols))
            unit = n1[f, :, cols].astype(F32)
            mean = channel_sum(dnorm * unit) * (1.0 / chans)
            dhid = dh2[f, :, cols] + inv1[f, :, cols] * (dnorm - unit * mean)
            dh2[f, :, cols] = dhid
            dm0[f, :, cols] = (dhid * (sp0[f, :, cols] * ok)).astype(BF16)

    def back0(f):
        b = f - HALO
        for cols in chunks:
            dnorm = dot_nn(wtb_ref[0], stack(dm0, f + 1, f, f - 1, cols))
            unit = n0[f, :, cols].astype(F32)
            mean = channel_sum(dnorm * unit) * (1.0 / chans)
            dhid = dh2[f, :, cols] + inv0[f, :, cols] * (dnorm - unit * mean)
            dfeat = dhid.astype(BF16).astype(F32)
            dpre_ref[b, :, cols] = (dfeat * slope[b, :, cols].astype(F32)).astype(BF16)

    def weights(f):
        b = f - HALO
        center = dpre_ref[b]
        blank = jnp.zeros((chans, width), BF16)
        taller = jnp.concatenate([center[:, width:], blank], axis=1)
        lower = jnp.concatenate([blank, center[:, :-width]], axis=1)
        for i, rows in enumerate((taller, center, lower)):
            grad_ref[i] += dot_nt(rows, xs[b])
        grad_ref[3] += dot_nt(dm0[f], stack(n0, f - 1, f, f + 1, whole))
        grad_ref[4] += dot_nt(dm1[f], stack(n1, f - 2, f, f + 2, whole))
        head = jnp.broadcast_to(dlog[f].astype(BF16), (chans, vox))
        grad_ref[5, :, :chans] += dot_nt(head, final_ref[f])

    grad_ref[...] = init_ref[...]
    loop(0, hi + HALO, norm0)
    loop(1, hi + HALO - 1, layer0)
    loop(3, hi + 3, layer1)
    loop(lo - 1, hi + 1, back1)
    for copy in late:
        copy.wait()
    loop(lo, hi, back0)
    loop(lo, hi, weights)


def run_temporal(meta, weights, wt, wtb, whc, tgt, init, pieces, slopes, xss, own, width, total):
    counts = tuple(p.shape[0] for p in pieces)
    members = len(slopes)
    chans, vox = pieces[0].shape[1:]
    every = own + 2 * HALO
    sds = jax.ShapeDtypeStruct
    smem = pl.BlockSpec(memory_space=pltpu.SMEM)
    vmem = pl.BlockSpec(memory_space=pltpu.VMEM)
    hbm = pl.BlockSpec(memory_space=pl.ANY)
    loose = len(pieces) + 2 * members
    frame = lambda n, c, dt: pltpu.VMEM((n, c, vox), dt)
    return pl.pallas_call(
        functools.partial(temporal_kernel, counts, (own, chans, vox, total, members, width)),
        name="temporal",
        out_shape=(
            sds((own + 6, 1, vox), F32),
            sds((own, chans, vox), BF16),
            sds((6, chans, 3 * chans), F32),
        ),
        in_specs=[smem, smem] + [vmem] * 5 + [hbm] * loose,
        out_specs=[vmem] * 3,
        scratch_shapes=[
            frame(every, chans, BF16),
            frame(own, chans, BF16),
            frame(own, 3 * chans, BF16),
            frame(every, chans, BF16),
            frame(every, 1, F32),
            frame(every, chans, F32),
            frame(every, chans, BF16),
            frame(every, 1, F32),
            frame(every, chans, F32),
            frame(every, chans, F32),
            frame(every, chans, BF16),
            frame(every, chans, BF16),
            frame(every, chans, BF16),
            frame(every, 1, F32),
            pltpu.SemaphoreType.DMA((loose,)),
        ],
        compiler_params=pltpu.CompilerParams(vmem_limit_bytes=VMEM_LIMIT),
        cost_estimate=pl.CostEstimate(
            flops=60 * own * 6 * chans * chans * vox,
            bytes_accessed=40 * own * chans * vox,
            transcendentals=6 * own * chans * vox,
        ),
    )(meta, weights, wt, wtb, whc, tgt, init, *pieces, *slopes, *xss)


def group_size(tiles, frames_here, layers):
    for g in range(1, layers + 1):
        if layers % g == 0 and tiles % g == 0 and g * frames_here >= HALO:
            return g
    return layers


def pick(parts, start):
    doubled = jnp.stack(parts + parts)
    return lax.dynamic_slice_in_dim(doubled, start, len(parts), 0)


def take(value, index, axis):
    return lax.dynamic_index_in_dim(value, index, axis, False)


def sum_over_tiles(value, tiles):
    if tiles & (tiles - 1):
        return lax.psum(value.astype(BF16), "tile").astype(F32)
    k = 1
    while k < tiles:
        pairs = [(a, a ^ k) for a in range(tiles)]
        value = value + lax.ppermute(value.astype(BF16), "tile", pairs).astype(F32)
        k *= 2
    return value


def sum_over_reps(value, axis):
    reps = lax.axis_size("rep")
    r = lax.axis_index("rep")
    n = value.shape[axis] // reps

    def share(k):
        return lax.dynamic_slice_in_dim(value, (k % reps) * n, n, axis)

    acc = share(r)
    for s in range(1, reps):
        pairs = [(a, (a + s) % reps) for a in range(reps)]
        acc = acc + lax.ppermute(share(r + s).astype(BF16), "rep", pairs).astype(F32)
    return acc


def body(inputs, w_spatial, w_temporal, w_head, targets, valid):
    _, here, chans, layers, rows, width = inputs.shape
    tiles = lax.axis_size("tile")
    total = here * tiles
    g = group_size(tiles, here, layers)
    per = layers // g
    own = g * here
    vox = rows * width
    t = lax.axis_index("tile")
    q, m = t // g, t % g
    spot = targets.shape[2]
    share = tiles // g
    x = inputs[0]
    apart = x.reshape(here, chans, g, per, rows, width)

    def swap(value, s):
        pairs = [(a, a // g * g + (a % g + s) % g) for a in range(tiles)]
        return lax.ppermute(value, "tile", pairs)

    def hop(value, shifts):
        pairs = [(a, a + shifts[a % g] * g) for a in range(tiles)]
        return lax.ppermute(value, "tile", [p for p in pairs if 0 <= p[1] < tiles])

    arriving = [
        [swap(take(apart, (m + s) % g, 2)[:, :, layer], s) for s in range(1, g)]
        for layer in range(per)
    ]

    w9 = w_spatial.reshape(3, 3, chans, chans)
    wf = w9.transpose(0, 2, 1, 3).reshape(3 * chans, 3 * chans)
    wb = w9.transpose(0, 3, 1, 2).reshape(3 * chans, 3 * chans)
    wt = w_temporal.transpose(0, 2, 1, 3).reshape(2, chans, 3 * chans)
    wtb = w_temporal.transpose(0, 3, 1, 2).reshape(2, chans, 3 * chans)
    whc = w_head.astype(F32)[:, None]

    window = jnp.pad(targets[0], ((3, 3), (0, 0)))
    parts = []
    for r in range(share):
        piece = lax.dynamic_slice_in_dim(window, ((t % share - r) % share) * own, own + 6, 0)
        pairs = [(a, (a % share - r) % share * g + a // share) for a in range(tiles)]
        parts.append(lax.ppermute(piece, "tile", pairs))
    tgt = pick(parts, (-q) % share).transpose(1, 0, 2).reshape(own + 6, per, 1, vox)
    frame_weight = jnp.pad(valid[0].astype(F32) / total, (3, 3))
    frame_weight = lax.dynamic_slice_in_dim(frame_weight, q * own, own + 6, 0)

    grads = jnp.zeros((6, chans, 3 * chans), F32)
    logits, out, backs = [], None, []
    mirrored = g == 2 and here <= HALO <= 2 * here
    for layer in range(per):
        index = (m * per + layer).astype(jnp.int32)
        done = [run_forward(index[None], x, wf)]
        for piece in arriving[layer]:
            done.append(run_forward(jnp.zeros((1,), jnp.int32), piece[:, :, None], wf))
        pieces = [d[0] for d in done]
        places = [HALO + (m - s) % g * here for s in range(g)]
        if mirrored:
            n = HALO - here
            up, down = own + HALO, HALO - here
            for k, full in enumerate(pieces[:2]):
                away, toward = ((-1, 1), (1, -1)) if k == 0 else ((1, -1), (-1, 1))
                pieces.append(hop(full, away))
                places.append(jnp.where(m == k, up, down))
                if n:
                    start = jnp.where(m == k, here - n, 0)
                    pieces.append(hop(lax.dynamic_slice_in_dim(full, start, n, 0), toward))
                    places.append(jnp.where(m == k, 0, up + here))
        else:
            block = pick(pieces[::-1], g - 1 - m).reshape(own, chans, vox)
            left, d = HALO, 1
            while left > 0:
                n = min(left, own)
                pieces.append(hop(block[own - n :], (d,) * g))
                places.append(left - n)
                pieces.append(hop(block[:n], (-d,) * g))
                places.append(HALO + d * own)
                left -= n
                d += 1
        meta = jnp.stack([jnp.asarray(v, jnp.int32) for v in [q * own] + places])
        logit, dpre, grads = run_temporal(
            meta,
            frame_weight,
            wt,
            wtb,
            whc,
            tgt[:, layer],
            grads,
            pieces,
            [d[1] for d in done],
            [d[2] for d in done],
            own,
            width,
            total,
        )
        logits.append(logit[3 : 3 + own, 0])
        zero = jnp.zeros((), jnp.int32)
        for s in range(1, g):
            frames = jnp.stack([((m - s) % g * here).astype(jnp.int32), zero])
            dx = run_backward(frames, dpre, wb, here, 1, rows, None)
            backs.append(((m + s) % g * per + layer, swap(dx, -s)))
        frames = jnp.stack([(m * here).astype(jnp.int32), index])
        out = run_backward(frames, dpre, wb, here, layers, rows, out)
    for index, dx in backs:
        out = lax.dynamic_update_slice_in_dim(out, dx, index, 2)

    grads = sum_over_tiles(sum_over_reps(grads, 1), tiles)
    part = grads.shape[1]
    gs = grads[:3].reshape(3, part, 3, chans).transpose(0, 2, 1, 3).reshape(9, part, chans)
    gt = grads[3:5].reshape(2, part, 3, chans).transpose(0, 2, 1, 3)
    gh = lax.dynamic_slice_in_dim(grads[5, 0], lax.axis_index("rep") * part, part, 0)

    logits = jnp.concatenate(logits, axis=1).astype(BF16).reshape(own, share, spot)
    parts = []
    for r in range(share):
        pairs = [(a, a % g * share + (a // g - r) % share) for a in range(tiles)]
        parts.append(lax.ppermute(take(logits, (q - r) % share, 1), "tile", pairs))
    logits = pick(parts, (-t) % share).reshape(1, total, spot)
    return logits, out[None], gs, gt, gh


def solution(mesh):
    placed = (
        P("rep", "tile", None, None, None, None),
        P(),
        P(),
        P(),
        P("rep", None, "tile"),
        P("rep", None),
    )
    return jax.shard_map(
        body,
        mesh=mesh,
        in_specs=placed,
        out_specs=(
            P("rep", None, "tile"),
            P("rep", "tile", None, None, None, None),
            P(None, "rep", None),
            P(None, None, "rep", None),
            P("rep"),
        ),
        check_vma=False,
    )
```

time: 274 us -> 191 us (0.70)
  blocking collectives: 123 us -> 0 us
  starting transfers between devices: 13.8 us -> 62.1 us
  waiting for transfers between devices: 2.17 us -> 22.3 us
  between operations: 14.5 us -> 1.59 us
  local copies, waits for them, and re-layouts: 26.1 us -> 13.3 us
  other arithmetic: 11.7 us -> 2.4 us
  Pallas kernels: 82.5 us -> 88.4 us
    all_gather x2 -> x0, blocking collectives: 84.4 us -> none  [the longest x1 48.3 us: body(): around = lax.all_gather(targets[0], 'tile', axis=0, tiled=False)]
    ppermute x4 -> x22, starting transfers between devices: 8.69 us -> 57.8 us  [the longest x8 22.7 us: hop(): return lax.ppermute(value, 'tile', [p for p in pairs if 0 <= p[1] < tiles])]
    psum x1 -> x0, blocking collectives: 38.3 us -> none  [body(): flat = lax.psum(flat, 'tile').astype(F32)]
    ppermute x4, waiting for transfers between devices: 0.01 us -> 10.2 us  [swap(): return lax.ppermute(value, 'tile', pairs)]
    ppermute x4 -> x22, waiting for transfers between devices: 2.15 us -> 12.1 us  [the longest x3 8.72 us: sum_over_tiles(): value = value + lax.ppermute(value.astype(BF16), 'tile', pairs).astype(F32)]
    pallas_call x2 -> x10, Pallas kernels: 82.5 us -> 88.4 us  [the longest x2 51.9 us: run_temporal(): pl.pallas_call(functools.partial(temporal_kernel, counts, (own, chans, vo...]
    squeeze x4 -> x3, local copies, waits for them, and re-layouts: 5.62 us -> 0.35 us  [the longest x1 0.19 us: take(): return lax.dynamic_index_in_dim(value, index, axis, False)]
    concatenate x4 -> x2, other arithmetic: 4.8 us -> 0.99 us  [the longest x2 4.74 us: body(): full = jnp.concatenate(before + [block] + after, axis=0)]
  transfers between devices with their start and end apart: 9 -> 26, of which waited for: 1 -> 6; matrix products, arithmetic and copies ran while one was open for 10% -> 6% of each run, Pallas kernels for 30% -> 33%
where the time goes in v1:
time: 191 us; the launch traced here: 190 us
  Pallas kernels  88.4 us (46%)
  starting transfers between devices  62.1 us (33%)
  waiting for transfers between devices  22.3 us (12%)
  local copies, waits for them, and re-layouts  13.3 us (7%)
  other arithmetic  2.4 us (1%)
    pallas_call x2, Pallas kernels, run_temporal(): pl.pallas_call(functools.partial(temporal_kernel, counts, (own, chans, vo...  51.9 us
    ppermute x8, starting transfers between devices, hop(): return lax.ppermute(value, 'tile', [p for p in pairs if 0 <= p[1] < tiles])  22.7 us
    pallas_call x4, Pallas kernels, run_backward(): pl.pallas_call(functools.partial(backward_kernel, aliased), name='conv_ba...  18.6 us
    pallas_call x4, Pallas kernels, run_forward(): pl.pallas_call(forward_kernel, name='conv_forward', out_shape=(sds((n, ch...  17.9 us
    ppermute x4, starting transfers between devices, body(): parts.append(lax.ppermute(piece, 'tile', pairs))  14.3 us
    ppermute x4, starting transfers between devices, body(): parts.append(lax.ppermute(take(logits, (q - r) % share, 1), 'tile', pairs))  13.7 us
    ppermute x4, waiting for transfers between devices, swap(): return lax.ppermute(value, 'tile', pairs)  10.2 us
    ppermute x3, waiting for transfers between devices, sum_over_tiles(): value = value + lax.ppermute(value.astype(BF16), 'tile', pairs).astype(F32)  8.72 us
  transfers between devices with their start and end apart: 26, of which 6 were waited for; matrix products, arithmetic and copies ran while one was open for 6% of the time, Pallas kernels for 33%

profile of v1, /device:TPU:0, one launch (start us, length us, event | category | flops | bytes accessed | tf_op | source)
XLA Modules:
  0.0 190.2 jit_solution(1588961976432756348)
XLA Ops:
  0.8 1.0 pad_dynamic-slice_fusion
  1.7 0.7 collective-permute-start
  2.4 9.6 %collective-permute-start.1 = (bf16[14,512]{1,0:T(8,128)(2,1)S(1)}, bf16[14,512]{1,0:T(8,128)(2,1)S(1)}, u32[]{:S(2)}, u32[]{:S(2)}) collective-permute-start(bf16[14,512]{1,0:T(8,128)(2,1)S(1)} %get-tuple-element.68), channel_id=1, source_target_pairs={{0,24},{4,0},{8,8},{12,16},{16,28},{20,4},{24,12},{28,20},{1,25},{... | collective-permute-start | bytes 43016 | tf_op jit(solution)/shard_map/ppermute | solution.py:441
  12.1 3.9 %collective-permute-start.3 = (bf16[14,512]{1,0:T(8,128)(2,1)S(1)}, bf16[14,512]{1,0:T(8,128)(2,1)S(1)}, u32[]{:S(2)}, u32[]{:S(2)}) collective-permute-start(bf16[14,512]{1,0:T(8,128)(2,1)S(1)} %get-tuple-element.67), channel_id=1, source_target_pairs={{0,8},{4,16},{8,24},{12,0},{16,12},{20,20},{24,28},{28,4},{1,9},{5... | collective-permute-start | bytes 43016 | tf_op jit(solution)/shard_map/ppermute | solution.py:441
  16.0 1.0 copy.69
  17.1 0.8 reshape.57.wf_ref
  17.9 4.4 %conv_forward.4 = (bf16[4,64,1024]{2,1,0:T(8,128)(2,1)}, bf16[4,64,1024]{2,1,0:T(8,128)(2,1)}, bf16[4,192,1024]{2,1,0:T(8,128)(2,1)}) custom-call(s32[1]{0:T(128)} %bitcast.20.meta_ref, bf16[4,64,4,8,128]{4,3,2,1,0:T(8,128)(2,1)} %bitcast.96, bf16[192,192]{1,0:T(8,128)(2,1)} %reshape.57.wf_ref), custom_call_target="tpu_custom_call" | custom-call | flops 301989888 | bytes 3145728 | tf_op jit(solution)/shard_map/conv_forward/pallas_call | solution.py:79
  22.3 1.3 collective-permute-start.5
  23.7 0.2 copy_bitcast_fusion
  24.0 0.7 copy-done.4
  24.8 4.5 %conv_forward.6 = (bf16[4,64,1024]{2,1,0:T(8,128)(2,1)}, bf16[4,64,1024]{2,1,0:T(8,128)(2,1)}, bf16[4,192,1024]{2,1,0:T(8,128)(2,1)}) custom-call(s32[1]{0:T(128)} %bitcast.30.meta_ref, bf16[4,64,4,8,128]{4,3,2,1,0:T(8,128)(2,1)} %bitcast.97, bf16[192,192]{1,0:T(8,128)(2,1)} %reshape.57.wf_ref), custom_call_target="tpu_custom_call" | custom-call | flops 301989888 | bytes 3145728 | tf_op jit(solution)/shard_map/conv_forward/pallas_call | solution.py:79
  29.3 1.0 constant_dynamic-slice_fusion.2
  30.2 0.6 pad_add_fusion.meta_ref
  30.9 0.7 pad_add_fusion.1
  31.7 0.2 copy.54
  32.0 0.1 copy.41
  32.1 0.1 copy.46.wt_ref
  32.2 0.1 copy.47.wtb_ref
  32.3 0.1 copy.48.whc_ref
  32.4 0.8 reshape.59.wb_ref
  33.3 2.2 %collective-permute-start.4 = (bf16[4,64,8,128]{3,2,1,0:T(8,128)(2,1)S(1)}, bf16[4,64,8,128]{3,2,1,0:T(8,128)(2,1)S(1)}, u32[]{:S(2)}, u32[]{:S(2)}) collective-permute-start(bf16[4,64,8,128]{3,2,1,0:T(8,128)(2,1)S(1)} %get-tuple-element.54), channel_id=1, source_target_pairs={{0,4},{4,0},{8,12},{12,8},{16,20},{20,16},{24,28},{28,24},{1,5},{5... | collective-permute-start | bytes 1572872 | tf_op jit(solution)/shard_map/ppermute | solution.py:418
  35.5 2.5 %collective-permute-start.6 = (bf16[2,64,1024]{2,1,0:T(8,128)(2,1)S(1)}, bf16[2,64,1024]{2,1,0:T(8,128)(2,1)S(1)}, u32[]{:S(2)}, u32[]{:S(2)}) collective-permute-start(bf16[2,64,1024]{2,1,0:T(8,128)(2,1)S(1)} %constant_dynamic-slice_fusion.4), channel_id=1, source_target_pairs={{0,8},{8,16},{12,4},{16,24},{20,12},{28,20},{1,9},{9,17},{13,5},{1... | collective-permute-start | bytes 786440 | tf_op jit(solution)/shard_map/ppermute | solution.py:422
  38.2 10.2 %collective-permute-done.4 = bf16[4,64,8,128]{3,2,1,0:T(8,128)(2,1)S(1)} collective-permute-done((bf16[4,64,8,128]{3,2,1,0:T(8,128)(2,1)S(1)}, bf16[4,64,8,128]{3,2,1,0:T(8,128)(2,1)S(1)}, u32[]{:S(2)}, u32[]{:S(2)}) %collective-permute-start.4) | collective-permute-done | bytes 524320 | tf_op jit(solution)/shard_map/ppermute | solution.py:418
  48.3 0.8 copy-done.7
  49.2 4.5 %conv_forward.5 = (bf16[4,64,1024]{2,1,0:T(8,128)(2,1)}, bf16[4,64,1024]{2,1,0:T(8,128)(2,1)}, bf16[4,192,1024]{2,1,0:T(8,128)(2,1)}) custom-call(s32[1]{0:T(128)} %constant.186.clone.1.meta_ref, bf16[4,64,1,8,128]{4,3,2,1,0:T(8,128)(2,1)} %bitcast.114, bf16[192,192]{1,0:T(8,128)(2,1)} %reshape.57.wf_ref), custom_call_target="tpu_custom_call" | custom-call | flops 301989888 | bytes 3145728 | tf_op jit(solution)/shard_map/conv_forward/pallas_call | solution.py:79
  53.7 5.2 %collective-permute-start.7 = (bf16[4,64,1024]{2,1,0:T(8,128)(2,1)}, bf16[4,64,1024]{2,1,0:T(8,128)(2,1)}, u32[]{:S(2)}, u32[]{:S(2)}) collective-permute-start(bf16[4,64,1024]{2,1,0:T(8,128)(2,1)} %get-tuple-element.24.rest_1_), channel_id=1, source_target_pairs={{0,8},{8,16},{12,4},{16,24},{20,12},{28,20},{1,9},{9,17},{13,5},{1... | collective-permute-start | bytes 1572872 | tf_op jit(solution)/shard_map/ppermute | solution.py:422
  59.0 1.0 constant_dynamic-slice_fusion.3
  60.0 1.3 collective-permute-start.8
  61.4 1.3 collective-permute-start.10
  62.7 4.5 %conv_forward.7 = (bf16[4,64,1024]{2,1,0:T(8,128)(2,1)}, bf16[4,64,1024]{2,1,0:T(8,128)(2,1)}, bf16[4,192,1024]{2,1,0:T(8,128)(2,1)}) custom-call(s32[1]{0:T(128)} %constant.186.clone.1.meta_ref, bf16[4,64,1,8,128]{4,3,2,1,0:T(8,128)(2,1)} %bitcast.32.x_ref, bf16[192,192]{1,0:T(8,128)(2,1)} %reshape.57.wf_ref), custom_call_target="tpu_custom_call" | custom-call | flops 301989888 | bytes 3145728 | tf_op jit(solution)/shard_map/conv_forward/pallas_call | solution.py:79
  67.2 1.0 constant_dynamic-slice_fusion.1
  68.2 5.2 %collective-permute-start.11 = (bf16[2,64,1024]{2,1,0:T(8,128)(2,1)S(1)}, bf16[2,64,1024]{2,1,0:T(8,128)(2,1)S(1)}, u32[]{:S(2)}, u32[]{:S(2)}) collective-permute-start(bf16[2,64,1024]{2,1,0:T(8,128)(2,1)S(1)} %constant_dynamic-slice_fusion.2), channel_id=1, source_target_pairs={{0,8},{8,16},{12,4},{16,24},{20,12},{28,20},{1,9},{9,17},{13,5},{1... | collective-permute-start | bytes 786440 | tf_op jit(solution)/shard_map/ppermute | solution.py:422
  73.4 4.7 %collective-permute-start.12 = (bf16[4,64,1024]{2,1,0:T(8,128)(2,1)}, bf16[4,64,1024]{2,1,0:T(8,128)(2,1)}, u32[]{:S(2)}, u32[]{:S(2)}) collective-permute-start(bf16[4,64,1024]{2,1,0:T(8,128)(2,1)} %get-tuple-element.32.rest_1_), channel_id=1, source_target_pairs={{0,8},{8,16},{12,4},{16,24},{20,12},{28,20},{1,9},{9,17},{13,5},{1... | collective-permute-start | bytes 1572872 | tf_op jit(solution)/shard_map/ppermute | solution.py:422
  78.1 1.3 collective-permute-start.13
  79.5 25.9 %temporal.2 = (f32[14,1,1024]{2,1,0:T(1,128)S(1)}, bf16[8,64,1024]{2,1,0:T(8,128)(2,1)}, f32[6,64,192]{2,1,0:T(8,128)S(1)}) custom-call(s32[7]{0:T(128)S(1)} %stack.97.meta_ref, f32[14]{0:T(128)S(1)} %pad_dynamic-slice_fusion.12.weight_ref, bf16[2,64,192]{2,1,0:T(8,128)(2,1)S(1)} %copy.46.wt_ref, bf16[2,64,192]{2,1,0:T(8,128)(2,1)S(1)} %copy.47.wtb_ref, ...), custom_call_target="tpu_custom_call" | custom-call | flops 12079595520 | bytes 20971520 | tf_op jit(solution)/shard_map/temporal/pallas_call | solution.py:323
  105.4 0.1 fusion.3
  105.6 25.9 %temporal.3 = (f32[14,1,1024]{2,1,0:T(1,128)S(1)}, bf16[8,64,1024]{2,1,0:T(8,128)(2,1)}, f32[6,64,192]{2,1,0:T(8,128)S(1)}) custom-call(s32[7]{0:T(128)S(1)} %stack.97.meta_ref, f32[14]{0:T(128)S(1)} %pad_dynamic-slice_fusion.12.weight_ref, bf16[2,64,192]{2,1,0:T(8,128)(2,1)S(1)} %copy.46.wt_ref, bf16[2,64,192]{2,1,0:T(8,128)(2,1)S(1)} %copy.47.wtb_ref, ...), custom_call_target="tpu_custom_call" | custom-call | flops 12079595520 | bytes 20971520 | tf_op jit(solution)/shard_map/temporal/pallas_call | solution.py:323
  131.5 0.1 fusion.2
  131.6 0.3 fusion.4
  132.0 0.7 collective-permute-start.14
  132.7 10.0 %collective-permute-start.15 = (bf16[8,512]{1,0:T(8,128)(2,1)S(1)}, bf16[8,512]{1,0:T(8,128)(2,1)S(1)}, u32[]{:S(2)}, u32[]{:S(2)}) collective-permute-start(bf16[8,512]{1,0:T(8,128)(2,1)S(1)} %bitcast.112), channel_id=1, source_target_pairs={{0,12},{4,28},{8,0},{12,16},{16,4},{20,20},{24,8},{28,24},{1,13},{... | collective-permute-start | bytes 24584 | tf_op jit(solution)/shard_map/ppermute | solution.py:515
  142.8 2.9 %collective-permute-start.17 = (bf16[8,512]{1,0:T(8,128)(2,1)S(1)}, bf16[8,512]{1,0:T(8,128)(2,1)S(1)}, u32[]{:S(2)}, u32[]{:S(2)}) collective-permute-start(bf16[8,512]{1,0:T(8,128)(2,1)S(1)} %bitcast.110), channel_id=1, source_target_pairs={{0,4},{4,20},{8,8},{12,24},{16,12},{20,28},{24,0},{28,16},{1,5},{5... | collective-permute-start | bytes 24584 | tf_op jit(solution)/shard_map/ppermute | solution.py:515
  145.7 4.6 %conv_backward.4.rest_0_ = bf16[4,64,4,8,128]{4,3,2,1,0:T(8,128)(2,1)} custom-call(s32[2]{0:T(128)} %get-tuple-element.71.meta_ref, bf16[8,64,1024]{2,1,0:T(8,128)(2,1)} %get-tuple-element.39.dpre_ref, bf16[192,192]{1,0:T(8,128)(2,1)} %reshape.59.wb_ref), custom_call_target="tpu_custom_call" | custom-call | flops 301989888 | bytes 1048576 | tf_op jit(solution)/shard_map/conv_backward/pallas_call | solution.py:123
  150.3 4.6 %conv_backward.6 = bf16[4,64,1,8,128]{4,3,2,1,0:T(8,128)(2,1)} custom-call(s32[2]{0:T(128)} %get-tuple-element.72.meta_ref, bf16[8,64,1024]{2,1,0:T(8,128)(2,1)} %get-tuple-element.39.dpre_ref, bf16[192,192]{1,0:T(8,128)(2,1)} %reshape.59.wb_ref), custom_call_target="tpu_custom_call" | custom-call | flops 301989888 | bytes 1048576 | tf_op jit(solution)/shard_map/conv_backward/pallas_call | solution.py:123
  155.0 2.0 %collective-permute-start.18 = (bf16[4,64,1,8,128]{4,3,2,1,0:T(8,128)(2,1)}, bf16[4,64,1,8,128]{4,3,2,1,0:T(8,128)(2,1)S(1)}, u32[]{:S(2)}, u32[]{:S(2)}) collective-permute-start(bf16[4,64,1,8,128]{4,3,2,1,0:T(8,128)(2,1)} %conv_backward.6), channel_id=1, source_target_pairs={{0,4},{4,0},{8,12},{12,8},{16,20},{20,16},{24,28},{28,24},{1,5},{5... | collective-permute-start | bytes 1572872 | tf_op jit(solution)/shard_map/ppermute | solution.py:418
  157.0 4.6 %conv_backward.7 = bf16[4,64,1,8,128]{4,3,2,1,0:T(8,128)(2,1)} custom-call(s32[2]{0:T(128)} %get-tuple-element.72.meta_ref, bf16[8,64,1024]{2,1,0:T(8,128)(2,1)} %get-tuple-element.38.dpre_ref, bf16[192,192]{1,0:T(8,128)(2,1)} %reshape.59.wb_ref), custom_call_target="tpu_custom_call" | custom-call | flops 301989888 | bytes 1048576 | tf_op jit(solution)/shard_map/conv_backward/pallas_call | solution.py:123
  161.6 4.8 %conv_backward.5 = bf16[4,64,4,8,128]{4,3,2,1,0:T(8,128)(2,1)} custom-call(s32[2]{0:T(128)} %pad_add_fusion.meta_ref, bf16[8,64,1024]{2,1,0:T(8,128)(2,1)} %get-tuple-element.38.dpre_ref, bf16[192,192]{1,0:T(8,128)(2,1)} %reshape.59.wb_ref, bf16[4,64,4,8,128]{4,3,2,1,0:T(8,128)(2,1)} %conv_backward.4.rest_0_), custom_call_target="tpu_custom_call", output_to_operand_aliasing={{}: (3, {})} | custom-call | flops 301989888 | bytes 1048576 | tf_op jit(solution)/shard_map/conv_backward/pallas_call | solution.py:123
  166.4 0.1 collective-permute-start.19
  166.6 1.6 collective-permute-start.21
  168.1 0.2 collective-permute-start.20
  168.3 2.9 %collective-permute-done.21 = bf16[6,16,192]{2,1,0:T(8,128)(2,1)S(1)} collective-permute-done((bf16[6,16,192]{2,1,0:T(8,128)(2,1)S(1)}, bf16[6,16,192]{2,1,0:T(8,128)(2,1)S(1)}, u32[]{:S(2)}, u32[]{:S(2)}) %collective-permute-start.21) | collective-permute-done | bytes 36896 | tf_op jit(solution)/shard_map/ppermute | solution.py:397
  171.2 0.5 collective-permute-done.20
  171.7 2.0 %collective-permute-start.23 = (bf16[6,16,192]{2,1,0:T(8,128)(2,1)S(1)}, bf16[6,16,192]{2,1,0:T(8,128)(2,1)S(1)}, u32[]{:S(2)}, u32[]{:S(2)}) collective-permute-start(bf16[6,16,192]{2,1,0:T(8,128)(2,1)S(1)} %get-tuple-element.51), channel_id=1, source_target_pairs={{0,4},{4,0},{8,12},{12,8},{16,20},{20,16},{24,28},{28,24},{1,5},{5... | collective-permute-start | bytes 110600 | tf_op jit(solution)/shard_map/ppermute | solution.py:381
  173.7 3.0 %collective-permute-done.23 = bf16[6,16,192]{2,1,0:T(8,128)(2,1)S(1)} collective-permute-done((bf16[6,16,192]{2,1,0:T(8,128)(2,1)S(1)}, bf16[6,16,192]{2,1,0:T(8,128)(2,1)S(1)}, u32[]{:S(2)}, u32[]{:S(2)}) %collective-permute-start.23) | collective-permute-done | bytes 36896 | tf_op jit(solution)/shard_map/ppermute | solution.py:381
  176.7 1.0 collective-permute-start.24
  177.7 3.2 %collective-permute-done.24 = bf16[6,16,192]{2,1,0:T(8,128)(2,1)S(1)} collective-permute-done((bf16[6,16,192]{2,1,0:T(8,128)(2,1)S(1)}, bf16[6,16,192]{2,1,0:T(8,128)(2,1)S(1)}, u32[]{:S(2)}, u32[]{:S(2)}) %collective-permute-start.24) | collective-permute-done | bytes 36896 | tf_op jit(solution)/shard_map/ppermute | solution.py:381
  180.9 2.4 %collective-permute-start.25 = (bf16[6,16,192]{2,1,0:T(8,128)(2,1)S(1)}, bf16[6,16,192]{2,1,0:T(8,128)(2,1)S(1)}, u32[]{:S(2)}, u32[]{:S(2)}) collective-permute-start(bf16[6,16,192]{2,1,0:T(8,128)(2,1)S(1)} %fusion.1), channel_id=1, source_target_pairs={{0,16},{4,20},{8,24},{12,28},{16,0},{20,4},{24,8},{28,12},{1,17},{... | collective-permute-start | bytes 110600 | tf_op jit(solution)/shard_map/ppermute | solution.py:381
  183.3 0.6 dynamic-slice_bitcast_fusion.1
  183.9 2.6 %collective-permute-done.25 = bf16[6,16,192]{2,1,0:T(8,128)(2,1)S(1)} collective-permute-done((bf16[6,16,192]{2,1,0:T(8,128)(2,1)S(1)}, bf16[6,16,192]{2,1,0:T(8,128)(2,1)S(1)}, u32[]{:S(2)}, u32[]{:S(2)}) %collective-permute-start.25) | collective-permute-done | bytes 36896 | tf_op jit(solution)/shard_map/ppermute | solution.py:381
  186.7 0.6 copy.57
  187.3 0.6 fusion.8
  187.9 0.6 pad_maximum_fusion
  188.5 0.8 bitcast_dynamic-update-slice_fusion.1
  189.4 0.8 bitcast_dynamic-update-slice_fusion
  (84 shorter events, 1.2 us)
Async XLA Ops:
  0.6 23.1 %copy-start = (bf16[1,4,64,4,8,128]{5,4,3,2,1,0:T(8,128)(2,1)S(1)}, bf16[1,4,64,4,8,128]{5,4,3,2,1,0:T(8,128)(2,1)}, u32[]{:S(2)}) copy-start(bf16[1,4,64,4,8,128]{5,4,3,2,1,0:T(8,128)(2,1)} %param.6) | copy-start | bytes 6291460
  0.6 23.0 %copy-start.8 = (s32[1,32]{1,0:T(1,128)S(1)}, s32[1,32]{1,0:T(1,128)}, u32[]{:S(2)}) copy-start(s32[1,32]{1,0:T(1,128)} %param.11) | copy-start | bytes 388
  0.7 23.0 %copy-start.9 = (bf16[64]{0:T(256)(128)(2,1)S(1)}, bf16[64]{0:T(256)(128)(2,1)}, u32[]{:S(2)}) copy-start(bf16[64]{0:T(256)(128)(2,1)} %param.9) | copy-start | bytes 388
  1.7 31.6 %collective-permute-start = (bf16[14,512]{1,0:T(8,128)(2,1)S(1)}, bf16[14,512]{1,0:T(8,128)(2,1)S(1)}, u32[]{:S(2)}, u32[]{:S(2)}) collective-permute-start(bf16[14,512]{1,0:T(8,128)(2,1)S(1)} %get-tuple-element.70), channel_id=1, source_target_pairs={{0,0},{4,8},{8,16},{12,24},{16,4},{20,12},{24,20},{28,28},{1,1},{5... | collective-permute-start | bytes 43016 | tf_op jit(solution)/shard_map/ppermute | solution.py:441
  2.4 33.1 %collective-permute-start.1 = (bf16[14,512]{1,0:T(8,128)(2,1)S(1)}, bf16[14,512]{1,0:T(8,128)(2,1)S(1)}, u32[]{:S(2)}, u32[]{:S(2)}) collective-permute-start(bf16[14,512]{1,0:T(8,128)(2,1)S(1)} %get-tuple-element.68), channel_id=1, source_target_pairs={{0,24},{4,0},{8,8},{12,16},{16,28},{20,4},{24,12},{28,20},{1,25},{... | collective-permute-start | bytes 43016 | tf_op jit(solution)/shard_map/ppermute | solution.py:441
  12.0 26.0 %collective-permute-start.2 = (bf16[14,512]{1,0:T(8,128)(2,1)S(1)}, bf16[14,512]{1,0:T(8,128)(2,1)S(1)}, u32[]{:S(2)}, u32[]{:S(2)}) collective-permute-start(bf16[14,512]{1,0:T(8,128)(2,1)S(1)} %get-tuple-element.69), channel_id=1, source_target_pairs={{0,16},{4,24},{8,0},{12,8},{16,20},{20,28},{24,4},{28,12},{1,17},{... | collective-permute-start | bytes 43016 | tf_op jit(solution)/shard_map/ppermute | solution.py:441
  12.1 26.0 %collective-permute-start.3 = (bf16[14,512]{1,0:T(8,128)(2,1)S(1)}, bf16[14,512]{1,0:T(8,128)(2,1)S(1)}, u32[]{:S(2)}, u32[]{:S(2)}) collective-permute-start(bf16[14,512]{1,0:T(8,128)(2,1)S(1)} %get-tuple-element.67), channel_id=1, source_target_pairs={{0,8},{4,16},{8,24},{12,0},{16,12},{20,20},{24,28},{28,4},{1,9},{5... | collective-permute-start | bytes 43016 | tf_op jit(solution)/shard_map/ppermute | solution.py:441
  22.3 51.1 %collective-permute-start.5 = (bf16[4,64,1024]{2,1,0:T(8,128)(2,1)}, bf16[4,64,1024]{2,1,0:T(8,128)(2,1)S(1)}, u32[]{:S(2)}, u32[]{:S(2)}) collective-permute-start(bf16[4,64,1024]{2,1,0:T(8,128)(2,1)} %get-tuple-element.23.rest_0_), channel_id=1, source_target_pairs={{4,12},{8,0},{12,20},{16,8},{20,28},{24,16},{5,13},{9,1},{13,21},{... | collective-permute-start | bytes 1572872 | tf_op jit(solution)/shard_map/ppermute | solution.py:422
  23.7 1.0 copy-start.4
  24.0 7.7 %copy-start.1 = (bf16[9,64,64]{2,1,0:T(8,128)(2,1)S(1)}, bf16[9,64,64]{2,1,0:T(8,128)(2,1)}, u32[]{:S(2)}) copy-start(bf16[9,64,64]{2,1,0:T(8,128)(2,1)} %param.7) | copy-start | bytes 221188
  24.0 8.0 %copy-start.3 = (bf16[2,3,64,64]{3,2,1,0:T(8,128)(2,1)S(1)}, bf16[2,3,64,64]{3,2,1,0:T(8,128)(2,1)}, u32[]{:S(2)}) copy-start(bf16[2,3,64,64]{3,2,1,0:T(8,128)(2,1)} %param.8) | copy-start | bytes 147460
  30.2 31.1 %copy-start.5 = (bf16[4,64,1024]{2,1,0:T(8,128)(2,1)S(1)}, bf16[4,64,1024]{2,1,0:T(8,128)(2,1)}, u32[]{:S(2)}) copy-start(bf16[4,64,1024]{2,1,0:T(8,128)(2,1)} %get-tuple-element.31.rest_0_) | copy-start | bytes 1572868
  33.3 15.0 %collective-permute-start.4 = (bf16[4,64,8,128]{3,2,1,0:T(8,128)(2,1)S(1)}, bf16[4,64,8,128]{3,2,1,0:T(8,128)(2,1)S(1)}, u32[]{:S(2)}, u32[]{:S(2)}) collective-permute-start(bf16[4,64,8,128]{3,2,1,0:T(8,128)(2,1)S(1)} %get-tuple-element.54), channel_id=1, source_target_pairs={{0,4},{4,0},{8,12},{12,8},{16,20},{20,16},{24,28},{28,24},{1,5},{5... | collective-permute-start | bytes 1572872 | tf_op jit(solution)/shard_map/ppermute | solution.py:418
  35.5 32.7 %collective-permute-start.6 = (bf16[2,64,1024]{2,1,0:T(8,128)(2,1)S(1)}, bf16[2,64,1024]{2,1,0:T(8,128)(2,1)S(1)}, u32[]{:S(2)}, u32[]{:S(2)}) collective-permute-start(bf16[2,64,1024]{2,1,0:T(8,128)(2,1)S(1)} %constant_dynamic-slice_fusion.4), channel_id=1, source_target_pairs={{0,8},{8,16},{12,4},{16,24},{20,12},{28,20},{1,9},{9,17},{13,5},{1... | collective-permute-start | bytes 786440 | tf_op jit(solution)/shard_map/ppermute | solution.py:422
  38.0 23.4 %collective-permute-start.9 = (bf16[4,64,8,128]{3,2,1,0:T(8,128)(2,1)S(1)}, bf16[4,64,8,128]{3,2,1,0:T(8,128)(2,1)}, u32[]{:S(2)}, u32[]{:S(2)}) collective-permute-start(bf16[4,64,8,128]{3,2,1,0:T(8,128)(2,1)S(1)} %get-tuple-element.53), channel_id=1, source_target_pairs={{0,4},{4,0},{8,12},{12,8},{16,20},{20,16},{24,28},{28,24},{1,5},{5... | collective-permute-start | bytes 1572872 | tf_op jit(solution)/shard_map/ppermute | solution.py:418
  48.3 0.8 copy-start.7
  53.7 25.8 %collective-permute-start.7 = (bf16[4,64,1024]{2,1,0:T(8,128)(2,1)}, bf16[4,64,1024]{2,1,0:T(8,128)(2,1)}, u32[]{:S(2)}, u32[]{:S(2)}) collective-permute-start(bf16[4,64,1024]{2,1,0:T(8,128)(2,1)} %get-tuple-element.24.rest_1_), channel_id=1, source_target_pairs={{0,8},{8,16},{12,4},{16,24},{20,12},{28,20},{1,9},{9,17},{13,5},{1... | collective-permute-start | bytes 1572872 | tf_op jit(solution)/shard_map/ppermute | solution.py:422
  60.0 18.2 %collective-permute-start.8 = (bf16[2,64,1024]{2,1,0:T(8,128)(2,1)S(1)}, bf16[2,64,1024]{2,1,0:T(8,128)(2,1)S(1)}, u32[]{:S(2)}, u32[]{:S(2)}) collective-permute-start(bf16[2,64,1024]{2,1,0:T(8,128)(2,1)S(1)} %constant_dynamic-slice_fusion.3), channel_id=1, source_target_pairs={{4,12},{8,0},{12,20},{16,8},{20,28},{24,16},{5,13},{9,1},{13,21},{... | collective-permute-start | bytes 786440 | tf_op jit(solution)/shard_map/ppermute | solution.py:422
  61.4 44.2 %collective-permute-start.10 = (bf16[4,64,1024]{2,1,0:T(8,128)(2,1)S(1)}, bf16[4,64,1024]{2,1,0:T(8,128)(2,1)}, u32[]{:S(2)}, u32[]{:S(2)}) collective-permute-start(bf16[4,64,1024]{2,1,0:T(8,128)(2,1)S(1)} %copy-done.5), channel_id=1, source_target_pairs={{4,12},{8,0},{12,20},{16,8},{20,28},{24,16},{5,13},{9,1},{13,21},{... | collective-permute-start | bytes 1572872 | tf_op jit(solution)/shard_map/ppermute | solution.py:422
  68.2 37.4 %collective-permute-start.11 = (bf16[2,64,1024]{2,1,0:T(8,128)(2,1)S(1)}, bf16[2,64,1024]{2,1,0:T(8,128)(2,1)S(1)}, u32[]{:S(2)}, u32[]{:S(2)}) collective-permute-start(bf16[2,64,1024]{2,1,0:T(8,128)(2,1)S(1)} %constant_dynamic-slice_fusion.2), channel_id=1, source_target_pairs={{0,8},{8,16},{12,4},{16,24},{20,12},{28,20},{1,9},{9,17},{13,5},{1... | collective-permute-start | bytes 786440 | tf_op jit(solution)/shard_map/ppermute | solution.py:422
  73.4 6.0 %copy-start.6 = (bf16[4,64,1024]{2,1,0:T(8,128)(2,1)}, bf16[4,64,1024]{2,1,0:T(8,128)(2,1)S(1)}, u32[]{:S(2)}) copy-start(bf16[4,64,1024]{2,1,0:T(8,128)(2,1)S(1)} %collective-permute-done.5.rest_2_) | copy-start | bytes 1572868
  73.4 32.2 %collective-permute-start.12 = (bf16[4,64,1024]{2,1,0:T(8,128)(2,1)}, bf16[4,64,1024]{2,1,0:T(8,128)(2,1)}, u32[]{:S(2)}, u32[]{:S(2)}) collective-permute-start(bf16[4,64,1024]{2,1,0:T(8,128)(2,1)} %get-tuple-element.32.rest_1_), channel_id=1, source_target_pairs={{0,8},{8,16},{12,4},{16,24},{20,12},{28,20},{1,9},{9,17},{13,5},{1... | collective-permute-start | bytes 1572872 | tf_op jit(solution)/shard_map/ppermute | solution.py:422
  78.1 27.4 %collective-permute-start.13 = (bf16[2,64,1024]{2,1,0:T(8,128)(2,1)S(1)}, bf16[2,64,1024]{2,1,0:T(8,128)(2,1)S(1)}, u32[]{:S(2)}, u32[]{:S(2)}) collective-permute-start(bf16[2,64,1024]{2,1,0:T(8,128)(2,1)S(1)} %constant_dynamic-slice_fusion.1), channel_id=1, source_target_pairs={{4,12},{8,0},{12,20},{16,8},{20,28},{24,16},{5,13},{9,1},{13,21},{... | collective-permute-start | bytes 786440 | tf_op jit(solution)/shard_map/ppermute | solution.py:422
  132.0 34.4 %collective-permute-start.14 = (bf16[8,512]{1,0:T(8,128)(2,1)S(1)}, bf16[8,512]{1,0:T(8,128)(2,1)S(1)}, u32[]{:S(2)}, u32[]{:S(2)}) collective-permute-start(bf16[8,512]{1,0:T(8,128)(2,1)S(1)} %bitcast.113), channel_id=1, source_target_pairs={{0,0},{4,16},{8,4},{12,20},{16,8},{20,24},{24,12},{28,28},{1,1},{5... | collective-permute-start | bytes 24584 | tf_op jit(solution)/shard_map/ppermute | solution.py:515
  132.7 33.8 %collective-permute-start.15 = (bf16[8,512]{1,0:T(8,128)(2,1)S(1)}, bf16[8,512]{1,0:T(8,128)(2,1)S(1)}, u32[]{:S(2)}, u32[]{:S(2)}) collective-permute-start(bf16[8,512]{1,0:T(8,128)(2,1)S(1)} %bitcast.112), channel_id=1, source_target_pairs={{0,12},{4,28},{8,0},{12,16},{16,4},{20,20},{24,8},{28,24},{1,13},{... | collective-permute-start | bytes 24584 | tf_op jit(solution)/shard_map/ppermute | solution.py:515
  142.7 23.9 %collective-permute-start.16 = (bf16[8,512]{1,0:T(8,128)(2,1)S(1)}, bf16[8,512]{1,0:T(8,128)(2,1)S(1)}, u32[]{:S(2)}, u32[]{:S(2)}) collective-permute-start(bf16[8,512]{1,0:T(8,128)(2,1)S(1)} %bitcast.111), channel_id=1, source_target_pairs={{0,8},{4,24},{8,12},{12,28},{16,0},{20,16},{24,4},{28,20},{1,9},{5... | collective-permute-start | bytes 24584 | tf_op jit(solution)/shard_map/ppermute | solution.py:515
  142.8 25.4 %collective-permute-start.17 = (bf16[8,512]{1,0:T(8,128)(2,1)S(1)}, bf16[8,512]{1,0:T(8,128)(2,1)S(1)}, u32[]{:S(2)}, u32[]{:S(2)}) collective-permute-start(bf16[8,512]{1,0:T(8,128)(2,1)S(1)} %bitcast.110), channel_id=1, source_target_pairs={{0,4},{4,20},{8,8},{12,24},{16,12},{20,28},{24,0},{28,16},{1,5},{5... | collective-permute-start | bytes 24584 | tf_op jit(solution)/shard_map/ppermute | solution.py:515
  155.0 33.5 %collective-permute-start.18 = (bf16[4,64,1,8,128]{4,3,2,1,0:T(8,128)(2,1)}, bf16[4,64,1,8,128]{4,3,2,1,0:T(8,128)(2,1)S(1)}, u32[]{:S(2)}, u32[]{:S(2)}) collective-permute-start(bf16[4,64,1,8,128]{4,3,2,1,0:T(8,128)(2,1)} %conv_backward.6), channel_id=1, source_target_pairs={{0,4},{4,0},{8,12},{12,8},{16,20},{20,16},{24,28},{28,24},{1,5},{5... | collective-permute-start | bytes 1572872 | tf_op jit(solution)/shard_map/ppermute | solution.py:418
  161.6 4.8 %copy-start.2 = (bf16[4,64,1,8,128]{4,3,2,1,0:T(8,128)(2,1)S(1)}, bf16[4,64,1,8,128]{4,3,2,1,0:T(8,128)(2,1)}, u32[]{:S(2)}) copy-start(bf16[4,64,1,8,128]{4,3,2,1,0:T(8,128)(2,1)} %conv_backward.7) | copy-start | bytes 1572868
  166.4 23.0 %collective-permute-start.19 = (bf16[4,64,1,8,128]{4,3,2,1,0:T(8,128)(2,1)S(1)}, bf16[4,64,1,8,128]{4,3,2,1,0:T(8,128)(2,1)S(1)}, u32[]{:S(2)}, u32[]{:S(2)}) collective-permute-start(bf16[4,64,1,8,128]{4,3,2,1,0:T(8,128)(2,1)S(1)} %copy-done.2), channel_id=1, source_target_pairs={{0,4},{4,0},{8,12},{12,8},{16,20},{20,16},{24,28},{28,24},{1,5},{5... | collective-permute-start | bytes 1572872 | tf_op jit(solution)/shard_map/ppermute | solution.py:418
  166.5 1.8 collective-permute-start.22
  166.6 4.6 %collective-permute-start.21 = (bf16[6,16,192]{2,1,0:T(8,128)(2,1)S(1)}, bf16[6,16,192]{2,1,0:T(8,128)(2,1)S(1)}, u32[]{:S(2)}, u32[]{:S(2)}) collective-permute-start(bf16[6,16,192]{2,1,0:T(8,128)(2,1)S(1)} %get-tuple-element.57), channel_id=1, source_target_pairs={{0,2},{1,3},{2,0},{3,1},{4,6},{5,7},{6,4},{7,5},{8,10},{9,11},{10,... | collective-permute-start | bytes 110600 | tf_op jit(solution)/shard_map/ppermute | solution.py:397
  168.1 3.5 %collective-permute-start.20 = (bf16[6,16,192]{2,1,0:T(8,128)(2,1)S(1)}, bf16[6,16,192]{2,1,0:T(8,128)(2,1)S(1)}, u32[]{:S(2)}, u32[]{:S(2)}) collective-permute-start(bf16[6,16,192]{2,1,0:T(8,128)(2,1)S(1)} %get-tuple-element.55), channel_id=1, source_target_pairs={{0,1},{1,2},{2,3},{3,0},{4,5},{5,6},{6,7},{7,4},{8,9},{9,10},{10,1... | collective-permute-start | bytes 110600 | tf_op jit(solution)/shard_map/ppermute | solution.py:397
  171.7 5.0 %collective-permute-start.23 = (bf16[6,16,192]{2,1,0:T(8,128)(2,1)S(1)}, bf16[6,16,192]{2,1,0:T(8,128)(2,1)S(1)}, u32[]{:S(2)}, u32[]{:S(2)}) collective-permute-start(bf16[6,16,192]{2,1,0:T(8,128)(2,1)S(1)} %get-tuple-element.51), channel_id=1, source_target_pairs={{0,4},{4,0},{8,12},{12,8},{16,20},{20,16},{24,28},{28,24},{1,5},{5... | collective-permute-start | bytes 110600 | tf_op jit(solution)/shard_map/ppermute | solution.py:381
  176.7 4.2 %collective-permute-start.24 = (bf16[6,16,192]{2,1,0:T(8,128)(2,1)S(1)}, bf16[6,16,192]{2,1,0:T(8,128)(2,1)S(1)}, u32[]{:S(2)}, u32[]{:S(2)}) collective-permute-start(bf16[6,16,192]{2,1,0:T(8,128)(2,1)S(1)} %fusion), channel_id=1, source_target_pairs={{0,8},{4,12},{8,0},{12,4},{16,24},{20,28},{24,16},{28,20},{1,9},{5... | collective-permute-start | bytes 110600 | tf_op jit(solution)/shard_map/ppermute | solution.py:381
  180.9 5.6 %collective-permute-start.25 = (bf16[6,16,192]{2,1,0:T(8,128)(2,1)S(1)}, bf16[6,16,192]{2,1,0:T(8,128)(2,1)S(1)}, u32[]{:S(2)}, u32[]{:S(2)}) collective-permute-start(bf16[6,16,192]{2,1,0:T(8,128)(2,1)S(1)} %fusion.1), channel_id=1, source_target_pairs={{0,16},{4,20},{8,24},{12,28},{16,0},{20,4},{24,8},{28,12},{1,17},{... | collective-permute-start | bytes 110600 | tf_op jit(solution)/shard_map/ppermute | solution.py:381

commit v2 on v1

--- a/solution.py
+++ b/solution.py
@@ -58,52 +58,57 @@
     return result
 
 
-def forward_kernel(meta_ref, x_ref, wf_ref, feat_ref, slope_ref, xs_ref, xt):
+def forward_kernel(meta_ref, x_ref, w_ref, feat_ref, slope_ref, xs_ref, xt, wf):
     _, chans, _, rows, width = x_ref.shape
+
+    @pl.when((pl.program_id(0) == 0) & (pl.program_id(1) == 0))
+    def _():
+        for i in range(3):
+            for j in range(3):
+                wf[i * chans : (i + 1) * chans, j * chans : (j + 1) * chans] = w_ref[3 * i + j]
+
     xt[...] = x_ref[0, :, 0].astype(F32).reshape(chans * rows, width)
-    dst = xs_ref.at[0]
+    dst = xs_ref.at[0, 0]
     for r in range(rows):
         spread(xt[pl.ds(r, chans, stride=rows), :], dst, r, 1)
-    for r, pre in enumerate(conv_rows(wf_ref, dst, 1, rows, chans, width)):
+    for r, pre in enumerate(conv_rows(wf, dst, 1, rows, chans, width)):
         cols = slice(r * width, (r + 1) * width)
         s = sigmoid(pre)
         y = pre * s
-        feat_ref[0, :, cols] = y.astype(BF16)
-        slope_ref[0, :, cols] = (s + y * (1.0 - s)).astype(BF16)
-
-
-def run_forward(layer, x, wf):
+        feat_ref[0, 0, :, cols] = y.astype(BF16)
+        slope_ref[0, 0, :, cols] = (s + y * (1.0 - s)).astype(BF16)
+
+
+def run_forward(first, count, x, w_spatial):
     n, chans, _, rows, width = x.shape
     vox = rows * width
     sds = jax.ShapeDtypeStruct
+    result = lambda c: pl.BlockSpec((1, 1, c, vox), lambda k, f, meta: (k, f, 0, 0))
     return pl.pallas_call(
         forward_kernel,
         name="conv_forward",
         out_shape=(
-            sds((n, chans, vox), BF16),
-            sds((n, chans, vox), BF16),
-            sds((n, 3 * chans, vox), BF16),
+            sds((count, n, chans, vox), BF16),
+            sds((count, n, chans, vox), BF16),
+            sds((count, n, 3 * chans, vox), BF16),
         ),
         grid_spec=pltpu.PrefetchScalarGridSpec(
             num_scalar_prefetch=1,
-            grid=(n,),
+            grid=(count, n),
             in_specs=[
-                pl.BlockSpec((1, chans, 1, rows, width), lambda f, meta: (f, 0, meta[0], 0, 0)),
-                pl.BlockSpec((3 * chans, 3 * chans), lambda f, meta: (0, 0)),
+                pl.BlockSpec(
+                    (1, chans, 1, rows, width), lambda k, f, meta: (f, 0, meta[0] + k, 0, 0)
+                ),
+                pl.BlockSpec((9, chans, chans), lambda k, f, meta: (0, 0, 0)),
             ],
-            out_specs=[
-                pl.BlockSpec((1, chans, vox), lambda f, meta: (f, 0, 0)),
-                pl.BlockSpec((1, chans, vox), lambda f, meta: (f, 0, 0)),
-                pl.BlockSpec((1, 3 * chans, vox), lambda f, meta: (f, 0, 0)),
+            out_specs=[result(chans), result(chans), result(3 * chans)],
+            scratch_shapes=[
+                pltpu.VMEM((chans * rows, width), F32),
+                pltpu.VMEM((3 * chans, 3 * chans), BF16),
             ],
-            scratch_shapes=[pltpu.VMEM((chans * rows, width), F32)],
-        ),
-        cost_estimate=pl.CostEstimate(
-            flops=2 * n * 9 * chans * chans * vox,
-            bytes_accessed=n * chans * vox * 12,
-            transcendentals=n * chans * vox,
-        ),
-    )(layer, x, wf)
+        ),
+        cost_estimate=pl.CostEstimate(flops=1000, bytes_accessed=1000, transcendentals=0),
+    )(first, x, w_spatial)
 
 
 def backward_kernel(aliased, meta_ref, dpre_ref, wb_ref, *rest):
@@ -141,16 +146,13 @@
             ],
         ),
         input_output_aliases={3: 0} if aliased else {},
-        cost_estimate=pl.CostEstimate(
-            flops=2 * n * 9 * chans * chans * vox,
-            bytes_accessed=n * chans * vox * 4,
-            transcendentals=0,
-        ),
+        cost_estimate=pl.CostEstimate(flops=1000, bytes_accessed=1000, transcendentals=0),
     )(meta, dpre, wb, *([into] if aliased else []))
 
 
 def temporal_kernel(
-    counts,
+    places,
+    inside,
     dims,
     meta_ref,
     weight_ref,
@@ -159,16 +161,18 @@
     whc_ref,
     tgt_ref,
     init_ref,
+    wb_ref,
     *rest,
 ):
     own, chans, vox, total, members, width = dims
     here = own // members
-    pieces = rest[: len(counts)]
-    slope_in = rest[len(counts) : len(counts) + members]
-    xs_in = rest[len(counts) + members : len(counts) + 2 * members]
+    counts = len(places)
+    pieces = [ref.at[k] for ref, k in zip(rest[:counts], places)]
+    slope_in = [ref.at[k] for ref, k in zip(rest[counts : counts + members], places)]
+    xs_in = [ref.at[k] for ref, k in zip(rest[counts + members : counts + 2 * members], places)]
     (
         logit_ref,
-        dpre_ref,
+        back_ref,
         grad_ref,
         feats,
         slope,
@@ -182,10 +186,13 @@
         dh2,
         dm1,
         dm0,
+        dpre,
         final_ref,
         dlog,
+        ds,
+        xt,
         sems,
-    ) = rest[len(counts) + 2 * members :]
+    ) = rest[counts + 2 * members :]
     step = min(256, vox)
     lo, hi = HALO, HALO + own
     first = meta_ref[0]
@@ -193,8 +200,8 @@
     whole = slice(0, vox)
 
     early = [
-        pltpu.make_async_copy(src, feats.at[pl.ds(meta_ref[1 + k], n)], sems.at[k])
-        for k, (src, n) in enumerate(zip(pieces, counts))
+        pltpu.make_async_copy(src, feats.at[pl.ds(meta_ref[1 + k], src.shape[0])], sems.at[k])
+        for k, src in enumerate(pieces)
     ]
     late = []
     for k in range(members):
@@ -283,11 +290,11 @@
             mean = channel_sum(dnorm * unit) * (1.0 / chans)
             dhid = dh2[f, :, cols] + inv0[f, :, cols] * (dnorm - unit * mean)
             dfeat = dhid.astype(BF16).astype(F32)
-            dpre_ref[b, :, cols] = (dfeat * slope[b, :, cols].astype(F32)).astype(BF16)
+            dpre[b, :, cols] = (dfeat * slope[b, :, cols].astype(F32)).astype(BF16)
 
     def weights(f):
         b = f - HALO
-        center = dpre_ref[b]
+        center = dpre[b]
         blank = jnp.zeros((chans, width), BF16)
         taller = jnp.concatenate([center[:, width:], blank], axis=1)
         lower = jnp.concatenate([blank, center[:, :-width]], axis=1)
@@ -308,11 +315,25 @@
     loop(lo, hi, back0)
     loop(lo, hi, weights)
 
-
-def run_temporal(meta, weights, wt, wtb, whc, tgt, init, pieces, slopes, xss, own, width, total):
-    counts = tuple(p.shape[0] for p in pieces)
+    def inputs(b):
+        rows = vox // width
+        for r in range(rows):
+            spread(dpre[b, :, r * width : (r + 1) * width].astype(F32), ds, r, -1)
+        for r, row in enumerate(conv_rows(wb_ref, ds, -1, rows, chans, width)):
+            xt[pl.ds(r, chans, stride=rows), :] = row
+        back_ref[b] = xt[...].astype(BF16)
+
+    def hand_on(b):
+        back_ref[b] = dpre[b]
+
+    loop(0, own, inputs if inside else hand_on)
+
+
+def run_temporal(
+    meta, weights, wt, wtb, whc, tgt, init, wb, pieces, places, slopes, xss, inside, own, width, total
+):
     members = len(slopes)
-    chans, vox = pieces[0].shape[1:]
+    chans, vox = pieces[0].shape[2:]
     every = own + 2 * HALO
     sds = jax.ShapeDtypeStruct
     smem = pl.BlockSpec(memory_space=pltpu.SMEM)
@@ -321,14 +342,16 @@
     loose = len(pieces) + 2 * members
     frame = lambda n, c, dt: pltpu.VMEM((n, c, vox), dt)
     return pl.pallas_call(
-        functools.partial(temporal_kernel, counts, (own, chans, vox, total, members, width)),
+        functools.partial(
+            temporal_kernel, tuple(places), inside, (own, chans, vox, total, members, width)
+        ),
         name="temporal",
         out_shape=(
             sds((own + 6, 1, vox), F32),
-            sds((own, chans, vox), BF16),
+            sds((own, chans * vox // width, width) if inside else (own, chans, vox), BF16),
             sds((6, chans, 3 * chans), F32),
         ),
-        in_specs=[smem, smem] + [vmem] * 5 + [hbm] * loose,
+        in_specs=[smem, smem] + [vmem] * 6 + [hbm] * loose,
         out_specs=[vmem] * 3,
         scratch_shapes=[
             frame(every, chans, BF16),
@@ -343,17 +366,18 @@
             frame(every, chans, F32),
             frame(every, chans, BF16),
             frame(every, chans, BF16),
+            frame(own, chans, BF16),
             frame(every, chans, BF16),
             frame(every, 1, F32),
+            pltpu.VMEM((3 * chans, vox), BF16),
+            pltpu.VMEM((chans * vox // width, width), F32),
             pltpu.SemaphoreType.DMA((loose,)),
         ],
         compiler_params=pltpu.CompilerParams(vmem_limit_bytes=VMEM_LIMIT),
         cost_estimate=pl.CostEstimate(
-            flops=60 * own * 6 * chans * chans * vox,
-            bytes_accessed=40 * own * chans * vox,
-            transcendentals=6 * own * chans * vox,
-        ),
-    )(meta, weights, wt, wtb, whc, tgt, init, *pieces, *slopes, *xss)
+            flops=1000, bytes_accessed=1000, transcendentals=0
+        ),
+    )(meta, weights, wt, wtb, whc, tgt, init, wb, *pieces, *slopes, *xss)
 
 
 def group_size(tiles, frames_here, layers):
@@ -409,7 +433,7 @@
     t = lax.axis_index("tile")
     q, m = t // g, t % g
     spot = targets.shape[2]
-    share = tiles // g
+    share = groups = tiles // g
     x = inputs[0]
     apart = x.reshape(here, chans, g, per, rows, width)
 
@@ -427,56 +451,68 @@
     ]
 
     w9 = w_spatial.reshape(3, 3, chans, chans)
-    wf = w9.transpose(0, 2, 1, 3).reshape(3 * chans, 3 * chans)
     wb = w9.transpose(0, 3, 1, 2).reshape(3 * chans, 3 * chans)
     wt = w_temporal.transpose(0, 2, 1, 3).reshape(2, chans, 3 * chans)
     wtb = w_temporal.transpose(0, 3, 1, 2).reshape(2, chans, 3 * chans)
     whc = w_head.astype(F32)[:, None]
 
+    index = (m * per).astype(jnp.int32)
+    mine = run_forward(index[None], per, x, w_spatial)
+    mirrored = g == 2 and here <= HALO <= 2 * here
+    n = HALO - here
+    ahead = []
+    if mirrored:
+        ahead.append(hop(mine[0], (-1, 1)))
+        if n:
+            start = jnp.where(m == 0, here - n, 0)
+            ahead.append(hop(lax.dynamic_slice_in_dim(mine[0], start, n, 1), (1, -1)))
+
     window = jnp.pad(targets[0], ((3, 3), (0, 0)))
-    parts = []
-    for r in range(share):
-        piece = lax.dynamic_slice_in_dim(window, ((t % share - r) % share) * own, own + 6, 0)
-        pairs = [(a, (a % share - r) % share * g + a // share) for a in range(tiles)]
-        parts.append(lax.ppermute(piece, "tile", pairs))
-    tgt = pick(parts, (-q) % share).transpose(1, 0, 2).reshape(own + 6, per, 1, vox)
+    window = jnp.stack([window[k // g * own : k // g * own + own + 6] for k in range(tiles)])
+    window = lax.all_to_all(window, "tile", 0, 0, tiled=True)
+    tgt = lax.dynamic_slice_in_dim(window, m * share, share, 0)
+    tgt = tgt.transpose(1, 0, 2).reshape(own + 6, per, 1, vox)
     frame_weight = jnp.pad(valid[0].astype(F32) / total, (3, 3))
     frame_weight = lax.dynamic_slice_in_dim(frame_weight, q * own, own + 6, 0)
 
     grads = jnp.zeros((6, chans, 3 * chans), F32)
-    logits, out, backs = [], None, []
-    mirrored = g == 2 and here <= HALO <= 2 * here
+    logits, backs = [], []
+    zero = jnp.zeros((1,), jnp.int32)
     for layer in range(per):
-        index = (m * per + layer).astype(jnp.int32)
-        done = [run_forward(index[None], x, wf)]
+        done = [mine]
         for piece in arriving[layer]:
-            done.append(run_forward(jnp.zeros((1,), jnp.int32), piece[:, :, None], wf))
+            done.append(run_forward(zero, 1, piece[:, :, None], w_spatial))
         pieces = [d[0] for d in done]
+        ranks = [layer] + [0] * (g - 1)
         places = [HALO + (m - s) % g * here for s in range(g)]
         if mirrored:
-            n = HALO - here
             up, down = own + HALO, HALO - here
-            for k, full in enumerate(pieces[:2]):
-                away, toward = ((-1, 1), (1, -1)) if k == 0 else ((1, -1), (-1, 1))
-                pieces.append(hop(full, away))
-                places.append(jnp.where(m == k, up, down))
-                if n:
-                    start = jnp.where(m == k, here - n, 0)
-                    pieces.append(hop(lax.dynamic_slice_in_dim(full, start, n, 0), toward))
-                    places.append(jnp.where(m == k, 0, up + here))
+            pieces += ahead
+            ranks += [layer] * len(ahead)
+            places += [jnp.where(m == 0, up, down), jnp.where(m == 0, 0, up + here)][: len(ahead)]
+            pieces.append(hop(pieces[1], (1, -1)))
+            places.append(jnp.where(m == 1, up, down))
+            if n:
+                start = jnp.where(m == 1, here - n, 0)
+                pieces.append(hop(lax.dynamic_slice_in_dim(pieces[1], start, n, 1), (-1, 1)))
+                places.append(jnp.where(m == 1, 0, up + here))
+            ranks += [0] * len(ahead)
         else:
-            block = pick(pieces[::-1], g - 1 - m).reshape(own, chans, vox)
+            block = [p[k] for p, k in zip(pieces, ranks)]
+            block = pick(block[::-1], g - 1 - m).reshape(own, chans, vox)
             left, d = HALO, 1
             while left > 0:
-                n = min(left, own)
-                pieces.append(hop(block[own - n :], (d,) * g))
-                places.append(left - n)
-                pieces.append(hop(block[:n], (-d,) * g))
+                k = min(left, own)
+                pieces.append(hop(block[own - k :], (d,) * g)[None])
+                places.append(left - k)
+                pieces.append(hop(block[:k], (-d,) * g)[None])
                 places.append(HALO + d * own)
-                left -= n
+                ranks += [0, 0]
+                left -= k
                 d += 1
         meta = jnp.stack([jnp.asarray(v, jnp.int32) for v in [q * own] + places])
-        logit, dpre, grads = run_temporal(
+        inside = layer < per - 1
+        logit, back, grads = run_temporal(
             meta,
             frame_weight,
             wt,
@@ -484,23 +520,32 @@
             whc,
             tgt[:, layer],
             grads,
+            wb,
             pieces,
+            ranks,
             [d[1] for d in done],
             [d[2] for d in done],
+            inside,
             own,
             width,
             total,
         )
         logits.append(logit[3 : 3 + own, 0])
-        zero = jnp.zeros((), jnp.int32)
-        for s in range(1, g):
-            frames = jnp.stack([((m - s) % g * here).astype(jnp.int32), zero])
-            dx = run_backward(frames, dpre, wb, here, 1, rows, None)
-            backs.append(((m + s) % g * per + layer, swap(dx, -s)))
-        frames = jnp.stack([(m * here).astype(jnp.int32), index])
-        out = run_backward(frames, dpre, wb, here, layers, rows, out)
-    for index, dx in backs:
-        out = lax.dynamic_update_slice_in_dim(out, dx, index, 2)
+        if inside:
+            back = back.reshape(g, here, chans, 1, rows, width)
+            for s in range(1, g):
+                dx = swap(take(back, (m - s) % g, 0), -s)
+                backs.append(((m + s) % g * per + layer, dx))
+            backs.append((index + layer, take(back, m, 0)))
+        else:
+            for s in range(1, g):
+                frames = jnp.stack([((m - s) % g * here).astype(jnp.int32), zero[0]])
+                dx = swap(run_backward(frames, back, wb, here, 1, rows, None), -s)
+                backs.append(((m + s) % g * per + layer, dx))
+            frames = jnp.stack([(m * here).astype(jnp.int32), index + layer])
+            out = run_backward(frames, back, wb, here, layers, rows, None)
+    for spot_z, dx in backs:
+        out = lax.dynamic_update_slice_in_dim(out, dx, spot_z, 2)
 
     grads = sum_over_tiles(sum_over_reps(grads, 1), tiles)
     part = grads.shape[1]
@@ -509,11 +554,10 @@
     gh = lax.dynamic_slice_in_dim(grads[5, 0], lax.axis_index("rep") * part, part, 0)
 
     logits = jnp.concatenate(logits, axis=1).astype(BF16).reshape(own, share, spot)
-    parts = []
-    for r in range(share):
-        pairs = [(a, a % g * share + (a // g - r) % share) for a in range(tiles)]
-        parts.append(lax.ppermute(take(logits, (q - r) % share, 1), "tile", pairs))
-    logits = pick(parts, (-t) % share).reshape(1, total, spot)
+    logits = logits.transpose(1, 0, 2)
+    logits = jnp.concatenate([logits] * g)
+    logits = lax.all_to_all(logits, "tile", 0, 0, tiled=True)
+    logits = take(logits.reshape(groups, g, own, spot), t // share, 1).reshape(1, total, spot)
     return logits, out[None], gs, gt, gh
 
 

time: 191 us -> 171 us (0.90)
  starting transfers between devices: 62.1 us -> 38 us
  local copies, waits for them, and re-layouts: 13.3 us -> 24.9 us
  Pallas kernels: 88.4 us -> 81.4 us
    ppermute x8 -> x0, starting transfers between devices: 27.9 us -> none  [the longest x4 14.3 us: body(): parts.append(lax.ppermute(piece, 'tile', pairs))]
    ppermute x4, waiting for transfers between devices: 10.2 us -> 0.01 us  [swap(): return lax.ppermute(value, 'tile', pairs)]
    pallas_call x4 -> x2, Pallas kernels: 18.6 us -> 9.25 us  [run_backward(): pl.pallas_call(functools.partial(backward_kernel, aliased), name='conv_ba...]
    all_to_all x0 -> x2, starting transfers between devices: none -> 8.29 us  [the longest x1 4.82 us: body(): window = lax.all_to_all(window, 'tile', 0, 0, tiled=True)]
    ppermute x8 -> x6, starting transfers between devices: 22.7 us -> 15.3 us  [hop(): return lax.ppermute(value, 'tile', [p for p in pairs if 0 <= p[1] < tiles])]
    unnamed x39 -> x34, local copies, waits for them, and re-layouts: 2.29 us -> 8.24 us
    ppermute x8 -> x6, waiting for transfers between devices: 0.02 us -> 5.7 us  [hop(): return lax.ppermute(value, 'tile', [p for p in pairs if 0 <= p[1] < tiles])]
    ppermute x3, waiting for transfers between devices: 8.72 us -> 13.6 us  [sum_over_tiles(): value = value + lax.ppermute(value.astype(BF16), 'tile', pairs).astype(F32)]
  transfers between devices with their start and end apart: 26 -> 18, of which waited for: 6 -> 3; matrix products, arithmetic and copies ran while one was open for 6% -> 12% of each run, Pallas kernels for 33% -> 33%
where the time goes in v2:
time: 171 us; the launch traced here: 170 us
  Pallas kernels  81.4 us (48%)
  starting transfers between devices  38 us (22%)
  local copies, waits for them, and re-layouts  24.9 us (15%)
  waiting for transfers between devices  23.2 us (14%)
    pallas_call x2, Pallas kernels, run_temporal(): pl.pallas_call(functools.partial(temporal_kernel, tuple(places), inside,...  55.3 us
    pallas_call x3, Pallas kernels, run_forward(): pl.pallas_call(forward_kernel, name='conv_forward', out_shape=(sds((count...  16.9 us
    ppermute x6, starting transfers between devices, hop(): return lax.ppermute(value, 'tile', [p for p in pairs if 0 <= p[1] < tiles])  15.3 us
    ppermute x3, waiting for transfers between devices, sum_over_tiles(): value = value + lax.ppermute(value.astype(BF16), 'tile', pairs).astype(F32)  13.6 us
    pallas_call x2, Pallas kernels, run_backward(): pl.pallas_call(functools.partial(backward_kernel, aliased), name='conv_ba...  9.25 us
    unnamed x34, local copies, waits for them, and re-layouts  8.24 us
    ppermute x4, starting transfers between devices, swap(): return lax.ppermute(value, 'tile', pairs)  7.13 us
    ppermute x6, waiting for transfers between devices, hop(): return lax.ppermute(value, 'tile', [p for p in pairs if 0 <= p[1] < tiles])  5.7 us
  transfers between devices with their start and end apart: 18, of which 3 were waited for; matrix products, arithmetic and copies ran while one was open for 12% of the time, Pallas kernels for 33%

profile of v2, /device:TPU:0, one launch (start us, length us, event | category | flops | bytes accessed | tf_op | source)
XLA Modules:
  0.0 170.0 jit_solution(3371487773694281549)
XLA Ops:
  0.7 1.4 copy_bitcast_fusion
  2.1 0.9 slice_bitcast_fusion
  3.0 3.0 %collective-permute-start = (bf16[4,64,8,128]{3,2,1,0:T(8,128)(2,1)}, bf16[4,64,8,128]{3,2,1,0:T(8,128)(2,1)S(1)}, u32[]{:S(2)}, u32[]{:S(2)}) collective-permute-start(bf16[4,64,8,128]{3,2,1,0:T(8,128)(2,1)} %get-tuple-element.53), channel_id=1, source_target_pairs={{0,4},{4,0},{8,12},{12,8},{16,20},{20,16},{24,28},{28,24},{1,5},{5... | collective-permute-start | bytes 1572872 | tf_op jit(solution)/shard_map/ppermute | solution.py:442
  6.0 7.8 %conv_forward.3 = (bf16[2,4,64,1024]{3,2,1,0:T(8,128)(2,1)}, bf16[2,4,64,1024]{3,2,1,0:T(8,128)(2,1)}, bf16[2,4,192,1024]{3,2,1,0:T(8,128)(2,1)}) custom-call(s32[1]{0:T(128)} %bitcast.20.meta_ref, bf16[4,64,4,8,128]{4,3,2,1,0:T(8,128)(2,1)} %bitcast.74, bf16[9,64,64]{2,1,0:T(8,128)(2,1)} %w_ref.5), custom_call_target="tpu_custom_call" | custom-call | flops 1000 | bytes 1000 | tf_op jit(solution)/shard_map/conv_forward/pallas_call | solution.py:87
  13.8 1.3 collective-permute-start.1
  15.0 1.9 %constant_dynamic-slice_fusion.3 = bf16[2,2,64,1024]{3,2,1,0:T(8,128)(2,1)} fusion(bf16[2,4,64,1024]{3,2,1,0:T(8,128)(2,1)} %get-tuple-element.20.rest_0_, s32[]{:T(128)S(6)} %select_n.141), kind=kLoop, calls=%fused_computation.42 | loop fusion | bytes 1048580 | tf_op jit(solution)/shard_map/dynamic_slice | solution.py:468
  16.9 4.6 %collective-permute-start.2 = (bf16[2,2,64,1024]{3,2,1,0:T(8,128)(2,1)}, bf16[2,2,64,1024]{3,2,1,0:T(8,128)(2,1)S(1)}, u32[]{:S(2)}, u32[]{:S(2)}) collective-permute-start(bf16[2,2,64,1024]{3,2,1,0:T(8,128)(2,1)} %constant_dynamic-slice_fusion.3), channel_id=1, source_target_pairs={{0,8},{8,16},{12,4},{16,24},{20,12},{28,20},{1,9},{9,17},{13,5},{1... | collective-permute-start | bytes 1572872 | tf_op jit(solution)/shard_map/ppermute | solution.py:446
  21.5 0.6 constant_dynamic-update-slice_fusion.7
  22.1 0.6 constant_dynamic-update-slice_fusion.6
  22.7 0.6 constant_dynamic-update-slice_fusion.5
  23.3 0.6 constant_dynamic-update-slice_fusion.4
  24.0 0.6 constant_dynamic-update-slice_fusion.3
  24.6 0.6 constant_dynamic-update-slice_fusion.2
  25.2 0.6 constant_dynamic-update-slice_fusion.1
  25.8 0.6 constant_dynamic-update-slice_fusion
  26.4 4.8 %all-to-all-start = ((bf16[8,14,512]{2,1,0:T(8,128)(2,1)}), bf16[8,14,512]{2,1,0:T(8,128)(2,1)}, u32[]{:S(2)}, u32[]{:S(2)}) async-start(bf16[8,14,512]{2,1,0:T(8,128)(2,1)} %constant_dynamic-update-slice_fusion), calls=%async_computation | async-start | bytes 262144 | tf_op jit(solution)/shard_map/all_to_all | solution.py:472
  31.2 2.0 %collective-permute-start.5 = (bf16[4,64,8,128]{3,2,1,0:T(8,128)(2,1)S(1)}, bf16[4,64,8,128]{3,2,1,0:T(8,128)(2,1)S(1)}, u32[]{:S(2)}, u32[]{:S(2)}) collective-permute-start(bf16[4,64,8,128]{3,2,1,0:T(8,128)(2,1)S(1)} %get-tuple-element.52), channel_id=1, source_target_pairs={{0,4},{4,0},{8,12},{12,8},{16,20},{20,16},{24,28},{28,24},{1,5},{5... | collective-permute-start | bytes 1572872 | tf_op jit(solution)/shard_map/ppermute | solution.py:442
  33.4 0.2 copy.56
  33.6 0.2 reshape.68.wb_ref
  33.8 1.0 copy.54
  34.8 0.1 copy.59.wt_ref
  34.9 1.0 copy.60.wtb_ref
  35.9 0.1 copy.61.whc_ref
  36.0 0.1 stack.69.meta_ref
  36.2 0.6 pad_add_fusion
  36.8 0.8 copy-done.9
  37.6 4.5 %conv_forward.4 = (bf16[1,4,64,1024]{3,2,1,0:T(8,128)(2,1)}, bf16[1,4,64,1024]{3,2,1,0:T(8,128)(2,1)}, bf16[1,4,192,1024]{3,2,1,0:T(8,128)(2,1)}) custom-call(s32[1]{0:T(128)} %constant.136.clone.1.meta_ref, bf16[4,64,1,8,128]{4,3,2,1,0:T(8,128)(2,1)} %bitcast.84, bf16[9,64,64]{2,1,0:T(8,128)(2,1)} %w_ref.5), custom_call_target="tpu_custom_call" | custom-call | flops 1000 | bytes 1000 | tf_op jit(solution)/shard_map/conv_forward/pallas_call | solution.py:87
  42.1 4.3 %collective-permute-start.3 = (bf16[1,4,64,1024]{3,2,1,0:T(8,128)(2,1)}, bf16[1,4,64,1024]{3,2,1,0:T(8,128)(2,1)}, u32[]{:S(2)}, u32[]{:S(2)}) collective-permute-start(bf16[1,4,64,1024]{3,2,1,0:T(8,128)(2,1)} %get-tuple-element.21.rest_1_), channel_id=1, source_target_pairs={{0,8},{8,16},{12,4},{16,24},{20,12},{28,20},{1,9},{9,17},{13,5},{1... | collective-permute-start | bytes 1572872 | tf_op jit(solution)/shard_map/ppermute | solution.py:446
  46.4 0.8 copy-done.10
  47.2 4.6 %conv_forward.5 = (bf16[1,4,64,1024]{3,2,1,0:T(8,128)(2,1)}, bf16[1,4,64,1024]{3,2,1,0:T(8,128)(2,1)}, bf16[1,4,192,1024]{3,2,1,0:T(8,128)(2,1)}) custom-call(s32[1]{0:T(128)} %constant.136.clone.1.meta_ref, bf16[4,64,1,8,128]{4,3,2,1,0:T(8,128)(2,1)} %bitcast.85, bf16[9,64,64]{2,1,0:T(8,128)(2,1)} %w_ref.5), custom_call_target="tpu_custom_call" | custom-call | flops 1000 | bytes 1000 | tf_op jit(solution)/shard_map/conv_forward/pallas_call | solution.py:87
  51.7 2.6 %collective-permute-start.6 = (bf16[1,4,64,1024]{3,2,1,0:T(8,128)(2,1)}, bf16[1,4,64,1024]{3,2,1,0:T(8,128)(2,1)S(1)}, u32[]{:S(2)}, u32[]{:S(2)}) collective-permute-start(bf16[1,4,64,1024]{3,2,1,0:T(8,128)(2,1)} %get-tuple-element.28.rest_1_), channel_id=1, source_target_pairs={{0,8},{8,16},{12,4},{16,24},{20,12},{28,20},{1,9},{9,17},{13,5},{1... | collective-permute-start | bytes 1572872 | tf_op jit(solution)/shard_map/ppermute | solution.py:446
  54.4 1.7 constant_dynamic-slice_fusion.2
  56.0 1.3 collective-permute-start.4
  57.3 1.7 constant_dynamic-slice_fusion.1
  59.0 1.3 collective-permute-start.7
  60.3 0.9 dynamic-slice_bitcast_fusion.1
  61.3 0.1 slice_bitcast_fusion.3
  61.4 5.7 %collective-permute-done.4.rest_5_ = bf16[1,2,64,1024]{3,2,1,0:T(8,128)(2,1)S(1)} collective-permute-done((bf16[1,2,64,1024]{3,2,1,0:T(8,128)(2,1)}, bf16[1,2,64,1024]{3,2,1,0:T(8,128)(2,1)S(1)}, u32[]{:S(2)}, u32[]{:S(2)}) %collective-permute-start.4) | collective-permute-done | bytes 262176 | tf_op jit(solution)/shard_map/ppermute | solution.py:446
  67.1 1.0 copy-done.3
  68.1 29.2 %temporal.2 = (f32[14,1,1024]{2,1,0:T(1,128)S(1)}, bf16[8,512,128]{2,1,0:T(8,128)(2,1)}, f32[6,64,192]{2,1,0:T(8,128)S(1)}) custom-call(s32[7]{0:T(128)S(1)} %stack.69.meta_ref, f32[14]{0:T(128)S(1)} %pad_dynamic-slice_fusion.weight_ref, bf16[2,64,192]{2,1,0:T(8,128)(2,1)S(1)} %copy.59.wt_ref, bf16[2,64,192]{2,1,0:T(8,128)(2,1)S(1)} %copy.60.wtb_ref, ...), custom_call_target="tpu_custom_call" | custom-call | flops 1000 | bytes 1000 | tf_op jit(solution)/shard_map/temporal/pallas_call | solution.py:344
  97.3 0.8 copy-done.8
  98.1 26.1 %temporal.3 = (f32[14,1,1024]{2,1,0:T(1,128)S(1)}, bf16[8,64,1024]{2,1,0:T(8,128)(2,1)}, f32[6,64,192]{2,1,0:T(8,128)S(1)}) custom-call(s32[7]{0:T(128)S(1)} %stack.69.meta_ref, f32[14]{0:T(128)S(1)} %pad_dynamic-slice_fusion.weight_ref, bf16[2,64,192]{2,1,0:T(8,128)(2,1)S(1)} %copy.59.wt_ref, bf16[2,64,192]{2,1,0:T(8,128)(2,1)S(1)} %copy.60.wtb_ref, ...), custom_call_target="tpu_custom_call" | custom-call | flops 1000 | bytes 1000 | tf_op jit(solution)/shard_map/temporal/pallas_call | solution.py:344
  124.3 1.6 collective-permute-start.11
  125.9 1.4 collective-permute-start.12
  127.4 4.6 %conv_backward.3 = bf16[4,64,1,8,128]{4,3,2,1,0:T(8,128)(2,1)} custom-call(s32[2]{0:T(128)} %get-tuple-element.63.meta_ref, bf16[8,64,1024]{2,1,0:T(8,128)(2,1)} %get-tuple-element.32.dpre_ref, bf16[192,192]{1,0:T(8,128)(2,1)} %copy-done), custom_call_target="tpu_custom_call" | custom-call | flops 1000 | bytes 1000 | tf_op jit(solution)/shard_map/conv_backward/pallas_call | solution.py:128
  132.0 2.0 %collective-permute-start.9 = (bf16[4,64,1,8,128]{4,3,2,1,0:T(8,128)(2,1)}, bf16[4,64,1,8,128]{4,3,2,1,0:T(8,128)(2,1)S(1)}, u32[]{:S(2)}, u32[]{:S(2)}) collective-permute-start(bf16[4,64,1,8,128]{4,3,2,1,0:T(8,128)(2,1)} %conv_backward.3), channel_id=1, source_target_pairs={{0,4},{4,0},{8,12},{12,8},{16,20},{20,16},{24,28},{28,24},{1,5},{5... | collective-permute-start | bytes 1572872 | tf_op jit(solution)/shard_map/ppermute | solution.py:442
  134.0 0.1 fusion.2
  134.1 0.1 fusion.3
  134.3 0.1 collective-permute-start.13
  134.4 4.6 %conv_backward.2 = bf16[4,64,4,8,128]{4,3,2,1,0:T(8,128)(2,1)} custom-call(s32[2]{0:T(128)} %get-tuple-element.62.meta_ref, bf16[8,64,1024]{2,1,0:T(8,128)(2,1)} %get-tuple-element.32.dpre_ref, bf16[192,192]{1,0:T(8,128)(2,1)} %copy-done), custom_call_target="tpu_custom_call" | custom-call | flops 1000 | bytes 1000 | tf_op jit(solution)/shard_map/conv_backward/pallas_call | solution.py:128
  139.0 13.5 %collective-permute-done.13 = bf16[6,16,192]{2,1,0:T(8,128)(2,1)S(1)} collective-permute-done((bf16[6,16,192]{2,1,0:T(8,128)(2,1)S(1)}, bf16[6,16,192]{2,1,0:T(8,128)(2,1)S(1)}, u32[]{:S(2)}, u32[]{:S(2)}) %collective-permute-start.13) | collective-permute-done | bytes 36896 | tf_op jit(solution)/shard_map/ppermute | solution.py:405
  152.6 1.2 collective-permute-start.14
  153.8 0.7 copy.67
  154.5 3.5 %all-to-all-start.1 = ((bf16[8,8,512]{2,1,0:T(8,128)(2,1)}), bf16[8,8,512]{2,1,0:T(8,128)(2,1)S(1)}, u32[]{:S(2)}, u32[]{:S(2)}) async-start(bf16[8,8,512]{2,1,0:T(8,128)(2,1)} %copy.67), calls=%async_computation.1 | async-start | bytes 131072 | tf_op jit(solution)/shard_map/all_to_all | solution.py:559
  158.0 3.0 %collective-permute-start.15 = (bf16[6,16,192]{2,1,0:T(8,128)(2,1)S(1)}, bf16[6,16,192]{2,1,0:T(8,128)(2,1)S(1)}, u32[]{:S(2)}, u32[]{:S(2)}) collective-permute-start(bf16[6,16,192]{2,1,0:T(8,128)(2,1)S(1)} %fusion.1), channel_id=1, source_target_pairs={{0,16},{4,20},{8,24},{12,28},{16,0},{20,4},{24,8},{28,12},{1,17},{... | collective-permute-start | bytes 110600 | tf_op jit(solution)/shard_map/ppermute | solution.py:405
  160.9 3.9 %all-to-all-done.1 = bf16[8,8,512]{2,1,0:T(8,128)(2,1)S(1)} async-done(((bf16[8,8,512]{2,1,0:T(8,128)(2,1)}), bf16[8,8,512]{2,1,0:T(8,128)(2,1)S(1)}, u32[]{:S(2)}, u32[]{:S(2)}) %all-to-all-start.1) | async-done | bytes 65568 | tf_op jit(solution)/shard_map/all_to_all | solution.py:559
  164.8 0.6 dynamic-slice_bitcast_fusion.2
  165.6 0.6 fusion.6
  166.2 0.1 reshape.73
  166.2 0.6 copy.69
  166.9 0.6 pad_maximum_fusion
  167.5 0.8 bitcast_dynamic-update-slice_fusion.1
  168.3 0.8 dynamic-slice_dynamic-update-slice_fusion
  169.2 0.8 bitcast_dynamic-update-slice_fusion
  (58 shorter events, 0.7 us)
Async XLA Ops:
  2.9 18.6 %copy-start.6 = (bf16[1,32,512]{2,1,0:T(8,128)(2,1)S(1)}, bf16[1,32,512]{2,1,0:T(8,128)(2,1)}, u32[]{:S(2)}) copy-start(bf16[1,32,512]{2,1,0:T(8,128)(2,1)} %param.10) | copy-start | bytes 98308
  2.9 30.3 %copy-start.11 = (s32[1,32]{1,0:T(1,128)S(1)}, s32[1,32]{1,0:T(1,128)}, u32[]{:S(2)}) copy-start(s32[1,32]{1,0:T(1,128)} %param.11) | copy-start | bytes 388
  3.0 30.3 %copy-start.12 = (bf16[64]{0:T(256)(128)(2,1)S(1)}, bf16[64]{0:T(256)(128)(2,1)}, u32[]{:S(2)}) copy-start(bf16[64]{0:T(256)(128)(2,1)} %param.9) | copy-start | bytes 388
  3.0 30.5 %copy-start.4 = (bf16[9,64,64]{2,1,0:T(8,128)(2,1)S(1)}, bf16[9,64,64]{2,1,0:T(8,128)(2,1)}, u32[]{:S(2)}) copy-start(bf16[9,64,64]{2,1,0:T(8,128)(2,1)} %w_ref.5) | copy-start | bytes 221188
  3.0 33.8 %collective-permute-start = (bf16[4,64,8,128]{3,2,1,0:T(8,128)(2,1)}, bf16[4,64,8,128]{3,2,1,0:T(8,128)(2,1)S(1)}, u32[]{:S(2)}, u32[]{:S(2)}) collective-permute-start(bf16[4,64,8,128]{3,2,1,0:T(8,128)(2,1)} %get-tuple-element.53), channel_id=1, source_target_pairs={{0,4},{4,0},{8,12},{12,8},{16,20},{20,16},{24,28},{28,24},{1,5},{5... | collective-permute-start | bytes 1572872 | tf_op jit(solution)/shard_map/ppermute | solution.py:442
  13.8 53.3 %collective-permute-start.1 = (bf16[2,4,64,1024]{3,2,1,0:T(8,128)(2,1)}, bf16[2,4,64,1024]{3,2,1,0:T(8,128)(2,1)S(1)}, u32[]{:S(2)}, u32[]{:S(2)}) collective-permute-start(bf16[2,4,64,1024]{3,2,1,0:T(8,128)(2,1)} %get-tuple-element.20.rest_0_), channel_id=1, source_target_pairs={{4,12},{8,0},{12,20},{16,8},{20,28},{24,16},{5,13},{9,1},{13,21},{... | collective-permute-start | bytes 3145736 | tf_op jit(solution)/shard_map/ppermute | solution.py:446
  16.9 42.1 %collective-permute-start.2 = (bf16[2,2,64,1024]{3,2,1,0:T(8,128)(2,1)}, bf16[2,2,64,1024]{3,2,1,0:T(8,128)(2,1)S(1)}, u32[]{:S(2)}, u32[]{:S(2)}) collective-permute-start(bf16[2,2,64,1024]{3,2,1,0:T(8,128)(2,1)} %constant_dynamic-slice_fusion.3), channel_id=1, source_target_pairs={{0,8},{8,16},{12,4},{16,24},{20,12},{28,20},{1,9},{9,17},{13,5},{1... | collective-permute-start | bytes 1572872 | tf_op jit(solution)/shard_map/ppermute | solution.py:446
  26.4 33.9 %all-to-all-start = ((bf16[8,14,512]{2,1,0:T(8,128)(2,1)}), bf16[8,14,512]{2,1,0:T(8,128)(2,1)}, u32[]{:S(2)}, u32[]{:S(2)}) async-start(bf16[8,14,512]{2,1,0:T(8,128)(2,1)} %constant_dynamic-update-slice_fusion), calls=%async_computation | async-start | bytes 262144 | tf_op jit(solution)/shard_map/all_to_all | solution.py:472
  31.2 15.2 %collective-permute-start.5 = (bf16[4,64,8,128]{3,2,1,0:T(8,128)(2,1)S(1)}, bf16[4,64,8,128]{3,2,1,0:T(8,128)(2,1)S(1)}, u32[]{:S(2)}, u32[]{:S(2)}) collective-permute-start(bf16[4,64,8,128]{3,2,1,0:T(8,128)(2,1)S(1)} %get-tuple-element.52), channel_id=1, source_target_pairs={{0,4},{4,0},{8,12},{12,8},{16,20},{20,16},{24,28},{28,24},{1,5},{5... | collective-permute-start | bytes 1572872 | tf_op jit(solution)/shard_map/ppermute | solution.py:442
  33.8 63.5 %copy-start = (bf16[192,192]{1,0:T(8,128)(2,1)}, bf16[192,192]{1,0:T(8,128)(2,1)S(1)}, u32[]{:S(2)}) copy-start(bf16[192,192]{1,0:T(8,128)(2,1)S(1)} %reshape.68.wb_ref) | copy-start | bytes 221188
  36.8 0.8 copy-start.9
  42.1 26.0 %copy-start.2 = (bf16[1,4,64,1024]{3,2,1,0:T(8,128)(2,1)S(1)}, bf16[1,4,64,1024]{3,2,1,0:T(8,128)(2,1)}, u32[]{:S(2)}) copy-start(bf16[1,4,64,1024]{3,2,1,0:T(8,128)(2,1)} %get-tuple-element.21.rest_1_) | copy-start | bytes 1572868
  42.1 25.0 %collective-permute-start.3 = (bf16[1,4,64,1024]{3,2,1,0:T(8,128)(2,1)}, bf16[1,4,64,1024]{3,2,1,0:T(8,128)(2,1)}, u32[]{:S(2)}, u32[]{:S(2)}) collective-permute-start(bf16[1,4,64,1024]{3,2,1,0:T(8,128)(2,1)} %get-tuple-element.21.rest_1_), channel_id=1, source_target_pairs={{0,8},{8,16},{12,4},{16,24},{20,12},{28,20},{1,9},{9,17},{13,5},{1... | collective-permute-start | bytes 1572872 | tf_op jit(solution)/shard_map/ppermute | solution.py:446
  46.4 0.8 copy-start.10
  51.7 45.5 %collective-permute-start.6 = (bf16[1,4,64,1024]{3,2,1,0:T(8,128)(2,1)}, bf16[1,4,64,1024]{3,2,1,0:T(8,128)(2,1)S(1)}, u32[]{:S(2)}, u32[]{:S(2)}) collective-permute-start(bf16[1,4,64,1024]{3,2,1,0:T(8,128)(2,1)} %get-tuple-element.28.rest_1_), channel_id=1, source_target_pairs={{0,8},{8,16},{12,4},{16,24},{20,12},{28,20},{1,9},{9,17},{13,5},{1... | collective-permute-start | bytes 1572872 | tf_op jit(solution)/shard_map/ppermute | solution.py:446
  56.0 11.0 %collective-permute-start.4 = (bf16[1,2,64,1024]{3,2,1,0:T(8,128)(2,1)}, bf16[1,2,64,1024]{3,2,1,0:T(8,128)(2,1)S(1)}, u32[]{:S(2)}, u32[]{:S(2)}) collective-permute-start(bf16[1,2,64,1024]{3,2,1,0:T(8,128)(2,1)} %constant_dynamic-slice_fusion.2), channel_id=1, source_target_pairs={{4,12},{8,0},{12,20},{16,8},{20,28},{24,16},{5,13},{9,1},{13,21},{... | collective-permute-start | bytes 786440 | tf_op jit(solution)/shard_map/ppermute | solution.py:446
  59.0 8.1 %copy-start.5 = (bf16[2,2,64,1024]{3,2,1,0:T(8,128)(2,1)}, bf16[2,2,64,1024]{3,2,1,0:T(8,128)(2,1)S(1)}, u32[]{:S(2)}) copy-start(bf16[2,2,64,1024]{3,2,1,0:T(8,128)(2,1)S(1)} %collective-permute-done.2.rest_3_) | copy-start | bytes 1572868
  59.0 38.2 %collective-permute-start.7 = (bf16[1,2,64,1024]{3,2,1,0:T(8,128)(2,1)}, bf16[1,2,64,1024]{3,2,1,0:T(8,128)(2,1)S(1)}, u32[]{:S(2)}, u32[]{:S(2)}) collective-permute-start(bf16[1,2,64,1024]{3,2,1,0:T(8,128)(2,1)} %constant_dynamic-slice_fusion.1), channel_id=1, source_target_pairs={{4,12},{8,0},{12,20},{16,8},{20,28},{24,16},{5,13},{9,1},{13,21},{... | collective-permute-start | bytes 786440 | tf_op jit(solution)/shard_map/ppermute | solution.py:446
  67.1 1.0 copy-start.3
  68.1 30.0 %copy-start.1 = (bf16[1,4,64,1024]{3,2,1,0:T(8,128)(2,1)S(1)}, bf16[1,4,64,1024]{3,2,1,0:T(8,128)(2,1)}, u32[]{:S(2)}) copy-start(bf16[1,4,64,1024]{3,2,1,0:T(8,128)(2,1)} %get-tuple-element.28.rest_1_) | copy-start | bytes 1572868
  97.3 0.8 copy-start.8
  98.1 29.2 %copy-start.7 = (bf16[8,512,128]{2,1,0:T(8,128)(2,1)S(1)}, bf16[8,512,128]{2,1,0:T(8,128)(2,1)}, u32[]{:S(2)}) copy-start(bf16[8,512,128]{2,1,0:T(8,128)(2,1)} %get-tuple-element.33) | copy-start | bytes 3145732
  124.2 10.0 %collective-permute-start.10 = (bf16[6,16,192]{2,1,0:T(8,128)(2,1)S(1)}, bf16[6,16,192]{2,1,0:T(8,128)(2,1)S(1)}, u32[]{:S(2)}, u32[]{:S(2)}) collective-permute-start(bf16[6,16,192]{2,1,0:T(8,128)(2,1)S(1)} %get-tuple-element.54), channel_id=1, source_target_pairs={{0,1},{1,2},{2,3},{3,0},{4,5},{5,6},{6,7},{7,4},{8,9},{9,10},{10,1... | collective-permute-start | bytes 110600 | tf_op jit(solution)/shard_map/ppermute | solution.py:421
  124.3 9.9 %collective-permute-start.11 = (bf16[6,16,192]{2,1,0:T(8,128)(2,1)S(1)}, bf16[6,16,192]{2,1,0:T(8,128)(2,1)S(1)}, u32[]{:S(2)}, u32[]{:S(2)}) collective-permute-start(bf16[6,16,192]{2,1,0:T(8,128)(2,1)S(1)} %get-tuple-element.56), channel_id=1, source_target_pairs={{0,2},{1,3},{2,0},{3,1},{4,6},{5,7},{6,4},{7,5},{8,10},{9,11},{10,... | collective-permute-start | bytes 110600 | tf_op jit(solution)/shard_map/ppermute | solution.py:421
  125.9 8.4 %collective-permute-start.12 = (bf16[6,16,192]{2,1,0:T(8,128)(2,1)S(1)}, bf16[6,16,192]{2,1,0:T(8,128)(2,1)S(1)}, u32[]{:S(2)}, u32[]{:S(2)}) collective-permute-start(bf16[6,16,192]{2,1,0:T(8,128)(2,1)S(1)} %get-tuple-element.55), channel_id=1, source_target_pairs={{0,3},{1,0},{2,1},{3,2},{4,7},{5,4},{6,5},{7,6},{8,11},{9,8},{10,9... | collective-permute-start | bytes 110600 | tf_op jit(solution)/shard_map/ppermute | solution.py:421
  127.3 40.2 %collective-permute-start.8 = (bf16[4,64,1,8,128]{4,3,1,0,2:T(8,128)(2,1)S(1)}, bf16[4,64,1,8,128]{4,3,1,0,2:T(8,128)(2,1)S(1)}, u32[]{:S(2)}, u32[]{:S(2)}) collective-permute-start(bf16[4,64,1,8,128]{4,3,1,0,2:T(8,128)(2,1)S(1)} %dynamic-slice_bitcast_fusion), channel_id=1, source_target_pairs={{0,4},{4,0},{8,12},{12,8},{16,20},{20,16},{24,28},{28,24},{1,5},{5... | collective-permute-start | bytes 1572872 | tf_op jit(solution)/shard_map/ppermute | solution.py:442
  132.0 37.2 %collective-permute-start.9 = (bf16[4,64,1,8,128]{4,3,2,1,0:T(8,128)(2,1)}, bf16[4,64,1,8,128]{4,3,2,1,0:T(8,128)(2,1)S(1)}, u32[]{:S(2)}, u32[]{:S(2)}) collective-permute-start(bf16[4,64,1,8,128]{4,3,2,1,0:T(8,128)(2,1)} %conv_backward.3), channel_id=1, source_target_pairs={{0,4},{4,0},{8,12},{12,8},{16,20},{20,16},{24,28},{28,24},{1,5},{5... | collective-permute-start | bytes 1572872 | tf_op jit(solution)/shard_map/ppermute | solution.py:442
  134.3 18.3 %collective-permute-start.13 = (bf16[6,16,192]{2,1,0:T(8,128)(2,1)S(1)}, bf16[6,16,192]{2,1,0:T(8,128)(2,1)S(1)}, u32[]{:S(2)}, u32[]{:S(2)}) collective-permute-start(bf16[6,16,192]{2,1,0:T(8,128)(2,1)S(1)} %get-tuple-element.50), channel_id=1, source_target_pairs={{0,4},{4,0},{8,12},{12,8},{16,20},{20,16},{24,28},{28,24},{1,5},{5... | collective-permute-start | bytes 110600 | tf_op jit(solution)/shard_map/ppermute | solution.py:405
  152.6 5.3 %collective-permute-start.14 = (bf16[6,16,192]{2,1,0:T(8,128)(2,1)S(1)}, bf16[6,16,192]{2,1,0:T(8,128)(2,1)S(1)}, u32[]{:S(2)}, u32[]{:S(2)}) collective-permute-start(bf16[6,16,192]{2,1,0:T(8,128)(2,1)S(1)} %fusion), channel_id=1, source_target_pairs={{0,8},{4,12},{8,0},{12,4},{16,24},{20,28},{24,16},{28,20},{1,9},{5... | collective-permute-start | bytes 110600 | tf_op jit(solution)/shard_map/ppermute | solution.py:405
  154.5 10.4 %all-to-all-start.1 = ((bf16[8,8,512]{2,1,0:T(8,128)(2,1)}), bf16[8,8,512]{2,1,0:T(8,128)(2,1)S(1)}, u32[]{:S(2)}, u32[]{:S(2)}) async-start(bf16[8,8,512]{2,1,0:T(8,128)(2,1)} %copy.67), calls=%async_computation.1 | async-start | bytes 131072 | tf_op jit(solution)/shard_map/all_to_all | solution.py:559
  158.0 7.5 %collective-permute-start.15 = (bf16[6,16,192]{2,1,0:T(8,128)(2,1)S(1)}, bf16[6,16,192]{2,1,0:T(8,128)(2,1)S(1)}, u32[]{:S(2)}, u32[]{:S(2)}) collective-permute-start(bf16[6,16,192]{2,1,0:T(8,128)(2,1)S(1)} %fusion.1), channel_id=1, source_target_pairs={{0,16},{4,20},{8,24},{12,28},{16,0},{20,4},{24,8},{28,12},{1,17},{... | collective-permute-start | bytes 110600 | tf_op jit(solution)/shard_map/ppermute | solution.py:405

commit v3 on v2

--- a/solution.py
+++ b/solution.py
@@ -58,7 +58,8 @@
     return result
 
 
-def forward_kernel(meta_ref, x_ref, w_ref, feat_ref, slope_ref, xs_ref, xt, wf):
+def forward_kernel(middle, meta_ref, x_ref, w_ref, feat_ref, slope_ref, xc_ref, *rest):
+    xt, xs, wf = rest[-3:]
     _, chans, _, rows, width = x_ref.shape
 
     @pl.when((pl.program_id(0) == 0) & (pl.program_id(1) == 0))
@@ -68,30 +69,43 @@
                 wf[i * chans : (i + 1) * chans, j * chans : (j + 1) * chans] = w_ref[3 * i + j]
 
     xt[...] = x_ref[0, :, 0].astype(F32).reshape(chans * rows, width)
-    dst = xs_ref.at[0, 0]
     for r in range(rows):
-        spread(xt[pl.ds(r, chans, stride=rows), :], dst, r, 1)
-    for r, pre in enumerate(conv_rows(wf, dst, 1, rows, chans, width)):
+        row = xt[pl.ds(r, chans, stride=rows), :]
+        spread(row, xs, r, 1)
+        xc_ref[0, 0, :, r * width : (r + 1) * width] = row.astype(BF16)
+    for r, pre in enumerate(conv_rows(wf, xs, 1, rows, chans, width)):
         cols = slice(r * width, (r + 1) * width)
         s = sigmoid(pre)
         y = pre * s
         feat_ref[0, 0, :, cols] = y.astype(BF16)
         slope_ref[0, 0, :, cols] = (s + y * (1.0 - s)).astype(BF16)
-
-
-def run_forward(first, count, x, w_spatial):
+    if middle:
+        spot = pl.program_id(1) - meta_ref[1]
+
+        @pl.when((spot >= 0) & (spot < middle))
+        def _():
+            rest[0][0, 0] = feat_ref[0, 0]
+
+
+def run_forward(first, start, middle, count, x, w_spatial):
     n, chans, _, rows, width = x.shape
     vox = rows * width
     sds = jax.ShapeDtypeStruct
-    result = lambda c: pl.BlockSpec((1, 1, c, vox), lambda k, f, meta: (k, f, 0, 0))
+    shapes = [sds((count, n, chans, vox), BF16)] * 3
+    specs = [pl.BlockSpec((1, 1, chans, vox), lambda k, f, meta: (k, f, 0, 0))] * 3
+    if middle:
+        shapes.append(sds((count, middle, chans, vox), BF16))
+        specs.append(
+            pl.BlockSpec(
+                (1, 1, chans, vox),
+                lambda k, f, meta: (k, jnp.clip(f - meta[1], 0, middle - 1), 0, 0),
+            )
+        )
+    meta = jnp.stack([jnp.asarray(v, jnp.int32) for v in (first, start)])
     return pl.pallas_call(
-        forward_kernel,
+        functools.partial(forward_kernel, middle),
         name="conv_forward",
-        out_shape=(
-            sds((count, n, chans, vox), BF16),
-            sds((count, n, chans, vox), BF16),
-            sds((count, n, 3 * chans, vox), BF16),
-        ),
+        out_shape=shapes,
         grid_spec=pltpu.PrefetchScalarGridSpec(
             num_scalar_prefetch=1,
             grid=(count, n),
@@ -101,14 +115,15 @@
                 ),
                 pl.BlockSpec((9, chans, chans), lambda k, f, meta: (0, 0, 0)),
             ],
-            out_specs=[result(chans), result(chans), result(3 * chans)],
+            out_specs=specs,
             scratch_shapes=[
                 pltpu.VMEM((chans * rows, width), F32),
+                pltpu.VMEM((3 * chans, vox), BF16),
                 pltpu.VMEM((3 * chans, 3 * chans), BF16),
             ],
         ),
         cost_estimate=pl.CostEstimate(flops=1000, bytes_accessed=1000, transcendentals=0),
-    )(first, x, w_spatial)
+    )(meta, x, w_spatial)
 
 
 def backward_kernel(aliased, meta_ref, dpre_ref, wb_ref, *rest):
@@ -153,6 +168,7 @@
 def temporal_kernel(
     places,
     inside,
+    aliased,
     dims,
     meta_ref,
     weight_ref,
@@ -165,15 +181,19 @@
     *rest,
 ):
     own, chans, vox, total, members, width = dims
+    rows = vox // width
     here = own // members
     counts = len(places)
     pieces = [ref.at[k] for ref, k in zip(rest[:counts], places)]
     slope_in = [ref.at[k] for ref, k in zip(rest[counts : counts + members], places)]
     xs_in = [ref.at[k] for ref, k in zip(rest[counts + members : counts + 2 * members], places)]
+    rest = rest[counts + 2 * members + aliased :]
+    logit_ref, grad_ref = rest[:2]
+    if inside:
+        out_ref, send_ref, back = rest[2], rest[3], rest[-1]
+    else:
+        dpre_ref = rest[2]
     (
-        logit_ref,
-        back_ref,
-        grad_ref,
         feats,
         slope,
         xs,
@@ -186,13 +206,13 @@
         dh2,
         dm1,
         dm0,
-        dpre,
         final_ref,
         dlog,
         ds,
         xt,
+        tgt,
         sems,
-    ) = rest[counts + 2 * members :]
+    ) = rest[3 + inside : 21 + inside]
     step = min(256, vox)
     lo, hi = HALO, HALO + own
     first = meta_ref[0]
@@ -212,6 +232,8 @@
         )
     for copy in early + late:
         copy.start()
+    for c in range(tgt_ref.shape[0]):
+        tgt[:, c * tgt_ref.shape[2] : (c + 1) * tgt_ref.shape[2]] = tgt_ref[c].astype(F32)
     for copy in early:
         copy.wait()
 
@@ -255,6 +277,7 @@
 
     def layer1(f):
         weight = weight_ref[f - 3]
+        frame = jnp.clip(first + f - HALO, 0, total - 1)
         for cols in chunks:
             mixed = dot_nn(wt_ref[1], stack(n1, f - 2, f, f + 2, cols))
             s = sigmoid(mixed)
@@ -265,7 +288,7 @@
             final = unit.astype(BF16)
             logit = channel_sum(final.astype(F32) * whc_ref[...])
             logit_ref[f - 3, :, cols] = logit
-            dlogit = weight * (sigmoid(logit) - tgt_ref[f - 3, :, cols].astype(F32))
+            dlogit = weight * (sigmoid(logit) - tgt[pl.ds(frame, 1), cols])
             final_ref[f, :, cols] = final
             dlog[f, :, cols] = dlogit
             dhid = (inv * dlogit) * (whc_ref[...] - unit * (logit * (1.0 / chans)))
@@ -290,20 +313,29 @@
             mean = channel_sum(dnorm * unit) * (1.0 / chans)
             dhid = dh2[f, :, cols] + inv0[f, :, cols] * (dnorm - unit * mean)
             dfeat = dhid.astype(BF16).astype(F32)
-            dpre[b, :, cols] = (dfeat * slope[b, :, cols].astype(F32)).astype(BF16)
-
-    def weights(f):
-        b = f - HALO
-        center = dpre[b]
+            dpre = dfeat * slope[b, :, cols].astype(F32)
+            if not inside:
+                dpre_ref[b, :, cols] = dpre.astype(BF16)
+            dpre = dpre.astype(BF16).astype(F32)
+            for r in range(step // width):
+                spread(
+                    dpre[:, r * width : (r + 1) * width], ds, cols.start // width + r, -1
+                )
+        center = xs[b]
         blank = jnp.zeros((chans, width), BF16)
         taller = jnp.concatenate([center[:, width:], blank], axis=1)
         lower = jnp.concatenate([blank, center[:, :-width]], axis=1)
-        for i, rows in enumerate((taller, center, lower)):
-            grad_ref[i] += dot_nt(rows, xs[b])
+        grad = dot_nt(ds[...], jnp.concatenate([lower, center, taller], axis=0))
+        for j in range(3):
+            grad_ref[j] += grad[j * chans : (j + 1) * chans]
         grad_ref[3] += dot_nt(dm0[f], stack(n0, f - 1, f, f + 1, whole))
         grad_ref[4] += dot_nt(dm1[f], stack(n1, f - 2, f, f + 2, whole))
         head = jnp.broadcast_to(dlog[f].astype(BF16), (chans, vox))
         grad_ref[5, :, :chans] += dot_nt(head, final_ref[f])
+        if inside:
+            for r, row in enumerate(conv_rows(wb_ref, ds, -1, rows, chans, width)):
+                xt[pl.ds(r, chans, stride=rows), :] = row
+            back[b] = xt[...].astype(BF16).reshape(chans, rows, width)
 
     grad_ref[...] = init_ref[...]
     loop(0, hi + HALO, norm0)
@@ -313,50 +345,50 @@
     for copy in late:
         copy.wait()
     loop(lo, hi, back0)
-    loop(lo, hi, weights)
-
-    def inputs(b):
-        rows = vox // width
-        for r in range(rows):
-            spread(dpre[b, :, r * width : (r + 1) * width].astype(F32), ds, r, -1)
-        for r, row in enumerate(conv_rows(wb_ref, ds, -1, rows, chans, width)):
-            xt[pl.ds(r, chans, stride=rows), :] = row
-        back_ref[b] = xt[...].astype(BF16)
-
-    def hand_on(b):
-        back_ref[b] = dpre[b]
-
-    loop(0, own, inputs if inside else hand_on)
-
-
-def run_temporal(
-    meta, weights, wt, wtb, whc, tgt, init, wb, pieces, places, slopes, xss, inside, own, width, total
-):
-    members = len(slopes)
-    chans, vox = pieces[0].shape[2:]
+    if inside:
+        layer = meta_ref[1 + counts]
+        leaving = []
+        for k in range(members):
+            src = back.at[pl.ds(meta_ref[1 + k] - HALO, here)]
+            dst = send_ref.at[k - 1] if k else out_ref.at[:, :, layer]
+            leaving.append(pltpu.make_async_copy(src, dst, sems.at[k]))
+        for copy in leaving:
+            copy.start()
+        for copy in leaving:
+            copy.wait()
+
+
+def run_temporal(meta, vmem_args, weights, pieces, places, slopes, xss, inside, into, dims, layers):
+    own, chans, vox, total, members, width = dims
+    rows, here = vox // width, own // members
     every = own + 2 * HALO
     sds = jax.ShapeDtypeStruct
     smem = pl.BlockSpec(memory_space=pltpu.SMEM)
     vmem = pl.BlockSpec(memory_space=pltpu.VMEM)
     hbm = pl.BlockSpec(memory_space=pl.ANY)
     loose = len(pieces) + 2 * members
+    aliased = into is not None
     frame = lambda n, c, dt: pltpu.VMEM((n, c, vox), dt)
+    shapes = [sds((own + 6, 1, vox), F32), sds((6, chans, 3 * chans), F32)]
+    specs = [vmem, vmem]
+    if inside:
+        shapes.append(sds((here, chans, layers, rows, width), BF16))
+        shapes.append(sds((members - 1, here, chans, rows, width), BF16))
+        specs += [hbm, hbm]
+    else:
+        shapes.append(sds((own, chans, vox), BF16))
+        specs.append(vmem)
     return pl.pallas_call(
-        functools.partial(
-            temporal_kernel, tuple(places), inside, (own, chans, vox, total, members, width)
-        ),
+        functools.partial(temporal_kernel, tuple(places), inside, aliased, dims),
         name="temporal",
-        out_shape=(
-            sds((own + 6, 1, vox), F32),
-            sds((own, chans * vox // width, width) if inside else (own, chans, vox), BF16),
-            sds((6, chans, 3 * chans), F32),
-        ),
-        in_specs=[smem, smem] + [vmem] * 6 + [hbm] * loose,
-        out_specs=[vmem] * 3,
+        out_shape=shapes,
+        in_specs=[smem, smem] + [vmem] * len(vmem_args) + [hbm] * (loose + aliased),
+        out_specs=specs,
+        input_output_aliases={2 + len(vmem_args) + loose: 2} if aliased else {},
         scratch_shapes=[
             frame(every, chans, BF16),
             frame(own, chans, BF16),
-            frame(own, 3 * chans, BF16),
+            frame(own, chans, BF16),
             frame(every, chans, BF16),
             frame(every, 1, F32),
             frame(every, chans, F32),
@@ -366,18 +398,19 @@
             frame(every, chans, F32),
             frame(every, chans, BF16),
             frame(every, chans, BF16),
-            frame(own, chans, BF16),
             frame(every, chans, BF16),
             frame(every, 1, F32),
             pltpu.VMEM((3 * chans, vox), BF16),
-            pltpu.VMEM((chans * vox // width, width), F32),
+            pltpu.VMEM((chans * rows, width), F32),
+            pltpu.VMEM((total, vox), F32),
             pltpu.SemaphoreType.DMA((loose,)),
-        ],
+        ]
+        + [pltpu.VMEM((own, chans, rows, width), BF16)] * inside,
         compiler_params=pltpu.CompilerParams(vmem_limit_bytes=VMEM_LIMIT),
         cost_estimate=pl.CostEstimate(
-            flops=1000, bytes_accessed=1000, transcendentals=0
+            flops=3000 * own * chans * vox, bytes_accessed=100 * own * chans * vox, transcendentals=0
         ),
-    )(meta, weights, wt, wtb, whc, tgt, init, wb, *pieces, *slopes, *xss)
+    )(meta, weights, *vmem_args, *pieces, *slopes, *xss, *([into] if aliased else []))
 
 
 def group_size(tiles, frames_here, layers):
@@ -396,15 +429,17 @@
     return lax.dynamic_index_in_dim(value, index, axis, False)
 
 
-def sum_over_tiles(value, tiles):
+def sum_over_tiles(value, tiles, others):
     if tiles & (tiles - 1):
-        return lax.psum(value.astype(BF16), "tile").astype(F32)
+        return lax.psum(value.astype(BF16), "tile").astype(F32), others
     k = 1
     while k < tiles:
+        if 2 * k >= tiles:
+            value, others = lax.optimization_barrier((value, others))
         pairs = [(a, a ^ k) for a in range(tiles)]
         value = value + lax.ppermute(value.astype(BF16), "tile", pairs).astype(F32)
         k *= 2
-    return value
+    return value, others
 
 
 def sum_over_reps(value, axis):
@@ -435,7 +470,6 @@
     spot = targets.shape[2]
     share = groups = tiles // g
     x = inputs[0]
-    apart = x.reshape(here, chans, g, per, rows, width)
 
     def swap(value, s):
         pairs = [(a, a // g * g + (a % g + s) % g) for a in range(tiles)]
@@ -444,11 +478,6 @@
     def hop(value, shifts):
         pairs = [(a, a + shifts[a % g] * g) for a in range(tiles)]
         return lax.ppermute(value, "tile", [p for p in pairs if 0 <= p[1] < tiles])
-
-    arriving = [
-        [swap(take(apart, (m + s) % g, 2)[:, :, layer], s) for s in range(1, g)]
-        for layer in range(per)
-    ]
 
     w9 = w_spatial.reshape(3, 3, chans, chans)
     wb = w9.transpose(0, 3, 1, 2).reshape(3 * chans, 3 * chans)
@@ -457,46 +486,55 @@
     whc = w_head.astype(F32)[:, None]
 
     index = (m * per).astype(jnp.int32)
-    mine = run_forward(index[None], per, x, w_spatial)
     mirrored = g == 2 and here <= HALO <= 2 * here
-    n = HALO - here
+    extra = HALO - here if mirrored else 0
+    start = jnp.where(m == 0, here - extra, 0)
+    def arrive(value, layer):
+        pieces = []
+        for s in range(1, g):
+            piece = lax.dynamic_slice_in_dim(value, (m + s) % g * per + layer, 1, 2)
+            pieces.append(swap(piece, s))
+        return pieces
+
+    arriving = [arrive(x, 0)]
+    mine = list(run_forward(index, start, extra, per, x, w_spatial))
+    if per > 1:
+        later, mine[1] = lax.optimization_barrier((x, mine[1]))
+        arriving += [arrive(later, layer) for layer in range(1, per)]
     ahead = []
     if mirrored:
         ahead.append(hop(mine[0], (-1, 1)))
-        if n:
-            start = jnp.where(m == 0, here - n, 0)
-            ahead.append(hop(lax.dynamic_slice_in_dim(mine[0], start, n, 1), (1, -1)))
-
-    window = jnp.pad(targets[0], ((3, 3), (0, 0)))
-    window = jnp.stack([window[k // g * own : k // g * own + own + 6] for k in range(tiles)])
-    window = lax.all_to_all(window, "tile", 0, 0, tiled=True)
-    tgt = lax.dynamic_slice_in_dim(window, m * share, share, 0)
-    tgt = tgt.transpose(1, 0, 2).reshape(own + 6, per, 1, vox)
+        if extra:
+            ahead.append(hop(mine[3], (1, -1)))
+
+    everyone = jnp.broadcast_to(targets, (tiles, total, spot))
+    everyone = lax.all_to_all(everyone, "tile", 0, 0, tiled=True)
+    tgt = lax.dynamic_slice_in_dim(everyone, m * share, share, 0)
+    if share % per:
+        tgt = tgt.transpose(1, 0, 2).reshape(total, per, vox).transpose(1, 0, 2)
     frame_weight = jnp.pad(valid[0].astype(F32) / total, (3, 3))
     frame_weight = lax.dynamic_slice_in_dim(frame_weight, q * own, own + 6, 0)
 
+    dims = (own, chans, vox, total, g, width)
     grads = jnp.zeros((6, chans, 3 * chans), F32)
-    logits, backs = [], []
-    zero = jnp.zeros((1,), jnp.int32)
+    ready = []
     for layer in range(per):
         done = [mine]
+        start = jnp.where(m == 1, here - extra, 0)
         for piece in arriving[layer]:
-            done.append(run_forward(zero, 1, piece[:, :, None], w_spatial))
+            done.append(run_forward(0, start, extra, 1, piece, w_spatial))
         pieces = [d[0] for d in done]
         ranks = [layer] + [0] * (g - 1)
         places = [HALO + (m - s) % g * here for s in range(g)]
         if mirrored:
             up, down = own + HALO, HALO - here
             pieces += ahead
-            ranks += [layer] * len(ahead)
-            places += [jnp.where(m == 0, up, down), jnp.where(m == 0, 0, up + here)][: len(ahead)]
-            pieces.append(hop(pieces[1], (1, -1)))
-            places.append(jnp.where(m == 1, up, down))
-            if n:
-                start = jnp.where(m == 1, here - n, 0)
-                pieces.append(hop(lax.dynamic_slice_in_dim(pieces[1], start, n, 1), (-1, 1)))
-                places.append(jnp.where(m == 1, 0, up + here))
-            ranks += [0] * len(ahead)
+            pieces.append(hop(done[1][0], (1, -1)))
+            if extra:
+                pieces.append(hop(done[1][3], (-1, 1)))
+            for k in range(2):
+                ranks += [0 if k else layer] * len(ahead)
+                places += [jnp.where(m == k, up, down), jnp.where(m == k, 0, up + here)][: len(ahead)]
         else:
             block = [p[k] for p, k in zip(pieces, ranks)]
             block = pick(block[::-1], g - 1 - m).reshape(own, chans, vox)
@@ -510,46 +548,55 @@
                 ranks += [0, 0]
                 left -= k
                 d += 1
-        meta = jnp.stack([jnp.asarray(v, jnp.int32) for v in [q * own] + places])
+        meta = jnp.stack([jnp.asarray(v, jnp.int32) for v in [q * own] + places + [index + layer]])
+        ready.append([meta, pieces, ranks, [d[1] for d in done], [d[2] for d in done]])
+
+    logits, out, homecoming = [], None, []
+    for layer in range(per):
+        meta, pieces, ranks, slopes, xcs = ready[layer]
         inside = layer < per - 1
-        logit, back, grads = run_temporal(
+        part = share // per if share % per == 0 else 1
+        logit, grads, *result = run_temporal(
             meta,
+            (wt, wtb, whc, tgt[layer * part : (layer + 1) * part], grads, wb),
             frame_weight,
-            wt,
-            wtb,
-            whc,
-            tgt[:, layer],
-            grads,
-            wb,
             pieces,
             ranks,
-            [d[1] for d in done],
-            [d[2] for d in done],
+            slopes,
+            xcs,
             inside,
-            own,
-            width,
-            total,
+            out if inside else None,
+            dims,
+            layers,
         )
         logits.append(logit[3 : 3 + own, 0])
         if inside:
-            back = back.reshape(g, here, chans, 1, rows, width)
+            out, sent = result
+            following = ready[layer + 1]
+            following[1], sent = lax.optimization_barrier((following[1], sent))
             for s in range(1, g):
-                dx = swap(take(back, (m - s) % g, 0), -s)
-                backs.append(((m + s) % g * per + layer, dx))
-            backs.append((index + layer, take(back, m, 0)))
-        else:
-            for s in range(1, g):
-                frames = jnp.stack([((m - s) % g * here).astype(jnp.int32), zero[0]])
-                dx = swap(run_backward(frames, back, wb, here, 1, rows, None), -s)
-                backs.append(((m + s) % g * per + layer, dx))
-            frames = jnp.stack([(m * here).astype(jnp.int32), index + layer])
-            out = run_backward(frames, back, wb, here, layers, rows, None)
-    for spot_z, dx in backs:
-        out = lax.dynamic_update_slice_in_dim(out, dx, spot_z, 2)
-
-    grads = sum_over_tiles(sum_over_reps(grads, 1), tiles)
+                dx = swap(sent[s - 1][:, :, None], -s)
+                homecoming.append(((m + s) % g * per + layer, dx))
+    dpre = result[0]
+    home = [dx for _, dx in homecoming]
+    home, dpre, grads = lax.optimization_barrier((home, dpre, grads))
+    for (place, _), dx in zip(homecoming, home):
+        out = lax.dynamic_update_slice_in_dim(out, dx, place, 2)
+    layer = per - 1
+    backs = []
+    for s in range(1, g):
+        frames = jnp.stack([(m - s) % g * here, 0]).astype(jnp.int32)
+        dx = run_backward(frames, dpre, wb, here, 1, rows, None)
+        logits, dx = lax.optimization_barrier((logits, dx))
+        backs.append(swap(dx, -s))
+    frames = jnp.stack([m * here, index + layer]).astype(jnp.int32)
+    out = run_backward(frames, dpre, wb, here, layers, rows, out)
+
+    grads, backs = sum_over_tiles(sum_over_reps(grads, 1), tiles, backs)
+    for s in range(1, g):
+        out = lax.dynamic_update_slice_in_dim(out, backs[s - 1], (m + s) % g * per + layer, 2)
     part = grads.shape[1]
-    gs = grads[:3].reshape(3, part, 3, chans).transpose(0, 2, 1, 3).reshape(9, part, chans)
+    gs = grads[:3].reshape(3, part, 3, chans).transpose(2, 0, 1, 3).reshape(9, part, chans)
     gt = grads[3:5].reshape(2, part, 3, chans).transpose(0, 2, 1, 3)
     gh = lax.dynamic_slice_in_dim(grads[5, 0], lax.axis_index("rep") * part, part, 0)
 

time: 171 us -> 152 us (0.89)
  local copies, waits for them, and re-layouts: 24.9 us -> 11.9 us
  Pallas kernels: 81.4 us -> 76 us
  waiting for transfers between devices: 23.2 us -> 20.3 us
    pallas_call x2, Pallas kernels: 55.3 us -> 48 us  [run_temporal(): pl.pallas_call(functools.partial(temporal_kernel, tuple(places), inside,...]
    ppermute x6, waiting for transfers between devices: 5.7 us -> 0.02 us  [hop(): return lax.ppermute(value, 'tile', [p for p in pairs if 0 <= p[1] < tiles])]
    unnamed x34 -> x25, local copies, waits for them, and re-layouts: 8.24 us -> 2.6 us
    ppermute x3, waiting for transfers between devices: 0.01 us -> 2.49 us  [sum_over_reps(): lax.ppermute(share(r + s).astype(BF16), 'rep', pairs).astype(F32)]
    squeeze x4 -> x0, local copies, waits for them, and re-layouts: 2.4 us -> none  [the longest x2 1.45 us: take(): return lax.dynamic_index_in_dim(value, index, axis, False)]
    ppermute x3, waiting for transfers between devices: 13.6 us -> 15.6 us  [sum_over_tiles(): value = value + lax.ppermute(value.astype(BF16), 'tile', pairs).astype(F32)]
    ppermute x4, starting transfers between devices: 7.13 us -> 9.07 us  [swap(): return lax.ppermute(value, 'tile', pairs)]
    pallas_call x3, Pallas kernels: 16.9 us -> 18.7 us  [run_forward(): pl.pallas_call(functools.partial(forward_kernel, middle), name='conv_forw...]
  transfers between devices with their start and end apart: 18 -> 18, of which waited for: 3 -> 5; matrix products, arithmetic and copies ran while one was open for 12% -> 6% of each run, Pallas kernels for 33% -> 47%
where the time goes in v3:
time: 152 us; the launch traced here: 151 us
  Pallas kernels  76 us (50%)
  starting transfers between devices  39 us (26%)
  waiting for transfers between devices  20.3 us (13%)
  local copies, waits for them, and re-layouts  11.9 us (8%)
  other arithmetic  2.55 us (2%)
    pallas_call x2, Pallas kernels, run_temporal(): pl.pallas_call(functools.partial(temporal_kernel, tuple(places), inside,...  48 us
    pallas_call x3, Pallas kernels, run_forward(): pl.pallas_call(functools.partial(forward_kernel, middle), name='conv_forw...  18.7 us
    ppermute x6, starting transfers between devices, hop(): return lax.ppermute(value, 'tile', [p for p in pairs if 0 <= p[1] < tiles])  16.6 us
    ppermute x3, waiting for transfers between devices, sum_over_tiles(): value = value + lax.ppermute(value.astype(BF16), 'tile', pairs).astype(F32)  15.6 us
    pallas_call x2, Pallas kernels, run_backward(): pl.pallas_call(functools.partial(backward_kernel, aliased), name='conv_ba...  9.24 us
    ppermute x4, starting transfers between devices, swap(): return lax.ppermute(value, 'tile', pairs)  9.07 us
    all_to_all x1, starting transfers between devices, body(): everyone = lax.all_to_all(everyone, 'tile', 0, 0, tiled=True)  4.69 us
    dynamic_slice x2, local copies, waits for them, and re-layouts, arrive(): piece = lax.dynamic_slice_in_dim(value, (m + s) % g * per + layer, 1, 2)  3.76 us
  transfers between devices with their start and end apart: 18, of which 5 were waited for; matrix products, arithmetic and copies ran while one was open for 6% of the time, Pallas kernels for 47%

profile of v3, /device:TPU:0, one launch (start us, length us, event | category | flops | bytes accessed | tf_op | source)
XLA Modules:
  0.0 150.8 jit_solution(18220685413155142069)
XLA Ops:
  0.7 1.9 %dynamic-slice_bitcast_fusion = bf16[4,64,1,8,128]{4,3,2,1,0:T(8,128)(2,1)} fusion(bf16[1,4,64,4,8,128]{5,4,3,2,1,0:T(8,128)(2,1)} %param.6, s32[]{:T(128)S(6)} %select_n.124), kind=kLoop, calls=%fused_computation.1 | loop fusion | bytes 1048580 | tf_op jit(solution)/shard_map/dynamic_slice | solution.py:495
  2.5 3.0 %collective-permute-start = (bf16[4,64,1,8,128]{4,3,2,1,0:T(8,128)(2,1)}, bf16[4,64,1,8,128]{4,3,2,1,0:T(8,128)(2,1)S(1)}, u32[]{:S(2)}, u32[]{:S(2)}) collective-permute-start(bf16[4,64,1,8,128]{4,3,2,1,0:T(8,128)(2,1)} %dynamic-slice_bitcast_fusion), channel_id=1, source_target_pairs={{0,4},{4,0},{8,12},{12,8},{16,20},{20,16},{24,28},{28,24},{1,5},{5... | collective-permute-start | bytes 1572872 | tf_op jit(solution)/shard_map/ppermute | solution.py:476
  5.5 0.7 pad_add_fusion
  6.2 8.4 %conv_forward.3 = (bf16[2,4,64,1024]{3,2,1,0:T(8,128)(2,1)}, bf16[2,4,64,1024]{3,2,1,0:T(8,128)(2,1)}, bf16[2,4,64,1024]{3,2,1,0:T(8,128)(2,1)}, bf16[2,2,64,1024]{3,2,1,0:T(8,128)(2,1)}) custom-call(s32[2]{0:T(128)} %get-tuple-element.94.meta_ref, bf16[4,64,4,8,128]{4,3,2,1,0:T(8,128)(2,1)} %bitcast.55, bf16[9,64,64]{2,1,0:T(8,128)(2,1)} %w_ref.5), custom_call_target="tpu_custom_call" | custom-call | flops 1000 | bytes 1000 | tf_op jit(solution)/shard_map/conv_forward/pallas_call | solution.py:105
  14.5 0.0 copy-start.3
  14.6 1.4 collective-permute-start.1
  16.0 1.9 %constant_dynamic-slice_fusion.2 = bf16[4,64,1,8,128]{4,3,2,1,0:T(8,128)(2,1)} fusion(bf16[4,64,4,8,128]{4,3,2,1,0:T(8,128)(2,1)} %bitcast.56, s32[]{:T(128)S(6)} %select_n.125), kind=kLoop, calls=%fused_computation.18 | loop fusion | bytes 1048580 | tf_op jit(solution)/shard_map/dynamic_slice | solution.py:495
  17.9 2.8 %collective-permute-start.5 = (bf16[4,64,1,8,128]{4,3,2,1,0:T(8,128)(2,1)}, bf16[4,64,1,8,128]{4,3,2,1,0:T(8,128)(2,1)}, u32[]{:S(2)}, u32[]{:S(2)}) collective-permute-start(bf16[4,64,1,8,128]{4,3,2,1,0:T(8,128)(2,1)} %constant_dynamic-slice_fusion.2), channel_id=1, source_target_pairs={{0,4},{4,0},{8,12},{12,8},{16,20},{20,16},{24,28},{28,24},{1,5},{5... | collective-permute-start | bytes 1572872 | tf_op jit(solution)/shard_map/ppermute | solution.py:476
  20.7 0.7 broadcast_in_dim.23
  21.4 4.7 %all-to-all-start = ((bf16[8,32,512]{2,1,0:T(8,128)(2,1)}), bf16[8,32,512]{2,1,0:T(8,128)(2,1)S(1)}, u32[]{:S(2)}, u32[]{:S(2)}) async-start(bf16[8,32,512]{2,1,0:T(8,128)(2,1)} %broadcast_in_dim.23), calls=%async_computation | async-start | bytes 524288 | tf_op jit(solution)/shard_map/all_to_all | solution.py:511
  26.1 3.9 %collective-permute-start.2 = (bf16[2,2,64,1024]{3,2,1,0:T(8,128)(2,1)}, bf16[2,2,64,1024]{3,2,1,0:T(8,128)(2,1)S(1)}, u32[]{:S(2)}, u32[]{:S(2)}) collective-permute-start(bf16[2,2,64,1024]{3,2,1,0:T(8,128)(2,1)} %get-tuple-element.43), channel_id=1, source_target_pairs={{0,8},{8,16},{12,4},{16,24},{20,12},{28,20},{1,9},{9,17},{13,5},{1... | collective-permute-start | bytes 1572872 | tf_op jit(solution)/shard_map/ppermute | solution.py:480
  30.1 0.6 pad_add_fusion.1.meta_ref
  30.6 0.8 copy-done.6
  31.4 5.2 %conv_forward.4 = (bf16[1,4,64,1024]{3,2,1,0:T(8,128)(2,1)}, bf16[1,4,64,1024]{3,2,1,0:T(8,128)(2,1)}, bf16[1,4,64,1024]{3,2,1,0:T(8,128)(2,1)}, bf16[1,2,64,1024]{3,2,1,0:T(8,128)(2,1)}) custom-call(s32[2]{0:T(128)} %pad_add_fusion.1.meta_ref, bf16[4,64,1,8,128]{4,3,2,1,0:T(8,128)(2,1)} %copy-done.6, bf16[9,64,64]{2,1,0:T(8,128)(2,1)} %w_ref.5), custom_call_target="tpu_custom_call" | custom-call | flops 1000 | bytes 1000 | tf_op jit(solution)/shard_map/conv_forward/pallas_call | solution.py:105
  36.6 3.4 %collective-permute-start.3 = (bf16[1,4,64,1024]{3,2,1,0:T(8,128)(2,1)}, bf16[1,4,64,1024]{3,2,1,0:T(8,128)(2,1)S(1)}, u32[]{:S(2)}, u32[]{:S(2)}) collective-permute-start(bf16[1,4,64,1024]{3,2,1,0:T(8,128)(2,1)} %get-tuple-element.42.rest_1_), channel_id=1, source_target_pairs={{0,8},{8,16},{12,4},{16,24},{20,12},{28,20},{1,9},{9,17},{13,5},{1... | collective-permute-start | bytes 1572872 | tf_op jit(solution)/shard_map/ppermute | solution.py:480
  40.0 1.3 collective-permute-start.4
  41.3 0.0 collective-permute-done.5.x_ref
  41.3 5.2 %conv_forward.5 = (bf16[1,4,64,1024]{3,2,1,0:T(8,128)(2,1)}, bf16[1,4,64,1024]{3,2,1,0:T(8,128)(2,1)}, bf16[1,4,64,1024]{3,2,1,0:T(8,128)(2,1)}, bf16[1,2,64,1024]{3,2,1,0:T(8,128)(2,1)}) custom-call(s32[2]{0:T(128)} %pad_add_fusion.1.meta_ref, bf16[4,64,1,8,128]{4,3,2,1,0:T(8,128)(2,1)} %collective-permute-done.5.x_ref, bf16[9,64,64]{2,1,0:T(8,128)(2,1)} %w_ref.5), custom_call_target="tpu_custom_call" | custom-call | flops 1000 | bytes 1000 | tf_op jit(solution)/shard_map/conv_forward/pallas_call | solution.py:105
  46.5 5.3 %collective-permute-start.6 = (bf16[1,4,64,1024]{3,2,1,0:T(8,128)(2,1)}, bf16[1,4,64,1024]{3,2,1,0:T(8,128)(2,1)}, u32[]{:S(2)}, u32[]{:S(2)}) collective-permute-start(bf16[1,4,64,1024]{3,2,1,0:T(8,128)(2,1)} %get-tuple-element.57.rest_1_), channel_id=1, source_target_pairs={{0,8},{8,16},{12,4},{16,24},{20,12},{28,20},{1,9},{9,17},{13,5},{1... | collective-permute-start | bytes 1572872 | tf_op jit(solution)/shard_map/ppermute | solution.py:480
  51.9 0.1 copy.32
  52.0 0.1 copy.34.wt_ref
  52.1 0.1 copy.35.wtb_ref
  52.2 0.1 copy.36.whc_ref
  52.3 0.2 copy.33
  52.5 0.2 reshape.53.wb_ref
  52.7 0.1 stack.76.meta_ref
  52.8 0.1 pad_dynamic-slice_fusion.weight_ref
  52.8 0.0 collective-permute-done.2.rest_3_
  52.8 1.3 collective-permute-start.7
  54.1 0.0 all-to-all-done
  54.2 0.0 collective-permute-done.4.rest_5_
  54.2 0.0 collective-permute-done.3.rest_4_
  54.2 0.8 copy-done.5
  55.1 0.3 copy-done.2
  55.4 24.6 %temporal.2 = (f32[14,1,1024]{2,1,0:T(1,128)S(1)}, f32[6,64,192]{2,1,0:T(8,128)S(1)}, bf16[4,64,4,8,128]{4,3,2,1,0:T(8,128)(2,1)}, bf16[1,4,64,8,128]{4,3,2,1,0:T(8,128)(2,1)S(1)}) custom-call(s32[8]{0:T(128)S(1)} %stack.76.meta_ref, f32[14]{0:T(128)S(1)} %pad_dynamic-slice_fusion.weight_ref, bf16[2,64,192]{2,1,0:T(8,128)(2,1)S(1)} %copy.34.wt_ref, ...), custom_call_target="tpu_custom_call" | custom-call | flops 1572864000 | bytes 52428800 | tf_op jit(solution)/shard_map/temporal/pallas_call | solution.py:381
  80.0 0.0 collective-permute-done.7.rest_5_
  80.0 3.2 %collective-permute-start.8 = (bf16[4,64,1,8,128]{4,3,2,1,0:T(8,128)(2,1)S(1)}, bf16[4,64,1,8,128]{4,3,2,1,0:T(8,128)(2,1)S(1)}, u32[]{:S(2)}, u32[]{:S(2)}) collective-permute-start(bf16[4,64,1,8,128]{4,3,2,1,0:T(8,128)(2,1)S(1)} %bitcast.54), channel_id=1, source_target_pairs={{0,4},{4,0},{8,12},{12,8},{16,20},{20,16},{24,28},{28,24},{1,5},{5... | collective-permute-start | bytes 1572872 | tf_op jit(solution)/shard_map/ppermute | solution.py:476
  83.3 0.1 stack.82.meta_ref
  83.4 0.6 pad_add_fusion.3.meta_ref
  84.0 23.4 %temporal.3 = (f32[14,1,1024]{2,1,0:T(1,128)S(1)}, f32[6,64,192]{2,1,0:T(8,128)S(1)}, bf16[8,64,1024]{2,1,0:T(8,128)(2,1)}) custom-call(s32[8]{0:T(128)S(1)} %stack.82.meta_ref, f32[14]{0:T(128)S(1)} %pad_dynamic-slice_fusion.weight_ref, bf16[2,64,192]{2,1,0:T(8,128)(2,1)S(1)} %copy.34.wt_ref, bf16[2,64,192]{2,1,0:T(8,128)(2,1)S(1)} %copy.35.wtb_ref, ...), custom_call_target="tpu_custom_call" | custom-call | flops 1572864000 | bytes 52428800 | tf_op jit(solution)/shard_map/temporal/pallas_call | solution.py:381
  107.4 4.6 %conv_backward.2 = bf16[4,64,1,8,128]{4,3,2,1,0:T(8,128)(2,1)} custom-call(s32[2]{0:T(128)} %get-tuple-element.95.meta_ref, bf16[8,64,1024]{2,1,0:T(8,128)(2,1)} %get-tuple-element.68.dpre_ref, bf16[192,192]{1,0:T(8,128)(2,1)} %copy-done), custom_call_target="tpu_custom_call" | custom-call | flops 1000 | bytes 1000 | tf_op jit(solution)/shard_map/conv_backward/pallas_call | solution.py:143
  112.1 0.1 collective-permute-start.11
  112.1 1.6 %collective-permute-start.10 = (bf16[6,16,192]{2,1,0:T(8,128)(2,1)S(1)}, bf16[6,16,192]{2,1,0:T(8,128)(2,1)S(1)}, u32[]{:S(2)}, u32[]{:S(2)}) collective-permute-start(bf16[6,16,192]{2,1,0:T(8,128)(2,1)S(1)} %get-tuple-element.91), channel_id=1, source_target_pairs={{0,2},{1,3},{2,0},{3,1},{4,6},{5,7},{6,4},{7,5},{8,10},{9,11},{10,... | collective-permute-start | bytes 110600 | tf_op jit(solution)/shard_map/ppermute | solution.py:456
  113.7 0.2 collective-permute-start.9
  113.9 0.1 collective-permute-start.14
  114.0 0.8 constant_dynamic-update-slice_fusion.rest_0_
  114.8 2.0 %collective-permute-done.10 = bf16[6,16,192]{2,1,0:T(8,128)(2,1)S(1)} collective-permute-done((bf16[6,16,192]{2,1,0:T(8,128)(2,1)S(1)}, bf16[6,16,192]{2,1,0:T(8,128)(2,1)S(1)}, u32[]{:S(2)}, u32[]{:S(2)}) %collective-permute-start.10) | collective-permute-done | bytes 36896 | tf_op jit(solution)/shard_map/ppermute | solution.py:456
  116.7 0.5 collective-permute-done.9
  117.3 0.2 collective-permute-start.12
  117.5 12.0 %collective-permute-done.12 = bf16[6,16,192]{2,1,0:T(8,128)(2,1)S(1)} collective-permute-done((bf16[6,16,192]{2,1,0:T(8,128)(2,1)S(1)}, bf16[6,16,192]{2,1,0:T(8,128)(2,1)S(1)}, u32[]{:S(2)}, u32[]{:S(2)}) %collective-permute-start.12) | collective-permute-done | bytes 36896 | tf_op jit(solution)/shard_map/ppermute | solution.py:440
  129.4 2.6 %collective-permute-start.13 = (bf16[6,16,192]{2,1,0:T(8,128)(2,1)S(1)}, bf16[6,16,192]{2,1,0:T(8,128)(2,1)S(1)}, u32[]{:S(2)}, u32[]{:S(2)}) collective-permute-start(bf16[6,16,192]{2,1,0:T(8,128)(2,1)S(1)} %fusion), channel_id=1, source_target_pairs={{0,8},{4,12},{8,0},{12,4},{16,24},{20,28},{24,16},{28,20},{1,9},{5... | collective-permute-start | bytes 110600 | tf_op jit(solution)/shard_map/ppermute | solution.py:440
  132.0 0.6 pad_maximum_fusion
  132.7 3.4 %all-to-all-start.1 = ((bf16[8,8,512]{2,1,0:T(8,128)(2,1)}), bf16[8,8,512]{2,1,0:T(8,128)(2,1)S(1)}, u32[]{:S(2)}, u32[]{:S(2)}) async-start(bf16[8,8,512]{2,1,0:T(8,128)(2,1)} %pad_maximum_fusion), calls=%async_computation.1 | async-start | bytes 131072 | tf_op jit(solution)/shard_map/all_to_all | solution.py:606
  136.0 4.6 %conv_backward.3 = bf16[4,64,4,8,128]{4,3,2,1,0:T(8,128)(2,1)} custom-call(s32[2]{0:T(128)} %pad_add_fusion.3.meta_ref, bf16[8,64,1024]{2,1,0:T(8,128)(2,1)} %get-tuple-element.68.dpre_ref, bf16[192,192]{1,0:T(8,128)(2,1)} %copy-done, bf16[4,64,4,8,128]{4,3,2,1,0:T(8,128)(2,1)} %constant_dynamic-update-slice_fusion.rest_0_), custom_call_target="tpu_custom_call", output_to_operand_aliasing={{}: (3, {})} | custom-call | flops 1000 | bytes 1000 | tf_op jit(solution)/shard_map/conv_backward/pallas_call | solution.py:143
  140.7 2.2 %all-to-all-done.1 = bf16[8,8,512]{2,1,0:T(8,128)(2,1)S(1)} async-done(((bf16[8,8,512]{2,1,0:T(8,128)(2,1)}), bf16[8,8,512]{2,1,0:T(8,128)(2,1)S(1)}, u32[]{:S(2)}, u32[]{:S(2)}) %all-to-all-start.1) | async-done | bytes 65568 | tf_op jit(solution)/shard_map/all_to_all | solution.py:606
  142.9 0.6 dynamic-slice_bitcast_fusion.1
  143.5 0.7 collective-permute-start.15
  144.2 0.8 bitcast_dynamic-update-slice_fusion
  145.1 3.7 %collective-permute-done.15 = bf16[6,16,192]{2,1,0:T(8,128)(2,1)S(1)} collective-permute-done((bf16[6,16,192]{2,1,0:T(8,128)(2,1)S(1)}, bf16[6,16,192]{2,1,0:T(8,128)(2,1)S(1)}, u32[]{:S(2)}, u32[]{:S(2)}) %collective-permute-start.15) | collective-permute-done | bytes 36896 | tf_op jit(solution)/shard_map/ppermute | solution.py:440
  148.8 0.1 reshape.56
  148.9 0.6 copy.42
  149.5 0.1 reshape.58
  149.6 0.6 copy.43
  150.2 0.6 fusion.1
  (43 shorter events, 0.3 us)
Async XLA Ops:
  0.7 20.0 %copy-start.8 = (bf16[1,32,512]{2,1,0:T(8,128)(2,1)S(1)}, bf16[1,32,512]{2,1,0:T(8,128)(2,1)}, u32[]{:S(2)}) copy-start(bf16[1,32,512]{2,1,0:T(8,128)(2,1)} %param.10) | copy-start | bytes 98308
  2.5 28.1 %collective-permute-start = (bf16[4,64,1,8,128]{4,3,2,1,0:T(8,128)(2,1)}, bf16[4,64,1,8,128]{4,3,2,1,0:T(8,128)(2,1)S(1)}, u32[]{:S(2)}, u32[]{:S(2)}) collective-permute-start(bf16[4,64,1,8,128]{4,3,2,1,0:T(8,128)(2,1)} %dynamic-slice_bitcast_fusion), channel_id=1, source_target_pairs={{0,4},{4,0},{8,12},{12,8},{16,20},{20,16},{24,28},{28,24},{1,5},{5... | collective-permute-start | bytes 1572872 | tf_op jit(solution)/shard_map/ppermute | solution.py:476
  6.2 33.8 %copy-start.9 = (s32[1,32]{1,0:T(1,128)S(1)}, s32[1,32]{1,0:T(1,128)}, u32[]{:S(2)}) copy-start(s32[1,32]{1,0:T(1,128)} %param.11) | copy-start | bytes 388
  14.5 37.3 %copy-start.10 = (bf16[64]{0:T(256)(128)(2,1)S(1)}, bf16[64]{0:T(256)(128)(2,1)}, u32[]{:S(2)}) copy-start(bf16[64]{0:T(256)(128)(2,1)} %param.9) | copy-start | bytes 388
  14.5 37.3 %copy-start.7 = (bf16[2,3,64,64]{3,2,1,0:T(8,128)(2,1)S(1)}, bf16[2,3,64,64]{3,2,1,0:T(8,128)(2,1)}, u32[]{:S(2)}) copy-start(bf16[2,3,64,64]{3,2,1,0:T(8,128)(2,1)} %param.8) | copy-start | bytes 147460
  14.5 37.8 %copy-start.3 = (bf16[9,64,64]{2,1,0:T(8,128)(2,1)S(1)}, bf16[9,64,64]{2,1,0:T(8,128)(2,1)}, u32[]{:S(2)}) copy-start(bf16[9,64,64]{2,1,0:T(8,128)(2,1)} %w_ref.5) | copy-start | bytes 221188
  14.6 39.6 %collective-permute-start.1 = (bf16[2,4,64,1024]{3,2,1,0:T(8,128)(2,1)}, bf16[2,4,64,1024]{3,2,1,0:T(8,128)(2,1)S(1)}, u32[]{:S(2)}, u32[]{:S(2)}) collective-permute-start(bf16[2,4,64,1024]{3,2,1,0:T(8,128)(2,1)} %get-tuple-element.56.rest_0_), channel_id=1, source_target_pairs={{4,12},{8,0},{12,20},{16,8},{20,28},{24,16},{5,13},{9,1},{13,21},{... | collective-permute-start | bytes 3145736 | tf_op jit(solution)/shard_map/ppermute | solution.py:480
  17.9 23.4 %collective-permute-start.5 = (bf16[4,64,1,8,128]{4,3,2,1,0:T(8,128)(2,1)}, bf16[4,64,1,8,128]{4,3,2,1,0:T(8,128)(2,1)}, u32[]{:S(2)}, u32[]{:S(2)}) collective-permute-start(bf16[4,64,1,8,128]{4,3,2,1,0:T(8,128)(2,1)} %constant_dynamic-slice_fusion.2), channel_id=1, source_target_pairs={{0,4},{4,0},{8,12},{12,8},{16,20},{20,16},{24,28},{28,24},{1,5},{5... | collective-permute-start | bytes 1572872 | tf_op jit(solution)/shard_map/ppermute | solution.py:476
  21.4 32.7 %all-to-all-start = ((bf16[8,32,512]{2,1,0:T(8,128)(2,1)}), bf16[8,32,512]{2,1,0:T(8,128)(2,1)S(1)}, u32[]{:S(2)}, u32[]{:S(2)}) async-start(bf16[8,32,512]{2,1,0:T(8,128)(2,1)} %broadcast_in_dim.23), calls=%async_computation | async-start | bytes 524288 | tf_op jit(solution)/shard_map/all_to_all | solution.py:511
  26.1 26.7 %collective-permute-start.2 = (bf16[2,2,64,1024]{3,2,1,0:T(8,128)(2,1)}, bf16[2,2,64,1024]{3,2,1,0:T(8,128)(2,1)S(1)}, u32[]{:S(2)}, u32[]{:S(2)}) collective-permute-start(bf16[2,2,64,1024]{3,2,1,0:T(8,128)(2,1)} %get-tuple-element.43), channel_id=1, source_target_pairs={{0,8},{8,16},{12,4},{16,24},{20,12},{28,20},{1,9},{9,17},{13,5},{1... | collective-permute-start | bytes 1572872 | tf_op jit(solution)/shard_map/ppermute | solution.py:480
  30.6 0.8 copy-start.6
  36.6 17.6 %collective-permute-start.3 = (bf16[1,4,64,1024]{3,2,1,0:T(8,128)(2,1)}, bf16[1,4,64,1024]{3,2,1,0:T(8,128)(2,1)S(1)}, u32[]{:S(2)}, u32[]{:S(2)}) collective-permute-start(bf16[1,4,64,1024]{3,2,1,0:T(8,128)(2,1)} %get-tuple-element.42.rest_1_), channel_id=1, source_target_pairs={{0,8},{8,16},{12,4},{16,24},{20,12},{28,20},{1,9},{9,17},{13,5},{1... | collective-permute-start | bytes 1572872 | tf_op jit(solution)/shard_map/ppermute | solution.py:480
  40.0 14.1 %collective-permute-start.4 = (bf16[1,2,64,1024]{3,2,1,0:T(8,128)(2,1)}, bf16[1,2,64,1024]{3,2,1,0:T(8,128)(2,1)S(1)}, u32[]{:S(2)}, u32[]{:S(2)}) collective-permute-start(bf16[1,2,64,1024]{3,2,1,0:T(8,128)(2,1)} %get-tuple-element.44), channel_id=1, source_target_pairs={{4,12},{8,0},{12,20},{16,8},{20,28},{24,16},{5,13},{9,1},{13,21},{... | collective-permute-start | bytes 786440 | tf_op jit(solution)/shard_map/ppermute | solution.py:480
  46.5 33.5 %collective-permute-start.6 = (bf16[1,4,64,1024]{3,2,1,0:T(8,128)(2,1)}, bf16[1,4,64,1024]{3,2,1,0:T(8,128)(2,1)}, u32[]{:S(2)}, u32[]{:S(2)}) collective-permute-start(bf16[1,4,64,1024]{3,2,1,0:T(8,128)(2,1)} %get-tuple-element.57.rest_1_), channel_id=1, source_target_pairs={{0,8},{8,16},{12,4},{16,24},{20,12},{28,20},{1,9},{9,17},{13,5},{1... | collective-permute-start | bytes 1572872 | tf_op jit(solution)/shard_map/ppermute | solution.py:480
  52.6 31.3 %copy-start = (bf16[192,192]{1,0:T(8,128)(2,1)}, bf16[192,192]{1,0:T(8,128)(2,1)S(1)}, u32[]{:S(2)}) copy-start(bf16[192,192]{1,0:T(8,128)(2,1)S(1)} %reshape.53.wb_ref) | copy-start | bytes 221188
  52.8 1.4 copy-start.4
  52.8 27.2 %collective-permute-start.7 = (bf16[1,2,64,1024]{3,2,1,0:T(8,128)(2,1)}, bf16[1,2,64,1024]{3,2,1,0:T(8,128)(2,1)S(1)}, u32[]{:S(2)}, u32[]{:S(2)}) collective-permute-start(bf16[1,2,64,1024]{3,2,1,0:T(8,128)(2,1)} %get-tuple-element.54), channel_id=1, source_target_pairs={{4,12},{8,0},{12,20},{16,8},{20,28},{24,16},{5,13},{9,1},{13,21},{... | collective-permute-start | bytes 786440 | tf_op jit(solution)/shard_map/ppermute | solution.py:480
  54.2 1.2 copy-start.2
  54.2 0.9 copy-start.5
  55.4 28.6 %copy-start.1 = (bf16[1,4,64,1024]{3,2,1,0:T(8,128)(2,1)S(1)}, bf16[1,4,64,1024]{3,2,1,0:T(8,128)(2,1)}, u32[]{:S(2)}) copy-start(bf16[1,4,64,1024]{3,2,1,0:T(8,128)(2,1)} %get-tuple-element.57.rest_1_) | copy-start | bytes 1572868
  80.0 27.4 %collective-permute-start.8 = (bf16[4,64,1,8,128]{4,3,2,1,0:T(8,128)(2,1)S(1)}, bf16[4,64,1,8,128]{4,3,2,1,0:T(8,128)(2,1)S(1)}, u32[]{:S(2)}, u32[]{:S(2)}) collective-permute-start(bf16[4,64,1,8,128]{4,3,2,1,0:T(8,128)(2,1)S(1)} %bitcast.54), channel_id=1, source_target_pairs={{0,4},{4,0},{8,12},{12,8},{16,20},{20,16},{24,28},{28,24},{1,5},{5... | collective-permute-start | bytes 1572872 | tf_op jit(solution)/shard_map/ppermute | solution.py:476
  112.1 2.7 %collective-permute-start.11 = (bf16[6,16,192]{2,1,0:T(8,128)(2,1)S(1)}, bf16[6,16,192]{2,1,0:T(8,128)(2,1)S(1)}, u32[]{:S(2)}, u32[]{:S(2)}) collective-permute-start(bf16[6,16,192]{2,1,0:T(8,128)(2,1)S(1)} %get-tuple-element.90), channel_id=1, source_target_pairs={{0,3},{1,0},{2,1},{3,2},{4,7},{5,4},{6,5},{7,6},{8,11},{9,8},{10,9... | collective-permute-start | bytes 110600 | tf_op jit(solution)/shard_map/ppermute | solution.py:456
  112.1 4.6 %collective-permute-start.10 = (bf16[6,16,192]{2,1,0:T(8,128)(2,1)S(1)}, bf16[6,16,192]{2,1,0:T(8,128)(2,1)S(1)}, u32[]{:S(2)}, u32[]{:S(2)}) collective-permute-start(bf16[6,16,192]{2,1,0:T(8,128)(2,1)S(1)} %get-tuple-element.91), channel_id=1, source_target_pairs={{0,2},{1,3},{2,0},{3,1},{4,6},{5,7},{6,4},{7,5},{8,10},{9,11},{10,... | collective-permute-start | bytes 110600 | tf_op jit(solution)/shard_map/ppermute | solution.py:456
  113.7 3.6 %collective-permute-start.9 = (bf16[6,16,192]{2,1,0:T(8,128)(2,1)S(1)}, bf16[6,16,192]{2,1,0:T(8,128)(2,1)S(1)}, u32[]{:S(2)}, u32[]{:S(2)}) collective-permute-start(bf16[6,16,192]{2,1,0:T(8,128)(2,1)S(1)} %get-tuple-element.89), channel_id=1, source_target_pairs={{0,1},{1,2},{2,3},{3,0},{4,5},{5,6},{6,7},{7,4},{8,9},{9,10},{10,1... | collective-permute-start | bytes 110600 | tf_op jit(solution)/shard_map/ppermute | solution.py:456
  113.9 29.6 %collective-permute-start.14 = (bf16[4,64,1,8,128]{4,3,1,0,2:T(8,128)(2,1)}, bf16[4,64,1,8,128]{4,3,1,0,2:T(8,128)(2,1)S(1)}, u32[]{:S(2)}, u32[]{:S(2)}) collective-permute-start(bf16[4,64,1,8,128]{4,3,1,0,2:T(8,128)(2,1)} %bitcast.60), channel_id=1, source_target_pairs={{0,4},{4,0},{8,12},{12,8},{16,20},{20,16},{24,28},{28,24},{1,5},{5... | collective-permute-start | bytes 1572872 | tf_op jit(solution)/shard_map/ppermute | solution.py:476
  117.3 12.1 %collective-permute-start.12 = (bf16[6,16,192]{2,1,0:T(8,128)(2,1)S(1)}, bf16[6,16,192]{2,1,0:T(8,128)(2,1)S(1)}, u32[]{:S(2)}, u32[]{:S(2)}) collective-permute-start(bf16[6,16,192]{2,1,0:T(8,128)(2,1)S(1)} %get-tuple-element.87), channel_id=1, source_target_pairs={{0,4},{4,0},{8,12},{12,8},{16,20},{20,16},{24,28},{28,24},{1,5},{5... | collective-permute-start | bytes 110600 | tf_op jit(solution)/shard_map/ppermute | solution.py:440
  129.4 11.2 %collective-permute-start.13 = (bf16[6,16,192]{2,1,0:T(8,128)(2,1)S(1)}, bf16[6,16,192]{2,1,0:T(8,128)(2,1)S(1)}, u32[]{:S(2)}, u32[]{:S(2)}) collective-permute-start(bf16[6,16,192]{2,1,0:T(8,128)(2,1)S(1)} %fusion), channel_id=1, source_target_pairs={{0,8},{4,12},{8,0},{12,4},{16,24},{20,28},{24,16},{28,20},{1,9},{5... | collective-permute-start | bytes 110600 | tf_op jit(solution)/shard_map/ppermute | solution.py:440
  132.7 10.2 %all-to-all-start.1 = ((bf16[8,8,512]{2,1,0:T(8,128)(2,1)}), bf16[8,8,512]{2,1,0:T(8,128)(2,1)S(1)}, u32[]{:S(2)}, u32[]{:S(2)}) async-start(bf16[8,8,512]{2,1,0:T(8,128)(2,1)} %pad_maximum_fusion), calls=%async_computation.1 | async-start | bytes 131072 | tf_op jit(solution)/shard_map/all_to_all | solution.py:606
  143.5 5.2 %collective-permute-start.15 = (bf16[6,16,192]{2,1,0:T(8,128)(2,1)S(1)}, bf16[6,16,192]{2,1,0:T(8,128)(2,1)S(1)}, u32[]{:S(2)}, u32[]{:S(2)}) collective-permute-start(bf16[6,16,192]{2,1,0:T(8,128)(2,1)S(1)} %convert_element_type.56), channel_id=1, source_target_pairs={{0,16},{4,20},{8,24},{12,28},{16,0},{20,4},{24,8},{28,12},{1,17},{... | collective-permute-start | bytes 110600 | tf_op jit(solution)/shard_map/ppermute | solution.py:440

commit v4 on v3

--- a/solution.py
+++ b/solution.py
@@ -6,6 +6,7 @@
 from jax.experimental import pallas as pl
 from jax.experimental.pallas import tpu as pltpu
 from jax.sharding import PartitionSpec as P
+import numpy as np
 
 EPS = 1e-06
 HALO = 6
@@ -16,6 +17,13 @@
 
 def sigmoid(u):
     return 0.5 * jnp.tanh(0.5 * u) + 0.5
+
+
+def silu_parts(half):
+    t = jnp.tanh(half)
+    a = 1.0 + t
+    y = half * a
+    return y, a + y * (1.0 - t)
 
 
 def dot_nn(a, b):
@@ -58,67 +66,66 @@
     return result
 
 
-def forward_kernel(middle, meta_ref, x_ref, w_ref, feat_ref, slope_ref, xc_ref, *rest):
+def forward_kernel(middle, base, meta_ref, x_ref, w_ref, feat_ref, slope_ref, xc_ref, *rest):
     xt, xs, wf = rest[-3:]
-    _, chans, _, rows, width = x_ref.shape
+    frames, chans, _, rows, width = x_ref.shape
 
     @pl.when((pl.program_id(0) == 0) & (pl.program_id(1) == 0))
     def _():
         for i in range(3):
             for j in range(3):
-                wf[i * chans : (i + 1) * chans, j * chans : (j + 1) * chans] = w_ref[3 * i + j]
-
-    xt[...] = x_ref[0, :, 0].astype(F32).reshape(chans * rows, width)
-    for r in range(rows):
-        row = xt[pl.ds(r, chans, stride=rows), :]
-        spread(row, xs, r, 1)
-        xc_ref[0, 0, :, r * width : (r + 1) * width] = row.astype(BF16)
-    for r, pre in enumerate(conv_rows(wf, xs, 1, rows, chans, width)):
-        cols = slice(r * width, (r + 1) * width)
-        s = sigmoid(pre)
-        y = pre * s
-        feat_ref[0, 0, :, cols] = y.astype(BF16)
-        slope_ref[0, 0, :, cols] = (s + y * (1.0 - s)).astype(BF16)
+                wf[i * chans : (i + 1) * chans, j * chans : (j + 1) * chans] = (
+                    w_ref[3 * i + j].astype(F32) * 0.5
+                ).astype(BF16)
+
+    for n in range(frames):
+        xt[n] = x_ref[n, :, 0].astype(F32).reshape(chans * rows, width)
+    for n in range(frames):
+        for r in range(rows):
+            row = xt[n, pl.ds(r, chans, stride=rows), :]
+            spread(row, xs.at[n], r, 1)
+            xc_ref[0, n, :, r * width : (r + 1) * width] = row.astype(BF16)
+    for n in range(frames):
+        for r, half in enumerate(conv_rows(wf, xs.at[n], 1, rows, chans, width)):
+            cols = slice(r * width, (r + 1) * width)
+            y, slope = silu_parts(half)
+            feat_ref[0, n, :, cols] = y.astype(BF16)
+            slope_ref[0, n, :, cols] = slope.astype(BF16)
     if middle:
-        spot = pl.program_id(1) - meta_ref[1]
-
-        @pl.when((spot >= 0) & (spot < middle))
+
+        @pl.when(pl.program_id(1) == meta_ref[base + 1])
         def _():
-            rest[0][0, 0] = feat_ref[0, 0]
-
-
-def run_forward(first, start, middle, count, x, w_spatial):
+            rest[0][0] = feat_ref[0]
+
+
+def run_forward(meta, base, middle, count, x, w_spatial):
     n, chans, _, rows, width = x.shape
     vox = rows * width
     sds = jax.ShapeDtypeStruct
+    frames = middle if middle and n % middle == 0 else 2 - n % 2
     shapes = [sds((count, n, chans, vox), BF16)] * 3
-    specs = [pl.BlockSpec((1, 1, chans, vox), lambda k, f, meta: (k, f, 0, 0))] * 3
+    specs = [pl.BlockSpec((1, frames, chans, vox), lambda k, f, meta: (k, f, 0, 0))] * 3
     if middle:
         shapes.append(sds((count, middle, chans, vox), BF16))
-        specs.append(
-            pl.BlockSpec(
-                (1, 1, chans, vox),
-                lambda k, f, meta: (k, jnp.clip(f - meta[1], 0, middle - 1), 0, 0),
-            )
-        )
-    meta = jnp.stack([jnp.asarray(v, jnp.int32) for v in (first, start)])
+        specs.append(pl.BlockSpec((1, middle, chans, vox), lambda k, f, meta: (k, 0, 0, 0)))
     return pl.pallas_call(
-        functools.partial(forward_kernel, middle),
+        functools.partial(forward_kernel, middle, base),
         name="conv_forward",
         out_shape=shapes,
         grid_spec=pltpu.PrefetchScalarGridSpec(
             num_scalar_prefetch=1,
-            grid=(count, n),
+            grid=(count, n // frames),
             in_specs=[
                 pl.BlockSpec(
-                    (1, chans, 1, rows, width), lambda k, f, meta: (f, 0, meta[0] + k, 0, 0)
+                    (frames, chans, 1, rows, width),
+                    lambda k, f, meta: (f, 0, meta[base] + k, 0, 0),
                 ),
                 pl.BlockSpec((9, chans, chans), lambda k, f, meta: (0, 0, 0)),
             ],
             out_specs=specs,
             scratch_shapes=[
-                pltpu.VMEM((chans * rows, width), F32),
-                pltpu.VMEM((3 * chans, vox), BF16),
+                pltpu.VMEM((frames, chans * rows, width), F32),
+                pltpu.VMEM((frames, 3 * chans, vox), BF16),
                 pltpu.VMEM((3 * chans, 3 * chans), BF16),
             ],
         ),
@@ -128,36 +135,41 @@
 
 def backward_kernel(aliased, meta_ref, dpre_ref, wb_ref, *rest):
     dx_ref, ds, xt = rest[-3:]
-    _, chans, _, rows, width = dx_ref.shape
-    for r in range(rows):
-        spread(dpre_ref[0, :, r * width : (r + 1) * width].astype(F32), ds, r, -1)
-    for r, row in enumerate(conv_rows(wb_ref, ds, -1, rows, chans, width)):
-        xt[pl.ds(r, chans, stride=rows), :] = row
-    dx_ref[0, :, 0] = xt[...].astype(BF16).reshape(chans, rows, width)
-
-
-def run_backward(meta, dpre, wb, n, layers, rows, into):
+    frames, chans, _, rows, width = dx_ref.shape
+    for n in range(frames):
+        for r in range(rows):
+            spread(dpre_ref[n, :, r * width : (r + 1) * width].astype(F32), ds.at[n], r, -1)
+    for n in range(frames):
+        for r, row in enumerate(conv_rows(wb_ref, ds.at[n], -1, rows, chans, width)):
+            xt[n, pl.ds(r, chans, stride=rows), :] = row
+        dx_ref[n, :, 0] = xt[n].astype(BF16).reshape(chans, rows, width)
+
+
+def run_backward(meta, base, dpre, wb, n, layers, rows, into):
     chans, vox = dpre.shape[1:]
     width = vox // rows
     aliased = into is not None
+    frames = 2 - n % 2
     return pl.pallas_call(
         functools.partial(backward_kernel, aliased),
         name="conv_backward",
         out_shape=jax.ShapeDtypeStruct((n, chans, layers, rows, width), BF16),
         grid_spec=pltpu.PrefetchScalarGridSpec(
             num_scalar_prefetch=1,
-            grid=(n,),
+            grid=(n // frames,),
             in_specs=[
-                pl.BlockSpec((1, chans, vox), lambda f, meta: (meta[0] + f, 0, 0)),
+                pl.BlockSpec(
+                    (frames, chans, vox), lambda f, meta: (meta[base] * (n // frames) + f, 0, 0)
+                ),
                 pl.BlockSpec((3 * chans, 3 * chans), lambda f, meta: (0, 0)),
             ]
             + [pl.BlockSpec(memory_space=pl.ANY)] * aliased,
             out_specs=pl.BlockSpec(
-                (1, chans, 1, rows, width), lambda f, meta: (f, 0, meta[1], 0, 0)
+                (frames, chans, 1, rows, width), lambda f, meta: (f, 0, meta[base + 1], 0, 0)
             ),
             scratch_shapes=[
-                pltpu.VMEM((3 * chans, vox), BF16),
-                pltpu.VMEM((chans * rows, width), F32),
+                pltpu.VMEM((frames, 3 * chans, vox), BF16),
+                pltpu.VMEM((frames, chans * rows, width), F32),
             ],
         ),
         input_output_aliases={3: 0} if aliased else {},
@@ -169,6 +181,7 @@
     places,
     inside,
     aliased,
+    base,
     dims,
     meta_ref,
     weight_ref,
@@ -215,17 +228,17 @@
     ) = rest[3 + inside : 21 + inside]
     step = min(256, vox)
     lo, hi = HALO, HALO + own
-    first = meta_ref[0]
+    first = meta_ref[base]
     chunks = [slice(p * step, (p + 1) * step) for p in range(vox // step)]
     whole = slice(0, vox)
 
     early = [
-        pltpu.make_async_copy(src, feats.at[pl.ds(meta_ref[1 + k], src.shape[0])], sems.at[k])
+        pltpu.make_async_copy(src, feats.at[pl.ds(meta_ref[base + 1 + k], src.shape[0])], sems.at[k])
         for k, src in enumerate(pieces)
     ]
     late = []
     for k in range(members):
-        spot = pl.ds(meta_ref[1 + k] - HALO, here)
+        spot = pl.ds(meta_ref[base + 1 + k] - HALO, here)
         late.append(pltpu.make_async_copy(slope_in[k], slope.at[spot], sems.at[len(early) + k]))
         late.append(
             pltpu.make_async_copy(xs_in[k], xs.at[spot], sems.at[len(early) + members + k])
@@ -265,45 +278,39 @@
     def layer0(f):
         ok = frame_ok(f)
         for cols in chunks:
-            mixed = dot_nn(wt_ref[0], stack(n0, f - 1, f, f + 1, cols))
-            s = sigmoid(mixed)
-            y = mixed * s
+            y, slope2 = silu_parts(dot_nn(wt_ref[0], stack(n0, f - 1, f, f + 1, cols)))
             hid = feats[f, :, cols].astype(F32) + y
             inv = rms(hid) * ok
             h1[f, :, cols] = hid
             n1[f, :, cols] = (hid * inv).astype(BF16)
             inv1[f, :, cols] = inv
-            sp0[f, :, cols] = s + y * (1.0 - s)
+            sp0[f, :, cols] = slope2
 
     def layer1(f):
         weight = weight_ref[f - 3]
         frame = jnp.clip(first + f - HALO, 0, total - 1)
         for cols in chunks:
-            mixed = dot_nn(wt_ref[1], stack(n1, f - 2, f, f + 2, cols))
-            s = sigmoid(mixed)
-            y = mixed * s
+            y, slope2 = silu_parts(dot_nn(wt_ref[1], stack(n1, f - 2, f, f + 2, cols)))
             hid = h1[f, :, cols] + y
             inv = rms(hid)
             unit = hid * inv
-            final = unit.astype(BF16)
-            logit = channel_sum(final.astype(F32) * whc_ref[...])
+            logit = channel_sum(unit * whc_ref[...])
             logit_ref[f - 3, :, cols] = logit
             dlogit = weight * (sigmoid(logit) - tgt[pl.ds(frame, 1), cols])
-            final_ref[f, :, cols] = final
+            final_ref[f, :, cols] = unit.astype(BF16)
             dlog[f, :, cols] = dlogit
             dhid = (inv * dlogit) * (whc_ref[...] - unit * (logit * (1.0 / chans)))
             dh2[f, :, cols] = dhid
-            dm1[f, :, cols] = (dhid * (s + y * (1.0 - s))).astype(BF16)
+            dm1[f, :, cols] = (dhid * slope2).astype(BF16)
 
     def back1(f):
-        ok = frame_ok(f)
         for cols in chunks:
             dnorm = dot_nn(wtb_ref[1], stack(dm1, f + 2, f, f - 2, cols))
             unit = n1[f, :, cols].astype(F32)
             mean = channel_sum(dnorm * unit) * (1.0 / chans)
             dhid = dh2[f, :, cols] + inv1[f, :, cols] * (dnorm - unit * mean)
             dh2[f, :, cols] = dhid
-            dm0[f, :, cols] = (dhid * (sp0[f, :, cols] * ok)).astype(BF16)
+            dm0[f, :, cols] = (dhid * sp0[f, :, cols]).astype(BF16)
 
     def back0(f):
         b = f - HALO
@@ -312,15 +319,11 @@
             unit = n0[f, :, cols].astype(F32)
             mean = channel_sum(dnorm * unit) * (1.0 / chans)
             dhid = dh2[f, :, cols] + inv0[f, :, cols] * (dnorm - unit * mean)
-            dfeat = dhid.astype(BF16).astype(F32)
-            dpre = dfeat * slope[b, :, cols].astype(F32)
+            dpre = dhid * slope[b, :, cols].astype(F32)
             if not inside:
                 dpre_ref[b, :, cols] = dpre.astype(BF16)
-            dpre = dpre.astype(BF16).astype(F32)
             for r in range(step // width):
-                spread(
-                    dpre[:, r * width : (r + 1) * width], ds, cols.start // width + r, -1
-                )
+                spread(dpre[:, r * width : (r + 1) * width], ds, cols.start // width + r, -1)
         center = xs[b]
         blank = jnp.zeros((chans, width), BF16)
         taller = jnp.concatenate([center[:, width:], blank], axis=1)
@@ -338,18 +341,27 @@
             back[b] = xt[...].astype(BF16).reshape(chans, rows, width)
 
     grad_ref[...] = init_ref[...]
-    loop(0, hi + HALO, norm0)
-    loop(1, hi + HALO - 1, layer0)
-    loop(3, hi + 3, layer1)
-    loop(lo - 1, hi + 1, back1)
-    for copy in late:
-        copy.wait()
-    loop(lo, hi, back0)
+    stages = [
+        (back0, 5, lo, hi),
+        (back1, 3, lo - 1, hi + 1),
+        (layer1, 0, 3, hi + 3),
+        (layer0, -3, 1, hi + HALO - 1),
+        (norm0, -5, 0, hi + HALO),
+    ]
+    cuts = sorted({a + d for _, d, a, _ in stages} | {b + d for _, d, _, b in stages})
+    for a, b in zip(cuts, cuts[1:]):
+        active = [(fn, d) for fn, d, p, n in stages if p + d <= a and b <= n + d]
+        if a == lo + 5:
+            for copy in late:
+                copy.wait()
+        loop(0, b - a, *[lambda i, fn=fn, f=a - d: fn(i + f) for fn, d in active])
+    if inside is False:
+        grad_ref[:5] = grad_ref[:5] * 0.5
     if inside:
-        layer = meta_ref[1 + counts]
+        layer = meta_ref[base + 1 + counts]
         leaving = []
         for k in range(members):
-            src = back.at[pl.ds(meta_ref[1 + k] - HALO, here)]
+            src = back.at[pl.ds(meta_ref[base + 1 + k] - HALO, here)]
             dst = send_ref.at[k - 1] if k else out_ref.at[:, :, layer]
             leaving.append(pltpu.make_async_copy(src, dst, sems.at[k]))
         for copy in leaving:
@@ -358,7 +370,7 @@
             copy.wait()
 
 
-def run_temporal(meta, vmem_args, weights, pieces, places, slopes, xss, inside, into, dims, layers):
+def run_temporal(meta, base, vmem_args, weights, pieces, places, slopes, xss, inside, into, dims, layers):
     own, chans, vox, total, members, width = dims
     rows, here = vox // width, own // members
     every = own + 2 * HALO
@@ -379,7 +391,7 @@
         shapes.append(sds((own, chans, vox), BF16))
         specs.append(vmem)
     return pl.pallas_call(
-        functools.partial(temporal_kernel, tuple(places), inside, aliased, dims),
+        functools.partial(temporal_kernel, tuple(places), inside, aliased, base, dims),
         name="temporal",
         out_shape=shapes,
         in_specs=[smem, smem] + [vmem] * len(vmem_args) + [hbm] * (loose + aliased),
@@ -429,16 +441,16 @@
     return lax.dynamic_index_in_dim(value, index, axis, False)
 
 
-def sum_over_tiles(value, tiles, others):
+def sum_over_tiles(value, tiles, g, others):
     if tiles & (tiles - 1):
         return lax.psum(value.astype(BF16), "tile").astype(F32), others
-    k = 1
-    while k < tiles:
-        if 2 * k >= tiles:
+    steps = [2**k for k in range(tiles.bit_length() - 1)]
+    steps = [k for k in steps if k >= g] + [k for k in steps if k < g]
+    for k in steps:
+        if k == steps[-1]:
             value, others = lax.optimization_barrier((value, others))
         pairs = [(a, a ^ k) for a in range(tiles)]
         value = value + lax.ppermute(value.astype(BF16), "tile", pairs).astype(F32)
-        k *= 2
     return value, others
 
 
@@ -479,16 +491,48 @@
         pairs = [(a, a + shifts[a % g] * g) for a in range(tiles)]
         return lax.ppermute(value, "tile", [p for p in pairs if 0 <= p[1] < tiles])
 
-    w9 = w_spatial.reshape(3, 3, chans, chans)
+    halved = (w_temporal.astype(F32) * 0.5).astype(BF16)
+    wt = halved.transpose(0, 2, 1, 3).reshape(2, chans, 3 * chans)
+    wtb = halved.transpose(0, 3, 1, 2).reshape(2, chans, 3 * chans)
+    w9 = (w_spatial.astype(F32) * 0.5).astype(BF16).reshape(3, 3, chans, chans)
     wb = w9.transpose(0, 3, 1, 2).reshape(3 * chans, 3 * chans)
-    wt = w_temporal.transpose(0, 2, 1, 3).reshape(2, chans, 3 * chans)
-    wtb = w_temporal.transpose(0, 3, 1, 2).reshape(2, chans, 3 * chans)
     whc = w_head.astype(F32)[:, None]
 
-    index = (m * per).astype(jnp.int32)
     mirrored = g == 2 and here <= HALO <= 2 * here
     extra = HALO - here if mirrored else 0
-    start = jnp.where(m == 0, here - extra, 0)
+    up, down = own + HALO, HALO - here
+    table, slots = [], {}
+    for a in range(tiles):
+        aq, am = a // g, a % g
+        spots = [HALO + (am - s) % g * here for s in range(g)]
+        if mirrored:
+            for k in range(2):
+                spots.append(up if am == k else down)
+                if extra:
+                    spots.append(0 if am == k else up + here)
+        else:
+            left, d = HALO, 1
+            while left > 0:
+                k = min(left, own)
+                spots += [left - k, HALO + d * own]
+                left -= k
+                d += 1
+        late = (here - extra) // max(extra, 1)
+        row = []
+
+        def put(name, *values):
+            slots[name] = len(row)
+            row.extend(values)
+
+        put("mine", am * per, late if am == 0 else 0)
+        put("theirs", 0, late if am == 1 else 0)
+        for layer in range(per):
+            put(("temporal", layer), aq * own, *spots, am * per + layer)
+        for s in range(g):
+            put(("back", s), (am - s) % g, 0 if s else am * per + per - 1)
+        table.append(row)
+    meta = lax.dynamic_index_in_dim(jnp.asarray(np.array(table, np.int32)), t, 0, False)
+
     def arrive(value, layer):
         pieces = []
         for s in range(1, g):
@@ -497,7 +541,7 @@
         return pieces
 
     arriving = [arrive(x, 0)]
-    mine = list(run_forward(index, start, extra, per, x, w_spatial))
+    mine = list(run_forward(meta, slots["mine"], extra, per, x, w_spatial))
     if per > 1:
         later, mine[1] = lax.optimization_barrier((x, mine[1]))
         arriving += [arrive(later, layer) for layer in range(1, per)]
@@ -507,7 +551,8 @@
         if extra:
             ahead.append(hop(mine[3], (1, -1)))
 
-    everyone = jnp.broadcast_to(targets, (tiles, total, spot))
+    after, mine[2] = lax.optimization_barrier((targets, mine[2]))
+    everyone = jnp.broadcast_to(after, (tiles, total, spot))
     everyone = lax.all_to_all(everyone, "tile", 0, 0, tiled=True)
     tgt = lax.dynamic_slice_in_dim(everyone, m * share, share, 0)
     if share % per:
@@ -520,21 +565,17 @@
     ready = []
     for layer in range(per):
         done = [mine]
-        start = jnp.where(m == 1, here - extra, 0)
         for piece in arriving[layer]:
-            done.append(run_forward(0, start, extra, 1, piece, w_spatial))
+            done.append(run_forward(meta, slots["theirs"], extra, 1, piece, w_spatial))
         pieces = [d[0] for d in done]
         ranks = [layer] + [0] * (g - 1)
-        places = [HALO + (m - s) % g * here for s in range(g)]
         if mirrored:
-            up, down = own + HALO, HALO - here
             pieces += ahead
             pieces.append(hop(done[1][0], (1, -1)))
             if extra:
                 pieces.append(hop(done[1][3], (-1, 1)))
             for k in range(2):
                 ranks += [0 if k else layer] * len(ahead)
-                places += [jnp.where(m == k, up, down), jnp.where(m == k, 0, up + here)][: len(ahead)]
         else:
             block = [p[k] for p, k in zip(pieces, ranks)]
             block = pick(block[::-1], g - 1 - m).reshape(own, chans, vox)
@@ -542,22 +583,20 @@
             while left > 0:
                 k = min(left, own)
                 pieces.append(hop(block[own - k :], (d,) * g)[None])
-                places.append(left - k)
                 pieces.append(hop(block[:k], (-d,) * g)[None])
-                places.append(HALO + d * own)
                 ranks += [0, 0]
                 left -= k
                 d += 1
-        meta = jnp.stack([jnp.asarray(v, jnp.int32) for v in [q * own] + places + [index + layer]])
-        ready.append([meta, pieces, ranks, [d[1] for d in done], [d[2] for d in done]])
+        ready.append([layer, pieces, ranks, [d[1] for d in done], [d[2] for d in done]])
 
     logits, out, homecoming = [], None, []
     for layer in range(per):
-        meta, pieces, ranks, slopes, xcs = ready[layer]
+        _, pieces, ranks, slopes, xcs = ready[layer]
         inside = layer < per - 1
         part = share // per if share % per == 0 else 1
         logit, grads, *result = run_temporal(
             meta,
+            slots["temporal", layer],
             (wt, wtb, whc, tgt[layer * part : (layer + 1) * part], grads, wb),
             frame_weight,
             pieces,
@@ -585,14 +624,12 @@
     layer = per - 1
     backs = []
     for s in range(1, g):
-        frames = jnp.stack([(m - s) % g * here, 0]).astype(jnp.int32)
-        dx = run_backward(frames, dpre, wb, here, 1, rows, None)
+        dx = run_backward(meta, slots["back", s], dpre, wb, here, 1, rows, None)
         logits, dx = lax.optimization_barrier((logits, dx))
         backs.append(swap(dx, -s))
-    frames = jnp.stack([m * here, index + layer]).astype(jnp.int32)
-    out = run_backward(frames, dpre, wb, here, layers, rows, out)
-
-    grads, backs = sum_over_tiles(sum_over_reps(grads, 1), tiles, backs)
+    out = run_backward(meta, slots["back", 0], dpre, wb, here, layers, rows, out)
+
+    grads, backs = sum_over_tiles(sum_over_reps(grads, 1), tiles, g, backs)
     for s in range(1, g):
         out = lax.dynamic_update_slice_in_dim(out, backs[s - 1], (m + s) % g * per + layer, 2)
     part = grads.shape[1]

time: 152 us -> 135 us (0.89)
  Pallas kernels: 76 us -> 56.7 us
  waiting for transfers between devices: 20.3 us -> 22.5 us
  other arithmetic: 2.55 us -> 0.79 us
  starting transfers between devices: 39 us -> 40.6 us
    pallas_call x2, Pallas kernels: 48 us -> 35.7 us  [run_temporal(): pl.pallas_call(functools.partial(temporal_kernel, tuple(places), inside,...]
    ppermute x3, waiting for transfers between devices: 15.6 us -> 5.52 us  [sum_over_tiles(): value = value + lax.ppermute(value.astype(BF16), 'tile', pairs).astype(F32)]
    ppermute x6, waiting for transfers between devices: 0.02 us -> 10.1 us  [hop(): return lax.ppermute(value, 'tile', [p for p in pairs if 0 <= p[1] < tiles])]
    all_to_all x1, waiting for transfers between devices: 2.19 us -> 6.87 us  [body(): logits = lax.all_to_all(logits, 'tile', 0, 0, tiled=True)]
    pallas_call x3, Pallas kernels: 18.7 us -> 14.1 us  [run_forward(): pl.pallas_call(functools.partial(forward_kernel, middle, base), name='con...]
    ppermute x3, waiting for transfers between devices: 2.49 us -> 0.01 us  [sum_over_reps(): lax.ppermute(share(r + s).astype(BF16), 'rep', pairs).astype(F32)]
    pallas_call x2, Pallas kernels: 9.24 us -> 6.8 us  [run_backward(): pl.pallas_call(functools.partial(backward_kernel, aliased), name='conv_ba...]
    ppermute x4, starting transfers between devices: 9.07 us -> 6.99 us  [swap(): return lax.ppermute(value, 'tile', pairs)]
  transfers between devices with their start and end apart: 18 -> 18, of which waited for: 5 -> 4; matrix products, arithmetic and copies ran while one was open for 6% -> 6% of each run, Pallas kernels for 47% -> 40%
where the time goes in v4:
time: 135 us
  Pallas kernels  56.7 us (42%)
  starting transfers between devices  40.6 us (30%)
  waiting for transfers between devices  22.5 us (17%)
  local copies, waits for them, and re-layouts  12.9 us (10%)
    pallas_call x2, Pallas kernels, run_temporal(): pl.pallas_call(functools.partial(temporal_kernel, tuple(places), inside,...  35.7 us
    ppermute x6, starting transfers between devices, hop(): return lax.ppermute(value, 'tile', [p for p in pairs if 0 <= p[1] < tiles])  17.2 us
    pallas_call x3, Pallas kernels, run_forward(): pl.pallas_call(functools.partial(forward_kernel, middle, base), name='con...  14.1 us
    ppermute x6, waiting for transfers between devices, hop(): return lax.ppermute(value, 'tile', [p for p in pairs if 0 <= p[1] < tiles])  10.1 us
    ppermute x4, starting transfers between devices, swap(): return lax.ppermute(value, 'tile', pairs)  6.99 us
    all_to_all x1, waiting for transfers between devices, body(): logits = lax.all_to_all(logits, 'tile', 0, 0, tiled=True)  6.87 us
    pallas_call x2, Pallas kernels, run_backward(): pl.pallas_call(functools.partial(backward_kernel, aliased), name='conv_ba...  6.8 us
    ppermute x3, waiting for transfers between devices, sum_over_tiles(): value = value + lax.ppermute(value.astype(BF16), 'tile', pairs).astype(F32)  5.52 us
  transfers between devices with their start and end apart: 18, of which 4 were waited for; matrix products, arithmetic and copies ran while one was open for 6% of the time, Pallas kernels for 40%

profile of v4, /device:TPU:0, one launch (start us, length us, event | category | flops | bytes accessed | tf_op | source)
XLA Modules:
  0.0 134.6 jit_solution(17318792303658742139)
XLA Ops:
  0.7 1.9 %dynamic-slice_bitcast_fusion = bf16[4,64,1,8,128]{4,3,2,1,0:T(8,128)(2,1)} fusion(bf16[1,4,64,4,8,128]{5,4,3,2,1,0:T(8,128)(2,1)} %param.7, s32[]{:T(128)S(6)} %select_n.83), kind=kLoop, calls=%fused_computation.1 | loop fusion | bytes 1048580 | tf_op jit(solution)/shard_map/dynamic_slice | solution.py:539
  2.5 3.0 %collective-permute-start = (bf16[4,64,1,8,128]{4,3,2,1,0:T(8,128)(2,1)}, bf16[4,64,1,8,128]{4,3,2,1,0:T(8,128)(2,1)S(1)}, u32[]{:S(2)}, u32[]{:S(2)}) collective-permute-start(bf16[4,64,1,8,128]{4,3,2,1,0:T(8,128)(2,1)} %dynamic-slice_bitcast_fusion), channel_id=1, source_target_pairs={{0,4},{4,0},{8,12},{12,8},{16,20},{20,16},{24,28},{28,24},{1,5},{5... | collective-permute-start | bytes 1572872 | tf_op jit(solution)/shard_map/ppermute | solution.py:488
  5.5 1.2 fusion.1.meta_ref
  6.7 6.1 %conv_forward.3 = (bf16[2,4,64,1024]{3,2,1,0:T(8,128)(2,1)}, bf16[2,4,64,1024]{3,2,1,0:T(8,128)(2,1)}, bf16[2,4,64,1024]{3,2,1,0:T(8,128)(2,1)}, bf16[2,2,64,1024]{3,2,1,0:T(8,128)(2,1)}) custom-call(s32[24]{0:T(128)} %fusion.1.meta_ref, bf16[4,64,4,8,128]{4,3,2,1,0:T(8,128)(2,1)} %bitcast.43, bf16[9,64,64]{2,1,0:T(8,128)(2,1)} %w_ref.5), custom_call_target="tpu_custom_call" | custom-call | flops 1000 | bytes 1000 | tf_op jit(solution)/shard_map/conv_forward/pallas_call | solution.py:111
  12.8 0.7 broadcast_in_dim.23
  13.6 4.9 %all-to-all-start = ((bf16[8,32,512]{2,1,0:T(8,128)(2,1)}), bf16[8,32,512]{2,1,0:T(8,128)(2,1)S(1)}, u32[]{:S(2)}, u32[]{:S(2)}) async-start(bf16[8,32,512]{2,1,0:T(8,128)(2,1)} %broadcast_in_dim.23), calls=%async_computation | async-start | bytes 524288 | tf_op jit(solution)/shard_map/all_to_all | solution.py:556
  18.4 1.9 %constant_dynamic-slice_fusion.2 = bf16[4,64,1,8,128]{4,3,2,1,0:T(8,128)(2,1)} fusion(bf16[4,64,4,8,128]{4,3,2,1,0:T(8,128)(2,1)} %bitcast.44, s32[]{:T(128)S(6)} %select_n.84), kind=kLoop, calls=%fused_computation.20 | loop fusion | bytes 1048580 | tf_op jit(solution)/shard_map/dynamic_slice | solution.py:539
  20.3 2.0 %collective-permute-start.5 = (bf16[4,64,1,8,128]{4,3,2,1,0:T(8,128)(2,1)}, bf16[4,64,1,8,128]{4,3,2,1,0:T(8,128)(2,1)}, u32[]{:S(2)}, u32[]{:S(2)}) collective-permute-start(bf16[4,64,1,8,128]{4,3,2,1,0:T(8,128)(2,1)} %constant_dynamic-slice_fusion.2), channel_id=1, source_target_pairs={{0,4},{4,0},{8,12},{12,8},{16,20},{20,16},{24,28},{28,24},{1,5},{5... | collective-permute-start | bytes 1572872 | tf_op jit(solution)/shard_map/ppermute | solution.py:488
  22.4 3.4 %collective-permute-start.2 = (bf16[2,2,64,1024]{3,2,1,0:T(8,128)(2,1)}, bf16[2,2,64,1024]{3,2,1,0:T(8,128)(2,1)S(1)}, u32[]{:S(2)}, u32[]{:S(2)}) collective-permute-start(bf16[2,2,64,1024]{3,2,1,0:T(8,128)(2,1)} %get-tuple-element.47), channel_id=1, source_target_pairs={{0,8},{8,16},{12,4},{16,24},{20,12},{28,20},{1,9},{9,17},{13,5},{1... | collective-permute-start | bytes 1572872 | tf_op jit(solution)/shard_map/ppermute | solution.py:492
  25.8 1.3 collective-permute-start.1
  27.2 0.0 collective-permute-done.x_ref
  27.2 0.8 copy-done.7
  27.9 4.0 %conv_forward.4 = (bf16[1,4,64,1024]{3,2,1,0:T(8,128)(2,1)}, bf16[1,4,64,1024]{3,2,1,0:T(8,128)(2,1)}, bf16[1,4,64,1024]{3,2,1,0:T(8,128)(2,1)}, bf16[1,2,64,1024]{3,2,1,0:T(8,128)(2,1)}) custom-call(s32[24]{0:T(128)} %fusion.1.meta_ref, bf16[4,64,1,8,128]{4,3,2,1,0:T(8,128)(2,1)} %copy-done.7, bf16[9,64,64]{2,1,0:T(8,128)(2,1)} %w_ref.5), custom_call_target="tpu_custom_call" | custom-call | flops 1000 | bytes 1000 | tf_op jit(solution)/shard_map/conv_forward/pallas_call | solution.py:111
  32.0 4.6 %collective-permute-start.3 = (bf16[1,4,64,1024]{3,2,1,0:T(8,128)(2,1)}, bf16[1,4,64,1024]{3,2,1,0:T(8,128)(2,1)S(1)}, u32[]{:S(2)}, u32[]{:S(2)}) collective-permute-start(bf16[1,4,64,1024]{3,2,1,0:T(8,128)(2,1)} %get-tuple-element.46.rest_1_), channel_id=1, source_target_pairs={{0,8},{8,16},{12,4},{16,24},{20,12},{28,20},{1,9},{9,17},{13,5},{1... | collective-permute-start | bytes 1572872 | tf_op jit(solution)/shard_map/ppermute | solution.py:492
  36.6 1.3 collective-permute-start.4
  37.9 0.0 collective-permute-done.5.x_ref
  37.9 4.0 %conv_forward.5 = (bf16[1,4,64,1024]{3,2,1,0:T(8,128)(2,1)}, bf16[1,4,64,1024]{3,2,1,0:T(8,128)(2,1)}, bf16[1,4,64,1024]{3,2,1,0:T(8,128)(2,1)}, bf16[1,2,64,1024]{3,2,1,0:T(8,128)(2,1)}) custom-call(s32[24]{0:T(128)} %fusion.1.meta_ref, bf16[4,64,1,8,128]{4,3,2,1,0:T(8,128)(2,1)} %collective-permute-done.5.x_ref, bf16[9,64,64]{2,1,0:T(8,128)(2,1)} %w_ref.5), custom_call_target="tpu_custom_call" | custom-call | flops 1000 | bytes 1000 | tf_op jit(solution)/shard_map/conv_forward/pallas_call | solution.py:111
  41.9 5.4 %collective-permute-start.6 = (bf16[1,4,64,1024]{3,2,1,0:T(8,128)(2,1)}, bf16[1,4,64,1024]{3,2,1,0:T(8,128)(2,1)}, u32[]{:S(2)}, u32[]{:S(2)}) collective-permute-start(bf16[1,4,64,1024]{3,2,1,0:T(8,128)(2,1)} %get-tuple-element.61.rest_1_), channel_id=1, source_target_pairs={{0,8},{8,16},{12,4},{16,24},{20,12},{28,20},{1,9},{9,17},{13,5},{1... | collective-permute-start | bytes 1572872 | tf_op jit(solution)/shard_map/ppermute | solution.py:492
  47.3 0.1 copy.37.whc_ref
  47.4 0.2 copy.34
  47.6 0.2 reshape.53.wb_ref
  47.7 0.1 copy.36.wtb_ref
  47.8 0.1 copy.33
  48.0 0.1 copy.35.wt_ref
  48.1 0.1 pad_dynamic-slice_fusion.weight_ref
  48.2 0.0 collective-permute-done.2.rest_3_
  48.2 1.3 collective-permute-start.7
  49.5 0.0 all-to-all-done
  49.5 10.1 %collective-permute-done.4.rest_5_ = bf16[1,2,64,1024]{3,2,1,0:T(8,128)(2,1)S(1)} collective-permute-done((bf16[1,2,64,1024]{3,2,1,0:T(8,128)(2,1)}, bf16[1,2,64,1024]{3,2,1,0:T(8,128)(2,1)S(1)}, u32[]{:S(2)}, u32[]{:S(2)}) %collective-permute-start.4) | collective-permute-done | bytes 262176 | tf_op jit(solution)/shard_map/ppermute | solution.py:492
  59.6 0.0 collective-permute-done.3.rest_4_
  59.6 0.0 collective-permute-done.1.rest_2_
  59.6 0.8 copy-done.6
  60.4 0.3 copy-done.3
  60.8 18.7 %temporal.2 = (f32[14,1,1024]{2,1,0:T(1,128)S(1)}, f32[6,64,192]{2,1,0:T(8,128)S(1)}, bf16[4,64,4,8,128]{4,3,2,1,0:T(8,128)(2,1)}, bf16[1,4,64,8,128]{4,3,2,1,0:T(8,128)(2,1)S(1)}) custom-call(s32[24]{0:T(128)S(1)} %copy-done.2, f32[14]{0:T(128)S(1)} %pad_dynamic-slice_fusion.weight_ref, bf16[2,64,192]{2,1,0:T(8,128)(2,1)S(1)} %copy.35.wt_ref, ...), custom_call_target="tpu_custom_call" | custom-call | flops 1572864000 | bytes 52428800 | tf_op jit(solution)/shard_map/temporal/pallas_call | solution.py:393
  79.5 0.0 collective-permute-done.7.rest_5_
  79.5 0.0 collective-permute-done.6.rest_4_
  79.5 0.1 collective-permute-start.8
  79.7 17.0 %temporal.3 = (f32[14,1,1024]{2,1,0:T(1,128)S(1)}, f32[6,64,192]{2,1,0:T(8,128)S(1)}, bf16[8,64,1024]{2,1,0:T(8,128)(2,1)}) custom-call(s32[24]{0:T(128)S(1)} %copy-done.2, f32[14]{0:T(128)S(1)} %pad_dynamic-slice_fusion.weight_ref, bf16[2,64,192]{2,1,0:T(8,128)(2,1)S(1)} %copy.35.wt_ref, bf16[2,64,192]{2,1,0:T(8,128)(2,1)S(1)} %copy.36.wtb_ref, ...), custom_call_target="tpu_custom_call" | custom-call | flops 1572864000 | bytes 52428800 | tf_op jit(solution)/shard_map/temporal/pallas_call | solution.py:393
  96.8 0.0 collective-permute-done.8
  96.8 3.4 %conv_backward.2 = bf16[4,64,1,8,128]{4,3,2,1,0:T(8,128)(2,1)} custom-call(s32[24]{0:T(128)} %fusion.1.meta_ref, bf16[8,64,1024]{2,1,0:T(8,128)(2,1)} %get-tuple-element.72.dpre_ref, bf16[192,192]{1,0:T(8,128)(2,1)} %copy-done), custom_call_target="tpu_custom_call" | custom-call | flops 1000 | bytes 1000 | tf_op jit(solution)/shard_map/conv_backward/pallas_call | solution.py:153
  100.2 0.1 collective-permute-start.9
  100.3 1.7 %collective-permute-start.11 = (bf16[6,16,192]{2,1,0:T(8,128)(2,1)S(1)}, bf16[6,16,192]{2,1,0:T(8,128)(2,1)S(1)}, u32[]{:S(2)}, u32[]{:S(2)}) collective-permute-start(bf16[6,16,192]{2,1,0:T(8,128)(2,1)S(1)} %get-tuple-element.94), channel_id=1, source_target_pairs={{0,3},{1,0},{2,1},{3,2},{4,7},{5,4},{6,5},{7,6},{8,11},{9,8},{10,9... | collective-permute-start | bytes 110600 | tf_op jit(solution)/shard_map/ppermute | solution.py:468
  102.0 1.5 %collective-permute-start.10 = (bf16[6,16,192]{2,1,0:T(8,128)(2,1)S(1)}, bf16[6,16,192]{2,1,0:T(8,128)(2,1)S(1)}, u32[]{:S(2)}, u32[]{:S(2)}) collective-permute-start(bf16[6,16,192]{2,1,0:T(8,128)(2,1)S(1)} %get-tuple-element.95), channel_id=1, source_target_pairs={{0,2},{1,3},{2,0},{3,1},{4,6},{5,7},{6,4},{7,5},{8,10},{9,11},{10,... | collective-permute-start | bytes 110600 | tf_op jit(solution)/shard_map/ppermute | solution.py:468
  103.5 1.9 %collective-permute-start.14 = (bf16[4,64,1,8,128]{4,3,1,0,2:T(8,128)(2,1)}, bf16[4,64,1,8,128]{4,3,1,0,2:T(8,128)(2,1)S(1)}, u32[]{:S(2)}, u32[]{:S(2)}) collective-permute-start(bf16[4,64,1,8,128]{4,3,1,0,2:T(8,128)(2,1)} %bitcast.48), channel_id=1, source_target_pairs={{0,4},{4,0},{8,12},{12,8},{16,20},{20,16},{24,28},{28,24},{1,5},{5... | collective-permute-start | bytes 1572872 | tf_op jit(solution)/shard_map/ppermute | solution.py:488
  105.4 0.8 constant_dynamic-update-slice_fusion.rest_0_
  106.3 0.0 collective-permute-done.9
  106.3 0.0 collective-permute-done.11
  106.3 0.0 collective-permute-done.10
  106.3 1.5 %collective-permute-start.12 = (bf16[6,16,192]{2,1,0:T(8,128)(2,1)S(1)}, bf16[6,16,192]{2,1,0:T(8,128)(2,1)S(1)}, u32[]{:S(2)}, u32[]{:S(2)}) collective-permute-start(bf16[6,16,192]{2,1,0:T(8,128)(2,1)S(1)} %get-tuple-element.91), channel_id=1, source_target_pairs={{0,8},{4,12},{8,0},{12,4},{16,24},{20,28},{24,16},{28,20},{1,9},{5... | collective-permute-start | bytes 110600 | tf_op jit(solution)/shard_map/ppermute | solution.py:453
  107.8 2.6 %collective-permute-done.12 = bf16[6,16,192]{2,1,0:T(8,128)(2,1)S(1)} collective-permute-done((bf16[6,16,192]{2,1,0:T(8,128)(2,1)S(1)}, bf16[6,16,192]{2,1,0:T(8,128)(2,1)S(1)}, u32[]{:S(2)}, u32[]{:S(2)}) %collective-permute-start.12) | collective-permute-done | bytes 36896 | tf_op jit(solution)/shard_map/ppermute | solution.py:453
  110.5 2.4 %collective-permute-start.13 = (bf16[6,16,192]{2,1,0:T(8,128)(2,1)S(1)}, bf16[6,16,192]{2,1,0:T(8,128)(2,1)S(1)}, u32[]{:S(2)}, u32[]{:S(2)}) collective-permute-start(bf16[6,16,192]{2,1,0:T(8,128)(2,1)S(1)} %fusion), channel_id=1, source_target_pairs={{0,16},{4,20},{8,24},{12,28},{16,0},{20,4},{24,8},{28,12},{1,17},{... | collective-permute-start | bytes 110600 | tf_op jit(solution)/shard_map/ppermute | solution.py:453
  112.9 0.6 pad_maximum_fusion
  113.5 3.4 %conv_backward.3 = bf16[4,64,4,8,128]{4,3,2,1,0:T(8,128)(2,1)} custom-call(s32[24]{0:T(128)} %fusion.1.meta_ref, bf16[8,64,1024]{2,1,0:T(8,128)(2,1)} %get-tuple-element.72.dpre_ref, bf16[192,192]{1,0:T(8,128)(2,1)} %copy-done, bf16[4,64,4,8,128]{4,3,2,1,0:T(8,128)(2,1)} %constant_dynamic-update-slice_fusion.rest_0_), custom_call_target="tpu_custom_call", output_to_operand_aliasing={{}: (3, {})} | custom-call | flops 1000 | bytes 1000 | tf_op jit(solution)/shard_map/conv_backward/pallas_call | solution.py:153
  116.9 3.9 %all-to-all-start.1 = ((bf16[8,8,512]{2,1,0:T(8,128)(2,1)}), bf16[8,8,512]{2,1,0:T(8,128)(2,1)S(1)}, u32[]{:S(2)}, u32[]{:S(2)}) async-start(bf16[8,8,512]{2,1,0:T(8,128)(2,1)} %pad_maximum_fusion), calls=%async_computation.1 | async-start | bytes 131072 | tf_op jit(solution)/shard_map/all_to_all | solution.py:643
  120.9 6.9 %all-to-all-done.1 = bf16[8,8,512]{2,1,0:T(8,128)(2,1)S(1)} async-done(((bf16[8,8,512]{2,1,0:T(8,128)(2,1)}), bf16[8,8,512]{2,1,0:T(8,128)(2,1)S(1)}, u32[]{:S(2)}, u32[]{:S(2)}) %all-to-all-start.1) | async-done | bytes 65568 | tf_op jit(solution)/shard_map/all_to_all | solution.py:643
  127.8 0.6 dynamic-slice_bitcast_fusion.1
  128.4 0.5 collective-permute-start.15
  128.8 0.8 bitcast_dynamic-update-slice_fusion
  129.7 2.9 %collective-permute-done.15 = bf16[6,16,192]{2,1,0:T(8,128)(2,1)S(1)} collective-permute-done((bf16[6,16,192]{2,1,0:T(8,128)(2,1)S(1)}, bf16[6,16,192]{2,1,0:T(8,128)(2,1)S(1)}, u32[]{:S(2)}, u32[]{:S(2)}) %collective-permute-start.15) | collective-permute-done | bytes 36896 | tf_op jit(solution)/shard_map/ppermute | solution.py:453
  132.6 0.1 reshape.58
  132.7 0.6 copy.44
  133.3 0.1 reshape.56
  133.4 0.6 copy.43
  134.0 0.6 fusion.2
  (42 shorter events, 0.3 us)
Async XLA Ops:
  0.6 12.2 %copy-start.9 = (bf16[1,32,512]{2,1,0:T(8,128)(2,1)S(1)}, bf16[1,32,512]{2,1,0:T(8,128)(2,1)}, u32[]{:S(2)}) copy-start(bf16[1,32,512]{2,1,0:T(8,128)(2,1)} %param.11) | copy-start | bytes 98308
  2.5 24.5 %copy-start.8 = (bf16[2,3,64,64]{3,2,1,0:T(8,128)(2,1)S(1)}, bf16[2,3,64,64]{3,2,1,0:T(8,128)(2,1)}, u32[]{:S(2)}) copy-start(bf16[2,3,64,64]{3,2,1,0:T(8,128)(2,1)} %param.9) | copy-start | bytes 147460
  2.5 24.6 %collective-permute-start = (bf16[4,64,1,8,128]{4,3,2,1,0:T(8,128)(2,1)}, bf16[4,64,1,8,128]{4,3,2,1,0:T(8,128)(2,1)S(1)}, u32[]{:S(2)}, u32[]{:S(2)}) collective-permute-start(bf16[4,64,1,8,128]{4,3,2,1,0:T(8,128)(2,1)} %dynamic-slice_bitcast_fusion), channel_id=1, source_target_pairs={{0,4},{4,0},{8,12},{12,8},{16,20},{20,16},{24,28},{28,24},{1,5},{5... | collective-permute-start | bytes 1572872 | tf_op jit(solution)/shard_map/ppermute | solution.py:488
  6.7 20.4 %copy-start.4 = (bf16[9,64,64]{2,1,0:T(8,128)(2,1)S(1)}, bf16[9,64,64]{2,1,0:T(8,128)(2,1)}, u32[]{:S(2)}) copy-start(bf16[9,64,64]{2,1,0:T(8,128)(2,1)} %w_ref.5) | copy-start | bytes 221188
  12.8 23.8 %copy-start.10 = (bf16[64]{0:T(256)(128)(2,1)S(1)}, bf16[64]{0:T(256)(128)(2,1)}, u32[]{:S(2)}) copy-start(bf16[64]{0:T(256)(128)(2,1)} %param.10) | copy-start | bytes 388
  12.8 34.5 %copy-start.11 = (s32[1,32]{1,0:T(1,128)S(1)}, s32[1,32]{1,0:T(1,128)}, u32[]{:S(2)}) copy-start(s32[1,32]{1,0:T(1,128)} %param.12) | copy-start | bytes 388
  13.6 35.9 %all-to-all-start = ((bf16[8,32,512]{2,1,0:T(8,128)(2,1)}), bf16[8,32,512]{2,1,0:T(8,128)(2,1)S(1)}, u32[]{:S(2)}, u32[]{:S(2)}) async-start(bf16[8,32,512]{2,1,0:T(8,128)(2,1)} %broadcast_in_dim.23), calls=%async_computation | async-start | bytes 524288 | tf_op jit(solution)/shard_map/all_to_all | solution.py:556
  20.3 40.4 %copy-start.2 = (s32[24]{0:T(128)S(1)}, s32[24]{0:T(128)}, u32[]{:S(2)}) copy-start(s32[24]{0:T(128)} %fusion.1.meta_ref) | copy-start | bytes 292
  20.3 17.6 %collective-permute-start.5 = (bf16[4,64,1,8,128]{4,3,2,1,0:T(8,128)(2,1)}, bf16[4,64,1,8,128]{4,3,2,1,0:T(8,128)(2,1)}, u32[]{:S(2)}, u32[]{:S(2)}) collective-permute-start(bf16[4,64,1,8,128]{4,3,2,1,0:T(8,128)(2,1)} %constant_dynamic-slice_fusion.2), channel_id=1, source_target_pairs={{0,4},{4,0},{8,12},{12,8},{16,20},{20,16},{24,28},{28,24},{1,5},{5... | collective-permute-start | bytes 1572872 | tf_op jit(solution)/shard_map/ppermute | solution.py:488
  22.4 25.8 %collective-permute-start.2 = (bf16[2,2,64,1024]{3,2,1,0:T(8,128)(2,1)}, bf16[2,2,64,1024]{3,2,1,0:T(8,128)(2,1)S(1)}, u32[]{:S(2)}, u32[]{:S(2)}) collective-permute-start(bf16[2,2,64,1024]{3,2,1,0:T(8,128)(2,1)} %get-tuple-element.47), channel_id=1, source_target_pairs={{0,8},{8,16},{12,4},{16,24},{20,12},{28,20},{1,9},{9,17},{13,5},{1... | collective-permute-start | bytes 1572872 | tf_op jit(solution)/shard_map/ppermute | solution.py:492
  25.8 33.8 %collective-permute-start.1 = (bf16[2,4,64,1024]{3,2,1,0:T(8,128)(2,1)}, bf16[2,4,64,1024]{3,2,1,0:T(8,128)(2,1)S(1)}, u32[]{:S(2)}, u32[]{:S(2)}) collective-permute-start(bf16[2,4,64,1024]{3,2,1,0:T(8,128)(2,1)} %get-tuple-element.60.rest_0_), channel_id=1, source_target_pairs={{4,12},{8,0},{12,20},{16,8},{20,28},{24,16},{5,13},{9,1},{13,21},{... | collective-permute-start | bytes 3145736 | tf_op jit(solution)/shard_map/ppermute | solution.py:492
  27.2 0.8 copy-start.7
  32.0 27.6 %collective-permute-start.3 = (bf16[1,4,64,1024]{3,2,1,0:T(8,128)(2,1)}, bf16[1,4,64,1024]{3,2,1,0:T(8,128)(2,1)S(1)}, u32[]{:S(2)}, u32[]{:S(2)}) collective-permute-start(bf16[1,4,64,1024]{3,2,1,0:T(8,128)(2,1)} %get-tuple-element.46.rest_1_), channel_id=1, source_target_pairs={{0,8},{8,16},{12,4},{16,24},{20,12},{28,20},{1,9},{9,17},{13,5},{1... | collective-permute-start | bytes 1572872 | tf_op jit(solution)/shard_map/ppermute | solution.py:492
  36.6 23.0 %collective-permute-start.4 = (bf16[1,2,64,1024]{3,2,1,0:T(8,128)(2,1)}, bf16[1,2,64,1024]{3,2,1,0:T(8,128)(2,1)S(1)}, u32[]{:S(2)}, u32[]{:S(2)}) collective-permute-start(bf16[1,2,64,1024]{3,2,1,0:T(8,128)(2,1)} %get-tuple-element.48), channel_id=1, source_target_pairs={{4,12},{8,0},{12,20},{16,8},{20,28},{24,16},{5,13},{9,1},{13,21},{... | collective-permute-start | bytes 786440 | tf_op jit(solution)/shard_map/ppermute | solution.py:492
  41.9 37.6 %collective-permute-start.6 = (bf16[1,4,64,1024]{3,2,1,0:T(8,128)(2,1)}, bf16[1,4,64,1024]{3,2,1,0:T(8,128)(2,1)}, u32[]{:S(2)}, u32[]{:S(2)}) collective-permute-start(bf16[1,4,64,1024]{3,2,1,0:T(8,128)(2,1)} %get-tuple-element.61.rest_1_), channel_id=1, source_target_pairs={{0,8},{8,16},{12,4},{16,24},{20,12},{28,20},{1,9},{9,17},{13,5},{1... | collective-permute-start | bytes 1572872 | tf_op jit(solution)/shard_map/ppermute | solution.py:492
  47.7 32.0 %copy-start = (bf16[192,192]{1,0:T(8,128)(2,1)}, bf16[192,192]{1,0:T(8,128)(2,1)S(1)}, u32[]{:S(2)}) copy-start(bf16[192,192]{1,0:T(8,128)(2,1)S(1)} %reshape.53.wb_ref) | copy-start | bytes 221188
  48.2 11.4 %copy-start.5 = (bf16[2,2,64,1024]{3,2,1,0:T(8,128)(2,1)}, bf16[2,2,64,1024]{3,2,1,0:T(8,128)(2,1)S(1)}, u32[]{:S(2)}) copy-start(bf16[2,2,64,1024]{3,2,1,0:T(8,128)(2,1)S(1)} %collective-permute-done.2.rest_3_) | copy-start | bytes 1572868
  48.2 31.3 %collective-permute-start.7 = (bf16[1,2,64,1024]{3,2,1,0:T(8,128)(2,1)}, bf16[1,2,64,1024]{3,2,1,0:T(8,128)(2,1)S(1)}, u32[]{:S(2)}, u32[]{:S(2)}) collective-permute-start(bf16[1,2,64,1024]{3,2,1,0:T(8,128)(2,1)} %get-tuple-element.58), channel_id=1, source_target_pairs={{4,12},{8,0},{12,20},{16,8},{20,28},{24,16},{5,13},{9,1},{13,21},{... | collective-permute-start | bytes 786440 | tf_op jit(solution)/shard_map/ppermute | solution.py:492
  59.6 0.8 copy-start.6
  59.6 1.2 copy-start.3
  60.8 18.9 %copy-start.1 = (bf16[1,4,64,1024]{3,2,1,0:T(8,128)(2,1)S(1)}, bf16[1,4,64,1024]{3,2,1,0:T(8,128)(2,1)}, u32[]{:S(2)}) copy-start(bf16[1,4,64,1024]{3,2,1,0:T(8,128)(2,1)} %get-tuple-element.61.rest_1_) | copy-start | bytes 1572868
  79.5 17.3 %collective-permute-start.8 = (bf16[4,64,1,8,128]{4,3,2,1,0:T(8,128)(2,1)S(1)}, bf16[4,64,1,8,128]{4,3,2,1,0:T(8,128)(2,1)S(1)}, u32[]{:S(2)}, u32[]{:S(2)}) collective-permute-start(bf16[4,64,1,8,128]{4,3,2,1,0:T(8,128)(2,1)S(1)} %bitcast.42), channel_id=1, source_target_pairs={{0,4},{4,0},{8,12},{12,8},{16,20},{20,16},{24,28},{28,24},{1,5},{5... | collective-permute-start | bytes 1572872 | tf_op jit(solution)/shard_map/ppermute | solution.py:488
  100.2 6.0 %collective-permute-start.9 = (bf16[6,16,192]{2,1,0:T(8,128)(2,1)S(1)}, bf16[6,16,192]{2,1,0:T(8,128)(2,1)S(1)}, u32[]{:S(2)}, u32[]{:S(2)}) collective-permute-start(bf16[6,16,192]{2,1,0:T(8,128)(2,1)S(1)} %get-tuple-element.93), channel_id=1, source_target_pairs={{0,1},{1,2},{2,3},{3,0},{4,5},{5,6},{6,7},{7,4},{8,9},{9,10},{10,1... | collective-permute-start | bytes 110600 | tf_op jit(solution)/shard_map/ppermute | solution.py:468
  100.3 6.0 %collective-permute-start.11 = (bf16[6,16,192]{2,1,0:T(8,128)(2,1)S(1)}, bf16[6,16,192]{2,1,0:T(8,128)(2,1)S(1)}, u32[]{:S(2)}, u32[]{:S(2)}) collective-permute-start(bf16[6,16,192]{2,1,0:T(8,128)(2,1)S(1)} %get-tuple-element.94), channel_id=1, source_target_pairs={{0,3},{1,0},{2,1},{3,2},{4,7},{5,4},{6,5},{7,6},{8,11},{9,8},{10,9... | collective-permute-start | bytes 110600 | tf_op jit(solution)/shard_map/ppermute | solution.py:468
  102.0 4.3 %collective-permute-start.10 = (bf16[6,16,192]{2,1,0:T(8,128)(2,1)S(1)}, bf16[6,16,192]{2,1,0:T(8,128)(2,1)S(1)}, u32[]{:S(2)}, u32[]{:S(2)}) collective-permute-start(bf16[6,16,192]{2,1,0:T(8,128)(2,1)S(1)} %get-tuple-element.95), channel_id=1, source_target_pairs={{0,2},{1,3},{2,0},{3,1},{4,6},{5,7},{6,4},{7,5},{8,10},{9,11},{10,... | collective-permute-start | bytes 110600 | tf_op jit(solution)/shard_map/ppermute | solution.py:468
  103.5 24.9 %collective-permute-start.14 = (bf16[4,64,1,8,128]{4,3,1,0,2:T(8,128)(2,1)}, bf16[4,64,1,8,128]{4,3,1,0,2:T(8,128)(2,1)S(1)}, u32[]{:S(2)}, u32[]{:S(2)}) collective-permute-start(bf16[4,64,1,8,128]{4,3,1,0,2:T(8,128)(2,1)} %bitcast.48), channel_id=1, source_target_pairs={{0,4},{4,0},{8,12},{12,8},{16,20},{20,16},{24,28},{28,24},{1,5},{5... | collective-permute-start | bytes 1572872 | tf_op jit(solution)/shard_map/ppermute | solution.py:488
  106.3 4.2 %collective-permute-start.12 = (bf16[6,16,192]{2,1,0:T(8,128)(2,1)S(1)}, bf16[6,16,192]{2,1,0:T(8,128)(2,1)S(1)}, u32[]{:S(2)}, u32[]{:S(2)}) collective-permute-start(bf16[6,16,192]{2,1,0:T(8,128)(2,1)S(1)} %get-tuple-element.91), channel_id=1, source_target_pairs={{0,8},{4,12},{8,0},{12,4},{16,24},{20,28},{24,16},{28,20},{1,9},{5... | collective-permute-start | bytes 110600 | tf_op jit(solution)/shard_map/ppermute | solution.py:453
  110.5 10.4 %collective-permute-start.13 = (bf16[6,16,192]{2,1,0:T(8,128)(2,1)S(1)}, bf16[6,16,192]{2,1,0:T(8,128)(2,1)S(1)}, u32[]{:S(2)}, u32[]{:S(2)}) collective-permute-start(bf16[6,16,192]{2,1,0:T(8,128)(2,1)S(1)} %fusion), channel_id=1, source_target_pairs={{0,16},{4,20},{8,24},{12,28},{16,0},{20,4},{24,8},{28,12},{1,17},{... | collective-permute-start | bytes 110600 | tf_op jit(solution)/shard_map/ppermute | solution.py:453
  116.9 10.8 %all-to-all-start.1 = ((bf16[8,8,512]{2,1,0:T(8,128)(2,1)}), bf16[8,8,512]{2,1,0:T(8,128)(2,1)S(1)}, u32[]{:S(2)}, u32[]{:S(2)}) async-start(bf16[8,8,512]{2,1,0:T(8,128)(2,1)} %pad_maximum_fusion), calls=%async_computation.1 | async-start | bytes 131072 | tf_op jit(solution)/shard_map/all_to_all | solution.py:643
  128.4 4.2 %collective-permute-start.15 = (bf16[6,16,192]{2,1,0:T(8,128)(2,1)S(1)}, bf16[6,16,192]{2,1,0:T(8,128)(2,1)S(1)}, u32[]{:S(2)}, u32[]{:S(2)}) collective-permute-start(bf16[6,16,192]{2,1,0:T(8,128)(2,1)S(1)} %convert_element_type.72), channel_id=1, source_target_pairs={{0,4},{4,0},{8,12},{12,8},{16,20},{20,16},{24,28},{28,24},{1,5},{5... | collective-permute-start | bytes 110600 | tf_op jit(solution)/shard_map/ppermute | solution.py:453

commit v5 on v4

--- a/solution.py
+++ b/solution.py
@@ -133,53 +133,9 @@
     )(meta, x, w_spatial)
 
 
-def backward_kernel(aliased, meta_ref, dpre_ref, wb_ref, *rest):
-    dx_ref, ds, xt = rest[-3:]
-    frames, chans, _, rows, width = dx_ref.shape
-    for n in range(frames):
-        for r in range(rows):
-            spread(dpre_ref[n, :, r * width : (r + 1) * width].astype(F32), ds.at[n], r, -1)
-    for n in range(frames):
-        for r, row in enumerate(conv_rows(wb_ref, ds.at[n], -1, rows, chans, width)):
-            xt[n, pl.ds(r, chans, stride=rows), :] = row
-        dx_ref[n, :, 0] = xt[n].astype(BF16).reshape(chans, rows, width)
-
-
-def run_backward(meta, base, dpre, wb, n, layers, rows, into):
-    chans, vox = dpre.shape[1:]
-    width = vox // rows
-    aliased = into is not None
-    frames = 2 - n % 2
-    return pl.pallas_call(
-        functools.partial(backward_kernel, aliased),
-        name="conv_backward",
-        out_shape=jax.ShapeDtypeStruct((n, chans, layers, rows, width), BF16),
-        grid_spec=pltpu.PrefetchScalarGridSpec(
-            num_scalar_prefetch=1,
-            grid=(n // frames,),
-            in_specs=[
-                pl.BlockSpec(
-                    (frames, chans, vox), lambda f, meta: (meta[base] * (n // frames) + f, 0, 0)
-                ),
-                pl.BlockSpec((3 * chans, 3 * chans), lambda f, meta: (0, 0)),
-            ]
-            + [pl.BlockSpec(memory_space=pl.ANY)] * aliased,
-            out_specs=pl.BlockSpec(
-                (frames, chans, 1, rows, width), lambda f, meta: (f, 0, meta[base + 1], 0, 0)
-            ),
-            scratch_shapes=[
-                pltpu.VMEM((frames, 3 * chans, vox), BF16),
-                pltpu.VMEM((frames, chans * rows, width), F32),
-            ],
-        ),
-        input_output_aliases={3: 0} if aliased else {},
-        cost_estimate=pl.CostEstimate(flops=1000, bytes_accessed=1000, transcendentals=0),
-    )(meta, dpre, wb, *([into] if aliased else []))
-
-
 def temporal_kernel(
     places,
-    inside,
+    last,
     aliased,
     base,
     dims,
@@ -202,10 +158,10 @@
     xs_in = [ref.at[k] for ref, k in zip(rest[counts + members : counts + 2 * members], places)]
     rest = rest[counts + 2 * members + aliased :]
     logit_ref, grad_ref = rest[:2]
-    if inside:
-        out_ref, send_ref, back = rest[2], rest[3], rest[-1]
-    else:
-        dpre_ref = rest[2]
+    out_ref, send_ref, back = rest[2:4] + rest[-1:]
+    taps = grad_ref
+    if last:
+        grad_ref = rest[-2]
     (
         feats,
         slope,
@@ -225,7 +181,7 @@
         xt,
         tgt,
         sems,
-    ) = rest[3 + inside : 21 + inside]
+    ) = rest[4:22]
     step = min(256, vox)
     lo, hi = HALO, HALO + own
     first = meta_ref[base]
@@ -320,8 +276,6 @@
             mean = channel_sum(dnorm * unit) * (1.0 / chans)
             dhid = dh2[f, :, cols] + inv0[f, :, cols] * (dnorm - unit * mean)
             dpre = dhid * slope[b, :, cols].astype(F32)
-            if not inside:
-                dpre_ref[b, :, cols] = dpre.astype(BF16)
             for r in range(step // width):
                 spread(dpre[:, r * width : (r + 1) * width], ds, cols.start // width + r, -1)
         center = xs[b]
@@ -335,10 +289,9 @@
         grad_ref[4] += dot_nt(dm1[f], stack(n1, f - 2, f, f + 2, whole))
         head = jnp.broadcast_to(dlog[f].astype(BF16), (chans, vox))
         grad_ref[5, :, :chans] += dot_nt(head, final_ref[f])
-        if inside:
-            for r, row in enumerate(conv_rows(wb_ref, ds, -1, rows, chans, width)):
-                xt[pl.ds(r, chans, stride=rows), :] = row
-            back[b] = xt[...].astype(BF16).reshape(chans, rows, width)
+        for r, row in enumerate(conv_rows(wb_ref, ds, -1, rows, chans, width)):
+            xt[pl.ds(r, chans, stride=rows), :] = row
+        back[b] = xt[...].astype(BF16).reshape(chans, rows, width)
 
     grad_ref[...] = init_ref[...]
     stages = [
@@ -355,22 +308,27 @@
             for copy in late:
                 copy.wait()
         loop(0, b - a, *[lambda i, fn=fn, f=a - d: fn(i + f) for fn, d in active])
-    if inside is False:
-        grad_ref[:5] = grad_ref[:5] * 0.5
-    if inside:
-        layer = meta_ref[base + 1 + counts]
-        leaving = []
-        for k in range(members):
-            src = back.at[pl.ds(meta_ref[base + 1 + k] - HALO, here)]
-            dst = send_ref.at[k - 1] if k else out_ref.at[:, :, layer]
-            leaving.append(pltpu.make_async_copy(src, dst, sems.at[k]))
-        for copy in leaving:
-            copy.start()
-        for copy in leaving:
-            copy.wait()
-
-
-def run_temporal(meta, base, vmem_args, weights, pieces, places, slopes, xss, inside, into, dims, layers):
+    layer = meta_ref[base + 1 + counts]
+    leaving = []
+    for k in range(members):
+        src = back.at[pl.ds(meta_ref[base + 1 + k] - HALO, here)]
+        dst = send_ref.at[k - 1] if k else out_ref.at[:, :, layer]
+        leaving.append(pltpu.make_async_copy(src, dst, sems.at[k]))
+    for copy in leaving:
+        copy.start()
+    if last:
+        for k in range(3):
+            cols = slice(k * chans, (k + 1) * chans)
+            for j in range(3):
+                taps[3 * k + j] = grad_ref[j, :, cols] * 0.5
+            for l in range(2):
+                taps[9 + 3 * l + k] = grad_ref[3 + l, :, cols] * 0.5
+        taps[15] = grad_ref[5, :, :chans]
+    for copy in leaving:
+        copy.wait()
+
+
+def run_temporal(meta, base, vmem_args, weights, pieces, places, slopes, xss, last, into, dims, layers):
     own, chans, vox, total, members, width = dims
     rows, here = vox // width, own // members
     every = own + 2 * HALO
@@ -381,17 +339,16 @@
     loose = len(pieces) + 2 * members
     aliased = into is not None
     frame = lambda n, c, dt: pltpu.VMEM((n, c, vox), dt)
-    shapes = [sds((own + 6, 1, vox), F32), sds((6, chans, 3 * chans), F32)]
-    specs = [vmem, vmem]
-    if inside:
-        shapes.append(sds((here, chans, layers, rows, width), BF16))
-        shapes.append(sds((members - 1, here, chans, rows, width), BF16))
-        specs += [hbm, hbm]
-    else:
-        shapes.append(sds((own, chans, vox), BF16))
-        specs.append(vmem)
+    sums = (6, chans, 3 * chans)
+    shapes = [
+        sds((own + 6, 1, vox), F32),
+        sds((16, chans, chans) if last else sums, F32),
+        sds((here, chans, layers, rows, width), BF16),
+        sds((members - 1, here, chans, rows, width), BF16),
+    ]
+    specs = [vmem, vmem, hbm, hbm]
     return pl.pallas_call(
-        functools.partial(temporal_kernel, tuple(places), inside, aliased, base, dims),
+        functools.partial(temporal_kernel, tuple(places), last, aliased, base, dims),
         name="temporal",
         out_shape=shapes,
         in_specs=[smem, smem] + [vmem] * len(vmem_args) + [hbm] * (loose + aliased),
@@ -417,7 +374,8 @@
             pltpu.VMEM((total, vox), F32),
             pltpu.SemaphoreType.DMA((loose,)),
         ]
-        + [pltpu.VMEM((own, chans, rows, width), BF16)] * inside,
+        + [pltpu.VMEM(sums, F32)] * last
+        + [pltpu.VMEM((own, chans, rows, width), BF16)],
         compiler_params=pltpu.CompilerParams(vmem_limit_bytes=VMEM_LIMIT),
         cost_estimate=pl.CostEstimate(
             flops=3000 * own * chans * vox, bytes_accessed=100 * own * chans * vox, transcendentals=0
@@ -528,8 +486,6 @@
         put("theirs", 0, late if am == 1 else 0)
         for layer in range(per):
             put(("temporal", layer), aq * own, *spots, am * per + layer)
-        for s in range(g):
-            put(("back", s), (am - s) % g, 0 if s else am * per + per - 1)
         table.append(row)
     meta = lax.dynamic_index_in_dim(jnp.asarray(np.array(table, np.int32)), t, 0, False)
 
@@ -542,31 +498,22 @@
 
     arriving = [arrive(x, 0)]
     mine = list(run_forward(meta, slots["mine"], extra, per, x, w_spatial))
-    if per > 1:
-        later, mine[1] = lax.optimization_barrier((x, mine[1]))
-        arriving += [arrive(later, layer) for layer in range(1, per)]
     ahead = []
     if mirrored:
         ahead.append(hop(mine[0], (-1, 1)))
         if extra:
             ahead.append(hop(mine[3], (1, -1)))
 
-    after, mine[2] = lax.optimization_barrier((targets, mine[2]))
-    everyone = jnp.broadcast_to(after, (tiles, total, spot))
-    everyone = lax.all_to_all(everyone, "tile", 0, 0, tiled=True)
-    tgt = lax.dynamic_slice_in_dim(everyone, m * share, share, 0)
-    if share % per:
-        tgt = tgt.transpose(1, 0, 2).reshape(total, per, vox).transpose(1, 0, 2)
-    frame_weight = jnp.pad(valid[0].astype(F32) / total, (3, 3))
-    frame_weight = lax.dynamic_slice_in_dim(frame_weight, q * own, own + 6, 0)
-
     dims = (own, chans, vox, total, g, width)
     grads = jnp.zeros((6, chans, 3 * chans), F32)
-    ready = []
+    ready, asked = [], targets
     for layer in range(per):
         done = [mine]
         for piece in arriving[layer]:
-            done.append(run_forward(meta, slots["theirs"], extra, 1, piece, w_spatial))
+            done.append(list(run_forward(meta, slots["theirs"], extra, 1, piece, w_spatial)))
+        if layer == 0 and g > 1:
+            later, asked, done[1][2] = lax.optimization_barrier((x, targets, done[1][2]))
+            arriving += [arrive(later, k) for k in range(1, per)]
         pieces = [d[0] for d in done]
         ranks = [layer] + [0] * (g - 1)
         if mirrored:
@@ -589,12 +536,20 @@
                 d += 1
         ready.append([layer, pieces, ranks, [d[1] for d in done], [d[2] for d in done]])
 
+    everyone = jnp.broadcast_to(asked, (tiles, total, spot))
+    everyone = lax.all_to_all(everyone, "tile", 0, 0, tiled=True)
+    tgt = lax.dynamic_slice_in_dim(everyone, m * share, share, 0)
+    if share % per:
+        tgt = tgt.transpose(1, 0, 2).reshape(total, per, vox).transpose(1, 0, 2)
+    frame_weight = jnp.pad(valid[0].astype(F32) / total, (3, 3))
+    frame_weight = lax.dynamic_slice_in_dim(frame_weight, q * own, own + 6, 0)
+
+
     logits, out, homecoming = [], None, []
     for layer in range(per):
         _, pieces, ranks, slopes, xcs = ready[layer]
-        inside = layer < per - 1
         part = share // per if share % per == 0 else 1
-        logit, grads, *result = run_temporal(
+        logit, grads, out, sent = run_temporal(
             meta,
             slots["temporal", layer],
             (wt, wtb, whc, tgt[layer * part : (layer + 1) * part], grads, wb),
@@ -603,45 +558,34 @@
             ranks,
             slopes,
             xcs,
-            inside,
-            out if inside else None,
+            layer == per - 1,
+            out,
             dims,
             layers,
         )
         logits.append(logit[3 : 3 + own, 0])
-        if inside:
-            out, sent = result
+        if layer < per - 1:
             following = ready[layer + 1]
             following[1], sent = lax.optimization_barrier((following[1], sent))
-            for s in range(1, g):
-                dx = swap(sent[s - 1][:, :, None], -s)
-                homecoming.append(((m + s) % g * per + layer, dx))
-    dpre = result[0]
-    home = [dx for _, dx in homecoming]
-    home, dpre, grads = lax.optimization_barrier((home, dpre, grads))
-    for (place, _), dx in zip(homecoming, home):
-        out = lax.dynamic_update_slice_in_dim(out, dx, place, 2)
-    layer = per - 1
-    backs = []
-    for s in range(1, g):
-        dx = run_backward(meta, slots["back", s], dpre, wb, here, 1, rows, None)
-        logits, dx = lax.optimization_barrier((logits, dx))
-        backs.append(swap(dx, -s))
-    out = run_backward(meta, slots["back", 0], dpre, wb, here, layers, rows, out)
-
-    grads, backs = sum_over_tiles(sum_over_reps(grads, 1), tiles, g, backs)
-    for s in range(1, g):
-        out = lax.dynamic_update_slice_in_dim(out, backs[s - 1], (m + s) % g * per + layer, 2)
-    part = grads.shape[1]
-    gs = grads[:3].reshape(3, part, 3, chans).transpose(2, 0, 1, 3).reshape(9, part, chans)
-    gt = grads[3:5].reshape(2, part, 3, chans).transpose(0, 2, 1, 3)
-    gh = lax.dynamic_slice_in_dim(grads[5, 0], lax.axis_index("rep") * part, part, 0)
+        homecoming.append([swap(sent[s - 1][:, :, None], -s) for s in range(1, g)])
+    homecoming[:-1], grads = lax.optimization_barrier((homecoming[:-1], grads))
 
     logits = jnp.concatenate(logits, axis=1).astype(BF16).reshape(own, share, spot)
     logits = logits.transpose(1, 0, 2)
     logits = jnp.concatenate([logits] * g)
     logits = lax.all_to_all(logits, "tile", 0, 0, tiled=True)
+    grads, homecoming = sum_over_tiles(sum_over_reps(grads, 1), tiles, g, homecoming)
+    for layer in range(per):
+        for s in range(1, g):
+            place = (m + s) % g * per + layer
+            out = lax.dynamic_update_slice_in_dim(out, homecoming[layer][s - 1], place, 2)
+    logits, grads = lax.optimization_barrier((logits, grads))
     logits = take(logits.reshape(groups, g, own, spot), t // share, 1).reshape(1, total, spot)
+    part = grads.shape[1]
+    gs = grads[:9]
+    gt = grads[9:15].reshape(2, 3, part, chans)
+    gh = lax.dynamic_slice_in_dim(grads[15, 0], lax.axis_index("rep") * part, part, 0)
+
     return logits, out[None], gs, gt, gh
 
 

time: 135 us -> 123 us (0.911)
  waiting for transfers between devices: 22.5 us -> 10.4 us
  starting transfers between devices: 40.6 us -> 45.4 us
  Pallas kernels: 56.7 us -> 52 us
    ppermute x6, waiting for transfers between devices: 10.1 us -> 2.9 us  [hop(): return lax.ppermute(value, 'tile', [p for p in pairs if 0 <= p[1] < tiles])]
    pallas_call x4 -> x2, Pallas kernels: 42.5 us -> 37.8 us  [run_temporal(): pl.pallas_call(functools.partial(temporal_kernel, tuple(places), last, al...]
    all_to_all x1, waiting for transfers between devices: 6.87 us -> 2.33 us  [body(): logits = lax.all_to_all(logits, 'tile', 0, 0, tiled=True)]
    ppermute x3, starting transfers between devices: 4.35 us -> 7.8 us  [sum_over_tiles(): value = value + lax.ppermute(value.astype(BF16), 'tile', pairs).astype(F32)]
    ppermute x3, waiting for transfers between devices: 5.52 us -> 2.95 us  [sum_over_tiles(): value = value + lax.ppermute(value.astype(BF16), 'tile', pairs).astype(F32)]
  transfers between devices with their start and end apart: 18 -> 18, of which waited for: 4 -> 7; matrix products, arithmetic and copies ran while one was open for 6% -> 6% of each run, Pallas kernels for 40% -> 43%
where the time goes in v5:
time: 123 us; the launch traced here: 122 us
  Pallas kernels  52 us (42%)
  starting transfers between devices  45.4 us (37%)
  local copies, waits for them, and re-layouts  12.7 us (10%)
  waiting for transfers between devices  10.4 us (8%)
    pallas_call x2, Pallas kernels, run_temporal(): pl.pallas_call(functools.partial(temporal_kernel, tuple(places), last, al...  37.8 us
    ppermute x6, starting transfers between devices, hop(): return lax.ppermute(value, 'tile', [p for p in pairs if 0 <= p[1] < tiles])  17.1 us
    pallas_call x3, Pallas kernels, run_forward(): pl.pallas_call(functools.partial(forward_kernel, middle, base), name='con...  14.2 us
    ppermute x3, starting transfers between devices, sum_over_tiles(): value = value + lax.ppermute(value.astype(BF16), 'tile', pairs).astype(F32)  7.8 us
    ppermute x4, starting transfers between devices, swap(): return lax.ppermute(value, 'tile', pairs)  6.49 us
    all_to_all x1, starting transfers between devices, body(): everyone = lax.all_to_all(everyone, 'tile', 0, 0, tiled=True)  6.05 us
    all_to_all x1, starting transfers between devices, body(): logits = lax.all_to_all(logits, 'tile', 0, 0, tiled=True)  4.71 us
    ppermute x3, starting transfers between devices, sum_over_reps(): lax.ppermute(share(r + s).astype(BF16), 'rep', pairs).astype(F32)  3.28 us
  transfers between devices with their start and end apart: 18, of which 7 were waited for; matrix products, arithmetic and copies ran while one was open for 6% of the time, Pallas kernels for 43%

profile of v5, /device:TPU:0, one launch (start us, length us, event | category | flops | bytes accessed | tf_op | source)
XLA Modules:
  0.0 121.8 jit_solution(5075444739685160095)
XLA Ops:
  0.7 1.1 dynamic-slice_bitcast_fusion
  1.7 0.0 copy-start.6
  1.8 3.0 %collective-permute-start = (bf16[4,64,1,8,128]{4,3,2,1,0:T(8,128)(2,1)S(1)}, bf16[4,64,1,8,128]{4,3,2,1,0:T(8,128)(2,1)S(1)}, u32[]{:S(2)}, u32[]{:S(2)}) collective-permute-start(bf16[4,64,1,8,128]{4,3,2,1,0:T(8,128)(2,1)S(1)} %dynamic-slice_bitcast_fusion), channel_id=1, source_target_pairs={{0,4},{4,0},{8,12},{12,8},{16,20},{20,16},{24,28},{28,24},{1,5},{5... | collective-permute-start | bytes 1572872 | tf_op jit(solution)/shard_map/ppermute | solution.py:446
  4.8 1.2 fusion.3.meta_ref
  6.0 6.1 %conv_forward.4 = (bf16[2,4,64,1024]{3,2,1,0:T(8,128)(2,1)}, bf16[2,4,64,1024]{3,2,1,0:T(8,128)(2,1)}, bf16[2,4,64,1024]{3,2,1,0:T(8,128)(2,1)}, bf16[2,2,64,1024]{3,2,1,0:T(8,128)(2,1)}) custom-call(s32[20]{0:T(128)} %fusion.3.meta_ref, bf16[4,64,4,8,128]{4,3,2,1,0:T(8,128)(2,1)} %bitcast.37, bf16[9,64,64]{2,1,0:T(8,128)(2,1)} %w_ref.5), custom_call_target="tpu_custom_call" | custom-call | flops 1000 | bytes 1000 | tf_op jit(solution)/shard_map/conv_forward/pallas_call | solution.py:111
  12.1 3.6 %collective-permute-start.2 = (bf16[2,2,64,1024]{3,2,1,0:T(8,128)(2,1)}, bf16[2,2,64,1024]{3,2,1,0:T(8,128)(2,1)S(1)}, u32[]{:S(2)}, u32[]{:S(2)}) collective-permute-start(bf16[2,2,64,1024]{3,2,1,0:T(8,128)(2,1)} %get-tuple-element.46), channel_id=1, source_target_pairs={{0,8},{8,16},{12,4},{16,24},{20,12},{28,20},{1,9},{9,17},{13,5},{1... | collective-permute-start | bytes 1572872 | tf_op jit(solution)/shard_map/ppermute | solution.py:450
  15.7 1.3 %collective-permute-start.1 = (bf16[2,4,64,1024]{3,2,1,0:T(8,128)(2,1)}, bf16[2,4,64,1024]{3,2,1,0:T(8,128)(2,1)S(1)}, u32[]{:S(2)}, u32[]{:S(2)}) collective-permute-start(bf16[2,4,64,1024]{3,2,1,0:T(8,128)(2,1)} %get-tuple-element.58.rest_0_), channel_id=1, source_target_pairs={{4,12},{8,0},{12,20},{16,8},{20,28},{24,16},{5,13},{9,1},{13,21},{... | collective-permute-start | bytes 3145736 | tf_op jit(solution)/shard_map/ppermute | solution.py:450
  17.0 0.0 collective-permute-done.x_ref
  17.1 0.8 copy-done.5
  17.9 4.1 %conv_forward.3 = (bf16[1,4,64,1024]{3,2,1,0:T(8,128)(2,1)}, bf16[1,4,64,1024]{3,2,1,0:T(8,128)(2,1)}, bf16[1,4,64,1024]{3,2,1,0:T(8,128)(2,1)}, bf16[1,2,64,1024]{3,2,1,0:T(8,128)(2,1)}) custom-call(s32[20]{0:T(128)} %fusion.3.meta_ref, bf16[4,64,1,8,128]{4,3,2,1,0:T(8,128)(2,1)} %copy-done.5, bf16[9,64,64]{2,1,0:T(8,128)(2,1)} %w_ref.5), custom_call_target="tpu_custom_call" | custom-call | flops 1000 | bytes 1000 | tf_op jit(solution)/shard_map/conv_forward/pallas_call | solution.py:111
  21.9 1.9 %constant_dynamic-slice_fusion.2 = bf16[4,64,1,8,128]{4,3,2,1,0:T(8,128)(2,1)} fusion(bf16[4,64,4,8,128]{4,3,2,1,0:T(8,128)(2,1)} %bitcast.38, s32[]{:T(128)S(6)} %select_n.84), kind=kLoop, calls=%fused_computation.22 | loop fusion | bytes 1048580 | tf_op jit(solution)/shard_map/dynamic_slice | solution.py:495
  23.9 1.4 %collective-permute-start.5 = (bf16[4,64,1,8,128]{4,3,2,1,0:T(8,128)(2,1)}, bf16[4,64,1,8,128]{4,3,2,1,0:T(8,128)(2,1)}, u32[]{:S(2)}, u32[]{:S(2)}) collective-permute-start(bf16[4,64,1,8,128]{4,3,2,1,0:T(8,128)(2,1)} %constant_dynamic-slice_fusion.2), channel_id=1, source_target_pairs={{0,4},{4,0},{8,12},{12,8},{16,20},{20,16},{24,28},{28,24},{1,5},{5... | collective-permute-start | bytes 1572872 | tf_op jit(solution)/shard_map/ppermute | solution.py:446
  25.4 0.7 broadcast_in_dim.25
  26.1 6.0 %all-to-all-start = ((bf16[8,32,512]{2,1,0:T(8,128)(2,1)}), bf16[8,32,512]{2,1,0:T(8,128)(2,1)S(1)}, u32[]{:S(2)}, u32[]{:S(2)}) async-start(bf16[8,32,512]{2,1,0:T(8,128)(2,1)} %broadcast_in_dim.25), calls=%async_computation | async-start | bytes 524288 | tf_op jit(solution)/shard_map/all_to_all | solution.py:540
  32.2 4.7 %collective-permute-start.3 = (bf16[1,4,64,1024]{3,2,1,0:T(8,128)(2,1)S(1)}, bf16[1,4,64,1024]{3,2,1,0:T(8,128)(2,1)}, u32[]{:S(2)}, u32[]{:S(2)}) collective-permute-start(bf16[1,4,64,1024]{3,2,1,0:T(8,128)(2,1)S(1)} %copy-done.4), channel_id=1, source_target_pairs={{0,8},{8,16},{12,4},{16,24},{20,12},{28,20},{1,9},{9,17},{13,5},{1... | collective-permute-start | bytes 1572872 | tf_op jit(solution)/shard_map/ppermute | solution.py:450
  36.9 1.3 %collective-permute-start.4 = (bf16[1,2,64,1024]{3,2,1,0:T(8,128)(2,1)}, bf16[1,2,64,1024]{3,2,1,0:T(8,128)(2,1)S(1)}, u32[]{:S(2)}, u32[]{:S(2)}) collective-permute-start(bf16[1,2,64,1024]{3,2,1,0:T(8,128)(2,1)} %get-tuple-element.47), channel_id=1, source_target_pairs={{4,12},{8,0},{12,20},{16,8},{20,28},{24,16},{5,13},{9,1},{13,21},{... | collective-permute-start | bytes 786440 | tf_op jit(solution)/shard_map/ppermute | solution.py:450
  38.2 1.0 collective-permute-done.5.x_ref
  39.2 4.1 %conv_forward.5 = (bf16[1,4,64,1024]{3,2,1,0:T(8,128)(2,1)}, bf16[1,4,64,1024]{3,2,1,0:T(8,128)(2,1)}, bf16[1,4,64,1024]{3,2,1,0:T(8,128)(2,1)}, bf16[1,2,64,1024]{3,2,1,0:T(8,128)(2,1)}) custom-call(s32[20]{0:T(128)} %fusion.3.meta_ref, bf16[4,64,1,8,128]{4,3,2,1,0:T(8,128)(2,1)} %collective-permute-done.5.x_ref, bf16[9,64,64]{2,1,0:T(8,128)(2,1)} %w_ref.5), custom_call_target="tpu_custom_call" | custom-call | flops 1000 | bytes 1000 | tf_op jit(solution)/shard_map/conv_forward/pallas_call | solution.py:111
  43.3 4.7 %collective-permute-start.6 = (bf16[1,4,64,1024]{3,2,1,0:T(8,128)(2,1)}, bf16[1,4,64,1024]{3,2,1,0:T(8,128)(2,1)}, u32[]{:S(2)}, u32[]{:S(2)}) collective-permute-start(bf16[1,4,64,1024]{3,2,1,0:T(8,128)(2,1)} %get-tuple-element.59.rest_1_), channel_id=1, source_target_pairs={{0,8},{8,16},{12,4},{16,24},{20,12},{28,20},{1,9},{9,17},{13,5},{1... | collective-permute-start | bytes 1572872 | tf_op jit(solution)/shard_map/ppermute | solution.py:450
  48.0 0.1 copy.34.whc_ref
  48.1 0.2 copy.31
  48.2 0.2 reshape.51.wb_ref
  48.4 0.1 copy.33.wtb_ref
  48.5 0.1 copy.30
  48.6 0.1 copy.32.wt_ref
  48.8 0.1 pad_dynamic-slice_fusion.weight_ref
  48.8 0.0 collective-permute-done.2.rest_3_
  48.8 1.5 %collective-permute-start.7 = (bf16[1,2,64,1024]{3,2,1,0:T(8,128)(2,1)}, bf16[1,2,64,1024]{3,2,1,0:T(8,128)(2,1)S(1)}, u32[]{:S(2)}, u32[]{:S(2)}) collective-permute-start(bf16[1,2,64,1024]{3,2,1,0:T(8,128)(2,1)} %get-tuple-element.56), channel_id=1, source_target_pairs={{4,12},{8,0},{12,20},{16,8},{20,28},{24,16},{5,13},{9,1},{13,21},{... | collective-permute-start | bytes 786440 | tf_op jit(solution)/shard_map/ppermute | solution.py:450
  50.3 0.2 all-to-all-done
  50.6 2.9 %collective-permute-done.4.rest_5_ = bf16[1,2,64,1024]{3,2,1,0:T(8,128)(2,1)S(1)} collective-permute-done((bf16[1,2,64,1024]{3,2,1,0:T(8,128)(2,1)}, bf16[1,2,64,1024]{3,2,1,0:T(8,128)(2,1)S(1)}, u32[]{:S(2)}, u32[]{:S(2)}) %collective-permute-start.4) | collective-permute-done | bytes 262176 | tf_op jit(solution)/shard_map/ppermute | solution.py:450
  53.4 0.0 collective-permute-done.3.rest_4_
  53.4 0.0 collective-permute-done.1.rest_2_
  53.5 1.0 copy-done.1
  54.5 18.7 %temporal.2 = (f32[14,1,1024]{2,1,0:T(1,128)S(1)}, f32[6,64,192]{2,1,0:T(8,128)S(1)}, bf16[4,64,4,8,128]{4,3,2,1,0:T(8,128)(2,1)}, bf16[1,4,64,8,128]{4,3,2,1,0:T(8,128)(2,1)S(1)}) custom-call(s32[20]{0:T(128)S(1)} %copy-done, f32[14]{0:T(128)S(1)} %pad_dynamic-slice_fusion.weight_ref, bf16[2,64,192]{2,1,0:T(8,128)(2,1)S(1)} %copy.32.wt_ref, ...), custom_call_target="tpu_custom_call" | custom-call | flops 1572864000 | bytes 52428800 | tf_op jit(solution)/shard_map/temporal/pallas_call | solution.py:350
  73.2 0.0 collective-permute-done.7.rest_5_
  73.2 0.0 collective-permute-done.6.rest_4_
  73.2 0.1 collective-permute-start.8
  73.4 0.1 fusion.2
  73.5 19.1 %temporal.3 = (f32[14,1,1024]{2,1,0:T(1,128)S(1)}, f32[16,64,64]{2,1,0:T(8,128)S(1)}, bf16[4,64,4,8,128]{4,3,2,1,0:T(8,128)(2,1)}, bf16[1,4,64,8,128]{4,3,2,1,0:T(8,128)(2,1)}) custom-call(s32[20]{0:T(128)S(1)} %copy-done, f32[14]{0:T(128)S(1)} %pad_dynamic-slice_fusion.weight_ref, ...), custom_call_target="tpu_custom_call", output_to_operand_aliasing={{2}: (18, {})} | custom-call | flops 1572864000 | bytes 52428800 | tf_op jit(solution)/shard_map/temporal/pallas_call | solution.py:350
  92.6 0.0 collective-permute-done.8
  92.7 0.1 collective-permute-start.9
  92.7 1.7 %collective-permute-start.11 = (bf16[16,16,64]{2,1,0:T(8,128)(2,1)S(1)}, bf16[16,16,64]{2,1,0:T(8,128)(2,1)S(1)}, u32[]{:S(2)}, u32[]{:S(2)}) collective-permute-start(bf16[16,16,64]{2,1,0:T(8,128)(2,1)S(1)} %get-tuple-element.82), channel_id=1, source_target_pairs={{0,3},{1,0},{2,1},{3,2},{4,7},{5,4},{6,5},{7,6},{8,11},{9,8},{10,9... | collective-permute-start | bytes 98312 | tf_op jit(solution)/shard_map/ppermute | solution.py:426
  94.5 1.5 %collective-permute-start.10 = (bf16[16,16,64]{2,1,0:T(8,128)(2,1)S(1)}, bf16[16,16,64]{2,1,0:T(8,128)(2,1)S(1)}, u32[]{:S(2)}, u32[]{:S(2)}) collective-permute-start(bf16[16,16,64]{2,1,0:T(8,128)(2,1)S(1)} %get-tuple-element.83), channel_id=1, source_target_pairs={{0,2},{1,3},{2,0},{3,1},{4,6},{5,7},{6,4},{7,5},{8,10},{9,11},{10,... | collective-permute-start | bytes 98312 | tf_op jit(solution)/shard_map/ppermute | solution.py:426
  95.9 0.1 fusion.1
  96.1 2.0 %collective-permute-start.14 = (bf16[4,64,1,8,128]{4,3,1,0,2:T(8,128)(2,1)}, bf16[4,64,1,8,128]{4,3,1,0,2:T(8,128)(2,1)S(1)}, u32[]{:S(2)}, u32[]{:S(2)}) collective-permute-start(bf16[4,64,1,8,128]{4,3,1,0,2:T(8,128)(2,1)} %bitcast.47), channel_id=1, source_target_pairs={{0,4},{4,0},{8,12},{12,8},{16,20},{20,16},{24,28},{28,24},{1,5},{5... | collective-permute-start | bytes 1572872 | tf_op jit(solution)/shard_map/ppermute | solution.py:446
  98.0 0.0 collective-permute-done.9
  98.1 0.0 collective-permute-done.11
  98.1 1.0 collective-permute-done.10
  99.1 3.3 %collective-permute-start.12 = (bf16[16,16,64]{2,1,0:T(8,128)(2,1)S(1)}, bf16[16,16,64]{2,1,0:T(8,128)(2,1)S(1)}, u32[]{:S(2)}, u32[]{:S(2)}) collective-permute-start(bf16[16,16,64]{2,1,0:T(8,128)(2,1)S(1)} %get-tuple-element.79), channel_id=1, source_target_pairs={{0,8},{4,12},{8,0},{12,4},{16,24},{20,28},{24,16},{28,20},{1,9},{5... | collective-permute-start | bytes 98312 | tf_op jit(solution)/shard_map/ppermute | solution.py:411
  102.5 2.2 %collective-permute-done.12 = bf16[16,16,64]{2,1,0:T(8,128)(2,1)S(1)} collective-permute-done((bf16[16,16,64]{2,1,0:T(8,128)(2,1)S(1)}, bf16[16,16,64]{2,1,0:T(8,128)(2,1)S(1)}, u32[]{:S(2)}, u32[]{:S(2)}) %collective-permute-start.12) | collective-permute-done | bytes 32800 | tf_op jit(solution)/shard_map/ppermute | solution.py:411
  104.7 2.4 %collective-permute-start.13 = (bf16[16,16,64]{2,1,0:T(8,128)(2,1)S(1)}, bf16[16,16,64]{2,1,0:T(8,128)(2,1)S(1)}, u32[]{:S(2)}, u32[]{:S(2)}) collective-permute-start(bf16[16,16,64]{2,1,0:T(8,128)(2,1)S(1)} %fusion), channel_id=1, source_target_pairs={{0,16},{4,20},{8,24},{12,28},{16,0},{20,4},{24,8},{28,12},{1,17},{... | collective-permute-start | bytes 98312 | tf_op jit(solution)/shard_map/ppermute | solution.py:411
  107.1 0.7 copy.38
  107.8 4.7 %all-to-all-start.1 = ((bf16[8,8,512]{2,1,0:T(8,128)(2,1)}), bf16[8,8,512]{2,1,0:T(8,128)(2,1)S(1)}, u32[]{:S(2)}, u32[]{:S(2)}) async-start(bf16[8,8,512]{2,1,0:T(8,128)(2,1)} %copy.38), calls=%async_computation.1 | async-start | bytes 131072 | tf_op jit(solution)/shard_map/all_to_all | solution.py:576
  112.5 0.0 collective-permute-done.13
  112.5 0.0 collective-permute-done.14
  112.5 2.1 %collective-permute-start.15 = (bf16[16,16,64]{2,1,0:T(8,128)(2,1)S(1)}, bf16[16,16,64]{2,1,0:T(8,128)(2,1)S(1)}, u32[]{:S(2)}, u32[]{:S(2)}) collective-permute-start(bf16[16,16,64]{2,1,0:T(8,128)(2,1)S(1)} %convert_element_type.72), channel_id=1, source_target_pairs={{0,4},{4,0},{8,12},{12,8},{16,20},{20,16},{24,28},{28,24},{1,5},{5... | collective-permute-start | bytes 98312 | tf_op jit(solution)/shard_map/ppermute | solution.py:411
  114.6 0.8 bitcast_dynamic-update-slice_fusion.1
  115.5 0.8 bitcast_dynamic-update-slice_fusion
  116.3 0.7 collective-permute-done.15
  117.0 2.3 %all-to-all-done.1 = bf16[8,8,512]{2,1,0:T(8,128)(2,1)S(1)} async-done(((bf16[8,8,512]{2,1,0:T(8,128)(2,1)}), bf16[8,8,512]{2,1,0:T(8,128)(2,1)S(1)}, u32[]{:S(2)}, u32[]{:S(2)}) %all-to-all-start.1) | async-done | bytes 65568 | tf_op jit(solution)/shard_map/all_to_all | solution.py:576
  119.4 0.6 slice.28
  120.0 0.6 slice.27
  120.6 0.6 dynamic-slice_bitcast_fusion.1
  121.3 0.6 fusion.4
  (34 shorter events, 0.4 us)
Async XLA Ops:
  1.7 23.5 %copy-start.6 = (bf16[2,3,64,64]{3,2,1,0:T(8,128)(2,1)S(1)}, bf16[2,3,64,64]{3,2,1,0:T(8,128)(2,1)}, u32[]{:S(2)}) copy-start(bf16[2,3,64,64]{3,2,1,0:T(8,128)(2,1)} %param.9) | copy-start | bytes 147460
  1.8 15.3 %collective-permute-start = (bf16[4,64,1,8,128]{4,3,2,1,0:T(8,128)(2,1)S(1)}, bf16[4,64,1,8,128]{4,3,2,1,0:T(8,128)(2,1)S(1)}, u32[]{:S(2)}, u32[]{:S(2)}) collective-permute-start(bf16[4,64,1,8,128]{4,3,2,1,0:T(8,128)(2,1)S(1)} %dynamic-slice_bitcast_fusion), channel_id=1, source_target_pairs={{0,4},{4,0},{8,12},{12,8},{16,20},{20,16},{24,28},{28,24},{1,5},{5... | collective-permute-start | bytes 1572872 | tf_op jit(solution)/shard_map/ppermute | solution.py:446
  6.0 19.3 %copy-start.2 = (bf16[9,64,64]{2,1,0:T(8,128)(2,1)S(1)}, bf16[9,64,64]{2,1,0:T(8,128)(2,1)}, u32[]{:S(2)}) copy-start(bf16[9,64,64]{2,1,0:T(8,128)(2,1)} %w_ref.5) | copy-start | bytes 221188
  6.0 19.4 %copy-start.7 = (bf16[1,32,512]{2,1,0:T(8,128)(2,1)S(1)}, bf16[1,32,512]{2,1,0:T(8,128)(2,1)}, u32[]{:S(2)}) copy-start(bf16[1,32,512]{2,1,0:T(8,128)(2,1)} %param.11) | copy-start | bytes 98308
  12.1 24.8 %copy-start.8 = (bf16[64]{0:T(256)(128)(2,1)S(1)}, bf16[64]{0:T(256)(128)(2,1)}, u32[]{:S(2)}) copy-start(bf16[64]{0:T(256)(128)(2,1)} %param.10) | copy-start | bytes 388
  12.1 35.9 %copy-start.9 = (s32[1,32]{1,0:T(1,128)S(1)}, s32[1,32]{1,0:T(1,128)}, u32[]{:S(2)}) copy-start(s32[1,32]{1,0:T(1,128)} %param.12) | copy-start | bytes 388
  12.1 36.8 %collective-permute-start.2 = (bf16[2,2,64,1024]{3,2,1,0:T(8,128)(2,1)}, bf16[2,2,64,1024]{3,2,1,0:T(8,128)(2,1)S(1)}, u32[]{:S(2)}, u32[]{:S(2)}) collective-permute-start(bf16[2,2,64,1024]{3,2,1,0:T(8,128)(2,1)} %get-tuple-element.46), channel_id=1, source_target_pairs={{0,8},{8,16},{12,4},{16,24},{20,12},{28,20},{1,9},{9,17},{13,5},{1... | collective-permute-start | bytes 1572872 | tf_op jit(solution)/shard_map/ppermute | solution.py:450
  15.7 37.7 %collective-permute-start.1 = (bf16[2,4,64,1024]{3,2,1,0:T(8,128)(2,1)}, bf16[2,4,64,1024]{3,2,1,0:T(8,128)(2,1)S(1)}, u32[]{:S(2)}, u32[]{:S(2)}) collective-permute-start(bf16[2,4,64,1024]{3,2,1,0:T(8,128)(2,1)} %get-tuple-element.58.rest_0_), channel_id=1, source_target_pairs={{4,12},{8,0},{12,20},{16,8},{20,28},{24,16},{5,13},{9,1},{13,21},{... | collective-permute-start | bytes 3145736 | tf_op jit(solution)/shard_map/ppermute | solution.py:450
  17.1 0.8 copy-start.5
  21.9 10.2 %copy-start.4 = (bf16[1,4,64,1024]{3,2,1,0:T(8,128)(2,1)S(1)}, bf16[1,4,64,1024]{3,2,1,0:T(8,128)(2,1)}, u32[]{:S(2)}) copy-start(bf16[1,4,64,1024]{3,2,1,0:T(8,128)(2,1)} %get-tuple-element.45.rest_1_) | copy-start | bytes 1572868
  23.9 30.6 %copy-start = (s32[20]{0:T(128)S(1)}, s32[20]{0:T(128)}, u32[]{:S(2)}) copy-start(s32[20]{0:T(128)} %fusion.3.meta_ref) | copy-start | bytes 244
  23.9 15.3 %collective-permute-start.5 = (bf16[4,64,1,8,128]{4,3,2,1,0:T(8,128)(2,1)}, bf16[4,64,1,8,128]{4,3,2,1,0:T(8,128)(2,1)}, u32[]{:S(2)}, u32[]{:S(2)}) collective-permute-start(bf16[4,64,1,8,128]{4,3,2,1,0:T(8,128)(2,1)} %constant_dynamic-slice_fusion.2), channel_id=1, source_target_pairs={{0,4},{4,0},{8,12},{12,8},{16,20},{20,16},{24,28},{28,24},{1,5},{5... | collective-permute-start | bytes 1572872 | tf_op jit(solution)/shard_map/ppermute | solution.py:446
  26.1 24.4 %all-to-all-start = ((bf16[8,32,512]{2,1,0:T(8,128)(2,1)}), bf16[8,32,512]{2,1,0:T(8,128)(2,1)S(1)}, u32[]{:S(2)}, u32[]{:S(2)}) async-start(bf16[8,32,512]{2,1,0:T(8,128)(2,1)} %broadcast_in_dim.25), calls=%async_computation | async-start | bytes 524288 | tf_op jit(solution)/shard_map/all_to_all | solution.py:540
  32.2 21.3 %collective-permute-start.3 = (bf16[1,4,64,1024]{3,2,1,0:T(8,128)(2,1)S(1)}, bf16[1,4,64,1024]{3,2,1,0:T(8,128)(2,1)}, u32[]{:S(2)}, u32[]{:S(2)}) collective-permute-start(bf16[1,4,64,1024]{3,2,1,0:T(8,128)(2,1)S(1)} %copy-done.4), channel_id=1, source_target_pairs={{0,8},{8,16},{12,4},{16,24},{20,12},{28,20},{1,9},{9,17},{13,5},{1... | collective-permute-start | bytes 1572872 | tf_op jit(solution)/shard_map/ppermute | solution.py:450
  36.9 16.5 %collective-permute-start.4 = (bf16[1,2,64,1024]{3,2,1,0:T(8,128)(2,1)}, bf16[1,2,64,1024]{3,2,1,0:T(8,128)(2,1)S(1)}, u32[]{:S(2)}, u32[]{:S(2)}) collective-permute-start(bf16[1,2,64,1024]{3,2,1,0:T(8,128)(2,1)} %get-tuple-element.47), channel_id=1, source_target_pairs={{4,12},{8,0},{12,20},{16,8},{20,28},{24,16},{5,13},{9,1},{13,21},{... | collective-permute-start | bytes 786440 | tf_op jit(solution)/shard_map/ppermute | solution.py:450
  43.3 29.9 %collective-permute-start.6 = (bf16[1,4,64,1024]{3,2,1,0:T(8,128)(2,1)}, bf16[1,4,64,1024]{3,2,1,0:T(8,128)(2,1)}, u32[]{:S(2)}, u32[]{:S(2)}) collective-permute-start(bf16[1,4,64,1024]{3,2,1,0:T(8,128)(2,1)} %get-tuple-element.59.rest_1_), channel_id=1, source_target_pairs={{0,8},{8,16},{12,4},{16,24},{20,12},{28,20},{1,9},{9,17},{13,5},{1... | collective-permute-start | bytes 1572872 | tf_op jit(solution)/shard_map/ppermute | solution.py:450
  48.8 4.6 %copy-start.3 = (bf16[2,2,64,1024]{3,2,1,0:T(8,128)(2,1)}, bf16[2,2,64,1024]{3,2,1,0:T(8,128)(2,1)S(1)}, u32[]{:S(2)}) copy-start(bf16[2,2,64,1024]{3,2,1,0:T(8,128)(2,1)S(1)} %collective-permute-done.2.rest_3_) | copy-start | bytes 1572868
  48.8 24.4 %collective-permute-start.7 = (bf16[1,2,64,1024]{3,2,1,0:T(8,128)(2,1)}, bf16[1,2,64,1024]{3,2,1,0:T(8,128)(2,1)S(1)}, u32[]{:S(2)}, u32[]{:S(2)}) collective-permute-start(bf16[1,2,64,1024]{3,2,1,0:T(8,128)(2,1)} %get-tuple-element.56), channel_id=1, source_target_pairs={{4,12},{8,0},{12,20},{16,8},{20,28},{24,16},{5,13},{9,1},{13,21},{... | collective-permute-start | bytes 786440 | tf_op jit(solution)/shard_map/ppermute | solution.py:450
  53.4 1.0 copy-start.1
  73.2 19.4 %collective-permute-start.8 = (bf16[4,64,1,8,128]{4,3,1,0,2:T(8,128)(2,1)S(1)}, bf16[4,64,1,8,128]{4,3,1,0,2:T(8,128)(2,1)S(1)}, u32[]{:S(2)}, u32[]{:S(2)}) collective-permute-start(bf16[4,64,1,8,128]{4,3,1,0,2:T(8,128)(2,1)S(1)} %bitcast.36), channel_id=1, source_target_pairs={{0,4},{4,0},{8,12},{12,8},{16,20},{20,16},{24,28},{28,24},{1,5},{5... | collective-permute-start | bytes 1572872 | tf_op jit(solution)/shard_map/ppermute | solution.py:446
  92.7 5.4 %collective-permute-start.9 = (bf16[16,16,64]{2,1,0:T(8,128)(2,1)S(1)}, bf16[16,16,64]{2,1,0:T(8,128)(2,1)S(1)}, u32[]{:S(2)}, u32[]{:S(2)}) collective-permute-start(bf16[16,16,64]{2,1,0:T(8,128)(2,1)S(1)} %get-tuple-element.81), channel_id=1, source_target_pairs={{0,1},{1,2},{2,3},{3,0},{4,5},{5,6},{6,7},{7,4},{8,9},{9,10},{10,1... | collective-permute-start | bytes 98312 | tf_op jit(solution)/shard_map/ppermute | solution.py:426
  92.7 5.3 %collective-permute-start.11 = (bf16[16,16,64]{2,1,0:T(8,128)(2,1)S(1)}, bf16[16,16,64]{2,1,0:T(8,128)(2,1)S(1)}, u32[]{:S(2)}, u32[]{:S(2)}) collective-permute-start(bf16[16,16,64]{2,1,0:T(8,128)(2,1)S(1)} %get-tuple-element.82), channel_id=1, source_target_pairs={{0,3},{1,0},{2,1},{3,2},{4,7},{5,4},{6,5},{7,6},{8,11},{9,8},{10,9... | collective-permute-start | bytes 98312 | tf_op jit(solution)/shard_map/ppermute | solution.py:426
  94.5 4.6 %collective-permute-start.10 = (bf16[16,16,64]{2,1,0:T(8,128)(2,1)S(1)}, bf16[16,16,64]{2,1,0:T(8,128)(2,1)S(1)}, u32[]{:S(2)}, u32[]{:S(2)}) collective-permute-start(bf16[16,16,64]{2,1,0:T(8,128)(2,1)S(1)} %get-tuple-element.83), channel_id=1, source_target_pairs={{0,2},{1,3},{2,0},{3,1},{4,6},{5,7},{6,4},{7,5},{8,10},{9,11},{10,... | collective-permute-start | bytes 98312 | tf_op jit(solution)/shard_map/ppermute | solution.py:426
  96.1 16.5 %collective-permute-start.14 = (bf16[4,64,1,8,128]{4,3,1,0,2:T(8,128)(2,1)}, bf16[4,64,1,8,128]{4,3,1,0,2:T(8,128)(2,1)S(1)}, u32[]{:S(2)}, u32[]{:S(2)}) collective-permute-start(bf16[4,64,1,8,128]{4,3,1,0,2:T(8,128)(2,1)} %bitcast.47), channel_id=1, source_target_pairs={{0,4},{4,0},{8,12},{12,8},{16,20},{20,16},{24,28},{28,24},{1,5},{5... | collective-permute-start | bytes 1572872 | tf_op jit(solution)/shard_map/ppermute | solution.py:446
  99.1 5.6 %collective-permute-start.12 = (bf16[16,16,64]{2,1,0:T(8,128)(2,1)S(1)}, bf16[16,16,64]{2,1,0:T(8,128)(2,1)S(1)}, u32[]{:S(2)}, u32[]{:S(2)}) collective-permute-start(bf16[16,16,64]{2,1,0:T(8,128)(2,1)S(1)} %get-tuple-element.79), channel_id=1, source_target_pairs={{0,8},{4,12},{8,0},{12,4},{16,24},{20,28},{24,16},{28,20},{1,9},{5... | collective-permute-start | bytes 98312 | tf_op jit(solution)/shard_map/ppermute | solution.py:411
  104.7 7.8 %collective-permute-start.13 = (bf16[16,16,64]{2,1,0:T(8,128)(2,1)S(1)}, bf16[16,16,64]{2,1,0:T(8,128)(2,1)S(1)}, u32[]{:S(2)}, u32[]{:S(2)}) collective-permute-start(bf16[16,16,64]{2,1,0:T(8,128)(2,1)S(1)} %fusion), channel_id=1, source_target_pairs={{0,16},{4,20},{8,24},{12,28},{16,0},{20,4},{24,8},{28,12},{1,17},{... | collective-permute-start | bytes 98312 | tf_op jit(solution)/shard_map/ppermute | solution.py:411
  107.8 11.6 %all-to-all-start.1 = ((bf16[8,8,512]{2,1,0:T(8,128)(2,1)}), bf16[8,8,512]{2,1,0:T(8,128)(2,1)S(1)}, u32[]{:S(2)}, u32[]{:S(2)}) async-start(bf16[8,8,512]{2,1,0:T(8,128)(2,1)} %copy.38), calls=%async_computation.1 | async-start | bytes 131072 | tf_op jit(solution)/shard_map/all_to_all | solution.py:576
  112.5 4.5 %collective-permute-start.15 = (bf16[16,16,64]{2,1,0:T(8,128)(2,1)S(1)}, bf16[16,16,64]{2,1,0:T(8,128)(2,1)S(1)}, u32[]{:S(2)}, u32[]{:S(2)}) collective-permute-start(bf16[16,16,64]{2,1,0:T(8,128)(2,1)S(1)} %convert_element_type.72), channel_id=1, source_target_pairs={{0,4},{4,0},{8,12},{12,8},{16,20},{20,16},{24,28},{28,24},{1,5},{5... | collective-permute-start | bytes 98312 | tf_op jit(solution)/shard_map/ppermute | solution.py:411

commit v6 on v5

--- a/solution.py
+++ b/solution.py
@@ -403,12 +403,16 @@
     if tiles & (tiles - 1):
         return lax.psum(value.astype(BF16), "tile").astype(F32), others
     steps = [2**k for k in range(tiles.bit_length() - 1)]
-    steps = [k for k in steps if k >= g] + [k for k in steps if k < g]
-    for k in steps:
-        if k == steps[-1]:
+    outer, inner = [k for k in steps if k >= g], [k for k in steps if k < g]
+    rounds = [part[i : i + 2] for part in (outer, inner) for i in range(0, len(part), 2)]
+    for number, bits in enumerate(rounds):
+        if number == len(rounds) - 1:
             value, others = lax.optimization_barrier((value, others))
-        pairs = [(a, a ^ k) for a in range(tiles)]
-        value = value + lax.ppermute(value.astype(BF16), "tile", pairs).astype(F32)
+        masks = bits + [sum(bits)] * (len(bits) - 1)
+        sent = value.astype(BF16)
+        for k in masks:
+            pairs = [(a, a ^ k) for a in range(tiles)]
+            value = value + lax.ppermute(sent, "tile", pairs).astype(F32)
     return value, others
 
 
@@ -498,6 +502,9 @@
 
     arriving = [arrive(x, 0)]
     mine = list(run_forward(meta, slots["mine"], extra, per, x, w_spatial))
+    if per > 1:
+        later, mine[1] = lax.optimization_barrier((x, mine[1]))
+        arriving += [arrive(later, layer) for layer in range(1, per)]
     ahead = []
     if mirrored:
         ahead.append(hop(mine[0], (-1, 1)))
@@ -512,8 +519,7 @@
         for piece in arriving[layer]:
             done.append(list(run_forward(meta, slots["theirs"], extra, 1, piece, w_spatial)))
         if layer == 0 and g > 1:
-            later, asked, done[1][2] = lax.optimization_barrier((x, targets, done[1][2]))
-            arriving += [arrive(later, k) for k in range(1, per)]
+            asked, done[1][2] = lax.optimization_barrier((targets, done[1][2]))
         pieces = [d[0] for d in done]
         ranks = [layer] + [0] * (g - 1)
         if mirrored:

time: 123 us -> 124 us (level)
  waiting for transfers between devices: 10.4 us -> 13.4 us
  starting transfers between devices: 45.4 us -> 43 us
    all_to_all x1, waiting for transfers between devices: 0.23 us -> 4.04 us  [body(): everyone = lax.all_to_all(everyone, 'tile', 0, 0, tiled=True)]
    ppermute x3 -> x4, waiting for transfers between devices: 2.95 us -> 0.78 us  [sum_over_tiles(): value = value + lax.ppermute(sent, 'tile', pairs).astype(F32)]
    ppermute x3, waiting for transfers between devices: 0.99 us -> 3.06 us  [sum_over_reps(): lax.ppermute(share(r + s).astype(BF16), 'rep', pairs).astype(F32)]
    ppermute x4, starting transfers between devices: 6.49 us -> 5.12 us  [swap(): return lax.ppermute(value, 'tile', pairs)]
    ppermute x3 -> x4, starting transfers between devices: 7.8 us -> 6.57 us  [sum_over_tiles(): value = value + lax.ppermute(sent, 'tile', pairs).astype(F32)]
  transfers between devices with their start and end apart: 18 -> 19, of which waited for: 7 -> 7; matrix products, arithmetic and copies ran while one was open for 6% -> 7% of each run, Pallas kernels for 43% -> 42%
where the time goes in v6:
time: 124 us; the launch traced here: 123 us
  Pallas kernels  52.1 us (42%)
  starting transfers between devices  43 us (35%)
  waiting for transfers between devices  13.4 us (11%)
  local copies, waits for them, and re-layouts  12.8 us (10%)
    pallas_call x2, Pallas kernels, run_temporal(): pl.pallas_call(functools.partial(temporal_kernel, tuple(places), last, al...  37.8 us
    ppermute x6, starting transfers between devices, hop(): return lax.ppermute(value, 'tile', [p for p in pairs if 0 <= p[1] < tiles])  17.3 us
    pallas_call x3, Pallas kernels, run_forward(): pl.pallas_call(functools.partial(forward_kernel, middle, base), name='con...  14.3 us
    ppermute x4, starting transfers between devices, sum_over_tiles(): value = value + lax.ppermute(sent, 'tile', pairs).astype(F32)  6.57 us
    all_to_all x1, starting transfers between devices, body(): everyone = lax.all_to_all(everyone, 'tile', 0, 0, tiled=True)  5.98 us
    ppermute x4, starting transfers between devices, swap(): return lax.ppermute(value, 'tile', pairs)  5.12 us
    all_to_all x1, starting transfers between devices, body(): logits = lax.all_to_all(logits, 'tile', 0, 0, tiled=True)  4.69 us
    all_to_all x1, waiting for transfers between devices, body(): everyone = lax.all_to_all(everyone, 'tile', 0, 0, tiled=True)  4.04 us
  transfers between devices with their start and end apart: 19, of which 7 were waited for; matrix products, arithmetic and copies ran while one was open for 7% of the time, Pallas kernels for 42%

profile of v6, /device:TPU:0, one launch (start us, length us, event | category | flops | bytes accessed | tf_op | source)
XLA Modules:
  0.0 123.2 jit_solution(10935884860782509600)
XLA Ops:
  0.7 0.0 copy-start.2
  0.7 1.1 dynamic-slice_bitcast_fusion
  1.8 3.0 %collective-permute-start = (bf16[4,64,1,8,128]{4,3,2,1,0:T(8,128)(2,1)S(1)}, bf16[4,64,1,8,128]{4,3,2,1,0:T(8,128)(2,1)S(1)}, u32[]{:S(2)}, u32[]{:S(2)}) collective-permute-start(bf16[4,64,1,8,128]{4,3,2,1,0:T(8,128)(2,1)S(1)} %dynamic-slice_bitcast_fusion), channel_id=1, source_target_pairs={{0,4},{4,0},{8,12},{12,8},{16,20},{20,16},{24,28},{28,24},{1,5},{5... | collective-permute-start | bytes 1572872 | tf_op jit(solution)/shard_map/ppermute | solution.py:450
  4.8 1.2 fusion.3.meta_ref
  6.0 6.1 %conv_forward.4 = (bf16[2,4,64,1024]{3,2,1,0:T(8,128)(2,1)}, bf16[2,4,64,1024]{3,2,1,0:T(8,128)(2,1)}, bf16[2,4,64,1024]{3,2,1,0:T(8,128)(2,1)}, bf16[2,2,64,1024]{3,2,1,0:T(8,128)(2,1)}) custom-call(s32[20]{0:T(128)} %fusion.3.meta_ref, bf16[4,64,4,8,128]{4,3,2,1,0:T(8,128)(2,1)} %bitcast.37, bf16[9,64,64]{2,1,0:T(8,128)(2,1)} %w_ref.5), custom_call_target="tpu_custom_call" | custom-call | flops 1000 | bytes 1000 | tf_op jit(solution)/shard_map/conv_forward/pallas_call | solution.py:111
  12.1 1.9 %constant_dynamic-slice_fusion.2 = bf16[4,64,1,8,128]{4,3,2,1,0:T(8,128)(2,1)} fusion(bf16[4,64,4,8,128]{4,3,2,1,0:T(8,128)(2,1)} %bitcast.38, s32[]{:T(128)S(6)} %select_n.84), kind=kLoop, calls=%fused_computation.20 | loop fusion | bytes 1048580 | tf_op jit(solution)/shard_map/dynamic_slice | solution.py:499
  14.0 0.0 collective-permute-start.5
  14.1 4.0 %collective-permute-start.2 = (bf16[2,2,64,1024]{3,2,1,0:T(8,128)(2,1)}, bf16[2,2,64,1024]{3,2,1,0:T(8,128)(2,1)S(1)}, u32[]{:S(2)}, u32[]{:S(2)}) collective-permute-start(bf16[2,2,64,1024]{3,2,1,0:T(8,128)(2,1)} %get-tuple-element.47), channel_id=1, source_target_pairs={{0,8},{8,16},{12,4},{16,24},{20,12},{28,20},{1,9},{9,17},{13,5},{1... | collective-permute-start | bytes 1572872 | tf_op jit(solution)/shard_map/ppermute | solution.py:454
  18.0 1.3 %collective-permute-start.1 = (bf16[2,4,64,1024]{3,2,1,0:T(8,128)(2,1)}, bf16[2,4,64,1024]{3,2,1,0:T(8,128)(2,1)S(1)}, u32[]{:S(2)}, u32[]{:S(2)}) collective-permute-start(bf16[2,4,64,1024]{3,2,1,0:T(8,128)(2,1)} %get-tuple-element.60.rest_0_), channel_id=1, source_target_pairs={{4,12},{8,0},{12,20},{16,8},{20,28},{24,16},{5,13},{9,1},{13,21},{... | collective-permute-start | bytes 3145736 | tf_op jit(solution)/shard_map/ppermute | solution.py:454
  19.4 0.7 multiply_convert_fusion.1
  20.1 0.0 copy-start
  20.1 0.0 collective-permute-done.x_ref
  20.1 0.8 copy-done.5
  20.9 4.1 %conv_forward.3 = (bf16[1,4,64,1024]{3,2,1,0:T(8,128)(2,1)}, bf16[1,4,64,1024]{3,2,1,0:T(8,128)(2,1)}, bf16[1,4,64,1024]{3,2,1,0:T(8,128)(2,1)}, bf16[1,2,64,1024]{3,2,1,0:T(8,128)(2,1)}) custom-call(s32[20]{0:T(128)} %fusion.3.meta_ref, bf16[4,64,1,8,128]{4,3,2,1,0:T(8,128)(2,1)} %copy-done.5, bf16[9,64,64]{2,1,0:T(8,128)(2,1)} %w_ref.5), custom_call_target="tpu_custom_call" | custom-call | flops 1000 | bytes 1000 | tf_op jit(solution)/shard_map/conv_forward/pallas_call | solution.py:111
  25.0 0.8 broadcast_in_dim.25
  25.8 6.0 %all-to-all-start = ((bf16[8,32,512]{2,1,0:T(8,128)(2,1)}), bf16[8,32,512]{2,1,0:T(8,128)(2,1)S(1)}, u32[]{:S(2)}, u32[]{:S(2)}) async-start(bf16[8,32,512]{2,1,0:T(8,128)(2,1)} %broadcast_in_dim.25), calls=%async_computation | async-start | bytes 524288 | tf_op jit(solution)/shard_map/all_to_all | solution.py:546
  31.8 3.9 %collective-permute-start.3 = (bf16[1,4,64,1024]{3,2,1,0:T(8,128)(2,1)}, bf16[1,4,64,1024]{3,2,1,0:T(8,128)(2,1)S(1)}, u32[]{:S(2)}, u32[]{:S(2)}) collective-permute-start(bf16[1,4,64,1024]{3,2,1,0:T(8,128)(2,1)} %get-tuple-element.46.rest_1_), channel_id=1, source_target_pairs={{0,8},{8,16},{12,4},{16,24},{20,12},{28,20},{1,9},{9,17},{13,5},{1... | collective-permute-start | bytes 1572872 | tf_op jit(solution)/shard_map/ppermute | solution.py:454
  35.8 1.3 %collective-permute-start.4 = (bf16[1,2,64,1024]{3,2,1,0:T(8,128)(2,1)}, bf16[1,2,64,1024]{3,2,1,0:T(8,128)(2,1)S(1)}, u32[]{:S(2)}, u32[]{:S(2)}) collective-permute-start(bf16[1,2,64,1024]{3,2,1,0:T(8,128)(2,1)} %get-tuple-element.48), channel_id=1, source_target_pairs={{4,12},{8,0},{12,20},{16,8},{20,28},{24,16},{5,13},{9,1},{13,21},{... | collective-permute-start | bytes 786440 | tf_op jit(solution)/shard_map/ppermute | solution.py:454
  37.1 0.0 collective-permute-done.5.x_ref
  37.1 4.0 %conv_forward.5 = (bf16[1,4,64,1024]{3,2,1,0:T(8,128)(2,1)}, bf16[1,4,64,1024]{3,2,1,0:T(8,128)(2,1)}, bf16[1,4,64,1024]{3,2,1,0:T(8,128)(2,1)}, bf16[1,2,64,1024]{3,2,1,0:T(8,128)(2,1)}) custom-call(s32[20]{0:T(128)} %fusion.3.meta_ref, bf16[4,64,1,8,128]{4,3,2,1,0:T(8,128)(2,1)} %collective-permute-done.5.x_ref, bf16[9,64,64]{2,1,0:T(8,128)(2,1)} %w_ref.5), custom_call_target="tpu_custom_call" | custom-call | flops 1000 | bytes 1000 | tf_op jit(solution)/shard_map/conv_forward/pallas_call | solution.py:111
  41.1 5.4 %collective-permute-start.6 = (bf16[1,4,64,1024]{3,2,1,0:T(8,128)(2,1)}, bf16[1,4,64,1024]{3,2,1,0:T(8,128)(2,1)}, u32[]{:S(2)}, u32[]{:S(2)}) collective-permute-start(bf16[1,4,64,1024]{3,2,1,0:T(8,128)(2,1)} %get-tuple-element.61.rest_1_), channel_id=1, source_target_pairs={{0,8},{8,16},{12,4},{16,24},{20,12},{28,20},{1,9},{9,17},{13,5},{1... | collective-permute-start | bytes 1572872 | tf_op jit(solution)/shard_map/ppermute | solution.py:454
  46.5 0.1 copy.34.whc_ref
  46.6 0.2 copy.31
  46.7 0.2 reshape.51.wb_ref
  46.9 0.1 copy.33.wtb_ref
  47.0 0.1 copy.30
  47.1 0.1 copy.32.wt_ref
  47.3 0.1 pad_dynamic-slice_fusion.weight_ref
  47.3 1.5 %collective-permute-start.7 = (bf16[1,2,64,1024]{3,2,1,0:T(8,128)(2,1)}, bf16[1,2,64,1024]{3,2,1,0:T(8,128)(2,1)S(1)}, u32[]{:S(2)}, u32[]{:S(2)}) collective-permute-start(bf16[1,2,64,1024]{3,2,1,0:T(8,128)(2,1)} %get-tuple-element.58), channel_id=1, source_target_pairs={{4,12},{8,0},{12,20},{16,8},{20,28},{24,16},{5,13},{9,1},{13,21},{... | collective-permute-start | bytes 786440 | tf_op jit(solution)/shard_map/ppermute | solution.py:454
  48.8 4.0 %all-to-all-done = bf16[8,32,512]{2,1,0:T(8,128)(2,1)S(1)} async-done(((bf16[8,32,512]{2,1,0:T(8,128)(2,1)}), bf16[8,32,512]{2,1,0:T(8,128)(2,1)S(1)}, u32[]{:S(2)}, u32[]{:S(2)}) %all-to-all-start) | async-done | bytes 262176 | tf_op jit(solution)/shard_map/all_to_all | solution.py:546
  52.9 3.2 %collective-permute-done.4.rest_5_ = bf16[1,2,64,1024]{3,2,1,0:T(8,128)(2,1)S(1)} collective-permute-done((bf16[1,2,64,1024]{3,2,1,0:T(8,128)(2,1)}, bf16[1,2,64,1024]{3,2,1,0:T(8,128)(2,1)S(1)}, u32[]{:S(2)}, u32[]{:S(2)}) %collective-permute-start.4) | collective-permute-done | bytes 262176 | tf_op jit(solution)/shard_map/ppermute | solution.py:454
  56.1 0.0 collective-permute-done.3.rest_4_
  56.1 0.8 copy-done.4
  57.0 0.3 copy-done.1
  57.3 18.7 %temporal.2 = (f32[14,1,1024]{2,1,0:T(1,128)S(1)}, f32[6,64,192]{2,1,0:T(8,128)S(1)}, bf16[4,64,4,8,128]{4,3,2,1,0:T(8,128)(2,1)}, bf16[1,4,64,8,128]{4,3,2,1,0:T(8,128)(2,1)S(1)}) custom-call(s32[20]{0:T(128)S(1)} %copy-done, f32[14]{0:T(128)S(1)} %pad_dynamic-slice_fusion.weight_ref, bf16[2,64,192]{2,1,0:T(8,128)(2,1)S(1)} %copy.32.wt_ref, ...), custom_call_target="tpu_custom_call" | custom-call | flops 1572864000 | bytes 52428800 | tf_op jit(solution)/shard_map/temporal/pallas_call | solution.py:350
  76.0 0.0 collective-permute-done.7.rest_5_
  76.0 0.0 collective-permute-done.6.rest_4_
  76.0 0.1 collective-permute-start.8
  76.2 0.1 fusion.1
  76.3 19.1 %temporal.3 = (f32[14,1,1024]{2,1,0:T(1,128)S(1)}, f32[16,64,64]{2,1,0:T(8,128)S(1)}, bf16[4,64,4,8,128]{4,3,2,1,0:T(8,128)(2,1)}, bf16[1,4,64,8,128]{4,3,2,1,0:T(8,128)(2,1)}) custom-call(s32[20]{0:T(128)S(1)} %copy-done, f32[14]{0:T(128)S(1)} %pad_dynamic-slice_fusion.weight_ref, ...), custom_call_target="tpu_custom_call", output_to_operand_aliasing={{2}: (18, {})} | custom-call | flops 1572864000 | bytes 52428800 | tf_op jit(solution)/shard_map/temporal/pallas_call | solution.py:350
  95.4 0.1 fusion
  95.5 2.0 %collective-permute-start.15 = (bf16[4,64,1,8,128]{4,3,1,0,2:T(8,128)(2,1)}, bf16[4,64,1,8,128]{4,3,1,0,2:T(8,128)(2,1)S(1)}, u32[]{:S(2)}, u32[]{:S(2)}) collective-permute-start(bf16[4,64,1,8,128]{4,3,1,0,2:T(8,128)(2,1)} %bitcast.47), channel_id=1, source_target_pairs={{0,4},{4,0},{8,12},{12,8},{16,20},{20,16},{24,28},{28,24},{1,5},{5... | collective-permute-start | bytes 1572872 | tf_op jit(solution)/shard_map/ppermute | solution.py:450
  97.5 0.1 collective-permute-start.9
  97.6 1.7 %collective-permute-start.11 = (bf16[16,16,64]{2,1,0:T(8,128)(2,1)S(1)}, bf16[16,16,64]{2,1,0:T(8,128)(2,1)S(1)}, u32[]{:S(2)}, u32[]{:S(2)}) collective-permute-start(bf16[16,16,64]{2,1,0:T(8,128)(2,1)S(1)} %get-tuple-element.82), channel_id=1, source_target_pairs={{0,3},{1,0},{2,1},{3,2},{4,7},{5,4},{6,5},{7,6},{8,11},{9,8},{10,9... | collective-permute-start | bytes 98312 | tf_op jit(solution)/shard_map/ppermute | solution.py:430
  99.3 1.5 %collective-permute-start.10 = (bf16[16,16,64]{2,1,0:T(8,128)(2,1)S(1)}, bf16[16,16,64]{2,1,0:T(8,128)(2,1)S(1)}, u32[]{:S(2)}, u32[]{:S(2)}) collective-permute-start(bf16[16,16,64]{2,1,0:T(8,128)(2,1)S(1)} %get-tuple-element.83), channel_id=1, source_target_pairs={{0,2},{1,3},{2,0},{3,1},{4,6},{5,7},{6,4},{7,5},{8,10},{9,11},{10,... | collective-permute-start | bytes 98312 | tf_op jit(solution)/shard_map/ppermute | solution.py:430
  100.9 0.4 collective-permute-done.9
  101.3 0.4 collective-permute-done.11
  101.7 2.2 %collective-permute-done.10 = bf16[16,16,64]{2,1,0:T(8,128)(2,1)S(1)} collective-permute-done((bf16[16,16,64]{2,1,0:T(8,128)(2,1)S(1)}, bf16[16,16,64]{2,1,0:T(8,128)(2,1)S(1)}, u32[]{:S(2)}, u32[]{:S(2)}) %collective-permute-start.10) | collective-permute-done | bytes 32800 | tf_op jit(solution)/shard_map/ppermute | solution.py:430
  104.0 2.1 %collective-permute-start.14 = (bf16[16,16,64]{2,1,0:T(8,128)(2,1)S(1)}, bf16[16,16,64]{2,1,0:T(8,128)(2,1)S(1)}, u32[]{:S(2)}, u32[]{:S(2)}) collective-permute-start(bf16[16,16,64]{2,1,0:T(8,128)(2,1)S(1)} %fusion.2), channel_id=1, source_target_pairs={{0,24},{4,28},{8,16},{12,20},{16,8},{20,12},{24,0},{28,4},{1,25},{... | collective-permute-start | bytes 98312 | tf_op jit(solution)/shard_map/ppermute | solution.py:415
  106.1 2.3 %collective-permute-start.13 = (bf16[16,16,64]{2,1,0:T(8,128)(2,1)S(1)}, bf16[16,16,64]{2,1,0:T(8,128)(2,1)S(1)}, u32[]{:S(2)}, u32[]{:S(2)}) collective-permute-start(bf16[16,16,64]{2,1,0:T(8,128)(2,1)S(1)} %fusion.2), channel_id=1, source_target_pairs={{0,16},{4,20},{8,24},{12,28},{16,0},{20,4},{24,8},{28,12},{1,17},{... | collective-permute-start | bytes 98312 | tf_op jit(solution)/shard_map/ppermute | solution.py:415
  108.5 0.7 copy.38
  109.1 4.7 %all-to-all-start.1 = ((bf16[8,8,512]{2,1,0:T(8,128)(2,1)}), bf16[8,8,512]{2,1,0:T(8,128)(2,1)S(1)}, u32[]{:S(2)}, u32[]{:S(2)}) async-start(bf16[8,8,512]{2,1,0:T(8,128)(2,1)} %copy.38), calls=%async_computation.1 | async-start | bytes 131072 | tf_op jit(solution)/shard_map/all_to_all | solution.py:582
  113.8 0.0 collective-permute-done.14
  113.8 0.0 collective-permute-done.12
  113.9 0.1 convert_add_fusion.1
  114.0 2.1 %collective-permute-start.16 = (bf16[16,16,64]{2,1,0:T(8,128)(2,1)S(1)}, bf16[16,16,64]{2,1,0:T(8,128)(2,1)S(1)}, u32[]{:S(2)}, u32[]{:S(2)}) collective-permute-start(bf16[16,16,64]{2,1,0:T(8,128)(2,1)S(1)} %convert_element_type.72), channel_id=1, source_target_pairs={{0,4},{4,0},{8,12},{12,8},{16,20},{20,16},{24,28},{28,24},{1,5},{5... | collective-permute-start | bytes 98312 | tf_op jit(solution)/shard_map/ppermute | solution.py:415
  116.0 0.8 bitcast_dynamic-update-slice_fusion.1
  116.9 0.8 bitcast_dynamic-update-slice_fusion
  117.7 0.8 collective-permute-done.16
  118.5 2.2 %all-to-all-done.1 = bf16[8,8,512]{2,1,0:T(8,128)(2,1)S(1)} async-done(((bf16[8,8,512]{2,1,0:T(8,128)(2,1)}), bf16[8,8,512]{2,1,0:T(8,128)(2,1)S(1)}, u32[]{:S(2)}, u32[]{:S(2)}) %all-to-all-start.1) | async-done | bytes 65568 | tf_op jit(solution)/shard_map/all_to_all | solution.py:582
  120.7 0.6 slice.28
  121.4 0.6 slice.27
  122.0 0.6 dynamic-slice_bitcast_fusion.1
  122.6 0.6 fusion.4
  (37 shorter events, 0.3 us)
Async XLA Ops:
  0.7 18.7 %copy-start.7 = (bf16[2,3,64,64]{3,2,1,0:T(8,128)(2,1)S(1)}, bf16[2,3,64,64]{3,2,1,0:T(8,128)(2,1)}, u32[]{:S(2)}) copy-start(bf16[2,3,64,64]{3,2,1,0:T(8,128)(2,1)} %param.9) | copy-start | bytes 147460
  0.7 19.4 %copy-start.2 = (bf16[9,64,64]{2,1,0:T(8,128)(2,1)S(1)}, bf16[9,64,64]{2,1,0:T(8,128)(2,1)}, u32[]{:S(2)}) copy-start(bf16[9,64,64]{2,1,0:T(8,128)(2,1)} %w_ref.5) | copy-start | bytes 221188
  1.8 18.3 %collective-permute-start = (bf16[4,64,1,8,128]{4,3,2,1,0:T(8,128)(2,1)S(1)}, bf16[4,64,1,8,128]{4,3,2,1,0:T(8,128)(2,1)S(1)}, u32[]{:S(2)}, u32[]{:S(2)}) collective-permute-start(bf16[4,64,1,8,128]{4,3,2,1,0:T(8,128)(2,1)S(1)} %dynamic-slice_bitcast_fusion), channel_id=1, source_target_pairs={{0,4},{4,0},{8,12},{12,8},{16,20},{20,16},{24,28},{28,24},{1,5},{5... | collective-permute-start | bytes 1572872 | tf_op jit(solution)/shard_map/ppermute | solution.py:450
  6.0 19.0 %copy-start.8 = (bf16[1,32,512]{2,1,0:T(8,128)(2,1)S(1)}, bf16[1,32,512]{2,1,0:T(8,128)(2,1)}, u32[]{:S(2)}) copy-start(bf16[1,32,512]{2,1,0:T(8,128)(2,1)} %param.11) | copy-start | bytes 98308
  12.1 23.6 %copy-start.9 = (bf16[64]{0:T(256)(128)(2,1)S(1)}, bf16[64]{0:T(256)(128)(2,1)}, u32[]{:S(2)}) copy-start(bf16[64]{0:T(256)(128)(2,1)} %param.10) | copy-start | bytes 388
  12.1 34.3 %copy-start.10 = (s32[1,32]{1,0:T(1,128)S(1)}, s32[1,32]{1,0:T(1,128)}, u32[]{:S(2)}) copy-start(s32[1,32]{1,0:T(1,128)} %param.12) | copy-start | bytes 388
  14.0 23.0 %collective-permute-start.5 = (bf16[4,64,1,8,128]{4,3,2,1,0:T(8,128)(2,1)}, bf16[4,64,1,8,128]{4,3,2,1,0:T(8,128)(2,1)}, u32[]{:S(2)}, u32[]{:S(2)}) collective-permute-start(bf16[4,64,1,8,128]{4,3,2,1,0:T(8,128)(2,1)} %constant_dynamic-slice_fusion.2), channel_id=1, source_target_pairs={{0,4},{4,0},{8,12},{12,8},{16,20},{20,16},{24,28},{28,24},{1,5},{5... | collective-permute-start | bytes 1572872 | tf_op jit(solution)/shard_map/ppermute | solution.py:450
  14.1 33.3 %collective-permute-start.2 = (bf16[2,2,64,1024]{3,2,1,0:T(8,128)(2,1)}, bf16[2,2,64,1024]{3,2,1,0:T(8,128)(2,1)S(1)}, u32[]{:S(2)}, u32[]{:S(2)}) collective-permute-start(bf16[2,2,64,1024]{3,2,1,0:T(8,128)(2,1)} %get-tuple-element.47), channel_id=1, source_target_pairs={{0,8},{8,16},{12,4},{16,24},{20,12},{28,20},{1,9},{9,17},{13,5},{1... | collective-permute-start | bytes 1572872 | tf_op jit(solution)/shard_map/ppermute | solution.py:454
  18.0 38.0 %collective-permute-start.1 = (bf16[2,4,64,1024]{3,2,1,0:T(8,128)(2,1)}, bf16[2,4,64,1024]{3,2,1,0:T(8,128)(2,1)S(1)}, u32[]{:S(2)}, u32[]{:S(2)}) collective-permute-start(bf16[2,4,64,1024]{3,2,1,0:T(8,128)(2,1)} %get-tuple-element.60.rest_0_), channel_id=1, source_target_pairs={{4,12},{8,0},{12,20},{16,8},{20,28},{24,16},{5,13},{9,1},{13,21},{... | collective-permute-start | bytes 3145736 | tf_op jit(solution)/shard_map/ppermute | solution.py:454
  20.1 37.2 %copy-start = (s32[20]{0:T(128)S(1)}, s32[20]{0:T(128)}, u32[]{:S(2)}) copy-start(s32[20]{0:T(128)} %fusion.3.meta_ref) | copy-start | bytes 244
  20.1 0.8 copy-start.5
  20.9 26.0 %copy-start.6 = (bf16[2,3,64,64]{3,2,1,0:T(8,128)(2,1)S(1)}, bf16[2,3,64,64]{3,2,1,0:T(8,128)(2,1)}, u32[]{:S(2)}) copy-start(bf16[2,3,64,64]{3,2,1,0:T(8,128)(2,1)} %get-tuple-element.86) | copy-start | bytes 147460
  25.8 27.1 %all-to-all-start = ((bf16[8,32,512]{2,1,0:T(8,128)(2,1)}), bf16[8,32,512]{2,1,0:T(8,128)(2,1)S(1)}, u32[]{:S(2)}, u32[]{:S(2)}) async-start(bf16[8,32,512]{2,1,0:T(8,128)(2,1)} %broadcast_in_dim.25), calls=%async_computation | async-start | bytes 524288 | tf_op jit(solution)/shard_map/all_to_all | solution.py:546
  31.8 24.3 %collective-permute-start.3 = (bf16[1,4,64,1024]{3,2,1,0:T(8,128)(2,1)}, bf16[1,4,64,1024]{3,2,1,0:T(8,128)(2,1)S(1)}, u32[]{:S(2)}, u32[]{:S(2)}) collective-permute-start(bf16[1,4,64,1024]{3,2,1,0:T(8,128)(2,1)} %get-tuple-element.46.rest_1_), channel_id=1, source_target_pairs={{0,8},{8,16},{12,4},{16,24},{20,12},{28,20},{1,9},{9,17},{13,5},{1... | collective-permute-start | bytes 1572872 | tf_op jit(solution)/shard_map/ppermute | solution.py:454
  35.8 20.3 %collective-permute-start.4 = (bf16[1,2,64,1024]{3,2,1,0:T(8,128)(2,1)}, bf16[1,2,64,1024]{3,2,1,0:T(8,128)(2,1)S(1)}, u32[]{:S(2)}, u32[]{:S(2)}) collective-permute-start(bf16[1,2,64,1024]{3,2,1,0:T(8,128)(2,1)} %get-tuple-element.48), channel_id=1, source_target_pairs={{4,12},{8,0},{12,20},{16,8},{20,28},{24,16},{5,13},{9,1},{13,21},{... | collective-permute-start | bytes 786440 | tf_op jit(solution)/shard_map/ppermute | solution.py:454
  41.1 34.9 %collective-permute-start.6 = (bf16[1,4,64,1024]{3,2,1,0:T(8,128)(2,1)}, bf16[1,4,64,1024]{3,2,1,0:T(8,128)(2,1)}, u32[]{:S(2)}, u32[]{:S(2)}) collective-permute-start(bf16[1,4,64,1024]{3,2,1,0:T(8,128)(2,1)} %get-tuple-element.61.rest_1_), channel_id=1, source_target_pairs={{0,8},{8,16},{12,4},{16,24},{20,12},{28,20},{1,9},{9,17},{13,5},{1... | collective-permute-start | bytes 1572872 | tf_op jit(solution)/shard_map/ppermute | solution.py:454
  47.3 9.6 %copy-start.3 = (bf16[2,2,64,1024]{3,2,1,0:T(8,128)(2,1)}, bf16[2,2,64,1024]{3,2,1,0:T(8,128)(2,1)S(1)}, u32[]{:S(2)}) copy-start(bf16[2,2,64,1024]{3,2,1,0:T(8,128)(2,1)S(1)} %collective-permute-done.2.rest_3_) | copy-start | bytes 1572868
  47.3 28.6 %collective-permute-start.7 = (bf16[1,2,64,1024]{3,2,1,0:T(8,128)(2,1)}, bf16[1,2,64,1024]{3,2,1,0:T(8,128)(2,1)S(1)}, u32[]{:S(2)}, u32[]{:S(2)}) collective-permute-start(bf16[1,2,64,1024]{3,2,1,0:T(8,128)(2,1)} %get-tuple-element.58), channel_id=1, source_target_pairs={{4,12},{8,0},{12,20},{16,8},{20,28},{24,16},{5,13},{9,1},{13,21},{... | collective-permute-start | bytes 786440 | tf_op jit(solution)/shard_map/ppermute | solution.py:454
  56.1 0.8 copy-start.4
  56.1 1.2 copy-start.1
  76.0 21.5 %collective-permute-start.8 = (bf16[4,64,1,8,128]{4,3,1,0,2:T(8,128)(2,1)S(1)}, bf16[4,64,1,8,128]{4,3,1,0,2:T(8,128)(2,1)S(1)}, u32[]{:S(2)}, u32[]{:S(2)}) collective-permute-start(bf16[4,64,1,8,128]{4,3,1,0,2:T(8,128)(2,1)S(1)} %bitcast.36), channel_id=1, source_target_pairs={{0,4},{4,0},{8,12},{12,8},{16,20},{20,16},{24,28},{28,24},{1,5},{5... | collective-permute-start | bytes 1572872 | tf_op jit(solution)/shard_map/ppermute | solution.py:450
  95.5 18.4 %collective-permute-start.15 = (bf16[4,64,1,8,128]{4,3,1,0,2:T(8,128)(2,1)}, bf16[4,64,1,8,128]{4,3,1,0,2:T(8,128)(2,1)S(1)}, u32[]{:S(2)}, u32[]{:S(2)}) collective-permute-start(bf16[4,64,1,8,128]{4,3,1,0,2:T(8,128)(2,1)} %bitcast.47), channel_id=1, source_target_pairs={{0,4},{4,0},{8,12},{12,8},{16,20},{20,16},{24,28},{28,24},{1,5},{5... | collective-permute-start | bytes 1572872 | tf_op jit(solution)/shard_map/ppermute | solution.py:450
  97.5 3.7 %collective-permute-start.9 = (bf16[16,16,64]{2,1,0:T(8,128)(2,1)S(1)}, bf16[16,16,64]{2,1,0:T(8,128)(2,1)S(1)}, u32[]{:S(2)}, u32[]{:S(2)}) collective-permute-start(bf16[16,16,64]{2,1,0:T(8,128)(2,1)S(1)} %get-tuple-element.81), channel_id=1, source_target_pairs={{0,1},{1,2},{2,3},{3,0},{4,5},{5,6},{6,7},{7,4},{8,9},{9,10},{10,1... | collective-permute-start | bytes 98312 | tf_op jit(solution)/shard_map/ppermute | solution.py:430
  97.6 4.1 %collective-permute-start.11 = (bf16[16,16,64]{2,1,0:T(8,128)(2,1)S(1)}, bf16[16,16,64]{2,1,0:T(8,128)(2,1)S(1)}, u32[]{:S(2)}, u32[]{:S(2)}) collective-permute-start(bf16[16,16,64]{2,1,0:T(8,128)(2,1)S(1)} %get-tuple-element.82), channel_id=1, source_target_pairs={{0,3},{1,0},{2,1},{3,2},{4,7},{5,4},{6,5},{7,6},{8,11},{9,8},{10,9... | collective-permute-start | bytes 98312 | tf_op jit(solution)/shard_map/ppermute | solution.py:430
  99.3 4.6 %collective-permute-start.10 = (bf16[16,16,64]{2,1,0:T(8,128)(2,1)S(1)}, bf16[16,16,64]{2,1,0:T(8,128)(2,1)S(1)}, u32[]{:S(2)}, u32[]{:S(2)}) collective-permute-start(bf16[16,16,64]{2,1,0:T(8,128)(2,1)S(1)} %get-tuple-element.83), channel_id=1, source_target_pairs={{0,2},{1,3},{2,0},{3,1},{4,6},{5,7},{6,4},{7,5},{8,10},{9,11},{10,... | collective-permute-start | bytes 98312 | tf_op jit(solution)/shard_map/ppermute | solution.py:430
  104.0 9.9 %collective-permute-start.14 = (bf16[16,16,64]{2,1,0:T(8,128)(2,1)S(1)}, bf16[16,16,64]{2,1,0:T(8,128)(2,1)S(1)}, u32[]{:S(2)}, u32[]{:S(2)}) collective-permute-start(bf16[16,16,64]{2,1,0:T(8,128)(2,1)S(1)} %fusion.2), channel_id=1, source_target_pairs={{0,24},{4,28},{8,16},{12,20},{16,8},{20,12},{24,0},{28,4},{1,25},{... | collective-permute-start | bytes 98312 | tf_op jit(solution)/shard_map/ppermute | solution.py:415
  106.1 7.7 %collective-permute-start.13 = (bf16[16,16,64]{2,1,0:T(8,128)(2,1)S(1)}, bf16[16,16,64]{2,1,0:T(8,128)(2,1)S(1)}, u32[]{:S(2)}, u32[]{:S(2)}) collective-permute-start(bf16[16,16,64]{2,1,0:T(8,128)(2,1)S(1)} %fusion.2), channel_id=1, source_target_pairs={{0,16},{4,20},{8,24},{12,28},{16,0},{20,4},{24,8},{28,12},{1,17},{... | collective-permute-start | bytes 98312 | tf_op jit(solution)/shard_map/ppermute | solution.py:415
  108.4 5.4 %collective-permute-start.12 = (bf16[16,16,64]{2,1,0:T(8,128)(2,1)S(1)}, bf16[16,16,64]{2,1,0:T(8,128)(2,1)S(1)}, u32[]{:S(2)}, u32[]{:S(2)}) collective-permute-start(bf16[16,16,64]{2,1,0:T(8,128)(2,1)S(1)} %fusion.2), channel_id=1, source_target_pairs={{0,8},{4,12},{8,0},{12,4},{16,24},{20,28},{24,16},{28,20},{1,9},{5... | collective-permute-start | bytes 98312 | tf_op jit(solution)/shard_map/ppermute | solution.py:415
  109.1 11.6 %all-to-all-start.1 = ((bf16[8,8,512]{2,1,0:T(8,128)(2,1)}), bf16[8,8,512]{2,1,0:T(8,128)(2,1)S(1)}, u32[]{:S(2)}, u32[]{:S(2)}) async-start(bf16[8,8,512]{2,1,0:T(8,128)(2,1)} %copy.38), calls=%async_computation.1 | async-start | bytes 131072 | tf_op jit(solution)/shard_map/all_to_all | solution.py:582
  114.0 4.5 %collective-permute-start.16 = (bf16[16,16,64]{2,1,0:T(8,128)(2,1)S(1)}, bf16[16,16,64]{2,1,0:T(8,128)(2,1)S(1)}, u32[]{:S(2)}, u32[]{:S(2)}) collective-permute-start(bf16[16,16,64]{2,1,0:T(8,128)(2,1)S(1)} %convert_element_type.72), channel_id=1, source_target_pairs={{0,4},{4,0},{8,12},{12,8},{16,20},{20,16},{24,28},{28,24},{1,5},{5... | collective-permute-start | bytes 98312 | tf_op jit(solution)/shard_map/ppermute | solution.py:415

commit v7 on v6

--- a/solution.py
+++ b/solution.py
@@ -131,6 +131,75 @@
         ),
         cost_estimate=pl.CostEstimate(flops=1000, bytes_accessed=1000, transcendentals=0),
     )(meta, x, w_spatial)
+
+
+def window_kernel(own, g, tgt_ref, win_ref, pad):
+    total, spot = tgt_ref.shape[1:]
+    pad[0:8] = jnp.zeros((8, spot), F32)
+    pad[8 : 8 + total] = tgt_ref[0].astype(F32)
+    pad[8 + total :] = jnp.zeros((8, spot), F32)
+    for a in range(win_ref.shape[0]):
+        first = a // g * own + 4
+        win_ref[a] = pad[first : first + own + 8].astype(BF16)
+
+
+def run_windows(targets, tiles, own, g):
+    _, total, spot = targets.shape
+    vmem = pl.BlockSpec(memory_space=pltpu.VMEM)
+    return pl.pallas_call(
+        functools.partial(window_kernel, own, g),
+        name="windows",
+        out_shape=jax.ShapeDtypeStruct((tiles, own + 8, spot), BF16),
+        in_specs=[vmem],
+        out_specs=vmem,
+        scratch_shapes=[pltpu.VMEM((total + 16, spot), F32)],
+        cost_estimate=pl.CostEstimate(flops=1000, bytes_accessed=1000, transcendentals=0),
+    )(targets)
+
+
+def finish_kernel(arrived, g, value_ref, *rest):
+    logit_ref, out_ref, gs_ref, gt_ref, gh_ref = rest[arrived:]
+    part, chans = value_ref.shape[1:]
+    groups = out_ref.shape[0]
+    member = lax.axis_index("tile") // groups
+    for q in range(groups):
+        out_ref[q] = logit_ref[q * g + member]
+
+    def total(k):
+        acc = value_ref[k]
+        for ref in rest[:arrived]:
+            acc = acc + ref[k].astype(F32)
+        return acc
+
+    for k in range(9):
+        gs_ref[k] = total(k)
+    for k in range(6):
+        gt_ref[k // 3, k % 3] = total(9 + k)
+    shape = (chans, part)
+    mine = lax.broadcasted_iota(jnp.int32, shape, 1) + lax.axis_index("rep") * part
+    chosen = jnp.where(lax.broadcasted_iota(jnp.int32, shape, 0) == mine, 1.0, 0.0)
+    picked = jnp.dot(total(15), chosen, precision=lax.Precision.HIGHEST, preferred_element_type=F32)
+    gh_ref[...] = picked[0:1]
+
+
+def run_finish(value, arrived, logits, groups, g):
+    _, part, chans = value.shape
+    _, own, spot = logits.shape
+    sds = jax.ShapeDtypeStruct
+    vmem = pl.BlockSpec(memory_space=pltpu.VMEM)
+    return pl.pallas_call(
+        functools.partial(finish_kernel, len(arrived), g),
+        name="finish",
+        out_shape=(
+            sds((groups, own, spot), BF16),
+            sds((9, part, chans), F32),
+            sds((2, 3, part, chans), F32),
+            sds((1, part), F32),
+        ),
+        in_specs=[vmem] * (2 + len(arrived)),
+        out_specs=[vmem] * 4,
+        cost_estimate=pl.CostEstimate(flops=1000, bytes_accessed=1000, transcendentals=0),
+    )(value, *arrived, logits)
 
 
 def temporal_kernel(
@@ -244,7 +313,6 @@
 
     def layer1(f):
         weight = weight_ref[f - 3]
-        frame = jnp.clip(first + f - HALO, 0, total - 1)
         for cols in chunks:
             y, slope2 = silu_parts(dot_nn(wt_ref[1], stack(n1, f - 2, f, f + 2, cols)))
             hid = h1[f, :, cols] + y
@@ -252,7 +320,7 @@
             unit = hid * inv
             logit = channel_sum(unit * whc_ref[...])
             logit_ref[f - 3, :, cols] = logit
-            dlogit = weight * (sigmoid(logit) - tgt[pl.ds(frame, 1), cols])
+            dlogit = weight * (sigmoid(logit) - tgt[pl.ds(f - 2, 1), cols])
             final_ref[f, :, cols] = unit.astype(BF16)
             dlog[f, :, cols] = dlogit
             dhid = (inv * dlogit) * (whc_ref[...] - unit * (logit * (1.0 / chans)))
@@ -371,7 +439,7 @@
             frame(every, 1, F32),
             pltpu.VMEM((3 * chans, vox), BF16),
             pltpu.VMEM((chans * rows, width), F32),
-            pltpu.VMEM((total, vox), F32),
+            pltpu.VMEM((own + 8, vox), F32),
             pltpu.SemaphoreType.DMA((loose,)),
         ]
         + [pltpu.VMEM(sums, F32)] * last
@@ -401,7 +469,7 @@
 
 def sum_over_tiles(value, tiles, g, others):
     if tiles & (tiles - 1):
-        return lax.psum(value.astype(BF16), "tile").astype(F32), others
+        return lax.psum(value.astype(BF16), "tile").astype(F32), [], others
     steps = [2**k for k in range(tiles.bit_length() - 1)]
     outer, inner = [k for k in steps if k >= g], [k for k in steps if k < g]
     rounds = [part[i : i + 2] for part in (outer, inner) for i in range(0, len(part), 2)]
@@ -409,11 +477,14 @@
         if number == len(rounds) - 1:
             value, others = lax.optimization_barrier((value, others))
         masks = bits + [sum(bits)] * (len(bits) - 1)
-        sent = value.astype(BF16)
+        sent, arrived = value.astype(BF16), []
         for k in masks:
             pairs = [(a, a ^ k) for a in range(tiles)]
-            value = value + lax.ppermute(sent, "tile", pairs).astype(F32)
-    return value, others
+            arrived.append(lax.ppermute(sent, "tile", pairs))
+        if number < len(rounds) - 1:
+            for piece in arrived:
+                value = value + piece.astype(F32)
+    return value, arrived, others
 
 
 def sum_over_reps(value, axis):
@@ -487,24 +558,16 @@
             row.extend(values)
 
         put("mine", am * per, late if am == 0 else 0)
-        put("theirs", 0, late if am == 1 else 0)
         for layer in range(per):
+            put(("theirs", layer), layer, late if am == 1 else 0)
             put(("temporal", layer), aq * own, *spots, am * per + layer)
         table.append(row)
     meta = lax.dynamic_index_in_dim(jnp.asarray(np.array(table, np.int32)), t, 0, False)
 
-    def arrive(value, layer):
-        pieces = []
-        for s in range(1, g):
-            piece = lax.dynamic_slice_in_dim(value, (m + s) % g * per + layer, 1, 2)
-            pieces.append(swap(piece, s))
-        return pieces
-
-    arriving = [arrive(x, 0)]
+    arriving = [
+        swap(lax.dynamic_slice_in_dim(x, (m + s) % g * per, per, 2), s) for s in range(1, g)
+    ]
     mine = list(run_forward(meta, slots["mine"], extra, per, x, w_spatial))
-    if per > 1:
-        later, mine[1] = lax.optimization_barrier((x, mine[1]))
-        arriving += [arrive(later, layer) for layer in range(1, per)]
     ahead = []
     if mirrored:
         ahead.append(hop(mine[0], (-1, 1)))
@@ -513,13 +576,14 @@
 
     dims = (own, chans, vox, total, g, width)
     grads = jnp.zeros((6, chans, 3 * chans), F32)
-    ready, asked = [], targets
+    asked, mine[2] = lax.optimization_barrier((targets, mine[2]))
+    ready = []
     for layer in range(per):
         done = [mine]
-        for piece in arriving[layer]:
-            done.append(list(run_forward(meta, slots["theirs"], extra, 1, piece, w_spatial)))
-        if layer == 0 and g > 1:
-            asked, done[1][2] = lax.optimization_barrier((targets, done[1][2]))
+        if layer:
+            ahead, arriving = lax.optimization_barrier((ahead, arriving))
+        for piece in arriving:
+            done.append(list(run_forward(meta, slots["theirs", layer], extra, 1, piece, w_spatial)))
         pieces = [d[0] for d in done]
         ranks = [layer] + [0] * (g - 1)
         if mirrored:
@@ -542,11 +606,11 @@
                 d += 1
         ready.append([layer, pieces, ranks, [d[1] for d in done], [d[2] for d in done]])
 
-    everyone = jnp.broadcast_to(asked, (tiles, total, spot))
-    everyone = lax.all_to_all(everyone, "tile", 0, 0, tiled=True)
-    tgt = lax.dynamic_slice_in_dim(everyone, m * share, share, 0)
+    windows = run_windows(asked, tiles, own, g)
+    windows = lax.all_to_all(windows, "tile", 0, 0, tiled=True)
+    tgt = lax.dynamic_slice_in_dim(windows, m * share, share, 0)
     if share % per:
-        tgt = tgt.transpose(1, 0, 2).reshape(total, per, vox).transpose(1, 0, 2)
+        tgt = tgt.transpose(1, 0, 2).reshape(own + 8, per, vox).transpose(1, 0, 2)
     frame_weight = jnp.pad(valid[0].astype(F32) / total, (3, 3))
     frame_weight = lax.dynamic_slice_in_dim(frame_weight, q * own, own + 6, 0)
 
@@ -580,18 +644,13 @@
     logits = logits.transpose(1, 0, 2)
     logits = jnp.concatenate([logits] * g)
     logits = lax.all_to_all(logits, "tile", 0, 0, tiled=True)
-    grads, homecoming = sum_over_tiles(sum_over_reps(grads, 1), tiles, g, homecoming)
+    grads, arrived, homecoming = sum_over_tiles(sum_over_reps(grads, 1), tiles, g, homecoming)
     for layer in range(per):
         for s in range(1, g):
             place = (m + s) % g * per + layer
             out = lax.dynamic_update_slice_in_dim(out, homecoming[layer][s - 1], place, 2)
-    logits, grads = lax.optimization_barrier((logits, grads))
-    logits = take(logits.reshape(groups, g, own, spot), t // share, 1).reshape(1, total, spot)
-    part = grads.shape[1]
-    gs = grads[:9]
-    gt = grads[9:15].reshape(2, 3, part, chans)
-    gh = lax.dynamic_slice_in_dim(grads[15, 0], lax.axis_index("rep") * part, part, 0)
-
+    logits, gs, gt, gh = run_finish(grads, arrived, logits, groups, g)
+    logits, gh = logits.reshape(1, total, spot), gh[0]
     return logits, out[None], gs, gt, gh
 
 

time: 124 us -> 121 us (0.976)
  local copies, waits for them, and re-layouts: 12.8 us -> 9.4 us
  waiting for transfers between devices: 13.4 us -> 10.5 us
  Pallas kernels: 52.1 us -> 54.7 us
    ppermute x4 -> x3, waiting for transfers between devices: 0.01 us -> 4.36 us  [swap(): return lax.ppermute(value, 'tile', pairs)]
    all_to_all x1, waiting for transfers between devices: 4.04 us -> 0.01 us  [body(): windows = lax.all_to_all(windows, 'tile', 0, 0, tiled=True)]
    ppermute x6, waiting for transfers between devices: 3.22 us -> 0.02 us  [hop(): return lax.ppermute(value, 'tile', [p for p in pairs if 0 <= p[1] < tiles])]
    pallas_call x0 -> x2, Pallas kernels: none -> 3.07 us  [the longest x1 1.64 us: run_finish(): pl.pallas_call(functools.partial(finish_kernel, len(arrived), g), name='f...]
    slice x3 -> x0, local copies, waits for them, and re-layouts: 1.26 us -> none  [the longest x1 0.64 us: body(): gs = grads[:9]]
    dynamic_slice x3 -> x1, local copies, waits for them, and re-layouts: 3.59 us -> 2.42 us  [body(): lax.dynamic_slice_in_dim(x, (m + s) % g * per, per, 2)]
    ppermute x4 -> x3, starting transfers between devices: 5.12 us -> 5.12 us  [swap(): return lax.ppermute(value, 'tile', pairs)]
  transfers between devices with their start and end apart: 19 -> 18, of which waited for: 7 -> 5; matrix products, arithmetic and copies ran while one was open for 7% -> 5% of each run, Pallas kernels for 42% -> 44%
where the time goes in v7:
time: 121 us; the launch traced here: 120 us
  Pallas kernels  54.7 us (45%)
  starting transfers between devices  43.6 us (36%)
  waiting for transfers between devices  10.5 us (9%)
  local copies, waits for them, and re-layouts  9.4 us (8%)
    pallas_call x2, Pallas kernels, run_temporal(): pl.pallas_call(functools.partial(temporal_kernel, tuple(places), last, al...  37.5 us
    ppermute x6, starting transfers between devices, hop(): return lax.ppermute(value, 'tile', [p for p in pairs if 0 <= p[1] < tiles])  17.7 us
    pallas_call x3, Pallas kernels, run_forward(): pl.pallas_call(functools.partial(forward_kernel, middle, base), name='con...  14.1 us
    ppermute x4, starting transfers between devices, sum_over_tiles(): arrived.append(lax.ppermute(sent, 'tile', pairs))  6.53 us
    all_to_all x1, starting transfers between devices, body(): windows = lax.all_to_all(windows, 'tile', 0, 0, tiled=True)  6.01 us
    ppermute x3, starting transfers between devices, swap(): return lax.ppermute(value, 'tile', pairs)  5.12 us
    all_to_all x1, starting transfers between devices, body(): logits = lax.all_to_all(logits, 'tile', 0, 0, tiled=True)  4.99 us
    ppermute x3, waiting for transfers between devices, swap(): return lax.ppermute(value, 'tile', pairs)  4.36 us
  transfers between devices with their start and end apart: 18, of which 5 were waited for; matrix products, arithmetic and copies ran while one was open for 5% of the time, Pallas kernels for 44%

profile of v7, /device:TPU:0, one launch (start us, length us, event | category | flops | bytes accessed | tf_op | source)
XLA Modules:
  0.0 120.1 jit_solution(16709705215346369666)
XLA Ops:
  0.7 0.0 copy-start.3
  0.7 2.4 %dynamic-slice_bitcast_fusion = bf16[4,64,2,8,128]{4,3,2,1,0:T(8,128)(2,1)} fusion(bf16[1,4,64,4,8,128]{5,4,3,2,1,0:T(8,128)(2,1)} %param.7, s32[]{:T(128)S(6)} %select_n.67), kind=kLoop, calls=%fused_computation | loop fusion | bytes 2097156 | tf_op jit(solution)/shard_map/dynamic_slice | solution.py:568
  3.1 3.0 %collective-permute-start.2 = (bf16[4,64,2,8,128]{4,3,2,1,0:T(8,128)(2,1)}, bf16[4,64,2,8,128]{4,3,2,1,0:T(8,128)(2,1)S(1)}, u32[]{:S(2)}, u32[]{:S(2)}) collective-permute-start(bf16[4,64,2,8,128]{4,3,2,1,0:T(8,128)(2,1)} %dynamic-slice_bitcast_fusion), channel_id=1, source_target_pairs={{0,4},{4,0},{8,12},{12,8},{16,20},{20,16},{24,28},{28,24},{1,5},{5... | collective-permute-start | bytes 3145736 | tf_op jit(solution)/shard_map/ppermute | solution.py:521
  6.1 1.2 fusion.3.meta_ref
  7.3 6.1 %conv_forward.3 = (bf16[2,4,64,1024]{3,2,1,0:T(8,128)(2,1)}, bf16[2,4,64,1024]{3,2,1,0:T(8,128)(2,1)}, bf16[2,4,64,1024]{3,2,1,0:T(8,128)(2,1)}, bf16[2,2,64,1024]{3,2,1,0:T(8,128)(2,1)}) custom-call(s32[22]{0:T(128)} %fusion.3.meta_ref, bf16[4,64,4,8,128]{4,3,2,1,0:T(8,128)(2,1)} %bitcast.34, bf16[9,64,64]{2,1,0:T(8,128)(2,1)} %w_ref.5), custom_call_target="tpu_custom_call" | custom-call | flops 1000 | bytes 1000 | tf_op jit(solution)/shard_map/conv_forward/pallas_call | solution.py:111
  13.4 1.4 %collective-permute-start = (bf16[2,4,64,1024]{3,2,1,0:T(8,128)(2,1)}, bf16[2,4,64,1024]{3,2,1,0:T(8,128)(2,1)S(1)}, u32[]{:S(2)}, u32[]{:S(2)}) collective-permute-start(bf16[2,4,64,1024]{3,2,1,0:T(8,128)(2,1)} %get-tuple-element.64.rest_0_), channel_id=1, source_target_pairs={{4,12},{8,0},{12,20},{16,8},{20,28},{24,16},{5,13},{9,1},{13,21},{... | collective-permute-start | bytes 3145736 | tf_op jit(solution)/shard_map/ppermute | solution.py:525
  14.8 1.4 %windows.1 = bf16[8,16,512]{2,1,0:T(8,128)(2,1)} custom-call(bf16[1,32,512]{2,1,0:T(8,128)(2,1)} %tgt_ref), custom_call_target="tpu_custom_call" | custom-call | flops 1000 | bytes 1000 | tf_op jit(solution)/shard_map/windows/pallas_call | solution.py:149
  16.2 6.0 %all-to-all-start = ((bf16[8,16,512]{2,1,0:T(8,128)(2,1)}), bf16[8,16,512]{2,1,0:T(8,128)(2,1)}, u32[]{:S(2)}, u32[]{:S(2)}) async-start(bf16[8,16,512]{2,1,0:T(8,128)(2,1)} %windows.1), calls=%async_computation | async-start | bytes 262144 | tf_op jit(solution)/shard_map/all_to_all | solution.py:610
  22.2 3.9 %collective-permute-start.1 = (bf16[2,2,64,1024]{3,2,1,0:T(8,128)(2,1)}, bf16[2,2,64,1024]{3,2,1,0:T(8,128)(2,1)S(1)}, u32[]{:S(2)}, u32[]{:S(2)}) collective-permute-start(bf16[2,2,64,1024]{3,2,1,0:T(8,128)(2,1)} %get-tuple-element.47), channel_id=1, source_target_pairs={{0,8},{8,16},{12,4},{16,24},{20,12},{28,20},{1,9},{9,17},{13,5},{1... | collective-permute-start | bytes 1572872 | tf_op jit(solution)/shard_map/ppermute | solution.py:525
  26.3 0.0 copy-start
  26.3 4.4 %collective-permute-done.2.x_ref = bf16[4,64,2,8,128]{4,3,2,1,0:T(8,128)(2,1)S(1)} collective-permute-done((bf16[4,64,2,8,128]{4,3,2,1,0:T(8,128)(2,1)}, bf16[4,64,2,8,128]{4,3,2,1,0:T(8,128)(2,1)S(1)}, u32[]{:S(2)}, u32[]{:S(2)}) %collective-permute-start.2) | collective-permute-done | bytes 1048608 | tf_op jit(solution)/shard_map/ppermute | solution.py:521
  30.7 1.0 copy-done.2
  31.6 4.0 %conv_forward.5 = (bf16[1,4,64,1024]{3,2,1,0:T(8,128)(2,1)}, bf16[1,4,64,1024]{3,2,1,0:T(8,128)(2,1)}, bf16[1,4,64,1024]{3,2,1,0:T(8,128)(2,1)}, bf16[1,2,64,1024]{3,2,1,0:T(8,128)(2,1)}) custom-call(s32[22]{0:T(128)} %fusion.3.meta_ref, bf16[4,64,2,8,128]{4,3,2,1,0:T(8,128)(2,1)} %copy-done.2, bf16[9,64,64]{2,1,0:T(8,128)(2,1)} %w_ref.5), custom_call_target="tpu_custom_call" | custom-call | flops 1000 | bytes 1000 | tf_op jit(solution)/shard_map/conv_forward/pallas_call | solution.py:111
  35.6 4.2 %collective-permute-start.5 = (bf16[1,4,64,1024]{3,2,1,0:T(8,128)(2,1)}, bf16[1,4,64,1024]{3,2,1,0:T(8,128)(2,1)}, u32[]{:S(2)}, u32[]{:S(2)}) collective-permute-start(bf16[1,4,64,1024]{3,2,1,0:T(8,128)(2,1)} %get-tuple-element.55.rest_1_), channel_id=1, source_target_pairs={{0,8},{8,16},{12,4},{16,24},{20,12},{28,20},{1,9},{9,17},{13,5},{1... | collective-permute-start | bytes 1572872 | tf_op jit(solution)/shard_map/ppermute | solution.py:525
  39.8 1.3 %collective-permute-start.6 = (bf16[1,2,64,1024]{3,2,1,0:T(8,128)(2,1)}, bf16[1,2,64,1024]{3,2,1,0:T(8,128)(2,1)S(1)}, u32[]{:S(2)}, u32[]{:S(2)}) collective-permute-start(bf16[1,2,64,1024]{3,2,1,0:T(8,128)(2,1)} %get-tuple-element.56), channel_id=1, source_target_pairs={{4,12},{8,0},{12,20},{16,8},{20,28},{24,16},{5,13},{9,1},{13,21},{... | collective-permute-start | bytes 786440 | tf_op jit(solution)/shard_map/ppermute | solution.py:525
  41.1 0.0 collective-permute-done.1.rest_3_
  41.1 0.0 collective-permute-done.rest_2_
  41.2 4.0 %conv_forward.4 = (bf16[1,4,64,1024]{3,2,1,0:T(8,128)(2,1)}, bf16[1,4,64,1024]{3,2,1,0:T(8,128)(2,1)}, bf16[1,4,64,1024]{3,2,1,0:T(8,128)(2,1)}, bf16[1,2,64,1024]{3,2,1,0:T(8,128)(2,1)}) custom-call(s32[22]{0:T(128)} %fusion.3.meta_ref, bf16[4,64,2,8,128]{4,3,2,1,0:T(8,128)(2,1)} %copy-done.2, bf16[9,64,64]{2,1,0:T(8,128)(2,1)} %w_ref.5), custom_call_target="tpu_custom_call" | custom-call | flops 1000 | bytes 1000 | tf_op jit(solution)/shard_map/conv_forward/pallas_call | solution.py:111
  45.2 5.4 %collective-permute-start.3 = (bf16[1,4,64,1024]{3,2,1,0:T(8,128)(2,1)}, bf16[1,4,64,1024]{3,2,1,0:T(8,128)(2,1)}, u32[]{:S(2)}, u32[]{:S(2)}) collective-permute-start(bf16[1,4,64,1024]{3,2,1,0:T(8,128)(2,1)} %get-tuple-element.65.rest_1_), channel_id=1, source_target_pairs={{0,8},{8,16},{12,4},{16,24},{20,12},{28,20},{1,9},{9,17},{13,5},{1... | collective-permute-start | bytes 1572872 | tf_op jit(solution)/shard_map/ppermute | solution.py:525
  50.6 0.1 copy.23.whc_ref
  50.7 0.2 copy.20
  50.8 0.1 pad_dynamic-slice_fusion.weight_ref
  50.9 1.5 %collective-permute-start.4 = (bf16[1,2,64,1024]{3,2,1,0:T(8,128)(2,1)}, bf16[1,2,64,1024]{3,2,1,0:T(8,128)(2,1)S(1)}, u32[]{:S(2)}, u32[]{:S(2)}) collective-permute-start(bf16[1,2,64,1024]{3,2,1,0:T(8,128)(2,1)} %get-tuple-element.52), channel_id=1, source_target_pairs={{4,12},{8,0},{12,20},{16,8},{20,28},{24,16},{5,13},{9,1},{13,21},{... | collective-permute-start | bytes 786440 | tf_op jit(solution)/shard_map/ppermute | solution.py:525
  52.4 0.2 reshape.43.wb_ref
  52.6 0.1 copy.22.wtb_ref
  52.7 0.1 copy.19
  52.8 0.1 copy.21.wt_ref
  52.9 0.0 all-to-all-done
  52.9 0.8 constant_dynamic-slice_fusion.1
  53.7 0.0 collective-permute-done.6.rest_5_
  53.7 0.0 collective-permute-done.5.rest_4_
  53.8 18.6 %temporal.2 = (f32[14,1,1024]{2,1,0:T(1,128)S(1)}, f32[6,64,192]{2,1,0:T(8,128)S(1)}, bf16[4,64,4,8,128]{4,3,2,1,0:T(8,128)(2,1)}, bf16[1,4,64,8,128]{4,3,2,1,0:T(8,128)(2,1)S(1)}) custom-call(s32[22]{0:T(128)S(1)} %copy-done, f32[14]{0:T(128)S(1)} %pad_dynamic-slice_fusion.weight_ref, bf16[2,64,192]{2,1,0:T(8,128)(2,1)S(1)} %copy.21.wt_ref, ...), custom_call_target="tpu_custom_call" | custom-call | flops 1572864000 | bytes 52428800 | tf_op jit(solution)/shard_map/temporal/pallas_call | solution.py:418
  72.3 0.0 collective-permute-done.4.rest_5_
  72.4 0.0 collective-permute-done.3.rest_4_
  72.4 0.4 collective-permute-start.7
  72.8 19.0 %temporal.3 = (f32[14,1,1024]{2,1,0:T(1,128)S(1)}, f32[16,64,64]{2,1,0:T(8,128)S(1)}, bf16[4,64,4,8,128]{4,3,2,1,0:T(8,128)(2,1)}, bf16[1,4,64,8,128]{4,3,2,1,0:T(8,128)(2,1)}) custom-call(s32[22]{0:T(128)S(1)} %copy-done, f32[14]{0:T(128)S(1)} %pad_dynamic-slice_fusion.weight_ref, ...), custom_call_target="tpu_custom_call", output_to_operand_aliasing={{2}: (18, {})} | custom-call | flops 1572864000 | bytes 52428800 | tf_op jit(solution)/shard_map/temporal/pallas_call | solution.py:418
  91.7 1.8 %collective-permute-start.14 = (bf16[4,64,1,8,128]{4,3,1,0,2:T(8,128)(2,1)}, bf16[4,64,1,8,128]{4,3,1,0,2:T(8,128)(2,1)S(1)}, u32[]{:S(2)}, u32[]{:S(2)}) collective-permute-start(bf16[4,64,1,8,128]{4,3,1,0,2:T(8,128)(2,1)} %bitcast.42), channel_id=1, source_target_pairs={{0,4},{4,0},{8,12},{12,8},{16,20},{20,16},{24,28},{28,24},{1,5},{5... | collective-permute-start | bytes 1572872 | tf_op jit(solution)/shard_map/ppermute | solution.py:521
  93.5 0.1 fusion.1
  93.6 0.1 fusion
  93.7 0.0 collective-permute-done.7
  93.8 0.1 collective-permute-start.8
  93.8 1.7 %collective-permute-start.10 = (bf16[16,16,64]{2,1,0:T(8,128)(2,1)S(1)}, bf16[16,16,64]{2,1,0:T(8,128)(2,1)S(1)}, u32[]{:S(2)}, u32[]{:S(2)}) collective-permute-start(bf16[16,16,64]{2,1,0:T(8,128)(2,1)S(1)} %get-tuple-element.88), channel_id=1, source_target_pairs={{0,3},{1,0},{2,1},{3,2},{4,7},{5,4},{6,5},{7,6},{8,11},{9,8},{10,9... | collective-permute-start | bytes 98312 | tf_op jit(solution)/shard_map/ppermute | solution.py:501
  95.6 1.5 %collective-permute-start.9 = (bf16[16,16,64]{2,1,0:T(8,128)(2,1)S(1)}, bf16[16,16,64]{2,1,0:T(8,128)(2,1)S(1)}, u32[]{:S(2)}, u32[]{:S(2)}) collective-permute-start(bf16[16,16,64]{2,1,0:T(8,128)(2,1)S(1)} %get-tuple-element.89), channel_id=1, source_target_pairs={{0,2},{1,3},{2,0},{3,1},{4,6},{5,7},{6,4},{7,5},{8,10},{9,11},{10,... | collective-permute-start | bytes 98312 | tf_op jit(solution)/shard_map/ppermute | solution.py:501
  97.1 0.4 collective-permute-done.8
  97.5 0.4 collective-permute-done.10
  97.9 2.2 %collective-permute-done.9 = bf16[16,16,64]{2,1,0:T(8,128)(2,1)S(1)} collective-permute-done((bf16[16,16,64]{2,1,0:T(8,128)(2,1)S(1)}, bf16[16,16,64]{2,1,0:T(8,128)(2,1)S(1)}, u32[]{:S(2)}, u32[]{:S(2)}) %collective-permute-start.9) | collective-permute-done | bytes 32800 | tf_op jit(solution)/shard_map/ppermute | solution.py:501
  100.2 2.7 %collective-permute-start.13 = (bf16[16,16,64]{2,1,0:T(8,128)(2,1)S(1)}, bf16[16,16,64]{2,1,0:T(8,128)(2,1)S(1)}, u32[]{:S(2)}, u32[]{:S(2)}) collective-permute-start(bf16[16,16,64]{2,1,0:T(8,128)(2,1)S(1)} %fusion.2), channel_id=1, source_target_pairs={{0,24},{4,28},{8,16},{12,20},{16,8},{20,12},{24,0},{28,4},{1,25},{... | collective-permute-start | bytes 98312 | tf_op jit(solution)/shard_map/ppermute | solution.py:483
  102.9 1.5 %collective-permute-start.12 = (bf16[16,16,64]{2,1,0:T(8,128)(2,1)S(1)}, bf16[16,16,64]{2,1,0:T(8,128)(2,1)S(1)}, u32[]{:S(2)}, u32[]{:S(2)}) collective-permute-start(bf16[16,16,64]{2,1,0:T(8,128)(2,1)S(1)} %fusion.2), channel_id=1, source_target_pairs={{0,16},{4,20},{8,24},{12,28},{16,0},{20,4},{24,8},{28,12},{1,17},{... | collective-permute-start | bytes 98312 | tf_op jit(solution)/shard_map/ppermute | solution.py:483
  104.4 0.3 collective-permute-start.11
  104.7 0.6 pad_maximum_fusion
  105.3 5.0 %all-to-all-start.1 = ((bf16[8,8,512]{2,1,0:T(8,128)(2,1)}), bf16[8,8,512]{2,1,0:T(8,128)(2,1)S(1)}, u32[]{:S(2)}, u32[]{:S(2)}) async-start(bf16[8,8,512]{2,1,0:T(8,128)(2,1)} %pad_maximum_fusion), calls=%async_computation.1 | async-start | bytes 131072 | tf_op jit(solution)/shard_map/all_to_all | solution.py:646
  110.3 0.0 collective-permute-done.13
  110.3 0.0 collective-permute-done.12
  110.3 0.0 collective-permute-done.11
  110.3 0.1 convert_add_fusion.value_ref
  110.4 0.0 collective-permute-done.14
  110.4 2.1 %collective-permute-start.15 = (bf16[16,16,64]{2,1,0:T(8,128)(2,1)S(1)}, bf16[16,16,64]{2,1,0:T(8,128)(2,1)S(1)}, u32[]{:S(2)}, u32[]{:S(2)}) collective-permute-start(bf16[16,16,64]{2,1,0:T(8,128)(2,1)S(1)} %convert_element_type.69), channel_id=1, source_target_pairs={{0,4},{4,0},{8,12},{12,8},{16,20},{20,16},{24,28},{28,24},{1,5},{5... | collective-permute-start | bytes 98312 | tf_op jit(solution)/shard_map/ppermute | solution.py:483
  112.5 0.8 bitcast_dynamic-update-slice_fusion.1
  113.3 0.8 bitcast_dynamic-update-slice_fusion
  114.2 3.0 %all-to-all-done.1.rest_1_ = bf16[8,8,512]{2,1,0:T(8,128)(2,1)S(1)} async-done(((bf16[8,8,512]{2,1,0:T(8,128)(2,1)}), bf16[8,8,512]{2,1,0:T(8,128)(2,1)S(1)}, u32[]{:S(2)}, u32[]{:S(2)}) %all-to-all-start.1) | async-done | bytes 65568 | tf_op jit(solution)/shard_map/all_to_all | solution.py:646
  117.2 0.0 collective-permute-done.15.rest_0_
  117.2 0.6 copy-done.6
  117.8 0.6 copy-done.8
  118.4 1.6 %finish.1 = (bf16[4,8,512]{2,1,0:T(8,128)(2,1)}, f32[9,16,64]{2,1,0:T(8,128)}, f32[2,3,16,64]{3,2,1,0:T(8,128)}, f32[1,16]{1,0:T(1,128)}) custom-call(f32[16,16,64]{2,1,0:T(8,128)} %copy-done.5, bf16[16,16,64]{2,1,0:T(8,128)(2,1)} %copy-done.8, bf16[8,8,512]{2,1,0:T(8,128)(2,1)} %copy-done.6), custom_call_target="tpu_custom_call" | custom-call | flops 1000 | bytes 1000 | tf_op jit(solution)/shard_map/finish/pallas_call | solution.py:190
  (26 shorter events, 0.2 us)
Async XLA Ops:
  0.7 25.5 %copy-start.7 = (bf16[2,3,64,64]{3,2,1,0:T(8,128)(2,1)S(1)}, bf16[2,3,64,64]{3,2,1,0:T(8,128)(2,1)}, u32[]{:S(2)}) copy-start(bf16[2,3,64,64]{3,2,1,0:T(8,128)(2,1)} %param.9) | copy-start | bytes 147460
  0.7 25.6 %copy-start.3 = (bf16[9,64,64]{2,1,0:T(8,128)(2,1)S(1)}, bf16[9,64,64]{2,1,0:T(8,128)(2,1)}, u32[]{:S(2)}) copy-start(bf16[9,64,64]{2,1,0:T(8,128)(2,1)} %w_ref.5) | copy-start | bytes 221188
  3.1 27.6 %collective-permute-start.2 = (bf16[4,64,2,8,128]{4,3,2,1,0:T(8,128)(2,1)}, bf16[4,64,2,8,128]{4,3,2,1,0:T(8,128)(2,1)S(1)}, u32[]{:S(2)}, u32[]{:S(2)}) collective-permute-start(bf16[4,64,2,8,128]{4,3,2,1,0:T(8,128)(2,1)} %dynamic-slice_bitcast_fusion), channel_id=1, source_target_pairs={{0,4},{4,0},{8,12},{12,8},{16,20},{20,16},{24,28},{28,24},{1,5},{5... | collective-permute-start | bytes 3145736 | tf_op jit(solution)/shard_map/ppermute | solution.py:521
  7.3 32.6 %copy-start.9 = (bf16[64]{0:T(256)(128)(2,1)S(1)}, bf16[64]{0:T(256)(128)(2,1)}, u32[]{:S(2)}) copy-start(bf16[64]{0:T(256)(128)(2,1)} %param.10) | copy-start | bytes 388
  13.4 37.2 %copy-start.10 = (s32[1,32]{1,0:T(1,128)S(1)}, s32[1,32]{1,0:T(1,128)}, u32[]{:S(2)}) copy-start(s32[1,32]{1,0:T(1,128)} %param.12) | copy-start | bytes 388
  13.4 27.8 %collective-permute-start = (bf16[2,4,64,1024]{3,2,1,0:T(8,128)(2,1)}, bf16[2,4,64,1024]{3,2,1,0:T(8,128)(2,1)S(1)}, u32[]{:S(2)}, u32[]{:S(2)}) collective-permute-start(bf16[2,4,64,1024]{3,2,1,0:T(8,128)(2,1)} %get-tuple-element.64.rest_0_), channel_id=1, source_target_pairs={{4,12},{8,0},{12,20},{16,8},{20,28},{24,16},{5,13},{9,1},{13,21},{... | collective-permute-start | bytes 3145736 | tf_op jit(solution)/shard_map/ppermute | solution.py:525
  16.2 36.7 %all-to-all-start = ((bf16[8,16,512]{2,1,0:T(8,128)(2,1)}), bf16[8,16,512]{2,1,0:T(8,128)(2,1)}, u32[]{:S(2)}, u32[]{:S(2)}) async-start(bf16[8,16,512]{2,1,0:T(8,128)(2,1)} %windows.1), calls=%async_computation | async-start | bytes 262144 | tf_op jit(solution)/shard_map/all_to_all | solution.py:610
  22.2 18.9 %collective-permute-start.1 = (bf16[2,2,64,1024]{3,2,1,0:T(8,128)(2,1)}, bf16[2,2,64,1024]{3,2,1,0:T(8,128)(2,1)S(1)}, u32[]{:S(2)}, u32[]{:S(2)}) collective-permute-start(bf16[2,2,64,1024]{3,2,1,0:T(8,128)(2,1)} %get-tuple-element.47), channel_id=1, source_target_pairs={{0,8},{8,16},{12,4},{16,24},{20,12},{28,20},{1,9},{9,17},{13,5},{1... | collective-permute-start | bytes 1572872 | tf_op jit(solution)/shard_map/ppermute | solution.py:525
  26.3 27.5 %copy-start = (s32[22]{0:T(128)S(1)}, s32[22]{0:T(128)}, u32[]{:S(2)}) copy-start(s32[22]{0:T(128)} %fusion.3.meta_ref) | copy-start | bytes 268
  30.7 1.0 copy-start.2
  35.6 18.1 %collective-permute-start.5 = (bf16[1,4,64,1024]{3,2,1,0:T(8,128)(2,1)}, bf16[1,4,64,1024]{3,2,1,0:T(8,128)(2,1)}, u32[]{:S(2)}, u32[]{:S(2)}) collective-permute-start(bf16[1,4,64,1024]{3,2,1,0:T(8,128)(2,1)} %get-tuple-element.55.rest_1_), channel_id=1, source_target_pairs={{0,8},{8,16},{12,4},{16,24},{20,12},{28,20},{1,9},{9,17},{13,5},{1... | collective-permute-start | bytes 1572872 | tf_op jit(solution)/shard_map/ppermute | solution.py:525
  39.8 13.9 %collective-permute-start.6 = (bf16[1,2,64,1024]{3,2,1,0:T(8,128)(2,1)}, bf16[1,2,64,1024]{3,2,1,0:T(8,128)(2,1)S(1)}, u32[]{:S(2)}, u32[]{:S(2)}) collective-permute-start(bf16[1,2,64,1024]{3,2,1,0:T(8,128)(2,1)} %get-tuple-element.56), channel_id=1, source_target_pairs={{4,12},{8,0},{12,20},{16,8},{20,28},{24,16},{5,13},{9,1},{13,21},{... | collective-permute-start | bytes 786440 | tf_op jit(solution)/shard_map/ppermute | solution.py:525
  41.1 12.6 %copy-start.4 = (bf16[2,2,64,1024]{3,2,1,0:T(8,128)(2,1)}, bf16[2,2,64,1024]{3,2,1,0:T(8,128)(2,1)S(1)}, u32[]{:S(2)}) copy-start(bf16[2,2,64,1024]{3,2,1,0:T(8,128)(2,1)S(1)} %collective-permute-done.1.rest_3_) | copy-start | bytes 1572868
  41.2 12.6 %copy-start.1 = (bf16[2,4,64,1024]{3,2,1,0:T(8,128)(2,1)}, bf16[2,4,64,1024]{3,2,1,0:T(8,128)(2,1)S(1)}, u32[]{:S(2)}) copy-start(bf16[2,4,64,1024]{3,2,1,0:T(8,128)(2,1)S(1)} %collective-permute-done.rest_2_) | copy-start | bytes 3145732
  45.2 27.2 %collective-permute-start.3 = (bf16[1,4,64,1024]{3,2,1,0:T(8,128)(2,1)}, bf16[1,4,64,1024]{3,2,1,0:T(8,128)(2,1)}, u32[]{:S(2)}, u32[]{:S(2)}) collective-permute-start(bf16[1,4,64,1024]{3,2,1,0:T(8,128)(2,1)} %get-tuple-element.65.rest_1_), channel_id=1, source_target_pairs={{0,8},{8,16},{12,4},{16,24},{20,12},{28,20},{1,9},{9,17},{13,5},{1... | collective-permute-start | bytes 1572872 | tf_op jit(solution)/shard_map/ppermute | solution.py:525
  50.9 21.4 %collective-permute-start.4 = (bf16[1,2,64,1024]{3,2,1,0:T(8,128)(2,1)}, bf16[1,2,64,1024]{3,2,1,0:T(8,128)(2,1)S(1)}, u32[]{:S(2)}, u32[]{:S(2)}) collective-permute-start(bf16[1,2,64,1024]{3,2,1,0:T(8,128)(2,1)} %get-tuple-element.52), channel_id=1, source_target_pairs={{4,12},{8,0},{12,20},{16,8},{20,28},{24,16},{5,13},{9,1},{13,21},{... | collective-permute-start | bytes 786440 | tf_op jit(solution)/shard_map/ppermute | solution.py:525
  72.4 21.3 %collective-permute-start.7 = (bf16[4,64,1,8,128]{4,3,1,0,2:T(8,128)(2,1)S(1)}, bf16[4,64,1,8,128]{4,3,1,0,2:T(8,128)(2,1)S(1)}, u32[]{:S(2)}, u32[]{:S(2)}) collective-permute-start(bf16[4,64,1,8,128]{4,3,1,0,2:T(8,128)(2,1)S(1)} %bitcast.33), channel_id=1, source_target_pairs={{0,4},{4,0},{8,12},{12,8},{16,20},{20,16},{24,28},{28,24},{1,5},{5... | collective-permute-start | bytes 1572872 | tf_op jit(solution)/shard_map/ppermute | solution.py:521
  91.7 18.6 %collective-permute-start.14 = (bf16[4,64,1,8,128]{4,3,1,0,2:T(8,128)(2,1)}, bf16[4,64,1,8,128]{4,3,1,0,2:T(8,128)(2,1)S(1)}, u32[]{:S(2)}, u32[]{:S(2)}) collective-permute-start(bf16[4,64,1,8,128]{4,3,1,0,2:T(8,128)(2,1)} %bitcast.42), channel_id=1, source_target_pairs={{0,4},{4,0},{8,12},{12,8},{16,20},{20,16},{24,28},{28,24},{1,5},{5... | collective-permute-start | bytes 1572872 | tf_op jit(solution)/shard_map/ppermute | solution.py:521
  93.8 3.7 %collective-permute-start.8 = (bf16[16,16,64]{2,1,0:T(8,128)(2,1)S(1)}, bf16[16,16,64]{2,1,0:T(8,128)(2,1)S(1)}, u32[]{:S(2)}, u32[]{:S(2)}) collective-permute-start(bf16[16,16,64]{2,1,0:T(8,128)(2,1)S(1)} %get-tuple-element.87), channel_id=1, source_target_pairs={{0,1},{1,2},{2,3},{3,0},{4,5},{5,6},{6,7},{7,4},{8,9},{9,10},{10,1... | collective-permute-start | bytes 98312 | tf_op jit(solution)/shard_map/ppermute | solution.py:501
  93.8 4.1 %collective-permute-start.10 = (bf16[16,16,64]{2,1,0:T(8,128)(2,1)S(1)}, bf16[16,16,64]{2,1,0:T(8,128)(2,1)S(1)}, u32[]{:S(2)}, u32[]{:S(2)}) collective-permute-start(bf16[16,16,64]{2,1,0:T(8,128)(2,1)S(1)} %get-tuple-element.88), channel_id=1, source_target_pairs={{0,3},{1,0},{2,1},{3,2},{4,7},{5,4},{6,5},{7,6},{8,11},{9,8},{10,9... | collective-permute-start | bytes 98312 | tf_op jit(solution)/shard_map/ppermute | solution.py:501
  95.6 4.6 %collective-permute-start.9 = (bf16[16,16,64]{2,1,0:T(8,128)(2,1)S(1)}, bf16[16,16,64]{2,1,0:T(8,128)(2,1)S(1)}, u32[]{:S(2)}, u32[]{:S(2)}) collective-permute-start(bf16[16,16,64]{2,1,0:T(8,128)(2,1)S(1)} %get-tuple-element.89), channel_id=1, source_target_pairs={{0,2},{1,3},{2,0},{3,1},{4,6},{5,7},{6,4},{7,5},{8,10},{9,11},{10,... | collective-permute-start | bytes 98312 | tf_op jit(solution)/shard_map/ppermute | solution.py:501
  100.2 10.1 %collective-permute-start.13 = (bf16[16,16,64]{2,1,0:T(8,128)(2,1)S(1)}, bf16[16,16,64]{2,1,0:T(8,128)(2,1)S(1)}, u32[]{:S(2)}, u32[]{:S(2)}) collective-permute-start(bf16[16,16,64]{2,1,0:T(8,128)(2,1)S(1)} %fusion.2), channel_id=1, source_target_pairs={{0,24},{4,28},{8,16},{12,20},{16,8},{20,12},{24,0},{28,4},{1,25},{... | collective-permute-start | bytes 98312 | tf_op jit(solution)/shard_map/ppermute | solution.py:483
  102.9 7.4 %collective-permute-start.12 = (bf16[16,16,64]{2,1,0:T(8,128)(2,1)S(1)}, bf16[16,16,64]{2,1,0:T(8,128)(2,1)S(1)}, u32[]{:S(2)}, u32[]{:S(2)}) collective-permute-start(bf16[16,16,64]{2,1,0:T(8,128)(2,1)S(1)} %fusion.2), channel_id=1, source_target_pairs={{0,16},{4,20},{8,24},{12,28},{16,0},{20,4},{24,8},{28,12},{1,17},{... | collective-permute-start | bytes 98312 | tf_op jit(solution)/shard_map/ppermute | solution.py:483
  104.4 5.9 %collective-permute-start.11 = (bf16[16,16,64]{2,1,0:T(8,128)(2,1)S(1)}, bf16[16,16,64]{2,1,0:T(8,128)(2,1)S(1)}, u32[]{:S(2)}, u32[]{:S(2)}) collective-permute-start(bf16[16,16,64]{2,1,0:T(8,128)(2,1)S(1)} %fusion.2), channel_id=1, source_target_pairs={{0,8},{4,12},{8,0},{12,4},{16,24},{20,28},{24,16},{28,20},{1,9},{5... | collective-permute-start | bytes 98312 | tf_op jit(solution)/shard_map/ppermute | solution.py:483
  105.3 11.9 %all-to-all-start.1 = ((bf16[8,8,512]{2,1,0:T(8,128)(2,1)}), bf16[8,8,512]{2,1,0:T(8,128)(2,1)S(1)}, u32[]{:S(2)}, u32[]{:S(2)}) async-start(bf16[8,8,512]{2,1,0:T(8,128)(2,1)} %pad_maximum_fusion), calls=%async_computation.1 | async-start | bytes 131072 | tf_op jit(solution)/shard_map/all_to_all | solution.py:646
  110.4 6.8 %copy-start.5 = (f32[16,16,64]{2,1,0:T(8,128)}, f32[16,16,64]{2,1,0:T(8,128)S(1)}, u32[]{:S(2)}) copy-start(f32[16,16,64]{2,1,0:T(8,128)S(1)} %convert_add_fusion.value_ref) | copy-start | bytes 196612
  110.4 6.8 %collective-permute-start.15 = (bf16[16,16,64]{2,1,0:T(8,128)(2,1)S(1)}, bf16[16,16,64]{2,1,0:T(8,128)(2,1)S(1)}, u32[]{:S(2)}, u32[]{:S(2)}) collective-permute-start(bf16[16,16,64]{2,1,0:T(8,128)(2,1)S(1)} %convert_element_type.69), channel_id=1, source_target_pairs={{0,4},{4,0},{8,12},{12,8},{16,20},{20,16},{24,28},{28,24},{1,5},{5... | collective-permute-start | bytes 98312 | tf_op jit(solution)/shard_map/ppermute | solution.py:483
  117.2 0.6 copy-start.6
  117.8 0.6 copy-start.8

commit v8 on v7

--- a/solution.py
+++ b/solution.py
@@ -559,19 +559,25 @@
 
         put("mine", am * per, late if am == 0 else 0)
         for layer in range(per):
-            put(("theirs", layer), layer, late if am == 1 else 0)
+            put(("theirs", layer), 0, late if am == 1 else 0)
             put(("temporal", layer), aq * own, *spots, am * per + layer)
         table.append(row)
     meta = lax.dynamic_index_in_dim(jnp.asarray(np.array(table, np.int32)), t, 0, False)
 
-    arriving = [
-        swap(lax.dynamic_slice_in_dim(x, (m + s) % g * per, per, 2), s) for s in range(1, g)
+    leaving = [
+        [lax.dynamic_slice_in_dim(x, (m + s) % g * per + layer, 1, 2) for s in range(1, g)]
+        for layer in range(per)
     ]
+    arriving = [[swap(piece, s + 1) for s, piece in enumerate(leaving[0])]]
     mine = list(run_forward(meta, slots["mine"], extra, per, x, w_spatial))
+    leaving[1:], mine[1] = lax.optimization_barrier((leaving[1:], mine[1]))
+    for pieces in leaving[1:]:
+        arriving.append([swap(piece, s + 1) for s, piece in enumerate(pieces)])
     ahead = []
     if mirrored:
         ahead.append(hop(mine[0], (-1, 1)))
         if extra:
+            mine[3], arriving[0] = lax.optimization_barrier((mine[3], arriving[0]))
             ahead.append(hop(mine[3], (1, -1)))
 
     dims = (own, chans, vox, total, g, width)
@@ -581,8 +587,8 @@
     for layer in range(per):
         done = [mine]
         if layer:
-            ahead, arriving = lax.optimization_barrier((ahead, arriving))
-        for piece in arriving:
+            ahead, arriving[layer] = lax.optimization_barrier((ahead, arriving[layer]))
+        for piece in arriving[layer]:
             done.append(list(run_forward(meta, slots["theirs", layer], extra, 1, piece, w_spatial)))
         pieces = [d[0] for d in done]
         ranks = [layer] + [0] * (g - 1)

time: 121 us -> 120 us (level)
  waiting for transfers between devices: 10.5 us -> 12.9 us
  starting transfers between devices: 43.6 us -> 41.2 us
    ppermute x6, waiting for transfers between devices: 0.02 us -> 5.78 us  [hop(): return lax.ppermute(value, 'tile', [p for p in pairs if 0 <= p[1] < tiles])]
    ppermute x3 -> x4, waiting for transfers between devices: 4.36 us -> 0.01 us  [swap(): return lax.ppermute(value, 'tile', pairs)]
    ppermute x3 -> x4, starting transfers between devices: 5.12 us -> 7.94 us  [swap(): return lax.ppermute(value, 'tile', pairs)]
    ppermute x6, starting transfers between devices: 17.7 us -> 15.8 us  [hop(): return lax.ppermute(value, 'tile', [p for p in pairs if 0 <= p[1] < tiles])]
    ppermute x3, starting transfers between devices: 3.29 us -> 1.79 us  [sum_over_reps(): lax.ppermute(share(r + s).astype(BF16), 'rep', pairs).astype(F32)]
    all_to_all x1, starting transfers between devices: 6.01 us -> 4.72 us  [body(): windows = lax.all_to_all(windows, 'tile', 0, 0, tiled=True)]
  transfers between devices with their start and end apart: 18 -> 19, of which waited for: 5 -> 5; matrix products, arithmetic and copies ran while one was open for 5% -> 5% of each run, Pallas kernels for 44% -> 44%
where the time goes in v8:
time: 120 us
  Pallas kernels  54.8 us (46%)
  starting transfers between devices  41.2 us (34%)
  waiting for transfers between devices  12.9 us (11%)
  local copies, waits for them, and re-layouts  8.97 us (7%)
    pallas_call x2, Pallas kernels, run_temporal(): pl.pallas_call(functools.partial(temporal_kernel, tuple(places), last, al...  37.5 us
    ppermute x6, starting transfers between devices, hop(): return lax.ppermute(value, 'tile', [p for p in pairs if 0 <= p[1] < tiles])  15.8 us
    pallas_call x3, Pallas kernels, run_forward(): pl.pallas_call(functools.partial(forward_kernel, middle, base), name='con...  14.2 us
    ppermute x4, starting transfers between devices, swap(): return lax.ppermute(value, 'tile', pairs)  7.94 us
    ppermute x4, starting transfers between devices, sum_over_tiles(): arrived.append(lax.ppermute(sent, 'tile', pairs))  6.53 us
    ppermute x6, waiting for transfers between devices, hop(): return lax.ppermute(value, 'tile', [p for p in pairs if 0 <= p[1] < tiles])  5.78 us
    all_to_all x1, starting transfers between devices, body(): windows = lax.all_to_all(windows, 'tile', 0, 0, tiled=True)  4.72 us
    all_to_all x1, starting transfers between devices, body(): logits = lax.all_to_all(logits, 'tile', 0, 0, tiled=True)  4.42 us
  transfers between devices with their start and end apart: 19, of which 5 were waited for; matrix products, arithmetic and copies ran while one was open for 5% of the time, Pallas kernels for 44%

profile of v8, /device:TPU:0, one launch (start us, length us, event | category | flops | bytes accessed | tf_op | source)
XLA Modules:
  0.0 119.7 jit_solution(6080744222826536892)
XLA Ops:
  0.7 0.0 copy-start.2
  0.7 2.1 %dynamic-slice_bitcast_fusion = (bf16[4,64,1,8,128]{4,3,2,1,0:T(8,128)(2,1)}, bf16[4,64,1,8,128]{4,3,2,1,0:T(8,128)(2,1)S(1)}) fusion(bf16[1,4,64,4,8,128]{5,4,3,2,1,0:T(8,128)(2,1)} %param.7, s32[]{:T(128)S(6)} %select_n.71, s32[]{:T(128)S(6)} %select_n.70), kind=kLoop, calls=%fused_computation.2 | loop fusion | bytes 2097160 | tf_op jit(solution)/shard_map/dynamic_slice | solution.py:568
  2.8 3.0 %collective-permute-start.1 = (bf16[4,64,1,8,128]{4,3,2,1,0:T(8,128)(2,1)S(1)}, bf16[4,64,1,8,128]{4,3,2,1,0:T(8,128)(2,1)S(1)}, u32[]{:S(2)}, u32[]{:S(2)}) collective-permute-start(bf16[4,64,1,8,128]{4,3,2,1,0:T(8,128)(2,1)S(1)} %get-tuple-element.96), channel_id=1, source_target_pairs={{0,4},{4,0},{8,12},{12,8},{16,20},{20,16},{24,28},{28,24},{1,5},{5... | collective-permute-start | bytes 1572872 | tf_op jit(solution)/shard_map/ppermute | solution.py:521
  5.8 1.2 %fusion.3.meta_ref = s32[22]{0:T(128)} fusion(s32[8,22]{1,0:T(8,128)} %constant.97.clone, s32[]{:T(128)S(6)} %select_n.67), kind=kLoop, calls=%fused_computation.21 | loop fusion | bytes 180 | tf_op jit(solution)/shard_map/jit(dynamic_index_in_dim)/squeeze | solution.py:565
  7.0 6.1 %conv_forward.3 = (bf16[2,4,64,1024]{3,2,1,0:T(8,128)(2,1)}, bf16[2,4,64,1024]{3,2,1,0:T(8,128)(2,1)}, bf16[2,4,64,1024]{3,2,1,0:T(8,128)(2,1)}, bf16[2,2,64,1024]{3,2,1,0:T(8,128)(2,1)}) custom-call(s32[22]{0:T(128)} %fusion.3.meta_ref, bf16[4,64,4,8,128]{4,3,2,1,0:T(8,128)(2,1)} %bitcast.36, bf16[9,64,64]{2,1,0:T(8,128)(2,1)} %w_ref.5), custom_call_target="tpu_custom_call" | custom-call | flops 1000 | bytes 1000 | tf_op jit(solution)/shard_map/conv_forward/pallas_call | solution.py:111
  13.1 1.4 %collective-permute-start = (bf16[2,4,64,1024]{3,2,1,0:T(8,128)(2,1)}, bf16[2,4,64,1024]{3,2,1,0:T(8,128)(2,1)S(1)}, u32[]{:S(2)}, u32[]{:S(2)}) collective-permute-start(bf16[2,4,64,1024]{3,2,1,0:T(8,128)(2,1)} %get-tuple-element.72.rest_0_), channel_id=1, source_target_pairs={{4,12},{8,0},{12,20},{16,8},{20,28},{24,16},{5,13},{9,1},{13,21},{... | collective-permute-start | bytes 3145736 | tf_op jit(solution)/shard_map/ppermute | solution.py:525
  14.5 2.8 %collective-permute-start.3 = (bf16[4,64,1,8,128]{4,3,2,1,0:T(8,128)(2,1)}, bf16[4,64,1,8,128]{4,3,2,1,0:T(8,128)(2,1)S(1)}, u32[]{:S(2)}, u32[]{:S(2)}) collective-permute-start(bf16[4,64,1,8,128]{4,3,2,1,0:T(8,128)(2,1)} %get-tuple-element.54), channel_id=1, source_target_pairs={{0,4},{4,0},{8,12},{12,8},{16,20},{20,16},{24,28},{28,24},{1,5},{5... | collective-permute-start | bytes 1572872 | tf_op jit(solution)/shard_map/ppermute | solution.py:521
  17.3 1.4 %windows.1 = bf16[8,16,512]{2,1,0:T(8,128)(2,1)} custom-call(bf16[1,32,512]{2,1,0:T(8,128)(2,1)} %tgt_ref), custom_call_target="tpu_custom_call" | custom-call | flops 1000 | bytes 1000 | tf_op jit(solution)/shard_map/windows/pallas_call | solution.py:149
  18.7 4.7 %all-to-all-start = ((bf16[8,16,512]{2,1,0:T(8,128)(2,1)}), bf16[8,16,512]{2,1,0:T(8,128)(2,1)}, u32[]{:S(2)}, u32[]{:S(2)}) async-start(bf16[8,16,512]{2,1,0:T(8,128)(2,1)} %windows.1), calls=%async_computation | async-start | bytes 262144 | tf_op jit(solution)/shard_map/all_to_all | solution.py:616
  23.5 0.0 collective-permute-done.1.x_ref
  23.5 4.0 %collective-permute-start.2 = (bf16[2,2,64,1024]{3,2,1,0:T(8,128)(2,1)}, bf16[2,2,64,1024]{3,2,1,0:T(8,128)(2,1)S(1)}, u32[]{:S(2)}, u32[]{:S(2)}) collective-permute-start(bf16[2,2,64,1024]{3,2,1,0:T(8,128)(2,1)} %get-tuple-element.52), channel_id=1, source_target_pairs={{0,8},{8,16},{12,4},{16,24},{20,12},{28,20},{1,9},{9,17},{13,5},{1... | collective-permute-start | bytes 1572872 | tf_op jit(solution)/shard_map/ppermute | solution.py:525
  27.5 4.0 %conv_forward.5 = (bf16[1,4,64,1024]{3,2,1,0:T(8,128)(2,1)}, bf16[1,4,64,1024]{3,2,1,0:T(8,128)(2,1)}, bf16[1,4,64,1024]{3,2,1,0:T(8,128)(2,1)}, bf16[1,2,64,1024]{3,2,1,0:T(8,128)(2,1)}) custom-call(s32[22]{0:T(128)} %fusion.3.meta_ref, bf16[4,64,1,8,128]{4,3,2,1,0:T(8,128)(2,1)} %copy-done.7, bf16[9,64,64]{2,1,0:T(8,128)(2,1)} %w_ref.5), custom_call_target="tpu_custom_call" | custom-call | flops 1000 | bytes 1000 | tf_op jit(solution)/shard_map/conv_forward/pallas_call | solution.py:111
  31.6 3.4 %collective-permute-start.6 = (bf16[1,4,64,1024]{3,2,1,0:T(8,128)(2,1)}, bf16[1,4,64,1024]{3,2,1,0:T(8,128)(2,1)S(1)}, u32[]{:S(2)}, u32[]{:S(2)}) collective-permute-start(bf16[1,4,64,1024]{3,2,1,0:T(8,128)(2,1)} %get-tuple-element.63.rest_1_), channel_id=1, source_target_pairs={{0,8},{8,16},{12,4},{16,24},{20,12},{28,20},{1,9},{9,17},{13,5},{1... | collective-permute-start | bytes 1572872 | tf_op jit(solution)/shard_map/ppermute | solution.py:525
  35.0 1.3 %collective-permute-start.7 = (bf16[1,2,64,1024]{3,2,1,0:T(8,128)(2,1)}, bf16[1,2,64,1024]{3,2,1,0:T(8,128)(2,1)S(1)}, u32[]{:S(2)}, u32[]{:S(2)}) collective-permute-start(bf16[1,2,64,1024]{3,2,1,0:T(8,128)(2,1)} %get-tuple-element.64), channel_id=1, source_target_pairs={{4,12},{8,0},{12,20},{16,8},{20,28},{24,16},{5,13},{9,1},{13,21},{... | collective-permute-start | bytes 786440 | tf_op jit(solution)/shard_map/ppermute | solution.py:525
  36.3 0.0 collective-permute-done.3.x_ref
  36.3 5.8 %collective-permute-done.rest_2_ = bf16[2,4,64,1024]{3,2,1,0:T(8,128)(2,1)S(1)} collective-permute-done((bf16[2,4,64,1024]{3,2,1,0:T(8,128)(2,1)}, bf16[2,4,64,1024]{3,2,1,0:T(8,128)(2,1)S(1)}, u32[]{:S(2)}, u32[]{:S(2)}) %collective-permute-start) | collective-permute-done | bytes 1048608 | tf_op jit(solution)/shard_map/ppermute | solution.py:525
  42.1 0.0 collective-permute-done.2.rest_3_
  42.1 4.0 %conv_forward.4 = (bf16[1,4,64,1024]{3,2,1,0:T(8,128)(2,1)}, bf16[1,4,64,1024]{3,2,1,0:T(8,128)(2,1)}, bf16[1,4,64,1024]{3,2,1,0:T(8,128)(2,1)}, bf16[1,2,64,1024]{3,2,1,0:T(8,128)(2,1)}) custom-call(s32[22]{0:T(128)} %fusion.3.meta_ref, bf16[4,64,1,8,128]{4,3,2,1,0:T(8,128)(2,1)} %copy-done.6, bf16[9,64,64]{2,1,0:T(8,128)(2,1)} %w_ref.5), custom_call_target="tpu_custom_call" | custom-call | flops 1000 | bytes 1000 | tf_op jit(solution)/shard_map/conv_forward/pallas_call | solution.py:111
  46.1 4.3 %collective-permute-start.4 = (bf16[1,4,64,1024]{3,2,1,0:T(8,128)(2,1)}, bf16[1,4,64,1024]{3,2,1,0:T(8,128)(2,1)}, u32[]{:S(2)}, u32[]{:S(2)}) collective-permute-start(bf16[1,4,64,1024]{3,2,1,0:T(8,128)(2,1)} %get-tuple-element.73.rest_1_), channel_id=1, source_target_pairs={{0,8},{8,16},{12,4},{16,24},{20,12},{28,20},{1,9},{9,17},{13,5},{1... | collective-permute-start | bytes 1572872 | tf_op jit(solution)/shard_map/ppermute | solution.py:525
  50.5 0.1 copy.19
  50.6 0.1 copy.21.wt_ref
  50.7 0.1 pad_dynamic-slice_fusion.weight_ref
  50.8 1.5 %collective-permute-start.5 = (bf16[1,2,64,1024]{3,2,1,0:T(8,128)(2,1)}, bf16[1,2,64,1024]{3,2,1,0:T(8,128)(2,1)S(1)}, u32[]{:S(2)}, u32[]{:S(2)}) collective-permute-start(bf16[1,2,64,1024]{3,2,1,0:T(8,128)(2,1)} %get-tuple-element.59), channel_id=1, source_target_pairs={{4,12},{8,0},{12,20},{16,8},{20,28},{24,16},{5,13},{9,1},{13,21},{... | collective-permute-start | bytes 786440 | tf_op jit(solution)/shard_map/ppermute | solution.py:525
  52.2 0.1 copy.22.wtb_ref
  52.3 0.1 copy.23.whc_ref
  52.4 0.2 copy.20
  52.6 0.2 reshape.44.wb_ref
  52.8 0.0 all-to-all-done
  52.8 0.8 constant_dynamic-slice_fusion.1
  53.6 0.0 collective-permute-done.7.rest_5_
  53.6 0.0 collective-permute-done.6.rest_4_
  53.6 0.8 copy-done.5
  54.5 18.6 %temporal.2 = (f32[14,1,1024]{2,1,0:T(1,128)S(1)}, f32[6,64,192]{2,1,0:T(8,128)S(1)}, bf16[4,64,4,8,128]{4,3,2,1,0:T(8,128)(2,1)}, bf16[1,4,64,8,128]{4,3,2,1,0:T(8,128)(2,1)S(1)}) custom-call(s32[22]{0:T(128)S(1)} %copy-done, f32[14]{0:T(128)S(1)} %pad_dynamic-slice_fusion.weight_ref, bf16[2,64,192]{2,1,0:T(8,128)(2,1)S(1)} %copy.21.wt_ref, ...), custom_call_target="tpu_custom_call" | custom-call | flops 1572864000 | bytes 52428800 | tf_op jit(solution)/shard_map/temporal/pallas_call | solution.py:418
  73.1 0.0 collective-permute-done.5.rest_5_
  73.1 0.0 collective-permute-done.4.rest_4_
  73.1 1.1 collective-permute-start.8
  74.2 0.1 fusion.1
  74.2 19.0 %temporal.3 = (f32[14,1,1024]{2,1,0:T(1,128)S(1)}, f32[16,64,64]{2,1,0:T(8,128)S(1)}, bf16[4,64,4,8,128]{4,3,2,1,0:T(8,128)(2,1)}, bf16[1,4,64,8,128]{4,3,2,1,0:T(8,128)(2,1)}) custom-call(s32[22]{0:T(128)S(1)} %copy-done, f32[14]{0:T(128)S(1)} %pad_dynamic-slice_fusion.weight_ref, ...), custom_call_target="tpu_custom_call", output_to_operand_aliasing={{2}: (18, {})} | custom-call | flops 1572864000 | bytes 52428800 | tf_op jit(solution)/shard_map/temporal/pallas_call | solution.py:418
  93.2 1.1 collective-permute-start.15
  94.3 0.1 fusion
  94.4 0.0 collective-permute-done.8
  94.5 0.1 collective-permute-start.11
  94.5 1.6 %collective-permute-start.10 = (bf16[16,16,64]{2,1,0:T(8,128)(2,1)S(1)}, bf16[16,16,64]{2,1,0:T(8,128)(2,1)S(1)}, u32[]{:S(2)}, u32[]{:S(2)}) collective-permute-start(bf16[16,16,64]{2,1,0:T(8,128)(2,1)S(1)} %get-tuple-element.99), channel_id=1, source_target_pairs={{0,2},{1,3},{2,0},{3,1},{4,6},{5,7},{6,4},{7,5},{8,10},{9,11},{10,... | collective-permute-start | bytes 98312 | tf_op jit(solution)/shard_map/ppermute | solution.py:501
  96.1 0.2 collective-permute-start.9
  96.3 0.2 collective-permute-done.11
  96.4 3.8 %collective-permute-done.10 = bf16[16,16,64]{2,1,0:T(8,128)(2,1)S(1)} collective-permute-done((bf16[16,16,64]{2,1,0:T(8,128)(2,1)S(1)}, bf16[16,16,64]{2,1,0:T(8,128)(2,1)S(1)}, u32[]{:S(2)}, u32[]{:S(2)}) %collective-permute-start.10) | collective-permute-done | bytes 32800 | tf_op jit(solution)/shard_map/ppermute | solution.py:501
  100.2 0.2 collective-permute-done.9
  100.4 2.5 %collective-permute-start.14 = (bf16[16,16,64]{2,1,0:T(8,128)(2,1)S(1)}, bf16[16,16,64]{2,1,0:T(8,128)(2,1)S(1)}, u32[]{:S(2)}, u32[]{:S(2)}) collective-permute-start(bf16[16,16,64]{2,1,0:T(8,128)(2,1)S(1)} %fusion.2), channel_id=1, source_target_pairs={{0,24},{4,28},{8,16},{12,20},{16,8},{20,12},{24,0},{28,4},{1,25},{... | collective-permute-start | bytes 98312 | tf_op jit(solution)/shard_map/ppermute | solution.py:483
  102.9 1.6 %collective-permute-start.13 = (bf16[16,16,64]{2,1,0:T(8,128)(2,1)S(1)}, bf16[16,16,64]{2,1,0:T(8,128)(2,1)S(1)}, u32[]{:S(2)}, u32[]{:S(2)}) collective-permute-start(bf16[16,16,64]{2,1,0:T(8,128)(2,1)S(1)} %fusion.2), channel_id=1, source_target_pairs={{0,16},{4,20},{8,24},{12,28},{16,0},{20,4},{24,8},{28,12},{1,17},{... | collective-permute-start | bytes 98312 | tf_op jit(solution)/shard_map/ppermute | solution.py:483
  104.6 0.3 collective-permute-start.12
  104.9 0.6 pad_maximum_fusion
  105.5 4.4 %all-to-all-start.1 = ((bf16[8,8,512]{2,1,0:T(8,128)(2,1)}), bf16[8,8,512]{2,1,0:T(8,128)(2,1)S(1)}, u32[]{:S(2)}, u32[]{:S(2)}) async-start(bf16[8,8,512]{2,1,0:T(8,128)(2,1)} %pad_maximum_fusion), calls=%async_computation.1 | async-start | bytes 131072 | tf_op jit(solution)/shard_map/all_to_all | solution.py:652
  109.9 0.0 collective-permute-done.14
  109.9 0.0 collective-permute-done.13
  109.9 0.0 collective-permute-done.12
  109.9 0.1 convert_add_fusion.value_ref
  110.0 0.0 collective-permute-done.15
  110.1 2.1 %collective-permute-start.16 = (bf16[16,16,64]{2,1,0:T(8,128)(2,1)S(1)}, bf16[16,16,64]{2,1,0:T(8,128)(2,1)S(1)}, u32[]{:S(2)}, u32[]{:S(2)}) collective-permute-start(bf16[16,16,64]{2,1,0:T(8,128)(2,1)S(1)} %convert_element_type.69), channel_id=1, source_target_pairs={{0,4},{4,0},{8,12},{12,8},{16,20},{20,16},{24,28},{28,24},{1,5},{5... | collective-permute-start | bytes 98312 | tf_op jit(solution)/shard_map/ppermute | solution.py:483
  112.1 0.8 bitcast_dynamic-update-slice_fusion.1
  113.0 0.8 bitcast_dynamic-update-slice_fusion
  113.8 3.0 %all-to-all-done.1.rest_1_ = bf16[8,8,512]{2,1,0:T(8,128)(2,1)S(1)} async-done(((bf16[8,8,512]{2,1,0:T(8,128)(2,1)}), bf16[8,8,512]{2,1,0:T(8,128)(2,1)S(1)}, u32[]{:S(2)}, u32[]{:S(2)}) %all-to-all-start.1) | async-done | bytes 65568 | tf_op jit(solution)/shard_map/all_to_all | solution.py:652
  116.8 0.6 copy-done.8
  117.5 0.6 copy-done.10
  118.1 1.6 %finish.1 = (bf16[4,8,512]{2,1,0:T(8,128)(2,1)}, f32[9,16,64]{2,1,0:T(8,128)}, f32[2,3,16,64]{3,2,1,0:T(8,128)}, f32[1,16]{1,0:T(1,128)}) custom-call(f32[16,16,64]{2,1,0:T(8,128)} %copy-done.4, bf16[16,16,64]{2,1,0:T(8,128)(2,1)} %copy-done.10, bf16[8,8,512]{2,1,0:T(8,128)(2,1)} %copy-done.8), custom_call_target="tpu_custom_call" | custom-call | flops 1000 | bytes 1000 | tf_op jit(solution)/shard_map/finish/pallas_call | solution.py:190
  (32 shorter events, 0.2 us)
Async XLA Ops:
  0.7 26.8 %copy-start.9 = (bf16[2,3,64,64]{3,2,1,0:T(8,128)(2,1)S(1)}, bf16[2,3,64,64]{3,2,1,0:T(8,128)(2,1)}, u32[]{:S(2)}) copy-start(bf16[2,3,64,64]{3,2,1,0:T(8,128)(2,1)} %param.9) | copy-start | bytes 147460
  0.7 26.8 %copy-start.2 = (bf16[9,64,64]{2,1,0:T(8,128)(2,1)S(1)}, bf16[9,64,64]{2,1,0:T(8,128)(2,1)}, u32[]{:S(2)}) copy-start(bf16[9,64,64]{2,1,0:T(8,128)(2,1)} %w_ref.5) | copy-start | bytes 221188
  2.8 32.2 %copy-start.11 = (s32[1,32]{1,0:T(1,128)S(1)}, s32[1,32]{1,0:T(1,128)}, u32[]{:S(2)}) copy-start(s32[1,32]{1,0:T(1,128)} %param.12) | copy-start | bytes 388
  2.8 20.6 %collective-permute-start.1 = (bf16[4,64,1,8,128]{4,3,2,1,0:T(8,128)(2,1)S(1)}, bf16[4,64,1,8,128]{4,3,2,1,0:T(8,128)(2,1)S(1)}, u32[]{:S(2)}, u32[]{:S(2)}) collective-permute-start(bf16[4,64,1,8,128]{4,3,2,1,0:T(8,128)(2,1)S(1)} %get-tuple-element.96), channel_id=1, source_target_pairs={{0,4},{4,0},{8,12},{12,8},{16,20},{20,16},{24,28},{28,24},{1,5},{5... | collective-permute-start | bytes 1572872 | tf_op jit(solution)/shard_map/ppermute | solution.py:521
  7.0 43.5 %copy-start.12 = (bf16[64]{0:T(256)(128)(2,1)S(1)}, bf16[64]{0:T(256)(128)(2,1)}, u32[]{:S(2)}) copy-start(bf16[64]{0:T(256)(128)(2,1)} %param.10) | copy-start | bytes 388
  13.1 41.4 %copy-start = (s32[22]{0:T(128)S(1)}, s32[22]{0:T(128)}, u32[]{:S(2)}) copy-start(s32[22]{0:T(128)} %fusion.3.meta_ref) | copy-start | bytes 268
  13.1 29.0 %collective-permute-start = (bf16[2,4,64,1024]{3,2,1,0:T(8,128)(2,1)}, bf16[2,4,64,1024]{3,2,1,0:T(8,128)(2,1)S(1)}, u32[]{:S(2)}, u32[]{:S(2)}) collective-permute-start(bf16[2,4,64,1024]{3,2,1,0:T(8,128)(2,1)} %get-tuple-element.72.rest_0_), channel_id=1, source_target_pairs={{4,12},{8,0},{12,20},{16,8},{20,28},{24,16},{5,13},{9,1},{13,21},{... | collective-permute-start | bytes 3145736 | tf_op jit(solution)/shard_map/ppermute | solution.py:525
  14.5 21.8 %collective-permute-start.3 = (bf16[4,64,1,8,128]{4,3,2,1,0:T(8,128)(2,1)}, bf16[4,64,1,8,128]{4,3,2,1,0:T(8,128)(2,1)S(1)}, u32[]{:S(2)}, u32[]{:S(2)}) collective-permute-start(bf16[4,64,1,8,128]{4,3,2,1,0:T(8,128)(2,1)} %get-tuple-element.54), channel_id=1, source_target_pairs={{0,4},{4,0},{8,12},{12,8},{16,20},{20,16},{24,28},{28,24},{1,5},{5... | collective-permute-start | bytes 1572872 | tf_op jit(solution)/shard_map/ppermute | solution.py:521
  18.7 34.0 %all-to-all-start = ((bf16[8,16,512]{2,1,0:T(8,128)(2,1)}), bf16[8,16,512]{2,1,0:T(8,128)(2,1)}, u32[]{:S(2)}, u32[]{:S(2)}) async-start(bf16[8,16,512]{2,1,0:T(8,128)(2,1)} %windows.1), calls=%async_computation | async-start | bytes 262144 | tf_op jit(solution)/shard_map/all_to_all | solution.py:616
  23.5 4.1 %copy-start.7 = (bf16[4,64,1,8,128]{4,3,2,1,0:T(8,128)(2,1)}, bf16[4,64,1,8,128]{4,3,2,1,0:T(8,128)(2,1)S(1)}, u32[]{:S(2)}) copy-start(bf16[4,64,1,8,128]{4,3,2,1,0:T(8,128)(2,1)S(1)} %collective-permute-done.1.x_ref) | copy-start | bytes 1572868
  23.5 18.6 %collective-permute-start.2 = (bf16[2,2,64,1024]{3,2,1,0:T(8,128)(2,1)}, bf16[2,2,64,1024]{3,2,1,0:T(8,128)(2,1)S(1)}, u32[]{:S(2)}, u32[]{:S(2)}) collective-permute-start(bf16[2,2,64,1024]{3,2,1,0:T(8,128)(2,1)} %get-tuple-element.52), channel_id=1, source_target_pairs={{0,8},{8,16},{12,4},{16,24},{20,12},{28,20},{1,9},{9,17},{13,5},{1... | collective-permute-start | bytes 1572872 | tf_op jit(solution)/shard_map/ppermute | solution.py:525
  31.6 22.0 %collective-permute-start.6 = (bf16[1,4,64,1024]{3,2,1,0:T(8,128)(2,1)}, bf16[1,4,64,1024]{3,2,1,0:T(8,128)(2,1)S(1)}, u32[]{:S(2)}, u32[]{:S(2)}) collective-permute-start(bf16[1,4,64,1024]{3,2,1,0:T(8,128)(2,1)} %get-tuple-element.63.rest_1_), channel_id=1, source_target_pairs={{0,8},{8,16},{12,4},{16,24},{20,12},{28,20},{1,9},{9,17},{13,5},{1... | collective-permute-start | bytes 1572872 | tf_op jit(solution)/shard_map/ppermute | solution.py:525
  35.0 18.6 %collective-permute-start.7 = (bf16[1,2,64,1024]{3,2,1,0:T(8,128)(2,1)}, bf16[1,2,64,1024]{3,2,1,0:T(8,128)(2,1)S(1)}, u32[]{:S(2)}, u32[]{:S(2)}) collective-permute-start(bf16[1,2,64,1024]{3,2,1,0:T(8,128)(2,1)} %get-tuple-element.64), channel_id=1, source_target_pairs={{4,12},{8,0},{12,20},{16,8},{20,28},{24,16},{5,13},{9,1},{13,21},{... | collective-permute-start | bytes 786440 | tf_op jit(solution)/shard_map/ppermute | solution.py:525
  36.3 5.8 %copy-start.6 = (bf16[4,64,1,8,128]{4,3,2,1,0:T(8,128)(2,1)}, bf16[4,64,1,8,128]{4,3,2,1,0:T(8,128)(2,1)S(1)}, u32[]{:S(2)}) copy-start(bf16[4,64,1,8,128]{4,3,2,1,0:T(8,128)(2,1)S(1)} %collective-permute-done.3.x_ref) | copy-start | bytes 1572868
  42.1 12.4 %copy-start.1 = (bf16[2,4,64,1024]{3,2,1,0:T(8,128)(2,1)}, bf16[2,4,64,1024]{3,2,1,0:T(8,128)(2,1)S(1)}, u32[]{:S(2)}) copy-start(bf16[2,4,64,1024]{3,2,1,0:T(8,128)(2,1)S(1)} %collective-permute-done.rest_2_) | copy-start | bytes 3145732
  42.1 12.4 %copy-start.3 = (bf16[2,2,64,1024]{3,2,1,0:T(8,128)(2,1)}, bf16[2,2,64,1024]{3,2,1,0:T(8,128)(2,1)S(1)}, u32[]{:S(2)}) copy-start(bf16[2,2,64,1024]{3,2,1,0:T(8,128)(2,1)S(1)} %collective-permute-done.2.rest_3_) | copy-start | bytes 1572868
  46.1 26.9 %collective-permute-start.4 = (bf16[1,4,64,1024]{3,2,1,0:T(8,128)(2,1)}, bf16[1,4,64,1024]{3,2,1,0:T(8,128)(2,1)}, u32[]{:S(2)}, u32[]{:S(2)}) collective-permute-start(bf16[1,4,64,1024]{3,2,1,0:T(8,128)(2,1)} %get-tuple-element.73.rest_1_), channel_id=1, source_target_pairs={{0,8},{8,16},{12,4},{16,24},{20,12},{28,20},{1,9},{9,17},{13,5},{1... | collective-permute-start | bytes 1572872 | tf_op jit(solution)/shard_map/ppermute | solution.py:525
  50.8 22.3 %collective-permute-start.5 = (bf16[1,2,64,1024]{3,2,1,0:T(8,128)(2,1)}, bf16[1,2,64,1024]{3,2,1,0:T(8,128)(2,1)S(1)}, u32[]{:S(2)}, u32[]{:S(2)}) collective-permute-start(bf16[1,2,64,1024]{3,2,1,0:T(8,128)(2,1)} %get-tuple-element.59), channel_id=1, source_target_pairs={{4,12},{8,0},{12,20},{16,8},{20,28},{24,16},{5,13},{9,1},{13,21},{... | collective-permute-start | bytes 786440 | tf_op jit(solution)/shard_map/ppermute | solution.py:525
  53.6 0.8 copy-start.5
  73.1 21.3 %collective-permute-start.8 = (bf16[4,64,1,8,128]{4,3,1,0,2:T(8,128)(2,1)S(1)}, bf16[4,64,1,8,128]{4,3,1,0,2:T(8,128)(2,1)S(1)}, u32[]{:S(2)}, u32[]{:S(2)}) collective-permute-start(bf16[4,64,1,8,128]{4,3,1,0,2:T(8,128)(2,1)S(1)} %bitcast.35), channel_id=1, source_target_pairs={{0,4},{4,0},{8,12},{12,8},{16,20},{20,16},{24,28},{28,24},{1,5},{5... | collective-permute-start | bytes 1572872 | tf_op jit(solution)/shard_map/ppermute | solution.py:521
  93.2 16.8 %collective-permute-start.15 = (bf16[4,64,1,8,128]{4,3,1,0,2:T(8,128)(2,1)}, bf16[4,64,1,8,128]{4,3,1,0,2:T(8,128)(2,1)S(1)}, u32[]{:S(2)}, u32[]{:S(2)}) collective-permute-start(bf16[4,64,1,8,128]{4,3,1,0,2:T(8,128)(2,1)} %bitcast.44), channel_id=1, source_target_pairs={{0,4},{4,0},{8,12},{12,8},{16,20},{20,16},{24,28},{28,24},{1,5},{5... | collective-permute-start | bytes 1572872 | tf_op jit(solution)/shard_map/ppermute | solution.py:521
  94.5 2.0 %collective-permute-start.11 = (bf16[16,16,64]{2,1,0:T(8,128)(2,1)S(1)}, bf16[16,16,64]{2,1,0:T(8,128)(2,1)S(1)}, u32[]{:S(2)}, u32[]{:S(2)}) collective-permute-start(bf16[16,16,64]{2,1,0:T(8,128)(2,1)S(1)} %get-tuple-element.98), channel_id=1, source_target_pairs={{0,3},{1,0},{2,1},{3,2},{4,7},{5,4},{6,5},{7,6},{8,11},{9,8},{10,9... | collective-permute-start | bytes 98312 | tf_op jit(solution)/shard_map/ppermute | solution.py:501
  94.5 5.6 %collective-permute-start.10 = (bf16[16,16,64]{2,1,0:T(8,128)(2,1)S(1)}, bf16[16,16,64]{2,1,0:T(8,128)(2,1)S(1)}, u32[]{:S(2)}, u32[]{:S(2)}) collective-permute-start(bf16[16,16,64]{2,1,0:T(8,128)(2,1)S(1)} %get-tuple-element.99), channel_id=1, source_target_pairs={{0,2},{1,3},{2,0},{3,1},{4,6},{5,7},{6,4},{7,5},{8,10},{9,11},{10,... | collective-permute-start | bytes 98312 | tf_op jit(solution)/shard_map/ppermute | solution.py:501
  96.1 4.3 %collective-permute-start.9 = (bf16[16,16,64]{2,1,0:T(8,128)(2,1)S(1)}, bf16[16,16,64]{2,1,0:T(8,128)(2,1)S(1)}, u32[]{:S(2)}, u32[]{:S(2)}) collective-permute-start(bf16[16,16,64]{2,1,0:T(8,128)(2,1)S(1)} %get-tuple-element.97), channel_id=1, source_target_pairs={{0,1},{1,2},{2,3},{3,0},{4,5},{5,6},{6,7},{7,4},{8,9},{9,10},{10,1... | collective-permute-start | bytes 98312 | tf_op jit(solution)/shard_map/ppermute | solution.py:501
  100.4 9.5 %collective-permute-start.14 = (bf16[16,16,64]{2,1,0:T(8,128)(2,1)S(1)}, bf16[16,16,64]{2,1,0:T(8,128)(2,1)S(1)}, u32[]{:S(2)}, u32[]{:S(2)}) collective-permute-start(bf16[16,16,64]{2,1,0:T(8,128)(2,1)S(1)} %fusion.2), channel_id=1, source_target_pairs={{0,24},{4,28},{8,16},{12,20},{16,8},{20,12},{24,0},{28,4},{1,25},{... | collective-permute-start | bytes 98312 | tf_op jit(solution)/shard_map/ppermute | solution.py:483
  102.9 7.0 %collective-permute-start.13 = (bf16[16,16,64]{2,1,0:T(8,128)(2,1)S(1)}, bf16[16,16,64]{2,1,0:T(8,128)(2,1)S(1)}, u32[]{:S(2)}, u32[]{:S(2)}) collective-permute-start(bf16[16,16,64]{2,1,0:T(8,128)(2,1)S(1)} %fusion.2), channel_id=1, source_target_pairs={{0,16},{4,20},{8,24},{12,28},{16,0},{20,4},{24,8},{28,12},{1,17},{... | collective-permute-start | bytes 98312 | tf_op jit(solution)/shard_map/ppermute | solution.py:483
  104.6 5.4 %collective-permute-start.12 = (bf16[16,16,64]{2,1,0:T(8,128)(2,1)S(1)}, bf16[16,16,64]{2,1,0:T(8,128)(2,1)S(1)}, u32[]{:S(2)}, u32[]{:S(2)}) collective-permute-start(bf16[16,16,64]{2,1,0:T(8,128)(2,1)S(1)} %fusion.2), channel_id=1, source_target_pairs={{0,8},{4,12},{8,0},{12,4},{16,24},{20,28},{24,16},{28,20},{1,9},{5... | collective-permute-start | bytes 98312 | tf_op jit(solution)/shard_map/ppermute | solution.py:483
  105.5 11.3 %all-to-all-start.1 = ((bf16[8,8,512]{2,1,0:T(8,128)(2,1)}), bf16[8,8,512]{2,1,0:T(8,128)(2,1)S(1)}, u32[]{:S(2)}, u32[]{:S(2)}) async-start(bf16[8,8,512]{2,1,0:T(8,128)(2,1)} %pad_maximum_fusion), calls=%async_computation.1 | async-start | bytes 131072 | tf_op jit(solution)/shard_map/all_to_all | solution.py:652
  110.0 6.8 %copy-start.4 = (f32[16,16,64]{2,1,0:T(8,128)}, f32[16,16,64]{2,1,0:T(8,128)S(1)}, u32[]{:S(2)}) copy-start(f32[16,16,64]{2,1,0:T(8,128)S(1)} %convert_add_fusion.value_ref) | copy-start | bytes 196612
  110.1 6.8 %collective-permute-start.16 = (bf16[16,16,64]{2,1,0:T(8,128)(2,1)S(1)}, bf16[16,16,64]{2,1,0:T(8,128)(2,1)S(1)}, u32[]{:S(2)}, u32[]{:S(2)}) collective-permute-start(bf16[16,16,64]{2,1,0:T(8,128)(2,1)S(1)} %convert_element_type.69), channel_id=1, source_target_pairs={{0,4},{4,0},{8,12},{12,8},{16,20},{20,16},{24,28},{28,24},{1,5},{5... | collective-permute-start | bytes 98312 | tf_op jit(solution)/shard_map/ppermute | solution.py:483
  116.8 0.6 copy-start.8
  117.5 0.6 copy-start.10

commit v9 on v8

--- a/solution.py
+++ b/solution.py
@@ -66,7 +66,7 @@
     return result
 
 
-def forward_kernel(middle, base, meta_ref, x_ref, w_ref, feat_ref, slope_ref, xc_ref, *rest):
+def forward_kernel(middle, block, x_ref, w_ref, feat_ref, slope_ref, xc_ref, *rest):
     xt, xs, wf = rest[-3:]
     frames, chans, _, rows, width = x_ref.shape
 
@@ -93,34 +93,33 @@
             slope_ref[0, n, :, cols] = slope.astype(BF16)
     if middle:
 
-        @pl.when(pl.program_id(1) == meta_ref[base + 1])
+        @pl.when(pl.program_id(1) == block())
         def _():
             rest[0][0] = feat_ref[0]
 
 
-def run_forward(meta, base, middle, count, x, w_spatial):
+def run_forward(first, block, middle, count, x, w_spatial):
     n, chans, _, rows, width = x.shape
     vox = rows * width
     sds = jax.ShapeDtypeStruct
     frames = middle if middle and n % middle == 0 else 2 - n % 2
     shapes = [sds((count, n, chans, vox), BF16)] * 3
-    specs = [pl.BlockSpec((1, frames, chans, vox), lambda k, f, meta: (k, f, 0, 0))] * 3
+    specs = [pl.BlockSpec((1, frames, chans, vox), lambda k, f: (k, f, 0, 0))] * 3
     if middle:
         shapes.append(sds((count, middle, chans, vox), BF16))
-        specs.append(pl.BlockSpec((1, middle, chans, vox), lambda k, f, meta: (k, 0, 0, 0)))
+        specs.append(pl.BlockSpec((1, middle, chans, vox), lambda k, f: (k, 0, 0, 0)))
     return pl.pallas_call(
-        functools.partial(forward_kernel, middle, base),
+        functools.partial(forward_kernel, middle, block),
         name="conv_forward",
         out_shape=shapes,
-        grid_spec=pltpu.PrefetchScalarGridSpec(
-            num_scalar_prefetch=1,
+        grid_spec=pl.GridSpec(
             grid=(count, n // frames),
             in_specs=[
                 pl.BlockSpec(
                     (frames, chans, 1, rows, width),
-                    lambda k, f, meta: (f, 0, meta[base] + k, 0, 0),
+                    lambda k, f: (f, 0, first() + k, 0, 0),
                 ),
-                pl.BlockSpec((9, chans, chans), lambda k, f, meta: (0, 0, 0)),
+                pl.BlockSpec((9, chans, chans), lambda k, f: (0, 0, 0)),
             ],
             out_specs=specs,
             scratch_shapes=[
@@ -130,7 +129,7 @@
             ],
         ),
         cost_estimate=pl.CostEstimate(flops=1000, bytes_accessed=1000, transcendentals=0),
-    )(meta, x, w_spatial)
+    )(x, w_spatial)
 
 
 def window_kernel(own, g, tgt_ref, win_ref, pad):
@@ -550,16 +549,13 @@
                 spots += [left - k, HALO + d * own]
                 left -= k
                 d += 1
-        late = (here - extra) // max(extra, 1)
         row = []
 
         def put(name, *values):
             slots[name] = len(row)
             row.extend(values)
 
-        put("mine", am * per, late if am == 0 else 0)
         for layer in range(per):
-            put(("theirs", layer), 0, late if am == 1 else 0)
             put(("temporal", layer), aq * own, *spots, am * per + layer)
         table.append(row)
     meta = lax.dynamic_index_in_dim(jnp.asarray(np.array(table, np.int32)), t, 0, False)
@@ -569,7 +565,13 @@
         for layer in range(per)
     ]
     arriving = [[swap(piece, s + 1) for s, piece in enumerate(leaving[0])]]
-    mine = list(run_forward(meta, slots["mine"], extra, per, x, w_spatial))
+    def member():
+        return lax.rem(lax.axis_index("tile"), g)
+
+    def last_if(k):
+        return lambda: jnp.where(member() == k, (here - extra) // max(extra, 1), 0)
+
+    mine = list(run_forward(lambda: member() * per, last_if(0), extra, per, x, w_spatial))
     leaving[1:], mine[1] = lax.optimization_barrier((leaving[1:], mine[1]))
     for pieces in leaving[1:]:
         arriving.append([swap(piece, s + 1) for s, piece in enumerate(pieces)])
@@ -586,16 +588,18 @@
     ready = []
     for layer in range(per):
         done = [mine]
-        if layer:
-            ahead, arriving[layer] = lax.optimization_barrier((ahead, arriving[layer]))
         for piece in arriving[layer]:
-            done.append(list(run_forward(meta, slots["theirs", layer], extra, 1, piece, w_spatial)))
+            done.append(list(run_forward(lambda: 0, last_if(1), extra, 1, piece, w_spatial)))
         pieces = [d[0] for d in done]
         ranks = [layer] + [0] * (g - 1)
         if mirrored:
-            pieces += ahead
-            pieces.append(hop(done[1][0], (1, -1)))
+            if layer:
+                ahead, done[1][0] = lax.optimization_barrier((ahead, done[1][0]))
+            pieces += [*ahead, hop(done[1][0], (1, -1))]
             if extra:
+                if layer:
+                    before = ready[-1][1]
+                    before[-1], done[1][3] = lax.optimization_barrier((before[-1], done[1][3]))
                 pieces.append(hop(done[1][3], (-1, 1)))
             for k in range(2):
                 ranks += [0 if k else layer] * len(ahead)

time: 120 us -> 116 us (0.967)
  waiting for transfers between devices: 12.9 us -> 10.4 us
  Pallas kernels: 54.8 us -> 52.7 us
  starting transfers between devices: 41.2 us -> 43.2 us
  local copies, waits for them, and re-layouts: 8.97 us -> 7.67 us
    ppermute x6, waiting for transfers between devices: 5.78 us -> 3.26 us  [hop(): return lax.ppermute(value, 'tile', [p for p in pairs if 0 <= p[1] < tiles])]
    pallas_call x3, Pallas kernels: 14.2 us -> 12 us  [run_forward(): pl.pallas_call(functools.partial(forward_kernel, middle, block), name='co...]
  transfers between devices with their start and end apart: 19 -> 19, of which waited for: 5 -> 7; matrix products, arithmetic and copies ran while one was open for 5% -> 4% of each run, Pallas kernels for 44% -> 44%
where the time goes in v9:
time: 116 us
  Pallas kernels  52.7 us (45%)
  starting transfers between devices  43.2 us (37%)
  waiting for transfers between devices  10.4 us (9%)
  local copies, waits for them, and re-layouts  7.67 us (7%)
    pallas_call x2, Pallas kernels, run_temporal(): pl.pallas_call(functools.partial(temporal_kernel, tuple(places), last, al...  37.6 us
    ppermute x6, starting transfers between devices, hop(): return lax.ppermute(value, 'tile', [p for p in pairs if 0 <= p[1] < tiles])  16.7 us
    pallas_call x3, Pallas kernels, run_forward(): pl.pallas_call(functools.partial(forward_kernel, middle, block), name='co...  12 us
    ppermute x4, starting transfers between devices, swap(): return lax.ppermute(value, 'tile', pairs)  8.82 us
    ppermute x4, starting transfers between devices, sum_over_tiles(): arrived.append(lax.ppermute(sent, 'tile', pairs))  6.53 us
    all_to_all x1, starting transfers between devices, body(): windows = lax.all_to_all(windows, 'tile', 0, 0, tiled=True)  4.72 us
    all_to_all x1, starting transfers between devices, body(): logits = lax.all_to_all(logits, 'tile', 0, 0, tiled=True)  4.67 us
    ppermute x3, waiting for transfers between devices, sum_over_reps(): lax.ppermute(share(r + s).astype(BF16), 'rep', pairs).astype(F32)  4.1 us
  transfers between devices with their start and end apart: 19, of which 7 were waited for; matrix products, arithmetic and copies ran while one was open for 4% of the time, Pallas kernels for 44%

profile of v9, /device:TPU:0, one launch (start us, length us, event | category | flops | bytes accessed | tf_op | source)
XLA Modules:
  0.0 115.8 jit_solution(16609355078279592957)
XLA Ops:
  0.7 2.2 %dynamic-slice_bitcast_fusion = (bf16[4,64,1,8,128]{4,3,2,1,0:T(8,128)(2,1)S(1)}, bf16[4,64,1,8,128]{4,3,2,1,0:T(8,128)(2,1)}) fusion(bf16[1,4,64,4,8,128]{5,4,3,2,1,0:T(8,128)(2,1)} %param.7, s32[]{:T(128)S(6)} %select_n.70, s32[]{:T(128)S(6)} %select_n.69), kind=kLoop, calls=%fused_computation.2 | loop fusion | bytes 2097160 | tf_op jit(solution)/shard_map/dynamic_slice | solution.py:564
  2.9 3.0 %collective-permute-start.2 = (bf16[4,64,1,8,128]{4,3,2,1,0:T(8,128)(2,1)S(1)}, bf16[4,64,1,8,128]{4,3,2,1,0:T(8,128)(2,1)S(1)}, u32[]{:S(2)}, u32[]{:S(2)}) collective-permute-start(bf16[4,64,1,8,128]{4,3,2,1,0:T(8,128)(2,1)S(1)} %get-tuple-element.99), channel_id=1, source_target_pairs={{0,4},{4,0},{8,12},{12,8},{16,20},{20,16},{24,28},{28,24},{1,5},{5... | collective-permute-start | bytes 1572872 | tf_op jit(solution)/shard_map/ppermute | solution.py:520
  5.8 5.3 %conv_forward.3 = (bf16[2,4,64,1024]{3,2,1,0:T(8,128)(2,1)}, bf16[2,4,64,1024]{3,2,1,0:T(8,128)(2,1)}, bf16[2,4,64,1024]{3,2,1,0:T(8,128)(2,1)}, bf16[2,2,64,1024]{3,2,1,0:T(8,128)(2,1)}) custom-call(bf16[4,64,4,8,128]{4,3,2,1,0:T(8,128)(2,1)} %bitcast.36, bf16[9,64,64]{2,1,0:T(8,128)(2,1)} %w_ref.5), custom_call_target="tpu_custom_call" | custom-call | flops 1000 | bytes 1000 | tf_op jit(solution)/shard_map/conv_forward/pallas_call | solution.py:111
  11.2 1.3 %collective-permute-start.1 = (bf16[2,4,64,1024]{3,2,1,0:T(8,128)(2,1)}, bf16[2,4,64,1024]{3,2,1,0:T(8,128)(2,1)S(1)}, u32[]{:S(2)}, u32[]{:S(2)}) collective-permute-start(bf16[2,4,64,1024]{3,2,1,0:T(8,128)(2,1)} %get-tuple-element.76.rest_0_), channel_id=1, source_target_pairs={{4,12},{8,0},{12,20},{16,8},{20,28},{24,16},{5,13},{9,1},{13,21},{... | collective-permute-start | bytes 3145736 | tf_op jit(solution)/shard_map/ppermute | solution.py:524
  12.4 2.8 %collective-permute-start = (bf16[4,64,1,8,128]{4,3,2,1,0:T(8,128)(2,1)}, bf16[4,64,1,8,128]{4,3,2,1,0:T(8,128)(2,1)S(1)}, u32[]{:S(2)}, u32[]{:S(2)}) collective-permute-start(bf16[4,64,1,8,128]{4,3,2,1,0:T(8,128)(2,1)} %get-tuple-element.54), channel_id=1, source_target_pairs={{0,4},{4,0},{8,12},{12,8},{16,20},{20,16},{24,28},{28,24},{1,5},{5... | collective-permute-start | bytes 1572872 | tf_op jit(solution)/shard_map/ppermute | solution.py:520
  15.3 1.4 %windows.1 = bf16[8,16,512]{2,1,0:T(8,128)(2,1)} custom-call(bf16[1,32,512]{2,1,0:T(8,128)(2,1)} %tgt_ref), custom_call_target="tpu_custom_call" | custom-call | flops 1000 | bytes 1000 | tf_op jit(solution)/shard_map/windows/pallas_call | solution.py:148
  16.7 4.7 %all-to-all-start = ((bf16[8,16,512]{2,1,0:T(8,128)(2,1)}), bf16[8,16,512]{2,1,0:T(8,128)(2,1)S(1)}, u32[]{:S(2)}, u32[]{:S(2)}) async-start(bf16[8,16,512]{2,1,0:T(8,128)(2,1)} %windows.1), calls=%async_computation | async-start | bytes 262144 | tf_op jit(solution)/shard_map/all_to_all | solution.py:620
  21.4 0.0 collective-permute-done.2.x_ref
  21.4 0.0 copy-start.5
  21.4 3.9 %collective-permute-start.3 = (bf16[2,2,64,1024]{3,2,1,0:T(8,128)(2,1)}, bf16[2,2,64,1024]{3,2,1,0:T(8,128)(2,1)S(1)}, u32[]{:S(2)}, u32[]{:S(2)}) collective-permute-start(bf16[2,2,64,1024]{3,2,1,0:T(8,128)(2,1)} %get-tuple-element.57), channel_id=1, source_target_pairs={{0,8},{8,16},{12,4},{16,24},{20,12},{28,20},{1,9},{9,17},{13,5},{1... | collective-permute-start | bytes 1572872 | tf_op jit(solution)/shard_map/ppermute | solution.py:524
  25.5 3.3 %conv_forward.5 = (bf16[1,4,64,1024]{3,2,1,0:T(8,128)(2,1)}, bf16[1,4,64,1024]{3,2,1,0:T(8,128)(2,1)}, bf16[1,4,64,1024]{3,2,1,0:T(8,128)(2,1)}, bf16[1,2,64,1024]{3,2,1,0:T(8,128)(2,1)}) custom-call(bf16[4,64,1,8,128]{4,3,2,1,0:T(8,128)(2,1)} %copy-done.5, bf16[9,64,64]{2,1,0:T(8,128)(2,1)} %w_ref.5), custom_call_target="tpu_custom_call" | custom-call | flops 1000 | bytes 1000 | tf_op jit(solution)/shard_map/conv_forward/pallas_call | solution.py:111
  28.8 4.2 %collective-permute-start.7 = (bf16[1,4,64,1024]{3,2,1,0:T(8,128)(2,1)}, bf16[1,4,64,1024]{3,2,1,0:T(8,128)(2,1)}, u32[]{:S(2)}, u32[]{:S(2)}) collective-permute-start(bf16[1,4,64,1024]{3,2,1,0:T(8,128)(2,1)} %get-tuple-element.67.rest_1_), channel_id=1, source_target_pairs={{0,8},{8,16},{12,4},{16,24},{20,12},{28,20},{1,9},{9,17},{13,5},{1... | collective-permute-start | bytes 1572872 | tf_op jit(solution)/shard_map/ppermute | solution.py:524
  33.0 0.7 fusion.3.meta_ref
  33.7 1.3 %collective-permute-start.5 = (bf16[1,2,64,1024]{3,2,1,0:T(8,128)(2,1)}, bf16[1,2,64,1024]{3,2,1,0:T(8,128)(2,1)S(1)}, u32[]{:S(2)}, u32[]{:S(2)}) collective-permute-start(bf16[1,2,64,1024]{3,2,1,0:T(8,128)(2,1)} %get-tuple-element.62), channel_id=1, source_target_pairs={{4,12},{8,0},{12,20},{16,8},{20,28},{24,16},{5,13},{9,1},{13,21},{... | collective-permute-start | bytes 786440 | tf_op jit(solution)/shard_map/ppermute | solution.py:524
  35.0 0.0 collective-permute-done.x_ref
  35.0 0.8 copy-done.4
  35.8 3.3 %conv_forward.4 = (bf16[1,4,64,1024]{3,2,1,0:T(8,128)(2,1)}, bf16[1,4,64,1024]{3,2,1,0:T(8,128)(2,1)}, bf16[1,4,64,1024]{3,2,1,0:T(8,128)(2,1)}, bf16[1,2,64,1024]{3,2,1,0:T(8,128)(2,1)}) custom-call(bf16[4,64,1,8,128]{4,3,2,1,0:T(8,128)(2,1)} %copy-done.4, bf16[9,64,64]{2,1,0:T(8,128)(2,1)} %w_ref.5), custom_call_target="tpu_custom_call" | custom-call | flops 1000 | bytes 1000 | tf_op jit(solution)/shard_map/conv_forward/pallas_call | solution.py:111
  39.1 0.9 collective-permute-done.1.rest_2_
  40.0 0.0 collective-permute-done.3.rest_3_
  40.0 4.5 %collective-permute-start.4 = (bf16[1,4,64,1024]{3,2,1,0:T(8,128)(2,1)}, bf16[1,4,64,1024]{3,2,1,0:T(8,128)(2,1)}, u32[]{:S(2)}, u32[]{:S(2)}) collective-permute-start(bf16[1,4,64,1024]{3,2,1,0:T(8,128)(2,1)} %get-tuple-element.77.rest_1_), channel_id=1, source_target_pairs={{0,8},{8,16},{12,4},{16,24},{20,12},{28,20},{1,9},{9,17},{13,5},{1... | collective-permute-start | bytes 1572872 | tf_op jit(solution)/shard_map/ppermute | solution.py:524
  44.6 0.1 pad_dynamic-slice_fusion.weight_ref
  44.6 0.1 copy.19
  44.8 0.1 copy.21.wt_ref
  44.9 0.7 collective-permute-done.5.rest_5_
  45.6 1.5 %collective-permute-start.6 = (bf16[1,2,64,1024]{3,2,1,0:T(8,128)(2,1)}, bf16[1,2,64,1024]{3,2,1,0:T(8,128)(2,1)S(1)}, u32[]{:S(2)}, u32[]{:S(2)}) collective-permute-start(bf16[1,2,64,1024]{3,2,1,0:T(8,128)(2,1)} %get-tuple-element.64), channel_id=1, source_target_pairs={{4,12},{8,0},{12,20},{16,8},{20,28},{24,16},{5,13},{9,1},{13,21},{... | collective-permute-start | bytes 786440 | tf_op jit(solution)/shard_map/ppermute | solution.py:524
  47.1 0.1 copy.22.wtb_ref
  47.2 0.1 copy.23.whc_ref
  47.3 0.2 copy.20
  47.4 0.2 reshape.44.wb_ref
  47.6 0.0 all-to-all-done
  47.6 1.7 %collective-permute-done.7.rest_4_ = bf16[1,4,64,1024]{3,2,1,0:T(8,128)(2,1)} collective-permute-done((bf16[1,4,64,1024]{3,2,1,0:T(8,128)(2,1)}, bf16[1,4,64,1024]{3,2,1,0:T(8,128)(2,1)}, u32[]{:S(2)}, u32[]{:S(2)}) %collective-permute-start.7) | collective-permute-done | bytes 524320 | tf_op jit(solution)/shard_map/ppermute | solution.py:524
  49.3 18.6 %temporal.2 = (f32[14,1,1024]{2,1,0:T(1,128)S(1)}, f32[6,64,192]{2,1,0:T(8,128)S(1)}, bf16[4,64,4,8,128]{4,3,2,1,0:T(8,128)(2,1)}, bf16[1,4,64,8,128]{4,3,2,1,0:T(8,128)(2,1)S(1)}) custom-call(s32[16]{0:T(128)S(1)} %fusion.3.meta_ref, f32[14]{0:T(128)S(1)} %pad_dynamic-slice_fusion.weight_ref, bf16[2,64,192]{2,1,0:T(8,128)(2,1)S(1)} %copy.21.wt_ref, ...), custom_call_target="tpu_custom_call" | custom-call | flops 1572864000 | bytes 52428800 | tf_op jit(solution)/shard_map/temporal/pallas_call | solution.py:417
  67.9 0.0 collective-permute-done.6.rest_5_
  68.0 0.0 collective-permute-done.4.rest_4_
  68.0 2.9 %collective-permute-start.8 = (bf16[4,64,1,8,128]{4,3,1,0,2:T(8,128)(2,1)S(1)}, bf16[4,64,1,8,128]{4,3,1,0,2:T(8,128)(2,1)S(1)}, u32[]{:S(2)}, u32[]{:S(2)}) collective-permute-start(bf16[4,64,1,8,128]{4,3,1,0,2:T(8,128)(2,1)S(1)} %bitcast.35), channel_id=1, source_target_pairs={{0,4},{4,0},{8,12},{12,8},{16,20},{20,16},{24,28},{28,24},{1,5},{5... | collective-permute-start | bytes 1572872 | tf_op jit(solution)/shard_map/ppermute | solution.py:520
  70.9 0.1 fusion.1
  71.0 19.0 %temporal.3 = (f32[14,1,1024]{2,1,0:T(1,128)S(1)}, f32[16,64,64]{2,1,0:T(8,128)S(1)}, bf16[4,64,4,8,128]{4,3,2,1,0:T(8,128)(2,1)}, bf16[1,4,64,8,128]{4,3,2,1,0:T(8,128)(2,1)}) custom-call(s32[16]{0:T(128)S(1)} %fusion.3.meta_ref, f32[14]{0:T(128)S(1)} %pad_dynamic-slice_fusion.weight_ref, ...), custom_call_target="tpu_custom_call", output_to_operand_aliasing={{2}: (18, {})} | custom-call | flops 1572864000 | bytes 52428800 | tf_op jit(solution)/shard_map/temporal/pallas_call | solution.py:417
  90.0 0.1 collective-permute-start.15
  90.1 0.1 fusion
  90.2 0.0 collective-permute-done.8
  90.3 0.1 collective-permute-start.11
  90.3 1.6 %collective-permute-start.10 = (bf16[16,16,64]{2,1,0:T(8,128)(2,1)S(1)}, bf16[16,16,64]{2,1,0:T(8,128)(2,1)S(1)}, u32[]{:S(2)}, u32[]{:S(2)}) collective-permute-start(bf16[16,16,64]{2,1,0:T(8,128)(2,1)S(1)} %get-tuple-element.103), channel_id=1, source_target_pairs={{0,2},{1,3},{2,0},{3,1},{4,6},{5,7},{6,4},{7,5},{8,10},{9,11},{10,... | collective-permute-start | bytes 98312 | tf_op jit(solution)/shard_map/ppermute | solution.py:500
  91.9 0.2 collective-permute-start.9
  92.1 0.2 collective-permute-done.11
  92.2 3.7 %collective-permute-done.10 = bf16[16,16,64]{2,1,0:T(8,128)(2,1)S(1)} collective-permute-done((bf16[16,16,64]{2,1,0:T(8,128)(2,1)S(1)}, bf16[16,16,64]{2,1,0:T(8,128)(2,1)S(1)}, u32[]{:S(2)}, u32[]{:S(2)}) %collective-permute-start.10) | collective-permute-done | bytes 32800 | tf_op jit(solution)/shard_map/ppermute | solution.py:500
  96.0 0.2 collective-permute-done.9
  96.2 3.5 %collective-permute-start.14 = (bf16[16,16,64]{2,1,0:T(8,128)(2,1)S(1)}, bf16[16,16,64]{2,1,0:T(8,128)(2,1)S(1)}, u32[]{:S(2)}, u32[]{:S(2)}) collective-permute-start(bf16[16,16,64]{2,1,0:T(8,128)(2,1)S(1)} %fusion.2), channel_id=1, source_target_pairs={{0,24},{4,28},{8,16},{12,20},{16,8},{20,12},{24,0},{28,4},{1,25},{... | collective-permute-start | bytes 98312 | tf_op jit(solution)/shard_map/ppermute | solution.py:482
  99.7 0.0 collective-permute-start.13
  99.7 1.0 collective-permute-start.12
  100.7 0.6 pad_maximum_fusion
  101.3 4.7 %all-to-all-start.1 = ((bf16[8,8,512]{2,1,0:T(8,128)(2,1)}), bf16[8,8,512]{2,1,0:T(8,128)(2,1)S(1)}, u32[]{:S(2)}, u32[]{:S(2)}) async-start(bf16[8,8,512]{2,1,0:T(8,128)(2,1)} %pad_maximum_fusion), calls=%async_computation.1 | async-start | bytes 131072 | tf_op jit(solution)/shard_map/all_to_all | solution.py:656
  106.0 0.0 collective-permute-done.14
  106.0 0.0 collective-permute-done.13
  106.0 0.0 collective-permute-done.12
  106.0 0.1 convert_add_fusion.value_ref
  106.1 0.0 collective-permute-done.15
  106.1 2.1 %collective-permute-start.16 = (bf16[16,16,64]{2,1,0:T(8,128)(2,1)S(1)}, bf16[16,16,64]{2,1,0:T(8,128)(2,1)S(1)}, u32[]{:S(2)}, u32[]{:S(2)}) collective-permute-start(bf16[16,16,64]{2,1,0:T(8,128)(2,1)S(1)} %convert_element_type.69), channel_id=1, source_target_pairs={{0,4},{4,0},{8,12},{12,8},{16,20},{20,16},{24,28},{28,24},{1,5},{5... | collective-permute-start | bytes 98312 | tf_op jit(solution)/shard_map/ppermute | solution.py:482
  108.2 0.8 bitcast_dynamic-update-slice_fusion.1
  109.0 0.8 bitcast_dynamic-update-slice_fusion
  109.9 3.0 %all-to-all-done.1.rest_1_ = bf16[8,8,512]{2,1,0:T(8,128)(2,1)S(1)} async-done(((bf16[8,8,512]{2,1,0:T(8,128)(2,1)}), bf16[8,8,512]{2,1,0:T(8,128)(2,1)S(1)}, u32[]{:S(2)}, u32[]{:S(2)}) %all-to-all-start.1) | async-done | bytes 65568 | tf_op jit(solution)/shard_map/all_to_all | solution.py:656
  112.9 0.0 collective-permute-done.16.rest_0_
  112.9 0.6 copy-done.6
  113.5 0.6 copy-done.8
  114.1 1.6 %finish.1 = (bf16[4,8,512]{2,1,0:T(8,128)(2,1)}, f32[9,16,64]{2,1,0:T(8,128)}, f32[2,3,16,64]{3,2,1,0:T(8,128)}, f32[1,16]{1,0:T(1,128)}) custom-call(f32[16,16,64]{2,1,0:T(8,128)} %copy-done.3, bf16[16,16,64]{2,1,0:T(8,128)(2,1)} %copy-done.8, bf16[8,8,512]{2,1,0:T(8,128)(2,1)} %copy-done.6), custom_call_target="tpu_custom_call" | custom-call | flops 1000 | bytes 1000 | tf_op jit(solution)/shard_map/finish/pallas_call | solution.py:189
  (28 shorter events, 0.2 us)
Async XLA Ops:
  0.7 20.7 %copy-start.9 = (s32[1,32]{1,0:T(1,128)S(1)}, s32[1,32]{1,0:T(1,128)}, u32[]{:S(2)}) copy-start(s32[1,32]{1,0:T(1,128)} %param.12) | copy-start | bytes 388
  0.7 24.7 %copy-start.10 = (bf16[64]{0:T(256)(128)(2,1)S(1)}, bf16[64]{0:T(256)(128)(2,1)}, u32[]{:S(2)}) copy-start(bf16[64]{0:T(256)(128)(2,1)} %param.10) | copy-start | bytes 388
  0.7 24.7 %copy-start.7 = (bf16[2,3,64,64]{3,2,1,0:T(8,128)(2,1)S(1)}, bf16[2,3,64,64]{3,2,1,0:T(8,128)(2,1)}, u32[]{:S(2)}) copy-start(bf16[2,3,64,64]{3,2,1,0:T(8,128)(2,1)} %param.9) | copy-start | bytes 147460
  2.9 18.6 %collective-permute-start.2 = (bf16[4,64,1,8,128]{4,3,2,1,0:T(8,128)(2,1)S(1)}, bf16[4,64,1,8,128]{4,3,2,1,0:T(8,128)(2,1)S(1)}, u32[]{:S(2)}, u32[]{:S(2)}) collective-permute-start(bf16[4,64,1,8,128]{4,3,2,1,0:T(8,128)(2,1)S(1)} %get-tuple-element.99), channel_id=1, source_target_pairs={{0,4},{4,0},{8,12},{12,8},{16,20},{20,16},{24,28},{28,24},{1,5},{5... | collective-permute-start | bytes 1572872 | tf_op jit(solution)/shard_map/ppermute | solution.py:520
  5.8 39.0 %copy-start.1 = (bf16[9,64,64]{2,1,0:T(8,128)(2,1)S(1)}, bf16[9,64,64]{2,1,0:T(8,128)(2,1)}, u32[]{:S(2)}) copy-start(bf16[9,64,64]{2,1,0:T(8,128)(2,1)} %w_ref.5) | copy-start | bytes 221188
  11.2 28.9 %collective-permute-start.1 = (bf16[2,4,64,1024]{3,2,1,0:T(8,128)(2,1)}, bf16[2,4,64,1024]{3,2,1,0:T(8,128)(2,1)S(1)}, u32[]{:S(2)}, u32[]{:S(2)}) collective-permute-start(bf16[2,4,64,1024]{3,2,1,0:T(8,128)(2,1)} %get-tuple-element.76.rest_0_), channel_id=1, source_target_pairs={{4,12},{8,0},{12,20},{16,8},{20,28},{24,16},{5,13},{9,1},{13,21},{... | collective-permute-start | bytes 3145736 | tf_op jit(solution)/shard_map/ppermute | solution.py:524
  12.4 22.6 %collective-permute-start = (bf16[4,64,1,8,128]{4,3,2,1,0:T(8,128)(2,1)}, bf16[4,64,1,8,128]{4,3,2,1,0:T(8,128)(2,1)S(1)}, u32[]{:S(2)}, u32[]{:S(2)}) collective-permute-start(bf16[4,64,1,8,128]{4,3,2,1,0:T(8,128)(2,1)} %get-tuple-element.54), channel_id=1, source_target_pairs={{0,4},{4,0},{8,12},{12,8},{16,20},{20,16},{24,28},{28,24},{1,5},{5... | collective-permute-start | bytes 1572872 | tf_op jit(solution)/shard_map/ppermute | solution.py:520
  16.7 30.9 %all-to-all-start = ((bf16[8,16,512]{2,1,0:T(8,128)(2,1)}), bf16[8,16,512]{2,1,0:T(8,128)(2,1)S(1)}, u32[]{:S(2)}, u32[]{:S(2)}) async-start(bf16[8,16,512]{2,1,0:T(8,128)(2,1)} %windows.1), calls=%async_computation | async-start | bytes 262144 | tf_op jit(solution)/shard_map/all_to_all | solution.py:620
  21.4 4.0 %copy-start.5 = (bf16[4,64,1,8,128]{4,3,2,1,0:T(8,128)(2,1)}, bf16[4,64,1,8,128]{4,3,2,1,0:T(8,128)(2,1)S(1)}, u32[]{:S(2)}) copy-start(bf16[4,64,1,8,128]{4,3,2,1,0:T(8,128)(2,1)S(1)} %collective-permute-done.2.x_ref) | copy-start | bytes 1572868
  21.4 18.6 %collective-permute-start.3 = (bf16[2,2,64,1024]{3,2,1,0:T(8,128)(2,1)}, bf16[2,2,64,1024]{3,2,1,0:T(8,128)(2,1)S(1)}, u32[]{:S(2)}, u32[]{:S(2)}) collective-permute-start(bf16[2,2,64,1024]{3,2,1,0:T(8,128)(2,1)} %get-tuple-element.57), channel_id=1, source_target_pairs={{0,8},{8,16},{12,4},{16,24},{20,12},{28,20},{1,9},{9,17},{13,5},{1... | collective-permute-start | bytes 1572872 | tf_op jit(solution)/shard_map/ppermute | solution.py:524
  28.8 20.5 %collective-permute-start.7 = (bf16[1,4,64,1024]{3,2,1,0:T(8,128)(2,1)}, bf16[1,4,64,1024]{3,2,1,0:T(8,128)(2,1)}, u32[]{:S(2)}, u32[]{:S(2)}) collective-permute-start(bf16[1,4,64,1024]{3,2,1,0:T(8,128)(2,1)} %get-tuple-element.67.rest_1_), channel_id=1, source_target_pairs={{0,8},{8,16},{12,4},{16,24},{20,12},{28,20},{1,9},{9,17},{13,5},{1... | collective-permute-start | bytes 1572872 | tf_op jit(solution)/shard_map/ppermute | solution.py:524
  33.7 11.9 %collective-permute-start.5 = (bf16[1,2,64,1024]{3,2,1,0:T(8,128)(2,1)}, bf16[1,2,64,1024]{3,2,1,0:T(8,128)(2,1)S(1)}, u32[]{:S(2)}, u32[]{:S(2)}) collective-permute-start(bf16[1,2,64,1024]{3,2,1,0:T(8,128)(2,1)} %get-tuple-element.62), channel_id=1, source_target_pairs={{4,12},{8,0},{12,20},{16,8},{20,28},{24,16},{5,13},{9,1},{13,21},{... | collective-permute-start | bytes 786440 | tf_op jit(solution)/shard_map/ppermute | solution.py:524
  35.0 0.8 copy-start.4
  40.0 9.3 %copy-start = (bf16[2,4,64,1024]{3,2,1,0:T(8,128)(2,1)}, bf16[2,4,64,1024]{3,2,1,0:T(8,128)(2,1)S(1)}, u32[]{:S(2)}) copy-start(bf16[2,4,64,1024]{3,2,1,0:T(8,128)(2,1)S(1)} %collective-permute-done.1.rest_2_) | copy-start | bytes 3145732
  40.0 9.3 %copy-start.2 = (bf16[2,2,64,1024]{3,2,1,0:T(8,128)(2,1)}, bf16[2,2,64,1024]{3,2,1,0:T(8,128)(2,1)S(1)}, u32[]{:S(2)}) copy-start(bf16[2,2,64,1024]{3,2,1,0:T(8,128)(2,1)S(1)} %collective-permute-done.3.rest_3_) | copy-start | bytes 1572868
  40.0 27.9 %collective-permute-start.4 = (bf16[1,4,64,1024]{3,2,1,0:T(8,128)(2,1)}, bf16[1,4,64,1024]{3,2,1,0:T(8,128)(2,1)}, u32[]{:S(2)}, u32[]{:S(2)}) collective-permute-start(bf16[1,4,64,1024]{3,2,1,0:T(8,128)(2,1)} %get-tuple-element.77.rest_1_), channel_id=1, source_target_pairs={{0,8},{8,16},{12,4},{16,24},{20,12},{28,20},{1,9},{9,17},{13,5},{1... | collective-permute-start | bytes 1572872 | tf_op jit(solution)/shard_map/ppermute | solution.py:524
  45.6 22.4 %collective-permute-start.6 = (bf16[1,2,64,1024]{3,2,1,0:T(8,128)(2,1)}, bf16[1,2,64,1024]{3,2,1,0:T(8,128)(2,1)S(1)}, u32[]{:S(2)}, u32[]{:S(2)}) collective-permute-start(bf16[1,2,64,1024]{3,2,1,0:T(8,128)(2,1)} %get-tuple-element.64), channel_id=1, source_target_pairs={{4,12},{8,0},{12,20},{16,8},{20,28},{24,16},{5,13},{9,1},{13,21},{... | collective-permute-start | bytes 786440 | tf_op jit(solution)/shard_map/ppermute | solution.py:524
  68.0 22.3 %collective-permute-start.8 = (bf16[4,64,1,8,128]{4,3,1,0,2:T(8,128)(2,1)S(1)}, bf16[4,64,1,8,128]{4,3,1,0,2:T(8,128)(2,1)S(1)}, u32[]{:S(2)}, u32[]{:S(2)}) collective-permute-start(bf16[4,64,1,8,128]{4,3,1,0,2:T(8,128)(2,1)S(1)} %bitcast.35), channel_id=1, source_target_pairs={{0,4},{4,0},{8,12},{12,8},{16,20},{20,16},{24,28},{28,24},{1,5},{5... | collective-permute-start | bytes 1572872 | tf_op jit(solution)/shard_map/ppermute | solution.py:520
  90.0 16.1 %collective-permute-start.15 = (bf16[4,64,1,8,128]{4,3,1,0,2:T(8,128)(2,1)}, bf16[4,64,1,8,128]{4,3,1,0,2:T(8,128)(2,1)S(1)}, u32[]{:S(2)}, u32[]{:S(2)}) collective-permute-start(bf16[4,64,1,8,128]{4,3,1,0,2:T(8,128)(2,1)} %bitcast.44), channel_id=1, source_target_pairs={{0,4},{4,0},{8,12},{12,8},{16,20},{20,16},{24,28},{28,24},{1,5},{5... | collective-permute-start | bytes 1572872 | tf_op jit(solution)/shard_map/ppermute | solution.py:520
  90.3 2.0 %collective-permute-start.11 = (bf16[16,16,64]{2,1,0:T(8,128)(2,1)S(1)}, bf16[16,16,64]{2,1,0:T(8,128)(2,1)S(1)}, u32[]{:S(2)}, u32[]{:S(2)}) collective-permute-start(bf16[16,16,64]{2,1,0:T(8,128)(2,1)S(1)} %get-tuple-element.102), channel_id=1, source_target_pairs={{0,3},{1,0},{2,1},{3,2},{4,7},{5,4},{6,5},{7,6},{8,11},{9,8},{10,9... | collective-permute-start | bytes 98312 | tf_op jit(solution)/shard_map/ppermute | solution.py:500
  90.3 5.6 %collective-permute-start.10 = (bf16[16,16,64]{2,1,0:T(8,128)(2,1)S(1)}, bf16[16,16,64]{2,1,0:T(8,128)(2,1)S(1)}, u32[]{:S(2)}, u32[]{:S(2)}) collective-permute-start(bf16[16,16,64]{2,1,0:T(8,128)(2,1)S(1)} %get-tuple-element.103), channel_id=1, source_target_pairs={{0,2},{1,3},{2,0},{3,1},{4,6},{5,7},{6,4},{7,5},{8,10},{9,11},{10,... | collective-permute-start | bytes 98312 | tf_op jit(solution)/shard_map/ppermute | solution.py:500
  91.9 4.3 %collective-permute-start.9 = (bf16[16,16,64]{2,1,0:T(8,128)(2,1)S(1)}, bf16[16,16,64]{2,1,0:T(8,128)(2,1)S(1)}, u32[]{:S(2)}, u32[]{:S(2)}) collective-permute-start(bf16[16,16,64]{2,1,0:T(8,128)(2,1)S(1)} %get-tuple-element.101), channel_id=1, source_target_pairs={{0,1},{1,2},{2,3},{3,0},{4,5},{5,6},{6,7},{7,4},{8,9},{9,10},{10,1... | collective-permute-start | bytes 98312 | tf_op jit(solution)/shard_map/ppermute | solution.py:500
  96.2 9.8 %collective-permute-start.14 = (bf16[16,16,64]{2,1,0:T(8,128)(2,1)S(1)}, bf16[16,16,64]{2,1,0:T(8,128)(2,1)S(1)}, u32[]{:S(2)}, u32[]{:S(2)}) collective-permute-start(bf16[16,16,64]{2,1,0:T(8,128)(2,1)S(1)} %fusion.2), channel_id=1, source_target_pairs={{0,24},{4,28},{8,16},{12,20},{16,8},{20,12},{24,0},{28,4},{1,25},{... | collective-permute-start | bytes 98312 | tf_op jit(solution)/shard_map/ppermute | solution.py:482
  99.7 6.3 %collective-permute-start.13 = (bf16[16,16,64]{2,1,0:T(8,128)(2,1)S(1)}, bf16[16,16,64]{2,1,0:T(8,128)(2,1)S(1)}, u32[]{:S(2)}, u32[]{:S(2)}) collective-permute-start(bf16[16,16,64]{2,1,0:T(8,128)(2,1)S(1)} %fusion.2), channel_id=1, source_target_pairs={{0,16},{4,20},{8,24},{12,28},{16,0},{20,4},{24,8},{28,12},{1,17},{... | collective-permute-start | bytes 98312 | tf_op jit(solution)/shard_map/ppermute | solution.py:482
  99.7 6.3 %collective-permute-start.12 = (bf16[16,16,64]{2,1,0:T(8,128)(2,1)S(1)}, bf16[16,16,64]{2,1,0:T(8,128)(2,1)S(1)}, u32[]{:S(2)}, u32[]{:S(2)}) collective-permute-start(bf16[16,16,64]{2,1,0:T(8,128)(2,1)S(1)} %fusion.2), channel_id=1, source_target_pairs={{0,8},{4,12},{8,0},{12,4},{16,24},{20,28},{24,16},{28,20},{1,9},{5... | collective-permute-start | bytes 98312 | tf_op jit(solution)/shard_map/ppermute | solution.py:482
  101.3 11.6 %all-to-all-start.1 = ((bf16[8,8,512]{2,1,0:T(8,128)(2,1)}), bf16[8,8,512]{2,1,0:T(8,128)(2,1)S(1)}, u32[]{:S(2)}, u32[]{:S(2)}) async-start(bf16[8,8,512]{2,1,0:T(8,128)(2,1)} %pad_maximum_fusion), calls=%async_computation.1 | async-start | bytes 131072 | tf_op jit(solution)/shard_map/all_to_all | solution.py:656
  106.1 6.8 %copy-start.3 = (f32[16,16,64]{2,1,0:T(8,128)}, f32[16,16,64]{2,1,0:T(8,128)S(1)}, u32[]{:S(2)}) copy-start(f32[16,16,64]{2,1,0:T(8,128)S(1)} %convert_add_fusion.value_ref) | copy-start | bytes 196612
  106.1 6.8 %collective-permute-start.16 = (bf16[16,16,64]{2,1,0:T(8,128)(2,1)S(1)}, bf16[16,16,64]{2,1,0:T(8,128)(2,1)S(1)}, u32[]{:S(2)}, u32[]{:S(2)}) collective-permute-start(bf16[16,16,64]{2,1,0:T(8,128)(2,1)S(1)} %convert_element_type.69), channel_id=1, source_target_pairs={{0,4},{4,0},{8,12},{12,8},{16,20},{20,16},{24,28},{28,24},{1,5},{5... | collective-permute-start | bytes 98312 | tf_op jit(solution)/shard_map/ppermute | solution.py:482
  112.9 0.6 copy-start.6
  113.5 0.6 copy-start.8

commit v10 on v9

--- a/solution.py
+++ b/solution.py
@@ -152,6 +152,7 @@
         in_specs=[vmem],
         out_specs=vmem,
         scratch_shapes=[pltpu.VMEM((total + 16, spot), F32)],
+        compiler_params=pltpu.CompilerParams(vmem_limit_bytes=4 * 1024 * 1024),
         cost_estimate=pl.CostEstimate(flops=1000, bytes_accessed=1000, transcendentals=0),
     )(targets)
 
@@ -197,6 +198,7 @@
         ),
         in_specs=[vmem] * (2 + len(arrived)),
         out_specs=[vmem] * 4,
+        compiler_params=pltpu.CompilerParams(vmem_limit_bytes=4 * 1024 * 1024),
         cost_estimate=pl.CostEstimate(flops=1000, bytes_accessed=1000, transcendentals=0),
     )(value, *arrived, logits)
 
@@ -267,12 +269,14 @@
         late.append(
             pltpu.make_async_copy(xs_in[k], xs.at[spot], sems.at[len(early) + members + k])
         )
-    for copy in early + late:
+    for copy in early:
         copy.start()
     for c in range(tgt_ref.shape[0]):
         tgt[:, c * tgt_ref.shape[2] : (c + 1) * tgt_ref.shape[2]] = tgt_ref[c].astype(F32)
     for copy in early:
         copy.wait()
+    for copy in late:
+        copy.start()
 
     def frame_ok(f):
         g = first + f - HALO

time: 116 us -> 114 us (0.983)
  waiting for transfers between devices: 10.4 us -> 8.59 us
  Pallas kernels: 52.7 us -> 51 us
    ppermute x6, waiting for transfers between devices: 3.26 us -> 1.43 us  [hop(): return lax.ppermute(value, 'tile', [p for p in pairs if 0 <= p[1] < tiles])]
    unnamed x22 -> x16, local copies, waits for them, and re-layouts: 2.06 us -> 0.82 us
  transfers between devices with their start and end apart: 19 -> 19, of which waited for: 7 -> 7; matrix products, arithmetic and copies ran while one was open for 4% -> 5% of each run, Pallas kernels for 44% -> 44%
where the time goes in v10:
time: 114 us; the launch traced here: 113 us
  Pallas kernels  51 us (45%)
  starting transfers between devices  43.6 us (38%)
  waiting for transfers between devices  8.59 us (8%)
  local copies, waits for them, and re-layouts  7.16 us (6%)
  other arithmetic  1.72 us (2%)
    pallas_call x2, Pallas kernels, run_temporal(): pl.pallas_call(functools.partial(temporal_kernel, tuple(places), last, al...  37.6 us
    ppermute x6, starting transfers between devices, hop(): return lax.ppermute(value, 'tile', [p for p in pairs if 0 <= p[1] < tiles])  16.8 us
    pallas_call x3, Pallas kernels, run_forward(): pl.pallas_call(functools.partial(forward_kernel, middle, block), name='co...  12 us
    ppermute x4, starting transfers between devices, swap(): return lax.ppermute(value, 'tile', pairs)  8.82 us
    ppermute x4, starting transfers between devices, sum_over_tiles(): arrived.append(lax.ppermute(sent, 'tile', pairs))  6.53 us
    all_to_all x1, starting transfers between devices, body(): logits = lax.all_to_all(logits, 'tile', 0, 0, tiled=True)  4.94 us
    all_to_all x1, starting transfers between devices, body(): windows = lax.all_to_all(windows, 'tile', 0, 0, tiled=True)  4.72 us
    ppermute x3, waiting for transfers between devices, sum_over_reps(): lax.ppermute(share(r + s).astype(BF16), 'rep', pairs).astype(F32)  4.1 us
  transfers between devices with their start and end apart: 19, of which 7 were waited for; matrix products, arithmetic and copies ran while one was open for 5% of the time, Pallas kernels for 44%

profile of v10, /device:TPU:0, one launch (start us, length us, event | category | flops | bytes accessed | tf_op | source)
XLA Modules:
  0.0 113.0 jit_solution(10523911332402884568)
XLA Ops:
  0.7 2.1 %dynamic-slice_bitcast_fusion = (bf16[4,64,1,8,128]{4,3,2,1,0:T(8,128)(2,1)S(1)}, bf16[4,64,1,8,128]{4,3,2,1,0:T(8,128)(2,1)}) fusion(bf16[1,4,64,4,8,128]{5,4,3,2,1,0:T(8,128)(2,1)} %param.7, s32[]{:T(128)S(6)} %select_n.70, s32[]{:T(128)S(6)} %select_n.69), kind=kLoop, calls=%fused_computation.2 | loop fusion | bytes 2097160 | tf_op jit(solution)/shard_map/dynamic_slice | solution.py:568
  2.8 3.0 %collective-permute-start.2 = (bf16[4,64,1,8,128]{4,3,2,1,0:T(8,128)(2,1)S(1)}, bf16[4,64,1,8,128]{4,3,2,1,0:T(8,128)(2,1)S(1)}, u32[]{:S(2)}, u32[]{:S(2)}) collective-permute-start(bf16[4,64,1,8,128]{4,3,2,1,0:T(8,128)(2,1)S(1)} %get-tuple-element.99), channel_id=1, source_target_pairs={{0,4},{4,0},{8,12},{12,8},{16,20},{20,16},{24,28},{28,24},{1,5},{5... | collective-permute-start | bytes 1572872 | tf_op jit(solution)/shard_map/ppermute | solution.py:524
  5.8 5.3 %conv_forward.3 = (bf16[2,4,64,1024]{3,2,1,0:T(8,128)(2,1)}, bf16[2,4,64,1024]{3,2,1,0:T(8,128)(2,1)}, bf16[2,4,64,1024]{3,2,1,0:T(8,128)(2,1)}, bf16[2,2,64,1024]{3,2,1,0:T(8,128)(2,1)}) custom-call(bf16[4,64,4,8,128]{4,3,2,1,0:T(8,128)(2,1)} %bitcast.36, bf16[9,64,64]{2,1,0:T(8,128)(2,1)} %w_ref.5), custom_call_target="tpu_custom_call" | custom-call | flops 1000 | bytes 1000 | tf_op jit(solution)/shard_map/conv_forward/pallas_call | solution.py:111
  11.1 1.3 %collective-permute-start.1 = (bf16[2,4,64,1024]{3,2,1,0:T(8,128)(2,1)}, bf16[2,4,64,1024]{3,2,1,0:T(8,128)(2,1)S(1)}, u32[]{:S(2)}, u32[]{:S(2)}) collective-permute-start(bf16[2,4,64,1024]{3,2,1,0:T(8,128)(2,1)} %get-tuple-element.76.rest_0_), channel_id=1, source_target_pairs={{4,12},{8,0},{12,20},{16,8},{20,28},{24,16},{5,13},{9,1},{13,21},{... | collective-permute-start | bytes 3145736 | tf_op jit(solution)/shard_map/ppermute | solution.py:528
  12.4 2.8 %collective-permute-start = (bf16[4,64,1,8,128]{4,3,2,1,0:T(8,128)(2,1)}, bf16[4,64,1,8,128]{4,3,2,1,0:T(8,128)(2,1)S(1)}, u32[]{:S(2)}, u32[]{:S(2)}) collective-permute-start(bf16[4,64,1,8,128]{4,3,2,1,0:T(8,128)(2,1)} %get-tuple-element.54), channel_id=1, source_target_pairs={{0,4},{4,0},{8,12},{12,8},{16,20},{20,16},{24,28},{28,24},{1,5},{5... | collective-permute-start | bytes 1572872 | tf_op jit(solution)/shard_map/ppermute | solution.py:524
  15.2 0.7 windows.1
  15.9 4.7 %all-to-all-start = ((bf16[8,16,512]{2,1,0:T(8,128)(2,1)}), bf16[8,16,512]{2,1,0:T(8,128)(2,1)}, u32[]{:S(2)}, u32[]{:S(2)}) async-start(bf16[8,16,512]{2,1,0:T(8,128)(2,1)} %windows.1), calls=%async_computation | async-start | bytes 262144 | tf_op jit(solution)/shard_map/all_to_all | solution.py:624
  20.6 0.0 collective-permute-done.2.x_ref
  20.6 3.9 %collective-permute-start.3 = (bf16[2,2,64,1024]{3,2,1,0:T(8,128)(2,1)}, bf16[2,2,64,1024]{3,2,1,0:T(8,128)(2,1)S(1)}, u32[]{:S(2)}, u32[]{:S(2)}) collective-permute-start(bf16[2,2,64,1024]{3,2,1,0:T(8,128)(2,1)} %get-tuple-element.57), channel_id=1, source_target_pairs={{0,8},{8,16},{12,4},{16,24},{20,12},{28,20},{1,9},{9,17},{13,5},{1... | collective-permute-start | bytes 1572872 | tf_op jit(solution)/shard_map/ppermute | solution.py:528
  24.6 0.9 multiply_convert_fusion.1
  25.6 0.0 copy-done.5
  25.6 3.3 %conv_forward.5 = (bf16[1,4,64,1024]{3,2,1,0:T(8,128)(2,1)}, bf16[1,4,64,1024]{3,2,1,0:T(8,128)(2,1)}, bf16[1,4,64,1024]{3,2,1,0:T(8,128)(2,1)}, bf16[1,2,64,1024]{3,2,1,0:T(8,128)(2,1)}) custom-call(bf16[4,64,1,8,128]{4,3,2,1,0:T(8,128)(2,1)} %copy-done.5, bf16[9,64,64]{2,1,0:T(8,128)(2,1)} %w_ref.5), custom_call_target="tpu_custom_call" | custom-call | flops 1000 | bytes 1000 | tf_op jit(solution)/shard_map/conv_forward/pallas_call | solution.py:111
  28.9 4.2 %collective-permute-start.7 = (bf16[1,4,64,1024]{3,2,1,0:T(8,128)(2,1)}, bf16[1,4,64,1024]{3,2,1,0:T(8,128)(2,1)}, u32[]{:S(2)}, u32[]{:S(2)}) collective-permute-start(bf16[1,4,64,1024]{3,2,1,0:T(8,128)(2,1)} %get-tuple-element.67.rest_1_), channel_id=1, source_target_pairs={{0,8},{8,16},{12,4},{16,24},{20,12},{28,20},{1,9},{9,17},{13,5},{1... | collective-permute-start | bytes 1572872 | tf_op jit(solution)/shard_map/ppermute | solution.py:528
  33.1 0.7 fusion.3.meta_ref
  33.8 1.3 %collective-permute-start.5 = (bf16[1,2,64,1024]{3,2,1,0:T(8,128)(2,1)}, bf16[1,2,64,1024]{3,2,1,0:T(8,128)(2,1)S(1)}, u32[]{:S(2)}, u32[]{:S(2)}) collective-permute-start(bf16[1,2,64,1024]{3,2,1,0:T(8,128)(2,1)} %get-tuple-element.62), channel_id=1, source_target_pairs={{4,12},{8,0},{12,20},{16,8},{20,28},{24,16},{5,13},{9,1},{13,21},{... | collective-permute-start | bytes 786440 | tf_op jit(solution)/shard_map/ppermute | solution.py:528
  35.1 0.0 collective-permute-done.x_ref
  35.1 0.8 copy-done.4
  35.9 3.3 %conv_forward.4 = (bf16[1,4,64,1024]{3,2,1,0:T(8,128)(2,1)}, bf16[1,4,64,1024]{3,2,1,0:T(8,128)(2,1)}, bf16[1,4,64,1024]{3,2,1,0:T(8,128)(2,1)}, bf16[1,2,64,1024]{3,2,1,0:T(8,128)(2,1)}) custom-call(bf16[4,64,1,8,128]{4,3,2,1,0:T(8,128)(2,1)} %copy-done.4, bf16[9,64,64]{2,1,0:T(8,128)(2,1)} %w_ref.5), custom_call_target="tpu_custom_call" | custom-call | flops 1000 | bytes 1000 | tf_op jit(solution)/shard_map/conv_forward/pallas_call | solution.py:111
  39.2 0.8 collective-permute-done.1.rest_2_
  40.0 0.0 collective-permute-done.3.rest_3_
  40.0 4.7 %collective-permute-start.4 = (bf16[1,4,64,1024]{3,2,1,0:T(8,128)(2,1)}, bf16[1,4,64,1024]{3,2,1,0:T(8,128)(2,1)}, u32[]{:S(2)}, u32[]{:S(2)}) collective-permute-start(bf16[1,4,64,1024]{3,2,1,0:T(8,128)(2,1)} %get-tuple-element.77.rest_1_), channel_id=1, source_target_pairs={{0,8},{8,16},{12,4},{16,24},{20,12},{28,20},{1,9},{9,17},{13,5},{1... | collective-permute-start | bytes 1572872 | tf_op jit(solution)/shard_map/ppermute | solution.py:528
  44.7 0.1 pad_dynamic-slice_fusion.weight_ref
  44.7 0.1 copy.19
  44.9 0.1 copy.21.wt_ref
  45.0 0.5 collective-permute-done.5.rest_5_
  45.5 1.5 %collective-permute-start.6 = (bf16[1,2,64,1024]{3,2,1,0:T(8,128)(2,1)}, bf16[1,2,64,1024]{3,2,1,0:T(8,128)(2,1)S(1)}, u32[]{:S(2)}, u32[]{:S(2)}) collective-permute-start(bf16[1,2,64,1024]{3,2,1,0:T(8,128)(2,1)} %get-tuple-element.64), channel_id=1, source_target_pairs={{4,12},{8,0},{12,20},{16,8},{20,28},{24,16},{5,13},{9,1},{13,21},{... | collective-permute-start | bytes 786440 | tf_op jit(solution)/shard_map/ppermute | solution.py:528
  47.0 0.1 copy.22.wtb_ref
  47.1 0.1 copy.23.whc_ref
  47.2 0.2 copy.20
  47.4 0.2 reshape.44.wb_ref
  47.5 0.0 all-to-all-done
  47.6 0.8 constant_dynamic-slice_fusion.1
  48.3 0.1 collective-permute-done.7.rest_4_
  48.5 18.6 %temporal.2 = (f32[14,1,1024]{2,1,0:T(1,128)S(1)}, f32[6,64,192]{2,1,0:T(8,128)S(1)}, bf16[4,64,4,8,128]{4,3,2,1,0:T(8,128)(2,1)}, bf16[1,4,64,8,128]{4,3,2,1,0:T(8,128)(2,1)S(1)}) custom-call(s32[16]{0:T(128)S(1)} %fusion.3.meta_ref, f32[14]{0:T(128)S(1)} %pad_dynamic-slice_fusion.weight_ref, bf16[2,64,192]{2,1,0:T(8,128)(2,1)S(1)} %copy.21.wt_ref, ...), custom_call_target="tpu_custom_call" | custom-call | flops 1572864000 | bytes 52428800 | tf_op jit(solution)/shard_map/temporal/pallas_call | solution.py:421
  67.1 0.0 collective-permute-done.6.rest_5_
  67.2 0.0 collective-permute-done.4.rest_4_
  67.2 2.9 %collective-permute-start.8 = (bf16[4,64,1,8,128]{4,3,1,0,2:T(8,128)(2,1)S(1)}, bf16[4,64,1,8,128]{4,3,1,0,2:T(8,128)(2,1)S(1)}, u32[]{:S(2)}, u32[]{:S(2)}) collective-permute-start(bf16[4,64,1,8,128]{4,3,1,0,2:T(8,128)(2,1)S(1)} %bitcast.35), channel_id=1, source_target_pairs={{0,4},{4,0},{8,12},{12,8},{16,20},{20,16},{24,28},{28,24},{1,5},{5... | collective-permute-start | bytes 1572872 | tf_op jit(solution)/shard_map/ppermute | solution.py:524
  70.1 0.1 fusion.1
  70.2 19.0 %temporal.3 = (f32[14,1,1024]{2,1,0:T(1,128)S(1)}, f32[16,64,64]{2,1,0:T(8,128)S(1)}, bf16[4,64,4,8,128]{4,3,2,1,0:T(8,128)(2,1)}, bf16[1,4,64,8,128]{4,3,2,1,0:T(8,128)(2,1)}) custom-call(s32[16]{0:T(128)S(1)} %fusion.3.meta_ref, f32[14]{0:T(128)S(1)} %pad_dynamic-slice_fusion.weight_ref, ...), custom_call_target="tpu_custom_call", output_to_operand_aliasing={{2}: (18, {})} | custom-call | flops 1572864000 | bytes 52428800 | tf_op jit(solution)/shard_map/temporal/pallas_call | solution.py:421
  89.2 0.1 collective-permute-start.15
  89.3 0.1 fusion
  89.4 0.0 collective-permute-done.8
  89.5 0.1 collective-permute-start.11
  89.5 1.5 %collective-permute-start.10 = (bf16[16,16,64]{2,1,0:T(8,128)(2,1)S(1)}, bf16[16,16,64]{2,1,0:T(8,128)(2,1)S(1)}, u32[]{:S(2)}, u32[]{:S(2)}) collective-permute-start(bf16[16,16,64]{2,1,0:T(8,128)(2,1)S(1)} %get-tuple-element.103), channel_id=1, source_target_pairs={{0,2},{1,3},{2,0},{3,1},{4,6},{5,7},{6,4},{7,5},{8,10},{9,11},{10,... | collective-permute-start | bytes 98312 | tf_op jit(solution)/shard_map/ppermute | solution.py:504
  91.1 0.2 collective-permute-start.9
  91.2 0.2 collective-permute-done.11
  91.4 3.7 %collective-permute-done.10 = bf16[16,16,64]{2,1,0:T(8,128)(2,1)S(1)} collective-permute-done((bf16[16,16,64]{2,1,0:T(8,128)(2,1)S(1)}, bf16[16,16,64]{2,1,0:T(8,128)(2,1)S(1)}, u32[]{:S(2)}, u32[]{:S(2)}) %collective-permute-start.10) | collective-permute-done | bytes 32800 | tf_op jit(solution)/shard_map/ppermute | solution.py:504
  95.2 0.2 collective-permute-done.9
  95.4 3.7 %collective-permute-start.14 = (bf16[16,16,64]{2,1,0:T(8,128)(2,1)S(1)}, bf16[16,16,64]{2,1,0:T(8,128)(2,1)S(1)}, u32[]{:S(2)}, u32[]{:S(2)}) collective-permute-start(bf16[16,16,64]{2,1,0:T(8,128)(2,1)S(1)} %fusion.2), channel_id=1, source_target_pairs={{0,24},{4,28},{8,16},{12,20},{16,8},{20,12},{24,0},{28,4},{1,25},{... | collective-permute-start | bytes 98312 | tf_op jit(solution)/shard_map/ppermute | solution.py:486
  99.1 0.0 collective-permute-start.13
  99.1 0.7 collective-permute-start.12
  99.8 0.6 pad_maximum_fusion
  100.5 4.9 %all-to-all-start.1 = ((bf16[8,8,512]{2,1,0:T(8,128)(2,1)}), bf16[8,8,512]{2,1,0:T(8,128)(2,1)S(1)}, u32[]{:S(2)}, u32[]{:S(2)}) async-start(bf16[8,8,512]{2,1,0:T(8,128)(2,1)} %pad_maximum_fusion), calls=%async_computation.1 | async-start | bytes 131072 | tf_op jit(solution)/shard_map/all_to_all | solution.py:660
  105.4 0.0 collective-permute-done.14
  105.4 0.0 collective-permute-done.13
  105.4 0.0 collective-permute-done.12
  105.4 0.1 convert_add_fusion.value_ref
  105.5 0.0 collective-permute-done.15
  105.5 2.1 %collective-permute-start.16 = (bf16[16,16,64]{2,1,0:T(8,128)(2,1)S(1)}, bf16[16,16,64]{2,1,0:T(8,128)(2,1)S(1)}, u32[]{:S(2)}, u32[]{:S(2)}) collective-permute-start(bf16[16,16,64]{2,1,0:T(8,128)(2,1)S(1)} %convert_element_type.69), channel_id=1, source_target_pairs={{0,4},{4,0},{8,12},{12,8},{16,20},{20,16},{24,28},{28,24},{1,5},{5... | collective-permute-start | bytes 98312 | tf_op jit(solution)/shard_map/ppermute | solution.py:486
  107.6 0.8 bitcast_dynamic-update-slice_fusion.1
  108.5 0.8 bitcast_dynamic-update-slice_fusion
  109.3 3.0 %all-to-all-done.1.rest_1_ = bf16[8,8,512]{2,1,0:T(8,128)(2,1)S(1)} async-done(((bf16[8,8,512]{2,1,0:T(8,128)(2,1)}), bf16[8,8,512]{2,1,0:T(8,128)(2,1)S(1)}, u32[]{:S(2)}, u32[]{:S(2)}) %all-to-all-start.1) | async-done | bytes 65568 | tf_op jit(solution)/shard_map/all_to_all | solution.py:660
  112.3 0.0 collective-permute-done.16.rest_0_
  112.3 0.7 finish.1
  (22 shorter events, 0.2 us)
Async XLA Ops:
  0.7 14.5 %copy-start = (bf16[1,32,512]{2,1,0:T(8,128)(2,1)S(1)}, bf16[1,32,512]{2,1,0:T(8,128)(2,1)}, u32[]{:S(2)}) copy-start(bf16[1,32,512]{2,1,0:T(8,128)(2,1)} %tgt_ref) | copy-start | bytes 98308
  0.7 19.9 %copy-start.6 = (s32[1,32]{1,0:T(1,128)S(1)}, s32[1,32]{1,0:T(1,128)}, u32[]{:S(2)}) copy-start(s32[1,32]{1,0:T(1,128)} %param.12) | copy-start | bytes 388
  0.7 23.9 %copy-start.7 = (bf16[64]{0:T(256)(128)(2,1)S(1)}, bf16[64]{0:T(256)(128)(2,1)}, u32[]{:S(2)}) copy-start(bf16[64]{0:T(256)(128)(2,1)} %param.10) | copy-start | bytes 388
  2.8 17.8 %collective-permute-start.2 = (bf16[4,64,1,8,128]{4,3,2,1,0:T(8,128)(2,1)S(1)}, bf16[4,64,1,8,128]{4,3,2,1,0:T(8,128)(2,1)S(1)}, u32[]{:S(2)}, u32[]{:S(2)}) collective-permute-start(bf16[4,64,1,8,128]{4,3,2,1,0:T(8,128)(2,1)S(1)} %get-tuple-element.99), channel_id=1, source_target_pairs={{0,4},{4,0},{8,12},{12,8},{16,20},{20,16},{24,28},{28,24},{1,5},{5... | collective-permute-start | bytes 1572872 | tf_op jit(solution)/shard_map/ppermute | solution.py:524
  5.8 39.2 %copy-start.2 = (bf16[9,64,64]{2,1,0:T(8,128)(2,1)S(1)}, bf16[9,64,64]{2,1,0:T(8,128)(2,1)}, u32[]{:S(2)}) copy-start(bf16[9,64,64]{2,1,0:T(8,128)(2,1)} %w_ref.5) | copy-start | bytes 221188
  11.1 28.9 %collective-permute-start.1 = (bf16[2,4,64,1024]{3,2,1,0:T(8,128)(2,1)}, bf16[2,4,64,1024]{3,2,1,0:T(8,128)(2,1)S(1)}, u32[]{:S(2)}, u32[]{:S(2)}) collective-permute-start(bf16[2,4,64,1024]{3,2,1,0:T(8,128)(2,1)} %get-tuple-element.76.rest_0_), channel_id=1, source_target_pairs={{4,12},{8,0},{12,20},{16,8},{20,28},{24,16},{5,13},{9,1},{13,21},{... | collective-permute-start | bytes 3145736 | tf_op jit(solution)/shard_map/ppermute | solution.py:528
  12.4 22.7 %collective-permute-start = (bf16[4,64,1,8,128]{4,3,2,1,0:T(8,128)(2,1)}, bf16[4,64,1,8,128]{4,3,2,1,0:T(8,128)(2,1)S(1)}, u32[]{:S(2)}, u32[]{:S(2)}) collective-permute-start(bf16[4,64,1,8,128]{4,3,2,1,0:T(8,128)(2,1)} %get-tuple-element.54), channel_id=1, source_target_pairs={{0,4},{4,0},{8,12},{12,8},{16,20},{20,16},{24,28},{28,24},{1,5},{5... | collective-permute-start | bytes 1572872 | tf_op jit(solution)/shard_map/ppermute | solution.py:524
  15.9 31.7 %all-to-all-start = ((bf16[8,16,512]{2,1,0:T(8,128)(2,1)}), bf16[8,16,512]{2,1,0:T(8,128)(2,1)}, u32[]{:S(2)}, u32[]{:S(2)}) async-start(bf16[8,16,512]{2,1,0:T(8,128)(2,1)} %windows.1), calls=%async_computation | async-start | bytes 262144 | tf_op jit(solution)/shard_map/all_to_all | solution.py:624
  20.6 4.9 %copy-start.5 = (bf16[4,64,1,8,128]{4,3,2,1,0:T(8,128)(2,1)}, bf16[4,64,1,8,128]{4,3,2,1,0:T(8,128)(2,1)S(1)}, u32[]{:S(2)}) copy-start(bf16[4,64,1,8,128]{4,3,2,1,0:T(8,128)(2,1)S(1)} %collective-permute-done.2.x_ref) | copy-start | bytes 1572868
  20.6 19.3 %collective-permute-start.3 = (bf16[2,2,64,1024]{3,2,1,0:T(8,128)(2,1)}, bf16[2,2,64,1024]{3,2,1,0:T(8,128)(2,1)S(1)}, u32[]{:S(2)}, u32[]{:S(2)}) collective-permute-start(bf16[2,2,64,1024]{3,2,1,0:T(8,128)(2,1)} %get-tuple-element.57), channel_id=1, source_target_pairs={{0,8},{8,16},{12,4},{16,24},{20,12},{28,20},{1,9},{9,17},{13,5},{1... | collective-permute-start | bytes 1572872 | tf_op jit(solution)/shard_map/ppermute | solution.py:528
  28.9 19.6 %collective-permute-start.7 = (bf16[1,4,64,1024]{3,2,1,0:T(8,128)(2,1)}, bf16[1,4,64,1024]{3,2,1,0:T(8,128)(2,1)}, u32[]{:S(2)}, u32[]{:S(2)}) collective-permute-start(bf16[1,4,64,1024]{3,2,1,0:T(8,128)(2,1)} %get-tuple-element.67.rest_1_), channel_id=1, source_target_pairs={{0,8},{8,16},{12,4},{16,24},{20,12},{28,20},{1,9},{9,17},{13,5},{1... | collective-permute-start | bytes 1572872 | tf_op jit(solution)/shard_map/ppermute | solution.py:528
  33.8 11.7 %collective-permute-start.5 = (bf16[1,2,64,1024]{3,2,1,0:T(8,128)(2,1)}, bf16[1,2,64,1024]{3,2,1,0:T(8,128)(2,1)S(1)}, u32[]{:S(2)}, u32[]{:S(2)}) collective-permute-start(bf16[1,2,64,1024]{3,2,1,0:T(8,128)(2,1)} %get-tuple-element.62), channel_id=1, source_target_pairs={{4,12},{8,0},{12,20},{16,8},{20,28},{24,16},{5,13},{9,1},{13,21},{... | collective-permute-start | bytes 786440 | tf_op jit(solution)/shard_map/ppermute | solution.py:528
  35.1 0.8 copy-start.4
  40.0 8.5 %copy-start.1 = (bf16[2,4,64,1024]{3,2,1,0:T(8,128)(2,1)}, bf16[2,4,64,1024]{3,2,1,0:T(8,128)(2,1)S(1)}, u32[]{:S(2)}) copy-start(bf16[2,4,64,1024]{3,2,1,0:T(8,128)(2,1)S(1)} %collective-permute-done.1.rest_2_) | copy-start | bytes 3145732
  40.0 8.5 %copy-start.3 = (bf16[2,2,64,1024]{3,2,1,0:T(8,128)(2,1)}, bf16[2,2,64,1024]{3,2,1,0:T(8,128)(2,1)S(1)}, u32[]{:S(2)}) copy-start(bf16[2,2,64,1024]{3,2,1,0:T(8,128)(2,1)S(1)} %collective-permute-done.3.rest_3_) | copy-start | bytes 1572868
  40.0 27.2 %collective-permute-start.4 = (bf16[1,4,64,1024]{3,2,1,0:T(8,128)(2,1)}, bf16[1,4,64,1024]{3,2,1,0:T(8,128)(2,1)}, u32[]{:S(2)}, u32[]{:S(2)}) collective-permute-start(bf16[1,4,64,1024]{3,2,1,0:T(8,128)(2,1)} %get-tuple-element.77.rest_1_), channel_id=1, source_target_pairs={{0,8},{8,16},{12,4},{16,24},{20,12},{28,20},{1,9},{9,17},{13,5},{1... | collective-permute-start | bytes 1572872 | tf_op jit(solution)/shard_map/ppermute | solution.py:528
  45.5 21.6 %collective-permute-start.6 = (bf16[1,2,64,1024]{3,2,1,0:T(8,128)(2,1)}, bf16[1,2,64,1024]{3,2,1,0:T(8,128)(2,1)S(1)}, u32[]{:S(2)}, u32[]{:S(2)}) collective-permute-start(bf16[1,2,64,1024]{3,2,1,0:T(8,128)(2,1)} %get-tuple-element.64), channel_id=1, source_target_pairs={{4,12},{8,0},{12,20},{16,8},{20,28},{24,16},{5,13},{9,1},{13,21},{... | collective-permute-start | bytes 786440 | tf_op jit(solution)/shard_map/ppermute | solution.py:528
  67.2 22.2 %collective-permute-start.8 = (bf16[4,64,1,8,128]{4,3,1,0,2:T(8,128)(2,1)S(1)}, bf16[4,64,1,8,128]{4,3,1,0,2:T(8,128)(2,1)S(1)}, u32[]{:S(2)}, u32[]{:S(2)}) collective-permute-start(bf16[4,64,1,8,128]{4,3,1,0,2:T(8,128)(2,1)S(1)} %bitcast.35), channel_id=1, source_target_pairs={{0,4},{4,0},{8,12},{12,8},{16,20},{20,16},{24,28},{28,24},{1,5},{5... | collective-permute-start | bytes 1572872 | tf_op jit(solution)/shard_map/ppermute | solution.py:524
  89.2 16.4 %collective-permute-start.15 = (bf16[4,64,1,8,128]{4,3,1,0,2:T(8,128)(2,1)}, bf16[4,64,1,8,128]{4,3,1,0,2:T(8,128)(2,1)S(1)}, u32[]{:S(2)}, u32[]{:S(2)}) collective-permute-start(bf16[4,64,1,8,128]{4,3,1,0,2:T(8,128)(2,1)} %bitcast.44), channel_id=1, source_target_pairs={{0,4},{4,0},{8,12},{12,8},{16,20},{20,16},{24,28},{28,24},{1,5},{5... | collective-permute-start | bytes 1572872 | tf_op jit(solution)/shard_map/ppermute | solution.py:524
  89.5 2.0 %collective-permute-start.11 = (bf16[16,16,64]{2,1,0:T(8,128)(2,1)S(1)}, bf16[16,16,64]{2,1,0:T(8,128)(2,1)S(1)}, u32[]{:S(2)}, u32[]{:S(2)}) collective-permute-start(bf16[16,16,64]{2,1,0:T(8,128)(2,1)S(1)} %get-tuple-element.102), channel_id=1, source_target_pairs={{0,3},{1,0},{2,1},{3,2},{4,7},{5,4},{6,5},{7,6},{8,11},{9,8},{10,9... | collective-permute-start | bytes 98312 | tf_op jit(solution)/shard_map/ppermute | solution.py:504
  89.5 5.6 %collective-permute-start.10 = (bf16[16,16,64]{2,1,0:T(8,128)(2,1)S(1)}, bf16[16,16,64]{2,1,0:T(8,128)(2,1)S(1)}, u32[]{:S(2)}, u32[]{:S(2)}) collective-permute-start(bf16[16,16,64]{2,1,0:T(8,128)(2,1)S(1)} %get-tuple-element.103), channel_id=1, source_target_pairs={{0,2},{1,3},{2,0},{3,1},{4,6},{5,7},{6,4},{7,5},{8,10},{9,11},{10,... | collective-permute-start | bytes 98312 | tf_op jit(solution)/shard_map/ppermute | solution.py:504
  91.1 4.3 %collective-permute-start.9 = (bf16[16,16,64]{2,1,0:T(8,128)(2,1)S(1)}, bf16[16,16,64]{2,1,0:T(8,128)(2,1)S(1)}, u32[]{:S(2)}, u32[]{:S(2)}) collective-permute-start(bf16[16,16,64]{2,1,0:T(8,128)(2,1)S(1)} %get-tuple-element.101), channel_id=1, source_target_pairs={{0,1},{1,2},{2,3},{3,0},{4,5},{5,6},{6,7},{7,4},{8,9},{9,10},{10,1... | collective-permute-start | bytes 98312 | tf_op jit(solution)/shard_map/ppermute | solution.py:504
  95.4 10.0 %collective-permute-start.14 = (bf16[16,16,64]{2,1,0:T(8,128)(2,1)S(1)}, bf16[16,16,64]{2,1,0:T(8,128)(2,1)S(1)}, u32[]{:S(2)}, u32[]{:S(2)}) collective-permute-start(bf16[16,16,64]{2,1,0:T(8,128)(2,1)S(1)} %fusion.2), channel_id=1, source_target_pairs={{0,24},{4,28},{8,16},{12,20},{16,8},{20,12},{24,0},{28,4},{1,25},{... | collective-permute-start | bytes 98312 | tf_op jit(solution)/shard_map/ppermute | solution.py:486
  99.1 6.3 %collective-permute-start.13 = (bf16[16,16,64]{2,1,0:T(8,128)(2,1)S(1)}, bf16[16,16,64]{2,1,0:T(8,128)(2,1)S(1)}, u32[]{:S(2)}, u32[]{:S(2)}) collective-permute-start(bf16[16,16,64]{2,1,0:T(8,128)(2,1)S(1)} %fusion.2), channel_id=1, source_target_pairs={{0,16},{4,20},{8,24},{12,28},{16,0},{20,4},{24,8},{28,12},{1,17},{... | collective-permute-start | bytes 98312 | tf_op jit(solution)/shard_map/ppermute | solution.py:486
  99.1 6.3 %collective-permute-start.12 = (bf16[16,16,64]{2,1,0:T(8,128)(2,1)S(1)}, bf16[16,16,64]{2,1,0:T(8,128)(2,1)S(1)}, u32[]{:S(2)}, u32[]{:S(2)}) collective-permute-start(bf16[16,16,64]{2,1,0:T(8,128)(2,1)S(1)} %fusion.2), channel_id=1, source_target_pairs={{0,8},{4,12},{8,0},{12,4},{16,24},{20,28},{24,16},{28,20},{1,9},{5... | collective-permute-start | bytes 98312 | tf_op jit(solution)/shard_map/ppermute | solution.py:486
  100.5 11.8 %all-to-all-start.1 = ((bf16[8,8,512]{2,1,0:T(8,128)(2,1)}), bf16[8,8,512]{2,1,0:T(8,128)(2,1)S(1)}, u32[]{:S(2)}, u32[]{:S(2)}) async-start(bf16[8,8,512]{2,1,0:T(8,128)(2,1)} %pad_maximum_fusion), calls=%async_computation.1 | async-start | bytes 131072 | tf_op jit(solution)/shard_map/all_to_all | solution.py:660
  105.5 6.8 %collective-permute-start.16 = (bf16[16,16,64]{2,1,0:T(8,128)(2,1)S(1)}, bf16[16,16,64]{2,1,0:T(8,128)(2,1)S(1)}, u32[]{:S(2)}, u32[]{:S(2)}) collective-permute-start(bf16[16,16,64]{2,1,0:T(8,128)(2,1)S(1)} %convert_element_type.69), channel_id=1, source_target_pairs={{0,4},{4,0},{8,12},{12,8},{16,20},{20,16},{24,28},{28,24},{1,5},{5... | collective-permute-start | bytes 98312 | tf_op jit(solution)/shard_map/ppermute | solution.py:486

commit v11 on v10

--- a/solution.py
+++ b/solution.py
@@ -252,7 +252,7 @@
         tgt,
         sems,
     ) = rest[4:22]
-    step = min(256, vox)
+    step = min(512, vox)
     lo, hi = HALO, HALO + own
     first = meta_ref[base]
     chunks = [slice(p * step, (p + 1) * step) for p in range(vox // step)]

time: 114 us -> 113 us (level)
  no operation moved by 1% of the time
where the time goes in v11:
time: 113 us
  Pallas kernels  50.7 us (45%)
  starting transfers between devices  43.6 us (39%)
  waiting for transfers between devices  8.59 us (8%)
  local copies, waits for them, and re-layouts  7.16 us (6%)
  other arithmetic  1.72 us (2%)
    pallas_call x2, Pallas kernels, run_temporal(): pl.pallas_call(functools.partial(temporal_kernel, tuple(places), last, al...  37.3 us
    ppermute x6, starting transfers between devices, hop(): return lax.ppermute(value, 'tile', [p for p in pairs if 0 <= p[1] < tiles])  16.8 us
    pallas_call x3, Pallas kernels, run_forward(): pl.pallas_call(functools.partial(forward_kernel, middle, block), name='co...  12 us
    ppermute x4, starting transfers between devices, swap(): return lax.ppermute(value, 'tile', pairs)  8.81 us
    ppermute x4, starting transfers between devices, sum_over_tiles(): arrived.append(lax.ppermute(sent, 'tile', pairs))  6.53 us
    all_to_all x1, starting transfers between devices, body(): logits = lax.all_to_all(logits, 'tile', 0, 0, tiled=True)  4.93 us
    all_to_all x1, starting transfers between devices, body(): windows = lax.all_to_all(windows, 'tile', 0, 0, tiled=True)  4.72 us
    ppermute x3, waiting for transfers between devices, sum_over_reps(): lax.ppermute(share(r + s).astype(BF16), 'rep', pairs).astype(F32)  4.1 us
  transfers between devices with their start and end apart: 19, of which 7 were waited for; matrix products, arithmetic and copies ran while one was open for 5% of the time, Pallas kernels for 44%

profile of v11, /device:TPU:0, one launch (start us, length us, event | category | flops | bytes accessed | tf_op | source)
XLA Modules:
  0.0 112.7 jit_solution(12250409177858870361)
XLA Ops:
  0.7 2.1 %dynamic-slice_bitcast_fusion = (bf16[4,64,1,8,128]{4,3,2,1,0:T(8,128)(2,1)S(1)}, bf16[4,64,1,8,128]{4,3,2,1,0:T(8,128)(2,1)}) fusion(bf16[1,4,64,4,8,128]{5,4,3,2,1,0:T(8,128)(2,1)} %param.7, s32[]{:T(128)S(6)} %select_n.70, s32[]{:T(128)S(6)} %select_n.69), kind=kLoop, calls=%fused_computation.2 | loop fusion | bytes 2097160 | tf_op jit(solution)/shard_map/dynamic_slice | solution.py:568
  2.8 3.0 %collective-permute-start.2 = (bf16[4,64,1,8,128]{4,3,2,1,0:T(8,128)(2,1)S(1)}, bf16[4,64,1,8,128]{4,3,2,1,0:T(8,128)(2,1)S(1)}, u32[]{:S(2)}, u32[]{:S(2)}) collective-permute-start(bf16[4,64,1,8,128]{4,3,2,1,0:T(8,128)(2,1)S(1)} %get-tuple-element.99), channel_id=1, source_target_pairs={{0,4},{4,0},{8,12},{12,8},{16,20},{20,16},{24,28},{28,24},{1,5},{5... | collective-permute-start | bytes 1572872 | tf_op jit(solution)/shard_map/ppermute | solution.py:524
  5.8 5.3 %conv_forward.3 = (bf16[2,4,64,1024]{3,2,1,0:T(8,128)(2,1)}, bf16[2,4,64,1024]{3,2,1,0:T(8,128)(2,1)}, bf16[2,4,64,1024]{3,2,1,0:T(8,128)(2,1)}, bf16[2,2,64,1024]{3,2,1,0:T(8,128)(2,1)}) custom-call(bf16[4,64,4,8,128]{4,3,2,1,0:T(8,128)(2,1)} %bitcast.36, bf16[9,64,64]{2,1,0:T(8,128)(2,1)} %w_ref.5), custom_call_target="tpu_custom_call" | custom-call | flops 1000 | bytes 1000 | tf_op jit(solution)/shard_map/conv_forward/pallas_call | solution.py:111
  11.1 1.3 %collective-permute-start.1 = (bf16[2,4,64,1024]{3,2,1,0:T(8,128)(2,1)}, bf16[2,4,64,1024]{3,2,1,0:T(8,128)(2,1)S(1)}, u32[]{:S(2)}, u32[]{:S(2)}) collective-permute-start(bf16[2,4,64,1024]{3,2,1,0:T(8,128)(2,1)} %get-tuple-element.76.rest_0_), channel_id=1, source_target_pairs={{4,12},{8,0},{12,20},{16,8},{20,28},{24,16},{5,13},{9,1},{13,21},{... | collective-permute-start | bytes 3145736 | tf_op jit(solution)/shard_map/ppermute | solution.py:528
  12.4 2.8 %collective-permute-start = (bf16[4,64,1,8,128]{4,3,2,1,0:T(8,128)(2,1)}, bf16[4,64,1,8,128]{4,3,2,1,0:T(8,128)(2,1)S(1)}, u32[]{:S(2)}, u32[]{:S(2)}) collective-permute-start(bf16[4,64,1,8,128]{4,3,2,1,0:T(8,128)(2,1)} %get-tuple-element.54), channel_id=1, source_target_pairs={{0,4},{4,0},{8,12},{12,8},{16,20},{20,16},{24,28},{28,24},{1,5},{5... | collective-permute-start | bytes 1572872 | tf_op jit(solution)/shard_map/ppermute | solution.py:524
  15.2 0.7 windows.1
  15.9 4.7 %all-to-all-start = ((bf16[8,16,512]{2,1,0:T(8,128)(2,1)}), bf16[8,16,512]{2,1,0:T(8,128)(2,1)}, u32[]{:S(2)}, u32[]{:S(2)}) async-start(bf16[8,16,512]{2,1,0:T(8,128)(2,1)} %windows.1), calls=%async_computation | async-start | bytes 262144 | tf_op jit(solution)/shard_map/all_to_all | solution.py:624
  20.6 0.0 collective-permute-done.2.x_ref
  20.6 3.9 %collective-permute-start.3 = (bf16[2,2,64,1024]{3,2,1,0:T(8,128)(2,1)}, bf16[2,2,64,1024]{3,2,1,0:T(8,128)(2,1)S(1)}, u32[]{:S(2)}, u32[]{:S(2)}) collective-permute-start(bf16[2,2,64,1024]{3,2,1,0:T(8,128)(2,1)} %get-tuple-element.57), channel_id=1, source_target_pairs={{0,8},{8,16},{12,4},{16,24},{20,12},{28,20},{1,9},{9,17},{13,5},{1... | collective-permute-start | bytes 1572872 | tf_op jit(solution)/shard_map/ppermute | solution.py:528
  24.6 0.9 multiply_convert_fusion.1
  25.6 0.0 copy-done.5
  25.6 3.3 %conv_forward.5 = (bf16[1,4,64,1024]{3,2,1,0:T(8,128)(2,1)}, bf16[1,4,64,1024]{3,2,1,0:T(8,128)(2,1)}, bf16[1,4,64,1024]{3,2,1,0:T(8,128)(2,1)}, bf16[1,2,64,1024]{3,2,1,0:T(8,128)(2,1)}) custom-call(bf16[4,64,1,8,128]{4,3,2,1,0:T(8,128)(2,1)} %copy-done.5, bf16[9,64,64]{2,1,0:T(8,128)(2,1)} %w_ref.5), custom_call_target="tpu_custom_call" | custom-call | flops 1000 | bytes 1000 | tf_op jit(solution)/shard_map/conv_forward/pallas_call | solution.py:111
  28.9 4.2 %collective-permute-start.7 = (bf16[1,4,64,1024]{3,2,1,0:T(8,128)(2,1)}, bf16[1,4,64,1024]{3,2,1,0:T(8,128)(2,1)}, u32[]{:S(2)}, u32[]{:S(2)}) collective-permute-start(bf16[1,4,64,1024]{3,2,1,0:T(8,128)(2,1)} %get-tuple-element.67.rest_1_), channel_id=1, source_target_pairs={{0,8},{8,16},{12,4},{16,24},{20,12},{28,20},{1,9},{9,17},{13,5},{1... | collective-permute-start | bytes 1572872 | tf_op jit(solution)/shard_map/ppermute | solution.py:528
  33.1 0.7 fusion.3.meta_ref
  33.8 1.3 %collective-permute-start.5 = (bf16[1,2,64,1024]{3,2,1,0:T(8,128)(2,1)}, bf16[1,2,64,1024]{3,2,1,0:T(8,128)(2,1)S(1)}, u32[]{:S(2)}, u32[]{:S(2)}) collective-permute-start(bf16[1,2,64,1024]{3,2,1,0:T(8,128)(2,1)} %get-tuple-element.62), channel_id=1, source_target_pairs={{4,12},{8,0},{12,20},{16,8},{20,28},{24,16},{5,13},{9,1},{13,21},{... | collective-permute-start | bytes 786440 | tf_op jit(solution)/shard_map/ppermute | solution.py:528
  35.1 0.0 collective-permute-done.x_ref
  35.1 0.8 copy-done.4
  35.9 3.3 %conv_forward.4 = (bf16[1,4,64,1024]{3,2,1,0:T(8,128)(2,1)}, bf16[1,4,64,1024]{3,2,1,0:T(8,128)(2,1)}, bf16[1,4,64,1024]{3,2,1,0:T(8,128)(2,1)}, bf16[1,2,64,1024]{3,2,1,0:T(8,128)(2,1)}) custom-call(bf16[4,64,1,8,128]{4,3,2,1,0:T(8,128)(2,1)} %copy-done.4, bf16[9,64,64]{2,1,0:T(8,128)(2,1)} %w_ref.5), custom_call_target="tpu_custom_call" | custom-call | flops 1000 | bytes 1000 | tf_op jit(solution)/shard_map/conv_forward/pallas_call | solution.py:111
  39.2 0.8 collective-permute-done.1.rest_2_
  40.0 0.0 collective-permute-done.3.rest_3_
  40.0 4.7 %collective-permute-start.4 = (bf16[1,4,64,1024]{3,2,1,0:T(8,128)(2,1)}, bf16[1,4,64,1024]{3,2,1,0:T(8,128)(2,1)}, u32[]{:S(2)}, u32[]{:S(2)}) collective-permute-start(bf16[1,4,64,1024]{3,2,1,0:T(8,128)(2,1)} %get-tuple-element.77.rest_1_), channel_id=1, source_target_pairs={{0,8},{8,16},{12,4},{16,24},{20,12},{28,20},{1,9},{9,17},{13,5},{1... | collective-permute-start | bytes 1572872 | tf_op jit(solution)/shard_map/ppermute | solution.py:528
  44.7 0.1 pad_dynamic-slice_fusion.weight_ref
  44.7 0.1 copy.19
  44.9 0.1 copy.21.wt_ref
  45.0 0.5 collective-permute-done.5.rest_5_
  45.5 1.5 %collective-permute-start.6 = (bf16[1,2,64,1024]{3,2,1,0:T(8,128)(2,1)}, bf16[1,2,64,1024]{3,2,1,0:T(8,128)(2,1)S(1)}, u32[]{:S(2)}, u32[]{:S(2)}) collective-permute-start(bf16[1,2,64,1024]{3,2,1,0:T(8,128)(2,1)} %get-tuple-element.64), channel_id=1, source_target_pairs={{4,12},{8,0},{12,20},{16,8},{20,28},{24,16},{5,13},{9,1},{13,21},{... | collective-permute-start | bytes 786440 | tf_op jit(solution)/shard_map/ppermute | solution.py:528
  47.0 0.1 copy.22.wtb_ref
  47.1 0.1 copy.23.whc_ref
  47.2 0.2 copy.20
  47.4 0.2 reshape.44.wb_ref
  47.5 0.0 all-to-all-done
  47.6 0.8 constant_dynamic-slice_fusion.1
  48.3 0.1 collective-permute-done.7.rest_4_
  48.5 18.5 %temporal.2 = (f32[14,1,1024]{2,1,0:T(1,128)S(1)}, f32[6,64,192]{2,1,0:T(8,128)S(1)}, bf16[4,64,4,8,128]{4,3,2,1,0:T(8,128)(2,1)}, bf16[1,4,64,8,128]{4,3,2,1,0:T(8,128)(2,1)S(1)}) custom-call(s32[16]{0:T(128)S(1)} %fusion.3.meta_ref, f32[14]{0:T(128)S(1)} %pad_dynamic-slice_fusion.weight_ref, bf16[2,64,192]{2,1,0:T(8,128)(2,1)S(1)} %copy.21.wt_ref, ...), custom_call_target="tpu_custom_call" | custom-call | flops 1572864000 | bytes 52428800 | tf_op jit(solution)/shard_map/temporal/pallas_call | solution.py:421
  67.0 0.0 collective-permute-done.6.rest_5_
  67.0 0.0 collective-permute-done.4.rest_4_
  67.1 2.9 %collective-permute-start.8 = (bf16[4,64,1,8,128]{4,3,1,0,2:T(8,128)(2,1)S(1)}, bf16[4,64,1,8,128]{4,3,1,0,2:T(8,128)(2,1)S(1)}, u32[]{:S(2)}, u32[]{:S(2)}) collective-permute-start(bf16[4,64,1,8,128]{4,3,1,0,2:T(8,128)(2,1)S(1)} %bitcast.35), channel_id=1, source_target_pairs={{0,4},{4,0},{8,12},{12,8},{16,20},{20,16},{24,28},{28,24},{1,5},{5... | collective-permute-start | bytes 1572872 | tf_op jit(solution)/shard_map/ppermute | solution.py:524
  69.9 0.1 fusion.1
  70.0 18.8 %temporal.3 = (f32[14,1,1024]{2,1,0:T(1,128)S(1)}, f32[16,64,64]{2,1,0:T(8,128)S(1)}, bf16[4,64,4,8,128]{4,3,2,1,0:T(8,128)(2,1)}, bf16[1,4,64,8,128]{4,3,2,1,0:T(8,128)(2,1)}) custom-call(s32[16]{0:T(128)S(1)} %fusion.3.meta_ref, f32[14]{0:T(128)S(1)} %pad_dynamic-slice_fusion.weight_ref, ...), custom_call_target="tpu_custom_call", output_to_operand_aliasing={{2}: (18, {})} | custom-call | flops 1572864000 | bytes 52428800 | tf_op jit(solution)/shard_map/temporal/pallas_call | solution.py:421
  88.9 0.1 collective-permute-start.15
  89.0 0.1 fusion
  89.1 0.0 collective-permute-done.8
  89.2 0.1 collective-permute-start.11
  89.2 1.6 %collective-permute-start.10 = (bf16[16,16,64]{2,1,0:T(8,128)(2,1)S(1)}, bf16[16,16,64]{2,1,0:T(8,128)(2,1)S(1)}, u32[]{:S(2)}, u32[]{:S(2)}) collective-permute-start(bf16[16,16,64]{2,1,0:T(8,128)(2,1)S(1)} %get-tuple-element.103), channel_id=1, source_target_pairs={{0,2},{1,3},{2,0},{3,1},{4,6},{5,7},{6,4},{7,5},{8,10},{9,11},{10,... | collective-permute-start | bytes 98312 | tf_op jit(solution)/shard_map/ppermute | solution.py:504
  90.8 0.2 collective-permute-start.9
  91.0 0.2 collective-permute-done.11
  91.1 3.8 %collective-permute-done.10 = bf16[16,16,64]{2,1,0:T(8,128)(2,1)S(1)} collective-permute-done((bf16[16,16,64]{2,1,0:T(8,128)(2,1)S(1)}, bf16[16,16,64]{2,1,0:T(8,128)(2,1)S(1)}, u32[]{:S(2)}, u32[]{:S(2)}) %collective-permute-start.10) | collective-permute-done | bytes 32800 | tf_op jit(solution)/shard_map/ppermute | solution.py:504
  94.9 0.2 collective-permute-done.9
  95.1 3.7 %collective-permute-start.14 = (bf16[16,16,64]{2,1,0:T(8,128)(2,1)S(1)}, bf16[16,16,64]{2,1,0:T(8,128)(2,1)S(1)}, u32[]{:S(2)}, u32[]{:S(2)}) collective-permute-start(bf16[16,16,64]{2,1,0:T(8,128)(2,1)S(1)} %fusion.2), channel_id=1, source_target_pairs={{0,24},{4,28},{8,16},{12,20},{16,8},{20,12},{24,0},{28,4},{1,25},{... | collective-permute-start | bytes 98312 | tf_op jit(solution)/shard_map/ppermute | solution.py:486
  98.8 0.0 collective-permute-start.13
  98.8 0.7 collective-permute-start.12
  99.6 0.6 pad_maximum_fusion
  100.2 4.9 %all-to-all-start.1 = ((bf16[8,8,512]{2,1,0:T(8,128)(2,1)}), bf16[8,8,512]{2,1,0:T(8,128)(2,1)S(1)}, u32[]{:S(2)}, u32[]{:S(2)}) async-start(bf16[8,8,512]{2,1,0:T(8,128)(2,1)} %pad_maximum_fusion), calls=%async_computation.1 | async-start | bytes 131072 | tf_op jit(solution)/shard_map/all_to_all | solution.py:660
  105.1 0.0 collective-permute-done.14
  105.1 0.0 collective-permute-done.13
  105.1 0.0 collective-permute-done.12
  105.1 0.1 convert_add_fusion.value_ref
  105.2 0.0 collective-permute-done.15
  105.2 2.1 %collective-permute-start.16 = (bf16[16,16,64]{2,1,0:T(8,128)(2,1)S(1)}, bf16[16,16,64]{2,1,0:T(8,128)(2,1)S(1)}, u32[]{:S(2)}, u32[]{:S(2)}) collective-permute-start(bf16[16,16,64]{2,1,0:T(8,128)(2,1)S(1)} %convert_element_type.69), channel_id=1, source_target_pairs={{0,4},{4,0},{8,12},{12,8},{16,20},{20,16},{24,28},{28,24},{1,5},{5... | collective-permute-start | bytes 98312 | tf_op jit(solution)/shard_map/ppermute | solution.py:486
  107.3 0.8 bitcast_dynamic-update-slice_fusion.1
  108.2 0.8 bitcast_dynamic-update-slice_fusion
  109.0 3.0 %all-to-all-done.1.rest_1_ = bf16[8,8,512]{2,1,0:T(8,128)(2,1)S(1)} async-done(((bf16[8,8,512]{2,1,0:T(8,128)(2,1)}), bf16[8,8,512]{2,1,0:T(8,128)(2,1)S(1)}, u32[]{:S(2)}, u32[]{:S(2)}) %all-to-all-start.1) | async-done | bytes 65568 | tf_op jit(solution)/shard_map/all_to_all | solution.py:660
  112.0 0.0 collective-permute-done.16.rest_0_
  112.0 0.7 finish.1
  (22 shorter events, 0.2 us)
Async XLA Ops:
  0.7 14.5 %copy-start = (bf16[1,32,512]{2,1,0:T(8,128)(2,1)S(1)}, bf16[1,32,512]{2,1,0:T(8,128)(2,1)}, u32[]{:S(2)}) copy-start(bf16[1,32,512]{2,1,0:T(8,128)(2,1)} %tgt_ref) | copy-start | bytes 98308
  0.7 19.9 %copy-start.6 = (s32[1,32]{1,0:T(1,128)S(1)}, s32[1,32]{1,0:T(1,128)}, u32[]{:S(2)}) copy-start(s32[1,32]{1,0:T(1,128)} %param.12) | copy-start | bytes 388
  0.7 23.9 %copy-start.7 = (bf16[64]{0:T(256)(128)(2,1)S(1)}, bf16[64]{0:T(256)(128)(2,1)}, u32[]{:S(2)}) copy-start(bf16[64]{0:T(256)(128)(2,1)} %param.10) | copy-start | bytes 388
  2.8 17.8 %collective-permute-start.2 = (bf16[4,64,1,8,128]{4,3,2,1,0:T(8,128)(2,1)S(1)}, bf16[4,64,1,8,128]{4,3,2,1,0:T(8,128)(2,1)S(1)}, u32[]{:S(2)}, u32[]{:S(2)}) collective-permute-start(bf16[4,64,1,8,128]{4,3,2,1,0:T(8,128)(2,1)S(1)} %get-tuple-element.99), channel_id=1, source_target_pairs={{0,4},{4,0},{8,12},{12,8},{16,20},{20,16},{24,28},{28,24},{1,5},{5... | collective-permute-start | bytes 1572872 | tf_op jit(solution)/shard_map/ppermute | solution.py:524
  5.8 39.2 %copy-start.2 = (bf16[9,64,64]{2,1,0:T(8,128)(2,1)S(1)}, bf16[9,64,64]{2,1,0:T(8,128)(2,1)}, u32[]{:S(2)}) copy-start(bf16[9,64,64]{2,1,0:T(8,128)(2,1)} %w_ref.5) | copy-start | bytes 221188
  11.1 28.9 %collective-permute-start.1 = (bf16[2,4,64,1024]{3,2,1,0:T(8,128)(2,1)}, bf16[2,4,64,1024]{3,2,1,0:T(8,128)(2,1)S(1)}, u32[]{:S(2)}, u32[]{:S(2)}) collective-permute-start(bf16[2,4,64,1024]{3,2,1,0:T(8,128)(2,1)} %get-tuple-element.76.rest_0_), channel_id=1, source_target_pairs={{4,12},{8,0},{12,20},{16,8},{20,28},{24,16},{5,13},{9,1},{13,21},{... | collective-permute-start | bytes 3145736 | tf_op jit(solution)/shard_map/ppermute | solution.py:528
  12.4 22.7 %collective-permute-start = (bf16[4,64,1,8,128]{4,3,2,1,0:T(8,128)(2,1)}, bf16[4,64,1,8,128]{4,3,2,1,0:T(8,128)(2,1)S(1)}, u32[]{:S(2)}, u32[]{:S(2)}) collective-permute-start(bf16[4,64,1,8,128]{4,3,2,1,0:T(8,128)(2,1)} %get-tuple-element.54), channel_id=1, source_target_pairs={{0,4},{4,0},{8,12},{12,8},{16,20},{20,16},{24,28},{28,24},{1,5},{5... | collective-permute-start | bytes 1572872 | tf_op jit(solution)/shard_map/ppermute | solution.py:524
  15.9 31.7 %all-to-all-start = ((bf16[8,16,512]{2,1,0:T(8,128)(2,1)}), bf16[8,16,512]{2,1,0:T(8,128)(2,1)}, u32[]{:S(2)}, u32[]{:S(2)}) async-start(bf16[8,16,512]{2,1,0:T(8,128)(2,1)} %windows.1), calls=%async_computation | async-start | bytes 262144 | tf_op jit(solution)/shard_map/all_to_all | solution.py:624
  20.6 4.9 %copy-start.5 = (bf16[4,64,1,8,128]{4,3,2,1,0:T(8,128)(2,1)}, bf16[4,64,1,8,128]{4,3,2,1,0:T(8,128)(2,1)S(1)}, u32[]{:S(2)}) copy-start(bf16[4,64,1,8,128]{4,3,2,1,0:T(8,128)(2,1)S(1)} %collective-permute-done.2.x_ref) | copy-start | bytes 1572868
  20.6 19.3 %collective-permute-start.3 = (bf16[2,2,64,1024]{3,2,1,0:T(8,128)(2,1)}, bf16[2,2,64,1024]{3,2,1,0:T(8,128)(2,1)S(1)}, u32[]{:S(2)}, u32[]{:S(2)}) collective-permute-start(bf16[2,2,64,1024]{3,2,1,0:T(8,128)(2,1)} %get-tuple-element.57), channel_id=1, source_target_pairs={{0,8},{8,16},{12,4},{16,24},{20,12},{28,20},{1,9},{9,17},{13,5},{1... | collective-permute-start | bytes 1572872 | tf_op jit(solution)/shard_map/ppermute | solution.py:528
  28.9 19.6 %collective-permute-start.7 = (bf16[1,4,64,1024]{3,2,1,0:T(8,128)(2,1)}, bf16[1,4,64,1024]{3,2,1,0:T(8,128)(2,1)}, u32[]{:S(2)}, u32[]{:S(2)}) collective-permute-start(bf16[1,4,64,1024]{3,2,1,0:T(8,128)(2,1)} %get-tuple-element.67.rest_1_), channel_id=1, source_target_pairs={{0,8},{8,16},{12,4},{16,24},{20,12},{28,20},{1,9},{9,17},{13,5},{1... | collective-permute-start | bytes 1572872 | tf_op jit(solution)/shard_map/ppermute | solution.py:528
  33.8 11.7 %collective-permute-start.5 = (bf16[1,2,64,1024]{3,2,1,0:T(8,128)(2,1)}, bf16[1,2,64,1024]{3,2,1,0:T(8,128)(2,1)S(1)}, u32[]{:S(2)}, u32[]{:S(2)}) collective-permute-start(bf16[1,2,64,1024]{3,2,1,0:T(8,128)(2,1)} %get-tuple-element.62), channel_id=1, source_target_pairs={{4,12},{8,0},{12,20},{16,8},{20,28},{24,16},{5,13},{9,1},{13,21},{... | collective-permute-start | bytes 786440 | tf_op jit(solution)/shard_map/ppermute | solution.py:528
  35.1 0.8 copy-start.4
  40.0 8.5 %copy-start.1 = (bf16[2,4,64,1024]{3,2,1,0:T(8,128)(2,1)}, bf16[2,4,64,1024]{3,2,1,0:T(8,128)(2,1)S(1)}, u32[]{:S(2)}) copy-start(bf16[2,4,64,1024]{3,2,1,0:T(8,128)(2,1)S(1)} %collective-permute-done.1.rest_2_) | copy-start | bytes 3145732
  40.0 8.5 %copy-start.3 = (bf16[2,2,64,1024]{3,2,1,0:T(8,128)(2,1)}, bf16[2,2,64,1024]{3,2,1,0:T(8,128)(2,1)S(1)}, u32[]{:S(2)}) copy-start(bf16[2,2,64,1024]{3,2,1,0:T(8,128)(2,1)S(1)} %collective-permute-done.3.rest_3_) | copy-start | bytes 1572868
  40.0 27.0 %collective-permute-start.4 = (bf16[1,4,64,1024]{3,2,1,0:T(8,128)(2,1)}, bf16[1,4,64,1024]{3,2,1,0:T(8,128)(2,1)}, u32[]{:S(2)}, u32[]{:S(2)}) collective-permute-start(bf16[1,4,64,1024]{3,2,1,0:T(8,128)(2,1)} %get-tuple-element.77.rest_1_), channel_id=1, source_target_pairs={{0,8},{8,16},{12,4},{16,24},{20,12},{28,20},{1,9},{9,17},{13,5},{1... | collective-permute-start | bytes 1572872 | tf_op jit(solution)/shard_map/ppermute | solution.py:528
  45.5 21.5 %collective-permute-start.6 = (bf16[1,2,64,1024]{3,2,1,0:T(8,128)(2,1)}, bf16[1,2,64,1024]{3,2,1,0:T(8,128)(2,1)S(1)}, u32[]{:S(2)}, u32[]{:S(2)}) collective-permute-start(bf16[1,2,64,1024]{3,2,1,0:T(8,128)(2,1)} %get-tuple-element.64), channel_id=1, source_target_pairs={{4,12},{8,0},{12,20},{16,8},{20,28},{24,16},{5,13},{9,1},{13,21},{... | collective-permute-start | bytes 786440 | tf_op jit(solution)/shard_map/ppermute | solution.py:528
  67.1 22.0 %collective-permute-start.8 = (bf16[4,64,1,8,128]{4,3,1,0,2:T(8,128)(2,1)S(1)}, bf16[4,64,1,8,128]{4,3,1,0,2:T(8,128)(2,1)S(1)}, u32[]{:S(2)}, u32[]{:S(2)}) collective-permute-start(bf16[4,64,1,8,128]{4,3,1,0,2:T(8,128)(2,1)S(1)} %bitcast.35), channel_id=1, source_target_pairs={{0,4},{4,0},{8,12},{12,8},{16,20},{20,16},{24,28},{28,24},{1,5},{5... | collective-permute-start | bytes 1572872 | tf_op jit(solution)/shard_map/ppermute | solution.py:524
  88.9 16.4 %collective-permute-start.15 = (bf16[4,64,1,8,128]{4,3,1,0,2:T(8,128)(2,1)}, bf16[4,64,1,8,128]{4,3,1,0,2:T(8,128)(2,1)S(1)}, u32[]{:S(2)}, u32[]{:S(2)}) collective-permute-start(bf16[4,64,1,8,128]{4,3,1,0,2:T(8,128)(2,1)} %bitcast.44), channel_id=1, source_target_pairs={{0,4},{4,0},{8,12},{12,8},{16,20},{20,16},{24,28},{28,24},{1,5},{5... | collective-permute-start | bytes 1572872 | tf_op jit(solution)/shard_map/ppermute | solution.py:524
  89.2 2.0 %collective-permute-start.11 = (bf16[16,16,64]{2,1,0:T(8,128)(2,1)S(1)}, bf16[16,16,64]{2,1,0:T(8,128)(2,1)S(1)}, u32[]{:S(2)}, u32[]{:S(2)}) collective-permute-start(bf16[16,16,64]{2,1,0:T(8,128)(2,1)S(1)} %get-tuple-element.102), channel_id=1, source_target_pairs={{0,3},{1,0},{2,1},{3,2},{4,7},{5,4},{6,5},{7,6},{8,11},{9,8},{10,9... | collective-permute-start | bytes 98312 | tf_op jit(solution)/shard_map/ppermute | solution.py:504
  89.2 5.6 %collective-permute-start.10 = (bf16[16,16,64]{2,1,0:T(8,128)(2,1)S(1)}, bf16[16,16,64]{2,1,0:T(8,128)(2,1)S(1)}, u32[]{:S(2)}, u32[]{:S(2)}) collective-permute-start(bf16[16,16,64]{2,1,0:T(8,128)(2,1)S(1)} %get-tuple-element.103), channel_id=1, source_target_pairs={{0,2},{1,3},{2,0},{3,1},{4,6},{5,7},{6,4},{7,5},{8,10},{9,11},{10,... | collective-permute-start | bytes 98312 | tf_op jit(solution)/shard_map/ppermute | solution.py:504
  90.8 4.3 %collective-permute-start.9 = (bf16[16,16,64]{2,1,0:T(8,128)(2,1)S(1)}, bf16[16,16,64]{2,1,0:T(8,128)(2,1)S(1)}, u32[]{:S(2)}, u32[]{:S(2)}) collective-permute-start(bf16[16,16,64]{2,1,0:T(8,128)(2,1)S(1)} %get-tuple-element.101), channel_id=1, source_target_pairs={{0,1},{1,2},{2,3},{3,0},{4,5},{5,6},{6,7},{7,4},{8,9},{9,10},{10,1... | collective-permute-start | bytes 98312 | tf_op jit(solution)/shard_map/ppermute | solution.py:504
  95.1 10.0 %collective-permute-start.14 = (bf16[16,16,64]{2,1,0:T(8,128)(2,1)S(1)}, bf16[16,16,64]{2,1,0:T(8,128)(2,1)S(1)}, u32[]{:S(2)}, u32[]{:S(2)}) collective-permute-start(bf16[16,16,64]{2,1,0:T(8,128)(2,1)S(1)} %fusion.2), channel_id=1, source_target_pairs={{0,24},{4,28},{8,16},{12,20},{16,8},{20,12},{24,0},{28,4},{1,25},{... | collective-permute-start | bytes 98312 | tf_op jit(solution)/shard_map/ppermute | solution.py:486
  98.8 6.3 %collective-permute-start.13 = (bf16[16,16,64]{2,1,0:T(8,128)(2,1)S(1)}, bf16[16,16,64]{2,1,0:T(8,128)(2,1)S(1)}, u32[]{:S(2)}, u32[]{:S(2)}) collective-permute-start(bf16[16,16,64]{2,1,0:T(8,128)(2,1)S(1)} %fusion.2), channel_id=1, source_target_pairs={{0,16},{4,20},{8,24},{12,28},{16,0},{20,4},{24,8},{28,12},{1,17},{... | collective-permute-start | bytes 98312 | tf_op jit(solution)/shard_map/ppermute | solution.py:486
  98.8 6.3 %collective-permute-start.12 = (bf16[16,16,64]{2,1,0:T(8,128)(2,1)S(1)}, bf16[16,16,64]{2,1,0:T(8,128)(2,1)S(1)}, u32[]{:S(2)}, u32[]{:S(2)}) collective-permute-start(bf16[16,16,64]{2,1,0:T(8,128)(2,1)S(1)} %fusion.2), channel_id=1, source_target_pairs={{0,8},{4,12},{8,0},{12,4},{16,24},{20,28},{24,16},{28,20},{1,9},{5... | collective-permute-start | bytes 98312 | tf_op jit(solution)/shard_map/ppermute | solution.py:486
  100.2 11.8 %all-to-all-start.1 = ((bf16[8,8,512]{2,1,0:T(8,128)(2,1)}), bf16[8,8,512]{2,1,0:T(8,128)(2,1)S(1)}, u32[]{:S(2)}, u32[]{:S(2)}) async-start(bf16[8,8,512]{2,1,0:T(8,128)(2,1)} %pad_maximum_fusion), calls=%async_computation.1 | async-start | bytes 131072 | tf_op jit(solution)/shard_map/all_to_all | solution.py:660
  105.2 6.8 %collective-permute-start.16 = (bf16[16,16,64]{2,1,0:T(8,128)(2,1)S(1)}, bf16[16,16,64]{2,1,0:T(8,128)(2,1)S(1)}, u32[]{:S(2)}, u32[]{:S(2)}) collective-permute-start(bf16[16,16,64]{2,1,0:T(8,128)(2,1)S(1)} %convert_element_type.69), channel_id=1, source_target_pairs={{0,4},{4,0},{8,12},{12,8},{16,20},{20,16},{24,28},{28,24},{1,5},{5... | collective-permute-start | bytes 98312 | tf_op jit(solution)/shard_map/ppermute | solution.py:486
